TPU v7x, 32 devices: a whole 2x2x4 slice. The times are simulated.
32 devices in a mesh: mode: 8 (over z, y), rep: 4 (over x, core).
Axes of the slice: x: 2, y: 2, z: 4, core: 2. Of those that a mesh axis runs over, the one named last changes fastest.
Arguments:
- first_cores: float32 [2, 8, 128, 64], P(None, 'rep', 'mode'), may hold values from -6 to 6
- mid_cores: float32 [2, 8, 3, 128, 4096], P(None, 'rep', None, 'mode'), may hold values from -2 to 2
- last_cores: float32 [2, 8, 128, 64], P(None, 'rep', 'mode'), may hold values from -0.75 to 0.75
- sketch_mid: float32 [3, 128, 4096], P(None, 'mode'), may hold values from -0.0625 to 0.0625
- sketch_last: float32 [128, 64], P('mode'), may hold values from -0.5 to 0.5
- ranks: int32 [4], replicated, may hold values from 32 to 64, as said below
Outputs:
- rounded_first: float32 [2, 128, 64], P(None, 'mode')
- rounded_mid: float32 [2, 3, 128, 4096], P(None, None, 'mode')
- rounded_last: float32 [2, 128, 64], P(None, 'mode')
Inputs may be any that keep to these rules, and one draw needn't show every extreme that they name: `ranks`: some bond has rank 64.
All inputs are finite; a program needn't handle non-finite values.
Results may differ from a plain program's by a relative error of at most 0.00019.
Values sent between devices are 32-bit elements; how exact they have to be, the bound alone decides.
No kernel may reach another device: no remote copies, remote signals or barrier semaphores. Data moves between devices by JAX's collectives and lax.ppermute only.
A program may use at most 64 MiB of HBM per device.

v0:
```python
import functools

import jax
import jax.numpy as jnp
from jax import lax
from jax.experimental import pallas as pl
from jax.experimental.pallas import tpu as pltpu
from jax.sharding import PartitionSpec as P

PRECISE = lax.Precision.HIGHEST
FAST = lax.Precision.HIGH


def lower_inverse(gram_matrix):
    factor = jnp.linalg.cholesky(gram_matrix)
    identity = jnp.eye(gram_matrix.shape[-1], dtype=gram_matrix.dtype)
    return jax.scipy.linalg.solve_triangular(factor, identity, lower=True)


def flip(value, axis, bits):
    size = lax.axis_size(axis)
    return lax.ppermute(value, axis, [(index, index ^ bits) for index in range(size)])


def radices(size):
    stride, out = 1, []
    if (size.bit_length() - 1) % 2:
        out.append((2, stride))
        stride *= 2
    while stride < size:
        out.append((4, stride))
        stride *= 4
    return out


def total(value, axis, size=None):
    for radix, stride in radices(size or lax.axis_size(axis)):
        parts = [flip(value, axis, step * stride) for step in range(1, radix)]
        value = sum(parts, value)
    return value


def gathered(value, axis, dim):
    for radix, stride in radices(lax.axis_size(axis)):
        parts = [flip(value, axis, step * stride) for step in range(1, radix)]
        value = jnp.concatenate([value] + parts, axis=dim)
    return value


def general(first_cores, mid_cores, last_cores, sketch_mid, sketch_last, ranks):
    members, _, slices, rank_size = first_cores.shape
    middle = mid_cores.shape[2]
    total_slices = slices * lax.axis_size("mode")
    low = lax.axis_size("rep") // members
    member = lax.axis_index("rep") // low
    masks = (jnp.arange(rank_size, dtype=jnp.int32)[None, :] < ranks[:, None]).astype(jnp.float32)

    def own_and_other(value):
        kept = lax.dynamic_index_in_dim(value, member, 0, keepdims=False)
        sent = lax.dynamic_index_in_dim(value, 1 - member, 0, keepdims=False)
        return jnp.concatenate([kept, flip(sent, "rep", low)], axis=0)

    def both_members(value):
        other = flip(value, "rep", low)
        return jnp.stack(
            [jnp.where(member == 0, value, other), jnp.where(member == 0, other, value)]
        )

    last = own_and_other(last_cores)
    first = own_and_other(first_cores)
    cores = [None] * middle
    for position in range(middle - 1, -1, -1):
        cores[position] = own_and_other(
            mid_cores[:, :, position].reshape(members, -1, slices, rank_size, rank_size)
        )
    sketch_cores = sketch_mid.reshape(middle, slices, rank_size, rank_size)
    sketches = [None] * (middle + 1)
    mixed = [None] * middle
    sketches[middle] = (
        total(jnp.einsum("sic,ie->sce", last, sketch_last, precision=FAST), "mode") * masks[middle]
    )
    for position in range(middle - 1, -1, -1):
        mixed[position] = jnp.einsum(
            "sicd,sde->sice", cores[position], sketches[position + 1], precision=FAST
        )
        folded = jnp.einsum(
            "sice,ife->scf", mixed[position], sketch_cores[position], precision=FAST
        )
        sketches[position] = total(folded, "mode") * masks[position]

    everything = gathered(first, "mode", 1)
    mixture = total(
        jnp.einsum("sid,sde->ie", everything, sketches[0], precision=PRECISE), "rep", low
    )
    gram = jnp.einsum("ie,if->ef", mixture, mixture, precision=PRECISE)
    raw = jnp.einsum("ie,sid->sed", mixture, everything, precision=PRECISE)
    inverse = lower_inverse(gram / total_slices + jnp.diag(1.0 - masks[0]))
    carried = jnp.einsum("fe,sed->sfd", inverse, raw, precision=PRECISE) / total_slices
    basis = jnp.einsum("ie,fe->if", mixture[:slices], inverse, precision=PRECISE)
    rounded_first = both_members(basis)

    rows = total_slices * rank_size
    blocks = []
    for position in range(middle):
        mixture = total(
            jnp.einsum("sac,sice->iae", carried, mixed[position], precision=FAST), "rep", low
        )
        gram = jnp.einsum("iae,iaf->ef", mixture, mixture, precision=PRECISE)
        spread = jnp.einsum("sac,iae->sice", carried, mixture, precision=FAST)
        raw = jnp.einsum("sice,sicd->sed", spread, cores[position], precision=FAST)
        both = total(jnp.concatenate([raw, gram[None]], axis=0), "mode")
        raw, gram = both[:-1], both[-1]
        inverse = lower_inverse(gram / rows + jnp.diag(1.0 - masks[position + 1]))
        carried = jnp.einsum("fe,sed->sfd", inverse, raw, precision=PRECISE) / rows
        basis = jnp.einsum("iae,fe->iaf", mixture, inverse, precision=FAST)
        blocks.append(both_members(basis.reshape(slices, rank_size * rank_size)))
    rounded_mid = jnp.stack(blocks, axis=1)
    local_last = jnp.einsum("sac,sic->ia", carried, last, precision=PRECISE)
    rounded_last = both_members(total(local_last, "rep", low))
    return (rounded_first, rounded_mid, rounded_last)


LANES = 128
SUBLANES = 8
HALF = 64
NN = (((1,), (0,)), ((), ()))
NT = (((1,), (1,)), ((), ()))
TN = (((0,), (0,)), ((), ()))


def left_half(rows):
    return lax.broadcasted_iota(jnp.int32, (rows, LANES), 1) < HALF


def swap(value):
    return pltpu.roll(value, HALF, 1)


def pick(left, right):
    return jnp.where(left_half(left.shape[0]), left, right)


def split(value):
    high = value.astype(jnp.bfloat16)
    return high, (value - high.astype(jnp.float32)).astype(jnp.bfloat16)


def dot(left, right, dims=NN):
    return lax.dot_general(left, right, dims, preferred_element_type=jnp.float32)


def dot3(left, right, dims=NN):
    (lh, ll), (rh, rl) = left, right
    return dot(lh, rh, dims) + dot(lh, rl, dims) + dot(ll, rh, dims)


def exact(left, right, dims=NN):
    return lax.dot_general(
        left, right, dims, precision=PRECISE, preferred_element_type=jnp.float32
    )


def block_diagonal(value):
    zero = jnp.zeros_like(value)
    return jnp.concatenate([pick(value, zero), pick(zero, swap(value))], axis=0)


def spread_rows(packed, scratch):
    count = packed.shape[0]
    scratch[pl.ds(0, count, stride=2), :] = packed
    scratch[pl.ds(1, count, stride=2), :] = swap(packed)
    return scratch[pl.ds(0, 2 * count), :]


def start_kernel(member, last, first, sketch, keep, send, scratch):
    count = last.shape[1]
    for out, index in ((keep, member[0]), (send, 1 - member[0])):
        cores, heads = last[index], first[index]
        for s in range(count):
            scratch[pl.ds(s * HALF, HALF), pl.ds(0, HALF)] = exact(cores[s], sketch[...], TN)
        rows = count * 32
        even = scratch[pl.ds(0, rows, stride=2), :]
        odd = scratch[pl.ds(1, rows, stride=2), :]
        out[pl.ds(0, rows), :] = pick(even, swap(odd))
        slices = heads.shape[1]
        out[pl.ds(rows, slices), :] = jnp.concatenate([heads[0], heads[1]], axis=1)
        if out.shape[0] > rows + slices:
            out[pl.ds(rows + slices, slices), :] = jnp.concatenate([cores[0], cores[1]], axis=1)


def merge_kernel(n_parts, rows, slices, *refs):
    keeps, sends, out = refs[:n_parts], refs[n_parts : 2 * n_parts], refs[-1]
    for pair, parts in enumerate((keeps, sends)):
        out[pl.ds(pair * rows, rows), :] = added([part.at[pl.ds(0, rows)] for part in parts])
        for at, part in enumerate(parts):
            out[pl.ds(2 * rows + (pair * n_parts + at) * slices, slices), :] = part[
                pl.ds(rows, slices), :
            ]


def heads_of(parts, pair):
    rows = (parts[0].shape[0] - LANES) // 2
    return jnp.concatenate(
        [part[pl.ds(LANES + pair * rows, rows), :] for part in parts], axis=0
    )


def added(parts):
    value = parts[0][...]
    for part in parts[1:]:
        value = value + part[...]
    return value


def sketch_kernel(n_parts, *refs):
    parts, refs = refs[:n_parts], refs[n_parts:]
    mask, kept, other, sketch, out, high, low, wide, product, narrow = refs
    count = kept.shape[0]
    rows = kept.shape[1]
    tiles = rows // 256
    value = added([part.at[pl.ds(0, LANES)] for part in parts])
    natural = spread_rows(value * mask[...], wide)
    for half, cores in enumerate((kept, other)):
        for index in range(count):
            s = half * count + index
            weight = split(block_diagonal(natural[s * HALF : (s + 1) * HALF]))
            result = dot3(split(cores[index]), weight)
            for tile in range(tiles):
                product[pl.ds((tile * 2 * count + s) * 256, 256), :] = result[
                    tile * 256 : (tile + 1) * 256
                ]
    height = 2 * count * 32
    total_value = jnp.zeros(out.shape, jnp.float32)
    for tile in range(tiles):
        for sub in range(SUBLANES):
            i = tile * SUBLANES + sub
            packed = sketch[pl.ds(tile * 256 + sub, 32, stride=SUBLANES), :]
            weight = split(block_diagonal(spread_rows(packed, narrow.at[i])))
            own = split(product[pl.ds(tile * height * SUBLANES + sub, height, stride=SUBLANES), :])
            high[i] = own[0]
            low[i] = own[1]
            total_value = total_value + dot3(own, weight, NT)
    out[...] = total_value


def first_kernel(n_parts, *refs):
    parts, refs = refs[:n_parts], refs[n_parts:]
    heads, (mask, out, wide) = refs[:n_parts], refs[n_parts:]
    natural = spread_rows(added(parts) * mask[...], wide)
    natural = pick(natural, jnp.zeros_like(natural))
    value = exact(heads_of(heads, 0), natural[:LANES])
    out[...] = value + exact(heads_of(heads, 1), natural[LANES:])


def eliminate(gram, mask, row_count):
    size = gram.shape[0]
    row = lax.broadcasted_iota(jnp.int32, (size, LANES), 0)
    lane = lax.broadcasted_iota(jnp.int32, (size, LANES), 1)
    scaled = gram * (1.0 / row_count)
    diagonal = jnp.where(lane == row, 1.0 - mask, 0.0)
    work = jnp.where(lane < HALF, scaled + diagonal, jnp.where(lane - HALF == row, 1.0, 0.0))
    step = 4
    done = []
    for base in range(0, size, step):
        start = base - base % SUBLANES
        if base % SUBLANES == 0 and base:
            work = work[SUBLANES:]
        live = size - start
        offset = base - start
        columns = [
            jnp.broadcast_to(work[:, base + k : base + k + 1], (live, LANES)) for k in range(step)
        ]
        factors, pivots = [], []
        for k in range(step):
            at = offset + k
            column, pivot = columns[k], work[at : at + 1]
            for m in range(k):
                weight = factors[m][at : at + 1]
                column = column - factors[m] * weight
                pivot = pivot - pivots[m] * weight
            scale = lax.rsqrt(column[at : at + 1])
            factors.append(column * scale)
            pivots.append(pivot * scale)
        update = work
        for k in range(step):
            update = update - factors[k] * pivots[k]
        place = lax.broadcasted_iota(jnp.int32, (live, LANES), 0)
        work = jnp.where(place >= offset + step, update, work)
        for k in range(step):
            work = jnp.where(place == offset + k, pivots[k], work)
        if offset + step == SUBLANES:
            done.append(work[:SUBLANES])
    return jnp.concatenate(done, axis=0)


def project(raw, gram, mask, row_count, square):
    solved = eliminate(gram, mask, row_count)
    square[pl.ds(0, HALF), :] = solved
    planar = jnp.concatenate(
        [square[pl.ds(0, HALF // 2, stride=2), :], square[pl.ds(1, HALF // 2, stride=2), :]], axis=0
    )
    carried = exact(raw, block_diagonal(swap(planar)), NT) * (1.0 / row_count)
    square[...] = carried
    pairs = carried.shape[0] // HALF
    even = square[pl.ds(0, pairs * 32, stride=2), :]
    odd = square[pl.ds(1, pairs * 32, stride=2), :]
    first, second = pick(even, swap(odd)), pick(swap(even), odd)
    blocks = []
    for pair in range(pairs):
        blocks += [first[pair * 32 : (pair + 1) * 32], second[pair * 32 : (pair + 1) * 32]]
    return swap(solved), jnp.concatenate(blocks, axis=0)


def mix(carried, high, low, out):
    weight = split(carried.T)
    for i in range(high.shape[0]):
        tile, sub = i // SUBLANES, i % SUBLANES
        value = dot3(weight, (high[i], low[i]))
        straight = pick(value[0:32], value[96:128])
        crossed = pick(value[32:64], value[64:96])
        out[pl.ds(tile * 256 + sub, 32, stride=SUBLANES), :] = straight + swap(crossed)


def unpack_gram(packed):
    return jnp.concatenate([packed, swap(packed)], axis=0)


def bond_one_kernel(row_count, n_parts, kept, other, *refs):
    heads, (mask, high, low, *refs) = refs[:n_parts], refs[n_parts:]
    inverse, carried, basis, out, square = refs
    mixture = kept[...] + other[...]
    gram = exact(mixture, mixture, TN)[:HALF]
    raw = []
    for pair in range(2):
        value = exact(heads_of(heads, pair), mixture, TN)
        raw.append(pick(value[:HALF], swap(value[HALF:])))
    solved, moved = project(jnp.concatenate(raw, axis=0), gram, mask[...], row_count, square)
    inverse[...] = solved
    carried[...] = moved
    slices = basis.shape[0]
    full = jnp.concatenate([pick(solved, jnp.zeros_like(solved)), jnp.zeros_like(solved)], axis=0)
    basis[...] = exact(mixture[:slices], full, NT)
    mix(moved, high, low, out)


def bond_kernel(row_count, n_parts, *refs):
    parts, refs = refs[:n_parts], refs[n_parts:]
    mask, high, low, inverse, carried, out, square = refs
    value = added(parts)
    solved, moved = project(
        value[:LANES], unpack_gram(value[LANES:]), mask[...], row_count, square
    )
    inverse[...] = solved
    carried[...] = moved
    mix(moved, high, low, out)


def last_kernel(row_count, n_parts, *refs):
    parts, refs = refs[:n_parts], refs[n_parts:]
    mask, member, kept, traded, basis, out = refs
    value = added(parts)
    solved = swap(eliminate(unpack_gram(value[LANES:]), mask[...], row_count))
    carried = exact(value[:LANES], block_diagonal(solved), NT) * (1.0 / row_count)
    cores = kept[member[0]]
    slices = cores.shape[1]
    own = jnp.concatenate([cores[0], cores[1]], axis=1)
    term = None
    for pair, both in enumerate((own, traded[...])):
        side = carried[pair * HALF : (pair + 1) * HALF]
        zero = jnp.zeros_like(side)
        both = exact(both, jnp.concatenate([pick(side, zero), pick(swap(side), zero)], axis=0))
        term = both if term is None else term + both
    out[pl.ds(0, slices), :] = pick(term, swap(basis[...]))
    out[pl.ds(slices, HALF), :] = solved


def place_kernel(position, member, mine, theirs, *refs):
    out, sems = refs[-2:]
    here = member[0]
    copies = [
        pltpu.make_async_copy(mine, out.at[here, position], sems.at[0]),
        pltpu.make_async_copy(theirs, out.at[1 - here, position], sems.at[1]),
    ]
    for copy in copies:
        copy.start()
    for copy in copies:
        copy.wait()


def final_kernel(position, member, mine, near, far, across, mixture, away, before, *refs):
    first, last, out, blocks, sems = refs
    here = member[0]
    slices = first.shape[1]
    copies = []
    for at, (place, value, terms) in enumerate(
        ((here, mixture, (mine, near)), (1 - here, away, (far, across)))
    ):
        weight = split(block_diagonal(terms[0][pl.ds(slices, HALF), :]))
        blocks[at] = dot3(split(value[...]), weight, NT)
        copy = pltpu.make_async_copy(blocks.at[at], out.at[place, position], sems.at[at])
        copy.start()
        copies.append(copy)
        head = terms[0][pl.ds(0, slices), :]
        first[place] = swap(head)[:, :HALF]
        last[place] = (head + terms[1][pl.ds(0, slices), :])[:, :HALF]
    for copy in copies:
        copy.wait()


def gram_kernel(mine, theirs, carried, kept, other, mixture, out, spread):
    count, rows = kept.shape[0], kept.shape[1]
    tiles = rows // 256
    mixture[...] = mine[...] + theirs[...]
    everything = mixture[...]
    gram = exact(everything, everything, TN)
    weight = split(carried[...])
    height = 2 * count * 32
    for tile in range(tiles):
        for sub in range(SUBLANES):
            packed = mixture[pl.ds(tile * 256 + sub, 32, stride=SUBLANES), :]
            crossed = swap(packed)
            zero = jnp.zeros_like(packed)
            blocks = jnp.concatenate(
                [pick(packed, zero), pick(crossed, zero), pick(zero, crossed), pick(zero, packed)],
                axis=0,
            )
            spread[pl.ds(tile * height * SUBLANES + sub, height, stride=SUBLANES), :] = dot3(
                weight, split(blocks)
            )
    raw = []
    for half, cores in enumerate((kept, other)):
        for index in range(count):
            s = half * count + index
            own = jnp.concatenate(
                [spread[pl.ds((tile * 2 * count + s) * 256, 256), :] for tile in range(tiles)],
                axis=0,
            )
            raw.append(dot3(split(cores[index]), split(own), TN))
    for pair in range(count):
        even, odd = raw[2 * pair], raw[2 * pair + 1]
        out[pl.ds(pair * HALF, HALF), :] = pick(even[:HALF], odd[HALF:]) + swap(
            pick(odd[:HALF], even[HALF:])
        )
    gram = gram[:HALF] + swap(gram[HALF:])
    out[pl.ds(2 * HALF, 32), :] = pick(gram[:32], swap(gram[32:]))


def basis_kernel(mixture, inverse, out):
    weight = split(block_diagonal(inverse[...]))
    out[...] = dot3(split(mixture[...]), weight, NT)


def kernel_call(body, outs, scratch, *operands, aliases=None, in_hbm=()):
    moved = sum(x.size * x.dtype.itemsize for x in (*operands, *outs))
    specs = []
    for at, x in enumerate((*operands, *outs)):
        space = pltpu.VMEM
        if at in in_hbm:
            space = pltpu.HBM
        elif x.dtype == jnp.int32:
            space = pltpu.SMEM
        specs.append(pl.BlockSpec(memory_space=space))
    return pl.pallas_call(
        body,
        out_shape=outs,
        in_specs=specs[: len(operands)],
        out_specs=specs[len(operands) :],
        scratch_shapes=scratch,
        input_output_aliases=aliases or {},
        compiler_params=pltpu.CompilerParams(vmem_limit_bytes=24 << 20),
        cost_estimate=pl.CostEstimate(flops=0, bytes_accessed=moved, transcendentals=0),
    )(*operands)


def shape(*dims, dtype=jnp.float32):
    return jax.ShapeDtypeStruct(dims, dtype)


def scratch(*dims):
    return pltpu.VMEM(dims, jnp.float32)


def in_rows(value):
    lead, (slices, width) = value.shape[:-2], value.shape[-2:]
    value = value.reshape(*lead, slices // SUBLANES, SUBLANES, width // LANES, LANES)
    value = jnp.swapaxes(value, -2, -3)
    return value.reshape(*lead, slices * width // LANES, LANES)


def out_of_rows(value, slices):
    lead, (rows, _) = value.shape[:-2], value.shape[-2:]
    value = value.reshape(*lead, slices // SUBLANES, rows // slices, SUBLANES, LANES)
    value = jnp.swapaxes(value, -2, -3)
    return value.reshape(*lead, slices, rows // slices * LANES)


def spread(value, axis, step):
    radix, stride = step
    return [value] + [flip(value, axis, other * stride) for other in range(1, radix)]


def exchanged(value, axis):
    steps = radices(lax.axis_size(axis))
    for at, (radix, stride) in enumerate(steps):
        parts = spread(value, axis, (radix, stride))
        if at < len(steps) - 1:
            value = sum(parts[1:], parts[0])
    return parts


def tiled(first_cores, mid_cores, last_cores, sketch_mid, sketch_last, ranks):
    members, count, slices, rank_size = first_cores.shape
    middle = mid_cores.shape[2]
    width = mid_cores.shape[4]
    total_slices = slices * lax.axis_size("mode")
    low = lax.axis_size("rep") // members
    member = lax.axis_index("rep") // low
    here = member[None].astype(jnp.int32)
    masks = (jnp.arange(rank_size, dtype=jnp.int32)[None, :] < ranks[:, None]).astype(jnp.float32)
    masks = jnp.concatenate([masks, masks], axis=1)[:, None, :]
    height = 2 * count * 32
    rows = slices * 32
    inner, outer = radices(lax.axis_size("mode"))

    def half_of(position, index):
        part = lax.dynamic_slice(
            mid_cores, (index, 0, position, 0, 0), (1, count, 1, slices, width)
        )
        return in_rows(part.reshape(count, slices, width))

    keep, send = kernel_call(
        start_kernel,
        [shape(count * 32 + slices, LANES), shape(count * 32 + 2 * slices, LANES)],
        [scratch(2 * height, LANES)],
        here,
        last_cores,
        first_cores,
        sketch_last,
    )
    keeps, sends = [keep], []
    sends.append(flip(send, "rep", low))
    for step in range(1, inner[0]):
        bits = step * inner[1]
        keeps.append(flip(keep, "mode", bits))
        pairs = [
            ((m * 2 * low + r), ((m ^ bits) * 2 * low + (r ^ low)))
            for m in range(lax.axis_size("mode"))
            for r in range(2 * low)
        ]
        sends.append(lax.ppermute(send, ("mode", "rep"), pairs))
    traded = sends[0][count * 32 + slices :]
    (part,) = kernel_call(
        functools.partial(merge_kernel, len(keeps), count * 32, slices),
        [shape(height + 2 * len(keeps) * slices, LANES)],
        [],
        *keeps,
        *sends,
    )
    cores = [None] * middle
    for position in range(middle - 1, -1, -1):
        sent = half_of(position, 1 - member)
        cores[position] = (
            half_of(position, member),
            flip(sent, "rep", low),
        )
    sketch_rows = in_rows(sketch_mid)
    mixed = [None] * middle
    heads = None
    for position in range(middle - 1, -1, -1):
        parts = exchanged(part, "mode") if heads else spread(part, "mode", outer)
        heads = heads or parts
        wide = shape(slices, height, LANES, dtype=jnp.bfloat16)
        part, *mixed[position] = kernel_call(
            functools.partial(sketch_kernel, len(parts)),
            [shape(height, LANES), wide, wide],
            [
                scratch(2 * height, LANES),
                scratch(height * slices, LANES),
                scratch(slices, HALF, LANES),
            ],
            *parts,
            masks[position + 1],
            *cores[position],
            sketch_rows[position],
        )
    parts = exchanged(part, "mode")
    (part,) = kernel_call(
        functools.partial(first_kernel, len(parts)),
        [shape(total_slices, LANES)],
        [scratch(2 * height, LANES)],
        *parts,
        *heads,
        masks[0],
    )
    square = scratch(count * HALF, LANES)
    near = flip(part, "rep", 1)
    inverse, carried, basis, part = kernel_call(
        functools.partial(bond_one_kernel, float(total_slices), len(heads)),
        [shape(HALF, LANES), shape(height, LANES), shape(slices, LANES), shape(rows, LANES)],
        [square],
        part,
        near,
        *heads,
        masks[0],
        *mixed[0],
    )
    row_count = float(total_slices * rank_size)
    whole = shape(members, middle, rows, LANES)
    blocks = ()
    for position in range(middle):
        near = flip(part, "rep", 1)
        mixture, part = kernel_call(
            gram_kernel,
            [shape(rows, LANES), shape(2 * HALF + 32, LANES)],
            [scratch(height * slices, LANES)],
            part,
            near,
            carried,
            *cores[position],
        )
        parts = exchanged(part, "mode")
        mask = masks[position + 1]
        if position < middle - 1:
            inverse, carried, part = kernel_call(
                functools.partial(bond_kernel, row_count, len(parts)),
                [shape(HALF, LANES), shape(height, LANES), shape(rows, LANES)],
                [square],
                *parts,
                mask,
                *mixed[position + 1],
            )
            (own,) = kernel_call(basis_kernel, [shape(rows, LANES)], [], mixture, inverse)
            other = flip(own, "rep", low)
            blocks = kernel_call(
                functools.partial(place_kernel, position),
                [whole],
                [pltpu.SemaphoreType.DMA((2,))],
                here,
                own,
                other,
                *blocks,
                aliases={3: 0} if blocks else None,
                in_hbm=(3, 4),
            )
    away = flip(mixture, "rep", low)
    (last,) = kernel_call(
        functools.partial(last_kernel, row_count, len(parts)),
        [shape(slices + HALF, LANES)],
        [],
        *parts,
        mask,
        here,
        last_cores,
        traded,
        basis,
    )
    near, far, across = (flip(last, "rep", bits) for bits in (1, low, low + 1))
    rounded_first, rounded_last, blocks = kernel_call(
        functools.partial(final_kernel, middle - 1),
        [shape(members, slices, rank_size), shape(members, slices, rank_size), whole],
        [pltpu.VMEM((2, rows, LANES), jnp.float32), pltpu.SemaphoreType.DMA((2,))],
        here,
        last,
        near,
        far,
        across,
        mixture,
        away,
        *blocks,
        aliases={7: 2},
        in_hbm=(7, 10),
    )
    return (rounded_first, out_of_rows(blocks, slices), rounded_last)


def per_device(*arguments):
    members, count, slices, rank_size = arguments[0].shape
    steps = radices(lax.axis_size("mode"))
    fits = (
        members == 2
        and count == 2
        and rank_size == HALF
        and slices % SUBLANES == 0
        and slices * lax.axis_size("mode") == LANES
        and lax.axis_size("rep") == 2 * members
        and len(steps) == 2
    )
    return tiled(*arguments) if fits else general(*arguments)


def solution(mesh):
    return jax.shard_map(
        per_device,
        mesh=mesh,
        in_specs=(
            P(None, "rep", "mode", None),
            P(None, "rep", None, "mode", None),
            P(None, "rep", "mode", None),
            P(None, "mode", None),
            P("mode", None),
            P(),
        ),
        out_specs=(P(None, "mode", None), P(None, None, "mode", None), P(None, "mode", None)),
        check_vma=False,
    )
```

profile of v0, /device:TPU:0, one launch (start us, length us, event | category | flops | bytes accessed | tf_op | source)
XLA Modules:
  0.0 156.7 jit_solution(2709376877011336585)
XLA Ops:
  3.2 4.0 %collective-permute-start.2 = (f32[96,128]{1,0:T(8,128)S(1)}, f32[96,128]{1,0:T(8,128)S(1)}, u32[]{:S(2)}, u32[]{:S(2)}) collective-permute-start(f32[96,128]{1,0:T(8,128)S(1)} %get-tuple-element.33), channel_id=1, source_target_pairs={{0,6},{1,7},{2,4},{3,5},{4,2},{5,3},{6,0},{7,1},{8,14},{9,15},{10,... | collective-permute-start | bytes 147464 | tf_op jit(solution)/shard_map/ppermute | solution.py:550
  7.9 2.2 %constant_dynamic-slice_fusion = (f32[1,2,1,16,4096]{4,3,2,1,0:T(8,128)S(1)}, f32[1,2,1,16,4096]{4,3,2,1,0:T(8,128)S(1)}, f32[1,2,1,16,4096]{4,3,2,1,0:T(8,128)S...) fusion(f32[2,2,3,16,4096]{4,3,2,1,0:T(8,128)} %param.7, ...), kind=kLoop, calls=%fused_computation.2 | loop fusion | bytes 6291464 | tf_op jit(solution)/shard_map/dynamic_slice | solution.py:526
  10.1 2.0 %collective-permute-start.11 = (f32[2,512,128]{2,1,0:T(8,128)S(1)}, f32[2,512,128]{2,1,0:T(8,128)S(1)}, u32[]{:S(2)}, u32[]{:S(2)}) collective-permute-start(f32[2,512,128]{2,1,0:T(8,128)S(1)} %bitcast.54), channel_id=1, source_target_pairs={{0,2},{1,3},{2,0},{3,1},{4,6},{5,7},{6,4},{7,5},{8,10},{9,11},{10,... | collective-permute-start | bytes 1572872 | tf_op jit(solution)/shard_map/ppermute | solution.py:22
  12.3 1.9 %collective-permute-start.16 = (f32[2,512,128]{2,1,0:T(8,128)S(1)}, f32[2,512,128]{2,1,0:T(8,128)S(1)}, u32[]{:S(2)}, u32[]{:S(2)}) collective-permute-start(f32[2,512,128]{2,1,0:T(8,128)S(1)} %bitcast.53), channel_id=1, source_target_pairs={{0,2},{1,3},{2,0},{3,1},{4,6},{5,7},{6,4},{7,5},{8,10},{9,11},{10,... | collective-permute-start | bytes 1572872 | tf_op jit(solution)/shard_map/ppermute | solution.py:22
  14.3 3.7 %collective-permute-start.5 = (f32[192,128]{1,0:T(8,128)S(1)}, f32[192,128]{1,0:T(8,128)S(1)}, u32[]{:S(2)}, u32[]{:S(2)}) collective-permute-start(f32[192,128]{1,0:T(8,128)S(1)} %shard_map.86.refs_0_.refs_4_), channel_id=1, source_target_pairs={{0,24},{4,28},{8,16},{12,20},{16,8},{20,12},{24,0},{28,4},{1,25},{... | collective-permute-start | bytes 294920 | tf_op jit(solution)/shard_map/ppermute | solution.py:22
  18.0 3.1 %collective-permute-done.5.refs_3_.refs_7_ = f32[192,128]{1,0:T(8,128)S(1)} collective-permute-done((f32[192,128]{1,0:T(8,128)S(1)}, f32[192,128]{1,0:T(8,128)S(1)}, u32[]{:S(2)}, u32[]{:S(2)}) %collective-permute-start.5) | collective-permute-done | bytes 98336 | tf_op jit(solution)/shard_map/ppermute | solution.py:22
  21.1 3.1 %collective-permute-start.3 = (f32[192,128]{1,0:T(8,128)S(1)}, f32[192,128]{1,0:T(8,128)S(1)}, u32[]{:S(2)}, u32[]{:S(2)}) collective-permute-start(f32[192,128]{1,0:T(8,128)S(1)} %shard_map.86.refs_0_.refs_4_), channel_id=1, source_target_pairs={{0,8},{4,12},{8,0},{12,4},{16,24},{20,28},{24,16},{28,20},{1,9},{5... | collective-permute-start | bytes 294920 | tf_op jit(solution)/shard_map/ppermute | solution.py:22
  24.7 2.1 %collective-permute-done.3.refs_1_.refs_5_ = f32[192,128]{1,0:T(8,128)S(1)} collective-permute-done((f32[192,128]{1,0:T(8,128)S(1)}, f32[192,128]{1,0:T(8,128)S(1)}, u32[]{:S(2)}, u32[]{:S(2)}) %collective-permute-start.3) | collective-permute-done | bytes 98336 | tf_op jit(solution)/shard_map/ppermute | solution.py:22
  26.8 9.4 %collective-permute-done.6.refs_6_.other = f32[2,512,128]{2,1,0:T(8,128)S(1)} collective-permute-done((f32[2,512,128]{2,1,0:T(8,128)S(1)}, f32[2,512,128]{2,1,0:T(8,128)S(1)}, u32[]{:S(2)}, u32[]{:S(2)}) %collective-permute-start.6) | collective-permute-done | bytes 524320 | tf_op jit(solution)/shard_map/ppermute | solution.py:22
  36.2 2.6 %shard_map.87 = (f32[128,128]{1,0:T(8,128)S(1)}, bf16[16,128,128]{2,1,0:T(8,128)(2,1)S(1)}, bf16[16,128,128]{2,1,0:T(8,128)(2,1)S(1)}) custom-call(f32[192,128]{1,0:T(8,128)S(1)} %shard_map.86.refs_0_.refs_4_, f32[192,128]{1,0:T(8,128)S(1)} %collective-permute-done.3.refs_1_.refs_5_, f32[192,128]{1,0:T(8,128)S(1)} %collective-permute-done.4.refs_2_.refs_6_, ...), custom_call_target="tpu_custom_call" | custom-call | bytes 2818560 | tf_op jit(solution)/shard_map/pallas_call | solution.py:463
  38.8 2.0 %collective-permute-start.7 = (f32[128,128]{1,0:T(8,128)S(1)}, f32[128,128]{1,0:T(8,128)S(1)}, u32[]{:S(2)}, u32[]{:S(2)}) collective-permute-start(f32[128,128]{1,0:T(8,128)S(1)} %get-tuple-element.34), channel_id=1, source_target_pairs={{0,4},{4,0},{8,12},{12,8},{16,20},{20,16},{24,28},{28,24},{1,5},{5... | collective-permute-start | bytes 196616 | tf_op jit(solution)/shard_map/ppermute | solution.py:22
  40.8 2.3 %collective-permute-done.7 = f32[128,128]{1,0:T(8,128)S(1)} collective-permute-done((f32[128,128]{1,0:T(8,128)S(1)}, f32[128,128]{1,0:T(8,128)S(1)}, u32[]{:S(2)}, u32[]{:S(2)}) %collective-permute-start.7) | collective-permute-done | bytes 65568 | tf_op jit(solution)/shard_map/ppermute | solution.py:22
  43.1 4.1 %collective-permute-start.10 = (f32[128,128]{1,0:T(8,128)S(1)}, f32[128,128]{1,0:T(8,128)S(1)}, u32[]{:S(2)}, u32[]{:S(2)}) collective-permute-start(f32[128,128]{1,0:T(8,128)S(1)} %add.32.refs_0_), channel_id=1, source_target_pairs={{0,24},{4,28},{8,16},{12,20},{16,8},{20,12},{24,0},{28,4},{1,25},{... | collective-permute-start | bytes 196616 | tf_op jit(solution)/shard_map/ppermute | solution.py:22
  47.8 1.7 %collective-permute-done.10.refs_3_ = f32[128,128]{1,0:T(8,128)S(1)} collective-permute-done((f32[128,128]{1,0:T(8,128)S(1)}, f32[128,128]{1,0:T(8,128)S(1)}, u32[]{:S(2)}, u32[]{:S(2)}) %collective-permute-start.10) | collective-permute-done | bytes 65568 | tf_op jit(solution)/shard_map/ppermute | solution.py:22
  49.5 2.8 %collective-permute-done.9.refs_2_ = f32[128,128]{1,0:T(8,128)S(1)} collective-permute-done((f32[128,128]{1,0:T(8,128)S(1)}, f32[128,128]{1,0:T(8,128)S(1)}, u32[]{:S(2)}, u32[]{:S(2)}) %collective-permute-start.9) | collective-permute-done | bytes 65568 | tf_op jit(solution)/shard_map/ppermute | solution.py:22
  52.3 2.6 %shard_map.88 = (f32[128,128]{1,0:T(8,128)S(1)}, bf16[16,128,128]{2,1,0:T(8,128)(2,1)S(1)}, bf16[16,128,128]{2,1,0:T(8,128)(2,1)S(1)}) custom-call(f32[128,128]{1,0:T(8,128)S(1)} %add.32.refs_0_, f32[128,128]{1,0:T(8,128)S(1)} %collective-permute-done.8.refs_1_, f32[128,128]{1,0:T(8,128)S(1)} %collective-permute-done.9.refs_2_, ...), custom_call_target="tpu_custom_call" | custom-call | bytes 2687488 | tf_op jit(solution)/shard_map/pallas_call | solution.py:463
  54.9 1.6 %collective-permute-start.12 = (f32[128,128]{1,0:T(8,128)S(1)}, f32[128,128]{1,0:T(8,128)S(1)}, u32[]{:S(2)}, u32[]{:S(2)}) collective-permute-start(f32[128,128]{1,0:T(8,128)S(1)} %get-tuple-element.35), channel_id=1, source_target_pairs={{0,4},{4,0},{8,12},{12,8},{16,20},{20,16},{24,28},{28,24},{1,5},{5... | collective-permute-start | bytes 196616 | tf_op jit(solution)/shard_map/ppermute | solution.py:22
  56.5 2.7 %collective-permute-done.12 = f32[128,128]{1,0:T(8,128)S(1)} collective-permute-done((f32[128,128]{1,0:T(8,128)S(1)}, f32[128,128]{1,0:T(8,128)S(1)}, u32[]{:S(2)}, u32[]{:S(2)}) %collective-permute-start.12) | collective-permute-done | bytes 65568 | tf_op jit(solution)/shard_map/ppermute | solution.py:22
  59.3 1.7 %collective-permute-start.15 = (f32[128,128]{1,0:T(8,128)S(1)}, f32[128,128]{1,0:T(8,128)S(1)}, u32[]{:S(2)}, u32[]{:S(2)}) collective-permute-start(f32[128,128]{1,0:T(8,128)S(1)} %add.33.refs_0_), channel_id=1, source_target_pairs={{0,24},{4,28},{8,16},{12,20},{16,8},{20,12},{24,0},{28,4},{1,25},{... | collective-permute-start | bytes 196616 | tf_op jit(solution)/shard_map/ppermute | solution.py:22
  61.4 2.3 %collective-permute-start.13 = (f32[128,128]{1,0:T(8,128)S(1)}, f32[128,128]{1,0:T(8,128)S(1)}, u32[]{:S(2)}, u32[]{:S(2)}) collective-permute-start(f32[128,128]{1,0:T(8,128)S(1)} %add.33.refs_0_), channel_id=1, source_target_pairs={{0,8},{4,12},{8,0},{12,4},{16,24},{20,28},{24,16},{28,20},{1,9},{5... | collective-permute-start | bytes 196616 | tf_op jit(solution)/shard_map/ppermute | solution.py:22
  63.7 1.7 %collective-permute-done.15.refs_3_ = f32[128,128]{1,0:T(8,128)S(1)} collective-permute-done((f32[128,128]{1,0:T(8,128)S(1)}, f32[128,128]{1,0:T(8,128)S(1)}, u32[]{:S(2)}, u32[]{:S(2)}) %collective-permute-start.15) | collective-permute-done | bytes 65568 | tf_op jit(solution)/shard_map/ppermute | solution.py:22
  65.4 1.4 collective-permute-done.14.refs_2_
  66.8 2.6 %shard_map.89 = (f32[128,128]{1,0:T(8,128)S(1)}, bf16[16,128,128]{2,1,0:T(8,128)(2,1)S(1)}, bf16[16,128,128]{2,1,0:T(8,128)(2,1)S(1)}) custom-call(f32[128,128]{1,0:T(8,128)S(1)} %add.33.refs_0_, f32[128,128]{1,0:T(8,128)S(1)} %collective-permute-done.13.refs_1_, f32[128,128]{1,0:T(8,128)S(1)} %collective-permute-done.14.refs_2_, ...), custom_call_target="tpu_custom_call" | custom-call | bytes 2687488 | tf_op jit(solution)/shard_map/pallas_call | solution.py:463
  69.4 1.6 %collective-permute-start.17 = (f32[128,128]{1,0:T(8,128)S(1)}, f32[128,128]{1,0:T(8,128)S(1)}, u32[]{:S(2)}, u32[]{:S(2)}) collective-permute-start(f32[128,128]{1,0:T(8,128)S(1)} %get-tuple-element.36), channel_id=1, source_target_pairs={{0,4},{4,0},{8,12},{12,8},{16,20},{20,16},{24,28},{28,24},{1,5},{5... | collective-permute-start | bytes 196616 | tf_op jit(solution)/shard_map/ppermute | solution.py:22
  71.0 2.7 %collective-permute-done.17 = f32[128,128]{1,0:T(8,128)S(1)} collective-permute-done((f32[128,128]{1,0:T(8,128)S(1)}, f32[128,128]{1,0:T(8,128)S(1)}, u32[]{:S(2)}, u32[]{:S(2)}) %collective-permute-start.17) | collective-permute-done | bytes 65568 | tf_op jit(solution)/shard_map/ppermute | solution.py:22
  73.7 2.5 %collective-permute-start.20 = (f32[128,128]{1,0:T(8,128)S(1)}, f32[128,128]{1,0:T(8,128)S(1)}, u32[]{:S(2)}, u32[]{:S(2)}) collective-permute-start(f32[128,128]{1,0:T(8,128)S(1)} %add.34.refs_0_), channel_id=1, source_target_pairs={{0,24},{4,28},{8,16},{12,20},{16,8},{20,12},{24,0},{28,4},{1,25},{... | collective-permute-start | bytes 196616 | tf_op jit(solution)/shard_map/ppermute | solution.py:22
  76.4 1.7 %collective-permute-start.18 = (f32[128,128]{1,0:T(8,128)S(1)}, f32[128,128]{1,0:T(8,128)S(1)}, u32[]{:S(2)}, u32[]{:S(2)}) collective-permute-start(f32[128,128]{1,0:T(8,128)S(1)} %add.34.refs_0_), channel_id=1, source_target_pairs={{0,8},{4,12},{8,0},{12,4},{16,24},{20,28},{24,16},{28,20},{1,9},{5... | collective-permute-start | bytes 196616 | tf_op jit(solution)/shard_map/ppermute | solution.py:22
  78.2 1.7 %collective-permute-done.20.refs_3_ = f32[128,128]{1,0:T(8,128)S(1)} collective-permute-done((f32[128,128]{1,0:T(8,128)S(1)}, f32[128,128]{1,0:T(8,128)S(1)}, u32[]{:S(2)}, u32[]{:S(2)}) %collective-permute-start.20) | collective-permute-done | bytes 65568 | tf_op jit(solution)/shard_map/ppermute | solution.py:22
  79.9 1.5 collective-permute-done.19.refs_2_
  81.8 1.2 collective-permute-done.21.other
  83.1 3.6 %shard_map.91 = (f32[64,128]{1,0:T(8,128)}, f32[128,128]{1,0:T(8,128)S(1)}, f32[16,128]{1,0:T(8,128)S(1)}, f32[512,128]{1,0:T(8,128)S(1)}) custom-call(f32[128,128]{1,0:T(8,128)S(1)} %shard_map.90.kept, f32[128,128]{1,0:T(8,128)S(1)} %collective-permute-done.21.other, f32[192,128]{1,0:T(8,128)S(1)} %shard_map.86.refs_0_.refs_4_, ...), custom_call_target="tpu_custom_call" | custom-call | bytes 1942016 | tf_op jit(solution)/shard_map/pallas_call | solution.py:463
  86.9 1.4 collective-permute-done.22.theirs
  88.3 1.6 shard_map.92
  89.9 1.6 %collective-permute-start.23 = (f32[160,128]{1,0:T(8,128)S(1)}, f32[160,128]{1,0:T(8,128)S(1)}, u32[]{:S(2)}, u32[]{:S(2)}) collective-permute-start(f32[160,128]{1,0:T(8,128)S(1)} %get-tuple-element.41), channel_id=1, source_target_pairs={{0,4},{4,0},{8,12},{12,8},{16,20},{20,16},{24,28},{28,24},{1,5},{5... | collective-permute-start | bytes 245768 | tf_op jit(solution)/shard_map/ppermute | solution.py:22
  91.4 3.0 %collective-permute-done.23 = f32[160,128]{1,0:T(8,128)S(1)} collective-permute-done((f32[160,128]{1,0:T(8,128)S(1)}, f32[160,128]{1,0:T(8,128)S(1)}, u32[]{:S(2)}, u32[]{:S(2)}) %collective-permute-start.23) | collective-permute-done | bytes 81952 | tf_op jit(solution)/shard_map/ppermute | solution.py:22
  94.4 2.4 %collective-permute-start.26 = (f32[160,128]{1,0:T(8,128)S(1)}, f32[160,128]{1,0:T(8,128)S(1)}, u32[]{:S(2)}, u32[]{:S(2)}) collective-permute-start(f32[160,128]{1,0:T(8,128)S(1)} %add.35.refs_0_), channel_id=1, source_target_pairs={{0,24},{4,28},{8,16},{12,20},{16,8},{20,12},{24,0},{28,4},{1,25},{... | collective-permute-start | bytes 245768 | tf_op jit(solution)/shard_map/ppermute | solution.py:22
  97.0 1.9 %collective-permute-start.24 = (f32[160,128]{1,0:T(8,128)S(1)}, f32[160,128]{1,0:T(8,128)S(1)}, u32[]{:S(2)}, u32[]{:S(2)}) collective-permute-start(f32[160,128]{1,0:T(8,128)S(1)} %add.35.refs_0_), channel_id=1, source_target_pairs={{0,8},{4,12},{8,0},{12,4},{16,24},{20,28},{24,16},{28,20},{1,9},{5... | collective-permute-start | bytes 245768 | tf_op jit(solution)/shard_map/ppermute | solution.py:22
  98.9 2.4 %collective-permute-done.26.refs_3_ = f32[160,128]{1,0:T(8,128)S(1)} collective-permute-done((f32[160,128]{1,0:T(8,128)S(1)}, f32[160,128]{1,0:T(8,128)S(1)}, u32[]{:S(2)}, u32[]{:S(2)}) %collective-permute-start.26) | collective-permute-done | bytes 81952 | tf_op jit(solution)/shard_map/ppermute | solution.py:22
  101.2 3.1 %collective-permute-done.25.refs_2_ = f32[160,128]{1,0:T(8,128)S(1)} collective-permute-done((f32[160,128]{1,0:T(8,128)S(1)}, f32[160,128]{1,0:T(8,128)S(1)}, u32[]{:S(2)}, u32[]{:S(2)}) %collective-permute-start.25) | collective-permute-done | bytes 81952 | tf_op jit(solution)/shard_map/ppermute | solution.py:22
  104.3 3.6 %shard_map.93 = (f32[64,128]{1,0:T(8,128)S(1)}, f32[128,128]{1,0:T(8,128)S(1)}, f32[512,128]{1,0:T(8,128)S(1)}) custom-call(f32[160,128]{1,0:T(8,128)S(1)} %add.35.refs_0_, f32[160,128]{1,0:T(8,128)S(1)} %collective-permute-done.24.refs_1_, f32[160,128]{1,0:T(8,128)S(1)} %collective-permute-done.25.refs_2_, f32[160,128]{1,0:T(8,128)S(1)} %collective-permute-done.26.refs_3_, ...), custom_call_target="tpu_custom_call" | custom-call | bytes 1737216 | tf_op jit(solution)/shard_map/pallas_call | solution.py:463
  107.9 1.5 collective-permute-done.27.theirs
  109.5 1.6 %shard_map.94 = (f32[512,128]{1,0:T(8,128)S(1)}, f32[160,128]{1,0:T(8,128)S(1)}) custom-call(f32[512,128]{1,0:T(8,128)S(1)} %get-tuple-element.44.mine, f32[512,128]{1,0:T(8,128)S(1)} %collective-permute-done.27.theirs, f32[128,128]{1,0:T(8,128)S(1)} %get-tuple-element.45.carried, f32[2,512,128]{2,1,0:T(8,128)S(1)} %bitcast.45, ...), custom_call_target="tpu_custom_call" | custom-call | bytes 1982464 | tf_op jit(solution)/shard_map/pallas_call | solution.py:463
  111.0 1.6 %collective-permute-start.28 = (f32[160,128]{1,0:T(8,128)S(1)}, f32[160,128]{1,0:T(8,128)S(1)}, u32[]{:S(2)}, u32[]{:S(2)}) collective-permute-start(f32[160,128]{1,0:T(8,128)S(1)} %get-tuple-element.46), channel_id=1, source_target_pairs={{0,4},{4,0},{8,12},{12,8},{16,20},{20,16},{24,28},{28,24},{1,5},{5... | collective-permute-start | bytes 245768 | tf_op jit(solution)/shard_map/ppermute | solution.py:22
  112.6 3.0 %collective-permute-done.28 = f32[160,128]{1,0:T(8,128)S(1)} collective-permute-done((f32[160,128]{1,0:T(8,128)S(1)}, f32[160,128]{1,0:T(8,128)S(1)}, u32[]{:S(2)}, u32[]{:S(2)}) %collective-permute-start.28) | collective-permute-done | bytes 81952 | tf_op jit(solution)/shard_map/ppermute | solution.py:22
  115.6 2.4 %collective-permute-start.31 = (f32[160,128]{1,0:T(8,128)S(1)}, f32[160,128]{1,0:T(8,128)S(1)}, u32[]{:S(2)}, u32[]{:S(2)}) collective-permute-start(f32[160,128]{1,0:T(8,128)S(1)} %add.36.refs_0_), channel_id=1, source_target_pairs={{0,24},{4,28},{8,16},{12,20},{16,8},{20,12},{24,0},{28,4},{1,25},{... | collective-permute-start | bytes 245768 | tf_op jit(solution)/shard_map/ppermute | solution.py:22
  118.0 2.1 %collective-permute-start.29 = (f32[160,128]{1,0:T(8,128)S(1)}, f32[160,128]{1,0:T(8,128)S(1)}, u32[]{:S(2)}, u32[]{:S(2)}) collective-permute-start(f32[160,128]{1,0:T(8,128)S(1)} %add.36.refs_0_), channel_id=1, source_target_pairs={{0,8},{4,12},{8,0},{12,4},{16,24},{20,28},{24,16},{28,20},{1,9},{5... | collective-permute-start | bytes 245768 | tf_op jit(solution)/shard_map/ppermute | solution.py:22
  120.1 2.2 %collective-permute-done.31.refs_3_ = f32[160,128]{1,0:T(8,128)S(1)} collective-permute-done((f32[160,128]{1,0:T(8,128)S(1)}, f32[160,128]{1,0:T(8,128)S(1)}, u32[]{:S(2)}, u32[]{:S(2)}) %collective-permute-start.31) | collective-permute-done | bytes 81952 | tf_op jit(solution)/shard_map/ppermute | solution.py:22
  122.3 2.3 %collective-permute-done.30.refs_2_ = f32[160,128]{1,0:T(8,128)S(1)} collective-permute-done((f32[160,128]{1,0:T(8,128)S(1)}, f32[160,128]{1,0:T(8,128)S(1)}, u32[]{:S(2)}, u32[]{:S(2)}) %collective-permute-start.30) | collective-permute-done | bytes 81952 | tf_op jit(solution)/shard_map/ppermute | solution.py:22
  124.6 3.4 %shard_map.95 = (f32[64,128]{1,0:T(8,128)S(1)}, f32[128,128]{1,0:T(8,128)S(1)}, f32[512,128]{1,0:T(8,128)S(1)}) custom-call(f32[160,128]{1,0:T(8,128)S(1)} %add.36.refs_0_, f32[160,128]{1,0:T(8,128)S(1)} %collective-permute-done.29.refs_1_, f32[160,128]{1,0:T(8,128)S(1)} %collective-permute-done.30.refs_2_, f32[160,128]{1,0:T(8,128)S(1)} %collective-permute-done.31.refs_3_, ...), custom_call_target="tpu_custom_call" | custom-call | bytes 1737216 | tf_op jit(solution)/shard_map/pallas_call | solution.py:463
  128.3 1.6 collective-permute-start.42
  129.9 1.6 shard_map.96
  131.5 1.6 %collective-permute-start.33 = (f32[160,128]{1,0:T(8,128)S(1)}, f32[160,128]{1,0:T(8,128)S(1)}, u32[]{:S(2)}, u32[]{:S(2)}) collective-permute-start(f32[160,128]{1,0:T(8,128)S(1)} %get-tuple-element.51), channel_id=1, source_target_pairs={{0,4},{4,0},{8,12},{12,8},{16,20},{20,16},{24,28},{28,24},{1,5},{5... | collective-permute-start | bytes 245768 | tf_op jit(solution)/shard_map/ppermute | solution.py:22
  133.4 1.2 collective-permute-start.41
  134.6 0.9 collective-permute-start.40
  136.1 2.4 %collective-permute-start.36 = (f32[160,128]{1,0:T(8,128)S(1)}, f32[160,128]{1,0:T(8,128)S(1)}, u32[]{:S(2)}, u32[]{:S(2)}) collective-permute-start(f32[160,128]{1,0:T(8,128)S(1)} %add.37.refs_0_), channel_id=1, source_target_pairs={{0,24},{4,28},{8,16},{12,20},{16,8},{20,12},{24,0},{28,4},{1,25},{... | collective-permute-start | bytes 245768 | tf_op jit(solution)/shard_map/ppermute | solution.py:22
  138.5 4.2 %collective-permute-done.36.refs_3_ = f32[160,128]{1,0:T(8,128)S(1)} collective-permute-done((f32[160,128]{1,0:T(8,128)S(1)}, f32[160,128]{1,0:T(8,128)S(1)}, u32[]{:S(2)}, u32[]{:S(2)}) %collective-permute-start.36) | collective-permute-done | bytes 81952 | tf_op jit(solution)/shard_map/ppermute | solution.py:22
  142.7 2.5 %collective-permute-start.34 = (f32[160,128]{1,0:T(8,128)S(1)}, f32[160,128]{1,0:T(8,128)S(1)}, u32[]{:S(2)}, u32[]{:S(2)}) collective-permute-start(f32[160,128]{1,0:T(8,128)S(1)} %add.37.refs_0_), channel_id=1, source_target_pairs={{0,8},{4,12},{8,0},{12,4},{16,24},{20,28},{24,16},{28,20},{1,9},{5... | collective-permute-start | bytes 245768 | tf_op jit(solution)/shard_map/ppermute | solution.py:22
  145.1 0.8 collective-permute-done.35.refs_2_
  145.9 1.6 %collective-permute-done.34.refs_1_ = f32[160,128]{1,0:T(8,128)S(1)} collective-permute-done((f32[160,128]{1,0:T(8,128)S(1)}, f32[160,128]{1,0:T(8,128)S(1)}, u32[]{:S(2)}, u32[]{:S(2)}) %collective-permute-start.34) | collective-permute-done | bytes 81952 | tf_op jit(solution)/shard_map/ppermute | solution.py:22
  147.6 2.8 %shard_map.97.mine = f32[80,128]{1,0:T(8,128)S(1)} custom-call(f32[160,128]{1,0:T(8,128)S(1)} %add.37.refs_0_, f32[160,128]{1,0:T(8,128)S(1)} %collective-permute-done.34.refs_1_, f32[160,128]{1,0:T(8,128)S(1)} %collective-permute-done.35.refs_2_, f32[160,128]{1,0:T(8,128)S(1)} %collective-permute-done.36.refs_3_, f32[1,128]{1,0:T(1,128)S(1)} %get-tuple-element.73.refs_4_, ...), custom_call_target="tpu_custom_call" | custom-call | bytes 401924 | tf_op jit(solution)/shard_map/pallas_call | solution.py:463
  150.4 1.2 collective-permute-start.38
  152.3 0.8 shard_map.100.refs_0_
  153.1 0.8 shard_map.101.before
  154.6 1.9 %shard_map.102 = (f32[2,16,64]{2,1,0:T(8,128)}, f32[2,16,64]{2,1,0:T(8,128)}, f32[2,3,512,128]{3,2,1,0:T(8,128)}) custom-call(s32[1]{0:T(128)} %bitcast.member.refs_5_, f32[80,128]{1,0:T(8,128)S(1)} %shard_map.97.mine, f32[80,128]{1,0:T(8,128)S(1)} %collective-permute-done.37.near, ...), custom_call_target="tpu_custom_call", output_to_operand_aliasing={{2}: (7, {})} | custom-call | bytes 3850244 | tf_op jit(solution)/shard_map/pallas_call | solution.py:463
  (64 shorter events, 9.2 us)
Async XLA Ops:
  0.6 0.8 copy-start
  1.4 0.8 copy-start.2
  2.2 0.7 copy-start.3
  3.2 11.0 %collective-permute-start.2 = (f32[96,128]{1,0:T(8,128)S(1)}, f32[96,128]{1,0:T(8,128)S(1)}, u32[]{:S(2)}, u32[]{:S(2)}) collective-permute-start(f32[96,128]{1,0:T(8,128)S(1)} %get-tuple-element.33), channel_id=1, source_target_pairs={{0,6},{1,7},{2,4},{3,5},{4,2},{5,3},{6,0},{7,1},{8,14},{9,15},{10,... | collective-permute-start | bytes 147464 | tf_op jit(solution)/shard_map/ppermute | solution.py:550
  7.2 7.0 %collective-permute-start.1 = (f32[96,128]{1,0:T(8,128)S(1)}, f32[96,128]{1,0:T(8,128)S(1)}, u32[]{:S(2)}, u32[]{:S(2)}) collective-permute-start(f32[96,128]{1,0:T(8,128)S(1)} %get-tuple-element.33), channel_id=1, source_target_pairs={{0,2},{1,3},{2,0},{3,1},{4,6},{5,7},{6,4},{7,5},{8,10},{9,11},{10,... | collective-permute-start | bytes 147464 | tf_op jit(solution)/shard_map/ppermute | solution.py:22
  7.8 4.6 %collective-permute-start = (f32[80,128]{1,0:T(8,128)S(1)}, f32[80,128]{1,0:T(8,128)S(1)}, u32[]{:S(2)}, u32[]{:S(2)}) collective-permute-start(f32[80,128]{1,0:T(8,128)S(1)} %get-tuple-element.32.refs_0_), channel_id=1, source_target_pairs={{0,4},{4,0},{8,12},{12,8},{16,20},{20,16},{24,28},{28,24},{1,5},{5... | collective-permute-start | bytes 122888 | tf_op jit(solution)/shard_map/ppermute | solution.py:22
  7.9 4.3 %copy-start.4 = (f32[3,16,4096]{2,1,0:T(8,128)S(1)}, f32[3,16,4096]{2,1,0:T(8,128)}, u32[]{:S(2)}) copy-start(f32[3,16,4096]{2,1,0:T(8,128)} %param.9) | copy-start | bytes 2359300
  10.1 2.2 %copy-start.5 = (s32[4]{0:T(128)S(1)}, s32[4]{0:T(128)}, u32[]{:S(2)}) copy-start(s32[4]{0:T(128)} %param.11) | copy-start | bytes 52
  10.1 37.7 %collective-permute-start.11 = (f32[2,512,128]{2,1,0:T(8,128)S(1)}, f32[2,512,128]{2,1,0:T(8,128)S(1)}, u32[]{:S(2)}, u32[]{:S(2)}) collective-permute-start(f32[2,512,128]{2,1,0:T(8,128)S(1)} %bitcast.54), channel_id=1, source_target_pairs={{0,2},{1,3},{2,0},{3,1},{4,6},{5,7},{6,4},{7,5},{8,10},{9,11},{10,... | collective-permute-start | bytes 1572872 | tf_op jit(solution)/shard_map/ppermute | solution.py:22
  12.0 24.1 %collective-permute-start.6 = (f32[2,512,128]{2,1,0:T(8,128)S(1)}, f32[2,512,128]{2,1,0:T(8,128)S(1)}, u32[]{:S(2)}, u32[]{:S(2)}) collective-permute-start(f32[2,512,128]{2,1,0:T(8,128)S(1)} %bitcast.55), channel_id=1, source_target_pairs={{0,2},{1,3},{2,0},{3,1},{4,6},{5,7},{6,4},{7,5},{8,10},{9,11},{10,... | collective-permute-start | bytes 1572872 | tf_op jit(solution)/shard_map/ppermute | solution.py:22
  12.3 51.4 %collective-permute-start.16 = (f32[2,512,128]{2,1,0:T(8,128)S(1)}, f32[2,512,128]{2,1,0:T(8,128)S(1)}, u32[]{:S(2)}, u32[]{:S(2)}) collective-permute-start(f32[2,512,128]{2,1,0:T(8,128)S(1)} %bitcast.53), channel_id=1, source_target_pairs={{0,2},{1,3},{2,0},{3,1},{4,6},{5,7},{6,4},{7,5},{8,10},{9,11},{10,... | collective-permute-start | bytes 1572872 | tf_op jit(solution)/shard_map/ppermute | solution.py:22
  14.3 6.9 %collective-permute-start.5 = (f32[192,128]{1,0:T(8,128)S(1)}, f32[192,128]{1,0:T(8,128)S(1)}, u32[]{:S(2)}, u32[]{:S(2)}) collective-permute-start(f32[192,128]{1,0:T(8,128)S(1)} %shard_map.86.refs_0_.refs_4_), channel_id=1, source_target_pairs={{0,24},{4,28},{8,16},{12,20},{16,8},{20,12},{24,0},{28,4},{1,25},{... | collective-permute-start | bytes 294920 | tf_op jit(solution)/shard_map/ppermute | solution.py:22
  18.0 6.7 %collective-permute-start.4 = (f32[192,128]{1,0:T(8,128)S(1)}, f32[192,128]{1,0:T(8,128)S(1)}, u32[]{:S(2)}, u32[]{:S(2)}) collective-permute-start(f32[192,128]{1,0:T(8,128)S(1)} %shard_map.86.refs_0_.refs_4_), channel_id=1, source_target_pairs={{0,16},{4,20},{8,24},{12,28},{16,0},{20,4},{24,8},{28,12},{1,17},{... | collective-permute-start | bytes 294920 | tf_op jit(solution)/shard_map/ppermute | solution.py:22
  21.1 5.7 %collective-permute-start.3 = (f32[192,128]{1,0:T(8,128)S(1)}, f32[192,128]{1,0:T(8,128)S(1)}, u32[]{:S(2)}, u32[]{:S(2)}) collective-permute-start(f32[192,128]{1,0:T(8,128)S(1)} %shard_map.86.refs_0_.refs_4_), channel_id=1, source_target_pairs={{0,8},{4,12},{8,0},{12,4},{16,24},{20,28},{24,16},{28,20},{1,9},{5... | collective-permute-start | bytes 294920 | tf_op jit(solution)/shard_map/ppermute | solution.py:22
  38.8 4.3 %collective-permute-start.7 = (f32[128,128]{1,0:T(8,128)S(1)}, f32[128,128]{1,0:T(8,128)S(1)}, u32[]{:S(2)}, u32[]{:S(2)}) collective-permute-start(f32[128,128]{1,0:T(8,128)S(1)} %get-tuple-element.34), channel_id=1, source_target_pairs={{0,4},{4,0},{8,12},{12,8},{16,20},{20,16},{24,28},{28,24},{1,5},{5... | collective-permute-start | bytes 196616 | tf_op jit(solution)/shard_map/ppermute | solution.py:22
  43.1 6.4 %collective-permute-start.10 = (f32[128,128]{1,0:T(8,128)S(1)}, f32[128,128]{1,0:T(8,128)S(1)}, u32[]{:S(2)}, u32[]{:S(2)}) collective-permute-start(f32[128,128]{1,0:T(8,128)S(1)} %add.32.refs_0_), channel_id=1, source_target_pairs={{0,24},{4,28},{8,16},{12,20},{16,8},{20,12},{24,0},{28,4},{1,25},{... | collective-permute-start | bytes 196616 | tf_op jit(solution)/shard_map/ppermute | solution.py:22
  47.2 5.2 %collective-permute-start.9 = (f32[128,128]{1,0:T(8,128)S(1)}, f32[128,128]{1,0:T(8,128)S(1)}, u32[]{:S(2)}, u32[]{:S(2)}) collective-permute-start(f32[128,128]{1,0:T(8,128)S(1)} %add.32.refs_0_), channel_id=1, source_target_pairs={{0,16},{4,20},{8,24},{12,28},{16,0},{20,4},{24,8},{28,12},{1,17},{... | collective-permute-start | bytes 196616 | tf_op jit(solution)/shard_map/ppermute | solution.py:22
  47.2 5.2 %collective-permute-start.8 = (f32[128,128]{1,0:T(8,128)S(1)}, f32[128,128]{1,0:T(8,128)S(1)}, u32[]{:S(2)}, u32[]{:S(2)}) collective-permute-start(f32[128,128]{1,0:T(8,128)S(1)} %add.32.refs_0_), channel_id=1, source_target_pairs={{0,8},{4,12},{8,0},{12,4},{16,24},{20,28},{24,16},{28,20},{1,9},{5... | collective-permute-start | bytes 196616 | tf_op jit(solution)/shard_map/ppermute | solution.py:22
  54.9 4.3 %collective-permute-start.12 = (f32[128,128]{1,0:T(8,128)S(1)}, f32[128,128]{1,0:T(8,128)S(1)}, u32[]{:S(2)}, u32[]{:S(2)}) collective-permute-start(f32[128,128]{1,0:T(8,128)S(1)} %get-tuple-element.35), channel_id=1, source_target_pairs={{0,4},{4,0},{8,12},{12,8},{16,20},{20,16},{24,28},{28,24},{1,5},{5... | collective-permute-start | bytes 196616 | tf_op jit(solution)/shard_map/ppermute | solution.py:22
  59.3 6.1 %collective-permute-start.15 = (f32[128,128]{1,0:T(8,128)S(1)}, f32[128,128]{1,0:T(8,128)S(1)}, u32[]{:S(2)}, u32[]{:S(2)}) collective-permute-start(f32[128,128]{1,0:T(8,128)S(1)} %add.33.refs_0_), channel_id=1, source_target_pairs={{0,24},{4,28},{8,16},{12,20},{16,8},{20,12},{24,0},{28,4},{1,25},{... | collective-permute-start | bytes 196616 | tf_op jit(solution)/shard_map/ppermute | solution.py:22
  60.9 5.9 %collective-permute-start.14 = (f32[128,128]{1,0:T(8,128)S(1)}, f32[128,128]{1,0:T(8,128)S(1)}, u32[]{:S(2)}, u32[]{:S(2)}) collective-permute-start(f32[128,128]{1,0:T(8,128)S(1)} %add.33.refs_0_), channel_id=1, source_target_pairs={{0,16},{4,20},{8,24},{12,28},{16,0},{20,4},{24,8},{28,12},{1,17},{... | collective-permute-start | bytes 196616 | tf_op jit(solution)/shard_map/ppermute | solution.py:22
  61.4 5.4 %collective-permute-start.13 = (f32[128,128]{1,0:T(8,128)S(1)}, f32[128,128]{1,0:T(8,128)S(1)}, u32[]{:S(2)}, u32[]{:S(2)}) collective-permute-start(f32[128,128]{1,0:T(8,128)S(1)} %add.33.refs_0_), channel_id=1, source_target_pairs={{0,8},{4,12},{8,0},{12,4},{16,24},{20,28},{24,16},{28,20},{1,9},{5... | collective-permute-start | bytes 196616 | tf_op jit(solution)/shard_map/ppermute | solution.py:22
  69.4 4.3 %collective-permute-start.17 = (f32[128,128]{1,0:T(8,128)S(1)}, f32[128,128]{1,0:T(8,128)S(1)}, u32[]{:S(2)}, u32[]{:S(2)}) collective-permute-start(f32[128,128]{1,0:T(8,128)S(1)} %get-tuple-element.36), channel_id=1, source_target_pairs={{0,4},{4,0},{8,12},{12,8},{16,20},{20,16},{24,28},{28,24},{1,5},{5... | collective-permute-start | bytes 196616 | tf_op jit(solution)/shard_map/ppermute | solution.py:22
  73.7 6.1 %collective-permute-start.20 = (f32[128,128]{1,0:T(8,128)S(1)}, f32[128,128]{1,0:T(8,128)S(1)}, u32[]{:S(2)}, u32[]{:S(2)}) collective-permute-start(f32[128,128]{1,0:T(8,128)S(1)} %add.34.refs_0_), channel_id=1, source_target_pairs={{0,24},{4,28},{8,16},{12,20},{16,8},{20,12},{24,0},{28,4},{1,25},{... | collective-permute-start | bytes 196616 | tf_op jit(solution)/shard_map/ppermute | solution.py:22
  76.2 5.2 %collective-permute-start.19 = (f32[128,128]{1,0:T(8,128)S(1)}, f32[128,128]{1,0:T(8,128)S(1)}, u32[]{:S(2)}, u32[]{:S(2)}) collective-permute-start(f32[128,128]{1,0:T(8,128)S(1)} %add.34.refs_0_), channel_id=1, source_target_pairs={{0,16},{4,20},{8,24},{12,28},{16,0},{20,4},{24,8},{28,12},{1,17},{... | collective-permute-start | bytes 196616 | tf_op jit(solution)/shard_map/ppermute | solution.py:22
  76.4 5.0 %collective-permute-start.18 = (f32[128,128]{1,0:T(8,128)S(1)}, f32[128,128]{1,0:T(8,128)S(1)}, u32[]{:S(2)}, u32[]{:S(2)}) collective-permute-start(f32[128,128]{1,0:T(8,128)S(1)} %add.34.refs_0_), channel_id=1, source_target_pairs={{0,8},{4,12},{8,0},{12,4},{16,24},{20,28},{24,16},{28,20},{1,9},{5... | collective-permute-start | bytes 196616 | tf_op jit(solution)/shard_map/ppermute | solution.py:22
  81.8 1.3 collective-permute-start.21
  86.7 1.6 %collective-permute-start.22 = (f32[512,128]{1,0:T(8,128)S(1)}, f32[512,128]{1,0:T(8,128)S(1)}, u32[]{:S(2)}, u32[]{:S(2)}) collective-permute-start(f32[512,128]{1,0:T(8,128)S(1)} %get-tuple-element.39.mine), channel_id=1, source_target_pairs={{0,1},{1,0},{2,3},{3,2},{4,5},{5,4},{6,7},{7,6},{8,9},{9,8},{10,11... | collective-permute-start | bytes 786440 | tf_op jit(solution)/shard_map/ppermute | solution.py:22
  89.9 4.6 %collective-permute-start.23 = (f32[160,128]{1,0:T(8,128)S(1)}, f32[160,128]{1,0:T(8,128)S(1)}, u32[]{:S(2)}, u32[]{:S(2)}) collective-permute-start(f32[160,128]{1,0:T(8,128)S(1)} %get-tuple-element.41), channel_id=1, source_target_pairs={{0,4},{4,0},{8,12},{12,8},{16,20},{20,16},{24,28},{28,24},{1,5},{5... | collective-permute-start | bytes 245768 | tf_op jit(solution)/shard_map/ppermute | solution.py:22
  94.4 6.8 %collective-permute-start.26 = (f32[160,128]{1,0:T(8,128)S(1)}, f32[160,128]{1,0:T(8,128)S(1)}, u32[]{:S(2)}, u32[]{:S(2)}) collective-permute-start(f32[160,128]{1,0:T(8,128)S(1)} %add.35.refs_0_), channel_id=1, source_target_pairs={{0,24},{4,28},{8,16},{12,20},{16,8},{20,12},{24,0},{28,4},{1,25},{... | collective-permute-start | bytes 245768 | tf_op jit(solution)/shard_map/ppermute | solution.py:22
  96.8 7.5 %collective-permute-start.25 = (f32[160,128]{1,0:T(8,128)S(1)}, f32[160,128]{1,0:T(8,128)S(1)}, u32[]{:S(2)}, u32[]{:S(2)}) collective-permute-start(f32[160,128]{1,0:T(8,128)S(1)} %add.35.refs_0_), channel_id=1, source_target_pairs={{0,16},{4,20},{8,24},{12,28},{16,0},{20,4},{24,8},{28,12},{1,17},{... | collective-permute-start | bytes 245768 | tf_op jit(solution)/shard_map/ppermute | solution.py:22
  97.0 7.3 %collective-permute-start.24 = (f32[160,128]{1,0:T(8,128)S(1)}, f32[160,128]{1,0:T(8,128)S(1)}, u32[]{:S(2)}, u32[]{:S(2)}) collective-permute-start(f32[160,128]{1,0:T(8,128)S(1)} %add.35.refs_0_), channel_id=1, source_target_pairs={{0,8},{4,12},{8,0},{12,4},{16,24},{20,28},{24,16},{28,20},{1,9},{5... | collective-permute-start | bytes 245768 | tf_op jit(solution)/shard_map/ppermute | solution.py:22
  107.9 1.6 collective-permute-start.27
  111.0 4.5 %collective-permute-start.28 = (f32[160,128]{1,0:T(8,128)S(1)}, f32[160,128]{1,0:T(8,128)S(1)}, u32[]{:S(2)}, u32[]{:S(2)}) collective-permute-start(f32[160,128]{1,0:T(8,128)S(1)} %get-tuple-element.46), channel_id=1, source_target_pairs={{0,4},{4,0},{8,12},{12,8},{16,20},{20,16},{24,28},{28,24},{1,5},{5... | collective-permute-start | bytes 245768 | tf_op jit(solution)/shard_map/ppermute | solution.py:22
  115.6 6.7 %collective-permute-start.31 = (f32[160,128]{1,0:T(8,128)S(1)}, f32[160,128]{1,0:T(8,128)S(1)}, u32[]{:S(2)}, u32[]{:S(2)}) collective-permute-start(f32[160,128]{1,0:T(8,128)S(1)} %add.36.refs_0_), channel_id=1, source_target_pairs={{0,24},{4,28},{8,16},{12,20},{16,8},{20,12},{24,0},{28,4},{1,25},{... | collective-permute-start | bytes 245768 | tf_op jit(solution)/shard_map/ppermute | solution.py:22
  118.0 6.6 %collective-permute-start.30 = (f32[160,128]{1,0:T(8,128)S(1)}, f32[160,128]{1,0:T(8,128)S(1)}, u32[]{:S(2)}, u32[]{:S(2)}) collective-permute-start(f32[160,128]{1,0:T(8,128)S(1)} %add.36.refs_0_), channel_id=1, source_target_pairs={{0,16},{4,20},{8,24},{12,28},{16,0},{20,4},{24,8},{28,12},{1,17},{... | collective-permute-start | bytes 245768 | tf_op jit(solution)/shard_map/ppermute | solution.py:22
  118.0 6.6 %collective-permute-start.29 = (f32[160,128]{1,0:T(8,128)S(1)}, f32[160,128]{1,0:T(8,128)S(1)}, u32[]{:S(2)}, u32[]{:S(2)}) collective-permute-start(f32[160,128]{1,0:T(8,128)S(1)} %add.36.refs_0_), channel_id=1, source_target_pairs={{0,8},{4,12},{8,0},{12,4},{16,24},{20,28},{24,16},{28,20},{1,9},{5... | collective-permute-start | bytes 245768 | tf_op jit(solution)/shard_map/ppermute | solution.py:22
  128.0 19.6 %copy-start.1 = (f32[2,2,16,64]{3,2,1,0:T(8,128)S(1)}, f32[2,2,16,64]{3,2,1,0:T(8,128)}, u32[]{:S(2)}) copy-start(f32[2,2,16,64]{3,2,1,0:T(8,128)} %refs_6_.1) | copy-start | bytes 49156
  128.0 1.9 %collective-permute-start.32 = (f32[512,128]{1,0:T(8,128)S(1)}, f32[512,128]{1,0:T(8,128)S(1)}, u32[]{:S(2)}, u32[]{:S(2)}) collective-permute-start(f32[512,128]{1,0:T(8,128)S(1)} %get-tuple-element.49.mine), channel_id=1, source_target_pairs={{0,1},{1,0},{2,3},{3,2},{4,5},{5,4},{6,7},{7,6},{8,9},{9,8},{10,11... | collective-permute-start | bytes 786440 | tf_op jit(solution)/shard_map/ppermute | solution.py:22
  128.3 23.2 %collective-permute-start.42 = (f32[512,128]{1,0:T(8,128)S(1)}, f32[512,128]{1,0:T(8,128)S(1)}, u32[]{:S(2)}, u32[]{:S(2)}) collective-permute-start(f32[512,128]{1,0:T(8,128)S(1)} %shard_map.99.mine), channel_id=1, source_target_pairs={{0,2},{1,3},{2,0},{3,1},{4,6},{5,7},{6,4},{7,5},{8,10},{9,11},{10,... | collective-permute-start | bytes 786440 | tf_op jit(solution)/shard_map/ppermute | solution.py:22
  131.5 4.6 %collective-permute-start.33 = (f32[160,128]{1,0:T(8,128)S(1)}, f32[160,128]{1,0:T(8,128)S(1)}, u32[]{:S(2)}, u32[]{:S(2)}) collective-permute-start(f32[160,128]{1,0:T(8,128)S(1)} %get-tuple-element.51), channel_id=1, source_target_pairs={{0,4},{4,0},{8,12},{12,8},{16,20},{20,16},{24,28},{28,24},{1,5},{5... | collective-permute-start | bytes 245768 | tf_op jit(solution)/shard_map/ppermute | solution.py:22
  133.4 19.7 %collective-permute-start.41 = (f32[512,128]{1,0:T(8,128)S(1)}, f32[512,128]{1,0:T(8,128)S(1)}, u32[]{:S(2)}, u32[]{:S(2)}) collective-permute-start(f32[512,128]{1,0:T(8,128)S(1)} %shard_map.98.mine), channel_id=1, source_target_pairs={{0,2},{1,3},{2,0},{3,1},{4,6},{5,7},{6,4},{7,5},{8,10},{9,11},{10,... | collective-permute-start | bytes 786440 | tf_op jit(solution)/shard_map/ppermute | solution.py:22
  134.6 20.1 %collective-permute-start.40 = (f32[512,128]{1,0:T(8,128)S(1)}, f32[512,128]{1,0:T(8,128)S(1)}, u32[]{:S(2)}, u32[]{:S(2)}) collective-permute-start(f32[512,128]{1,0:T(8,128)S(1)} %get-tuple-element.53.mixture), channel_id=1, source_target_pairs={{0,2},{1,3},{2,0},{3,1},{4,6},{5,7},{6,4},{7,5},{8,10},{9,11},{10,... | collective-permute-start | bytes 786440 | tf_op jit(solution)/shard_map/ppermute | solution.py:22
  136.1 6.5 %collective-permute-start.36 = (f32[160,128]{1,0:T(8,128)S(1)}, f32[160,128]{1,0:T(8,128)S(1)}, u32[]{:S(2)}, u32[]{:S(2)}) collective-permute-start(f32[160,128]{1,0:T(8,128)S(1)} %add.37.refs_0_), channel_id=1, source_target_pairs={{0,24},{4,28},{8,16},{12,20},{16,8},{20,12},{24,0},{28,4},{1,25},{... | collective-permute-start | bytes 245768 | tf_op jit(solution)/shard_map/ppermute | solution.py:22
  138.5 7.4 %collective-permute-start.35 = (f32[160,128]{1,0:T(8,128)S(1)}, f32[160,128]{1,0:T(8,128)S(1)}, u32[]{:S(2)}, u32[]{:S(2)}) collective-permute-start(f32[160,128]{1,0:T(8,128)S(1)} %add.37.refs_0_), channel_id=1, source_target_pairs={{0,16},{4,20},{8,24},{12,28},{16,0},{20,4},{24,8},{28,12},{1,17},{... | collective-permute-start | bytes 245768 | tf_op jit(solution)/shard_map/ppermute | solution.py:22
  142.7 4.9 %collective-permute-start.34 = (f32[160,128]{1,0:T(8,128)S(1)}, f32[160,128]{1,0:T(8,128)S(1)}, u32[]{:S(2)}, u32[]{:S(2)}) collective-permute-start(f32[160,128]{1,0:T(8,128)S(1)} %add.37.refs_0_), channel_id=1, source_target_pairs={{0,8},{4,12},{8,0},{12,4},{16,24},{20,28},{24,16},{28,20},{1,9},{5... | collective-permute-start | bytes 245768 | tf_op jit(solution)/shard_map/ppermute | solution.py:22
  150.4 3.6 %collective-permute-start.39 = (f32[80,128]{1,0:T(8,128)S(1)}, f32[80,128]{1,0:T(8,128)S(1)}, u32[]{:S(2)}, u32[]{:S(2)}) collective-permute-start(f32[80,128]{1,0:T(8,128)S(1)} %shard_map.97.mine), channel_id=1, source_target_pairs={{0,3},{1,2},{2,1},{3,0},{4,7},{5,6},{6,5},{7,4},{8,11},{9,10},{10,... | collective-permute-start | bytes 122888 | tf_op jit(solution)/shard_map/ppermute | solution.py:22
  150.4 4.2 %collective-permute-start.38 = (f32[80,128]{1,0:T(8,128)S(1)}, f32[80,128]{1,0:T(8,128)S(1)}, u32[]{:S(2)}, u32[]{:S(2)}) collective-permute-start(f32[80,128]{1,0:T(8,128)S(1)} %shard_map.97.mine), channel_id=1, source_target_pairs={{0,2},{1,3},{2,0},{3,1},{4,6},{5,7},{6,4},{7,5},{8,10},{9,11},{10,... | collective-permute-start | bytes 122888 | tf_op jit(solution)/shard_map/ppermute | solution.py:22
  151.6 3.1 %collective-permute-start.37 = (f32[80,128]{1,0:T(8,128)S(1)}, f32[80,128]{1,0:T(8,128)S(1)}, u32[]{:S(2)}, u32[]{:S(2)}) collective-permute-start(f32[80,128]{1,0:T(8,128)S(1)} %shard_map.97.mine), channel_id=1, source_target_pairs={{0,1},{1,0},{2,3},{3,2},{4,5},{5,4},{6,7},{7,6},{8,9},{9,8},{10,11... | collective-permute-start | bytes 122888 | tf_op jit(solution)/shard_map/ppermute | solution.py:22
where the time goes:
time: 157 us
  waiting for transfers between devices  61.8 us (39%)
  starting transfers between devices  58.6 us (37%)
  Pallas kernels  30.6 us (19%)
  local copies, waits for them, and re-layouts  4.48 us (3%)
    ppermute x42, waiting for transfers between devices, flip(): lax.ppermute(value, axis, [(index, index ^ bits) for index in range(size)])  61.8 us
    ppermute x42, starting transfers between devices, flip(): lax.ppermute(value, axis, [(index, index ^ bits) for index in range(size)])  54.6 us
    pallas_call x18, Pallas kernels, kernel_call(): pl.pallas_call(body, out_shape=outs, in_specs=specs[:len(operands)], out_...  30.6 us
    ppermute x1, starting transfers between devices, tiled(): sends.append(lax.ppermute(send, ('mode', 'rep'), pairs))  3.99 us
  transfers between devices with their start and end apart: 43, of which 27 were waited for; matrix products, arithmetic and copies ran while one was open for 2% of the time, Pallas kernels for 8%

commit v1 on v0

--- a/solution.py
+++ b/solution.py
@@ -172,7 +172,17 @@
     return scratch[pl.ds(0, 2 * count), :]
 
 
-def start_kernel(member, last, first, sketch, keep, send, scratch):
+def start_kernel(member, *refs):
+    sources, (keep, send), (*local, sems, scratch) = refs[:3], refs[3:5], refs[5:]
+    copies = [
+        pltpu.make_async_copy(source, target, sems.at[at])
+        for at, (source, target) in enumerate(zip(sources, local))
+    ]
+    for copy in copies:
+        copy.start()
+    for copy in copies:
+        copy.wait()
+    last, first, sketch = local
     count = last.shape[1]
     for out, index in ((keep, member[0]), (send, 1 - member[0])):
         cores, heads = last[index], first[index]
@@ -450,7 +460,7 @@
     out[...] = dot3(split(mixture[...]), weight, NT)
 
 
-def kernel_call(body, outs, scratch, *operands, aliases=None, in_hbm=()):
+def kernel_call(body, outs, scratch, *operands, aliases=None, in_hbm=(), limit=24 << 20):
     moved = sum(x.size * x.dtype.itemsize for x in (*operands, *outs))
     specs = []
     for at, x in enumerate((*operands, *outs)):
@@ -467,7 +477,7 @@
         out_specs=specs[len(operands) :],
         scratch_shapes=scratch,
         input_output_aliases=aliases or {},
-        compiler_params=pltpu.CompilerParams(vmem_limit_bytes=24 << 20),
+        compiler_params=pltpu.CompilerParams(vmem_limit_bytes=limit),
         cost_estimate=pl.CostEstimate(flops=0, bytes_accessed=moved, transcendentals=0),
     )(*operands)
 
@@ -522,20 +532,28 @@
     rows = slices * 32
     inner, outer = radices(lax.axis_size("mode"))
 
-    def half_of(position, index):
+    def half_of(source, position, index):
         part = lax.dynamic_slice(
-            mid_cores, (index, 0, position, 0, 0), (1, count, 1, slices, width)
+            source, (index, 0, position, 0, 0), (1, count, 1, slices, width)
         )
         return in_rows(part.reshape(count, slices, width))
 
     keep, send = kernel_call(
         start_kernel,
         [shape(count * 32 + slices, LANES), shape(count * 32 + 2 * slices, LANES)],
-        [scratch(2 * height, LANES)],
+        [
+            scratch(*last_cores.shape),
+            scratch(*first_cores.shape),
+            scratch(*sketch_last.shape),
+            pltpu.SemaphoreType.DMA((3,)),
+            scratch(2 * height, LANES),
+        ],
         here,
         last_cores,
         first_cores,
         sketch_last,
+        in_hbm=(1, 2, 3),
+        limit=None,
     )
     keeps, sends = [keep], []
     sends.append(flip(send, "rep", low))
@@ -557,12 +575,13 @@
         *sends,
     )
     cores = [None] * middle
+    late_cores, part = lax.optimization_barrier((mid_cores, part))
     for position in range(middle - 1, -1, -1):
-        sent = half_of(position, 1 - member)
-        cores[position] = (
-            half_of(position, member),
-            flip(sent, "rep", low),
-        )
+        if position == middle - 1:
+            sent = half_of(mid_cores, position, 1 - member)
+        else:
+            sent = half_of(late_cores, position, 1 - member)
+        cores[position] = (half_of(late_cores, position, member), flip(sent, "rep", low))
     sketch_rows = in_rows(sketch_mid)
     mixed = [None] * middle
     heads = None

time: 157 us -> 148 us (0.943)
  waiting for transfers between devices: 61.8 us -> 56.3 us
  starting transfers between devices: 58.6 us -> 53.4 us
    ppermute x42, waiting for transfers between devices: 61.8 us -> 56.3 us  [flip(): lax.ppermute(value, axis, [(index, index ^ bits) for index in range(size)])]
    ppermute x42, starting transfers between devices: 54.6 us -> 49.4 us  [flip(): lax.ppermute(value, axis, [(index, index ^ bits) for index in range(size)])]
  transfers between devices with their start and end apart: 43 -> 43, of which waited for: 27 -> 27; matrix products, arithmetic and copies ran while one was open for 2% -> 3% of each run, Pallas kernels for 8% -> 8%
where the time goes in v1:
time: 148 us
  waiting for transfers between devices  56.3 us (38%)
  starting transfers between devices  53.4 us (36%)
  Pallas kernels  32.1 us (22%)
  local copies, waits for them, and re-layouts  4.9 us (3%)
    ppermute x42, waiting for transfers between devices, flip(): lax.ppermute(value, axis, [(index, index ^ bits) for index in range(size)])  56.3 us
    ppermute x42, starting transfers between devices, flip(): lax.ppermute(value, axis, [(index, index ^ bits) for index in range(size)])  49.4 us
    pallas_call x18, Pallas kernels, kernel_call(): pl.pallas_call(body, out_shape=outs, in_specs=specs[:len(operands)], out_...  32.1 us
    ppermute x1, starting transfers between devices, tiled(): sends.append(lax.ppermute(send, ('mode', 'rep'), pairs))  3.99 us
  transfers between devices with their start and end apart: 43, of which 27 were waited for; matrix products, arithmetic and copies ran while one was open for 3% of the time, Pallas kernels for 8%

profile of v1, /device:TPU:0, one launch (start us, length us, event | category | flops | bytes accessed | tf_op | source)
XLA Modules:
  0.0 148.0 jit_solution(11007062615164552930)
XLA Ops:
  0.6 1.8 %shard_map.85 = (f32[80,128]{1,0:T(8,128)}, f32[96,128]{1,0:T(8,128)}) custom-call(s32[1]{0:T(128)} %bitcast.member.refs_5_, f32[2,2,16,64]{3,2,1,0:T(8,128)} %refs_6_.1, f32[2,2,16,64]{3,2,1,0:T(8,128)} %refs_1_.1, f32[16,64]{1,0:T(8,128)} %refs_2_.1), custom_call_target="tpu_custom_call" | custom-call | bytes 126980 | tf_op jit(solution)/shard_map/pallas_call | solution.py:473
  2.5 4.0 %collective-permute-start.2 = (f32[96,128]{1,0:T(8,128)}, f32[96,128]{1,0:T(8,128)S(1)}, u32[]{:S(2)}, u32[]{:S(2)}) collective-permute-start(f32[96,128]{1,0:T(8,128)} %get-tuple-element.35), channel_id=1, source_target_pairs={{0,6},{1,7},{2,4},{3,5},{4,2},{5,3},{6,0},{7,1},{8,14},{9,15},{10,... | collective-permute-start | bytes 147464 | tf_op jit(solution)/shard_map/ppermute | solution.py:568
  7.1 1.1 constant_dynamic-slice_fusion.4
  8.2 2.0 %collective-permute-start.6 = (f32[2,512,128]{2,1,0:T(8,128)S(1)}, f32[2,512,128]{2,1,0:T(8,128)S(1)}, u32[]{:S(2)}, u32[]{:S(2)}) collective-permute-start(f32[2,512,128]{2,1,0:T(8,128)S(1)} %bitcast.53), channel_id=1, source_target_pairs={{0,2},{1,3},{2,0},{3,1},{4,6},{5,7},{6,4},{7,5},{8,10},{9,11},{10,... | collective-permute-start | bytes 1572872 | tf_op jit(solution)/shard_map/ppermute | solution.py:22
  10.1 1.2 fusion
  12.1 1.9 %constant_dynamic-slice_fusion = (f32[1,2,1,16,4096]{4,3,2,1,0:T(8,128)S(1)}, f32[1,2,1,16,4096]{4,3,2,1,0:T(8,128)S(1)}, f32[1,2,1,16,4096]{4,3,2,1,0:T(8,128)S...) fusion(f32[2,2,3,16,4096]{4,3,2,1,0:T(8,128)} %param.7, s32[]{:T(128)S(6)} %select_n.17, s32[]{:T(128)S(6)} %select_n.16), kind=kLoop, calls=%fused_computation.2 | loop fusion | bytes 5242888 | tf_op jit(solution)/shard_map/dynamic_slice | solution.py:536
  14.0 1.4 collective-permute-start.11
  15.5 3.6 %collective-permute-start.5 = (f32[192,128]{1,0:T(8,128)S(1)}, f32[192,128]{1,0:T(8,128)S(1)}, u32[]{:S(2)}, u32[]{:S(2)}) collective-permute-start(f32[192,128]{1,0:T(8,128)S(1)} %shard_map.86.refs_0_.refs_4_), channel_id=1, source_target_pairs={{0,24},{4,28},{8,16},{12,20},{16,8},{20,12},{24,0},{28,4},{1,25},{... | collective-permute-start | bytes 294920 | tf_op jit(solution)/shard_map/ppermute | solution.py:22
  19.9 2.6 %collective-permute-done.5.refs_3_.refs_7_ = f32[192,128]{1,0:T(8,128)S(1)} collective-permute-done((f32[192,128]{1,0:T(8,128)S(1)}, f32[192,128]{1,0:T(8,128)S(1)}, u32[]{:S(2)}, u32[]{:S(2)}) %collective-permute-start.5) | collective-permute-done | bytes 98336 | tf_op jit(solution)/shard_map/ppermute | solution.py:22
  22.5 3.2 %collective-permute-start.3 = (f32[192,128]{1,0:T(8,128)S(1)}, f32[192,128]{1,0:T(8,128)S(1)}, u32[]{:S(2)}, u32[]{:S(2)}) collective-permute-start(f32[192,128]{1,0:T(8,128)S(1)} %shard_map.86.refs_0_.refs_4_), channel_id=1, source_target_pairs={{0,8},{4,12},{8,0},{12,4},{16,24},{20,28},{24,16},{28,20},{1,9},{5... | collective-permute-start | bytes 294920 | tf_op jit(solution)/shard_map/ppermute | solution.py:22
  26.4 1.9 %collective-permute-done.3.refs_1_.refs_5_ = f32[192,128]{1,0:T(8,128)S(1)} collective-permute-done((f32[192,128]{1,0:T(8,128)S(1)}, f32[192,128]{1,0:T(8,128)S(1)}, u32[]{:S(2)}, u32[]{:S(2)}) %collective-permute-start.3) | collective-permute-done | bytes 98336 | tf_op jit(solution)/shard_map/ppermute | solution.py:22
  28.3 2.6 %shard_map.87 = (f32[128,128]{1,0:T(8,128)S(1)}, bf16[16,128,128]{2,1,0:T(8,128)(2,1)S(1)}, bf16[16,128,128]{2,1,0:T(8,128)(2,1)S(1)}) custom-call(f32[192,128]{1,0:T(8,128)S(1)} %shard_map.86.refs_0_.refs_4_, f32[192,128]{1,0:T(8,128)S(1)} %collective-permute-done.3.refs_1_.refs_5_, f32[192,128]{1,0:T(8,128)S(1)} %collective-permute-done.4.refs_2_.refs_6_, ...), custom_call_target="tpu_custom_call" | custom-call | bytes 2818560 | tf_op jit(solution)/shard_map/pallas_call | solution.py:473
  31.4 3.8 %collective-permute-done.7 = f32[128,128]{1,0:T(8,128)S(1)} collective-permute-done((f32[128,128]{1,0:T(8,128)S(1)}, f32[128,128]{1,0:T(8,128)S(1)}, u32[]{:S(2)}, u32[]{:S(2)}) %collective-permute-start.7) | collective-permute-done | bytes 65568 | tf_op jit(solution)/shard_map/ppermute | solution.py:22
  35.2 2.9 %collective-permute-start.10 = (f32[128,128]{1,0:T(8,128)S(1)}, f32[128,128]{1,0:T(8,128)S(1)}, u32[]{:S(2)}, u32[]{:S(2)}) collective-permute-start(f32[128,128]{1,0:T(8,128)S(1)} %add.32.refs_0_), channel_id=1, source_target_pairs={{0,24},{4,28},{8,16},{12,20},{16,8},{20,12},{24,0},{28,4},{1,25},{... | collective-permute-start | bytes 196616 | tf_op jit(solution)/shard_map/ppermute | solution.py:22
  39.7 1.8 %collective-permute-done.10.refs_3_ = f32[128,128]{1,0:T(8,128)S(1)} collective-permute-done((f32[128,128]{1,0:T(8,128)S(1)}, f32[128,128]{1,0:T(8,128)S(1)}, u32[]{:S(2)}, u32[]{:S(2)}) %collective-permute-start.10) | collective-permute-done | bytes 65568 | tf_op jit(solution)/shard_map/ppermute | solution.py:22
  41.5 2.5 %collective-permute-done.9.refs_2_ = f32[128,128]{1,0:T(8,128)S(1)} collective-permute-done((f32[128,128]{1,0:T(8,128)S(1)}, f32[128,128]{1,0:T(8,128)S(1)}, u32[]{:S(2)}, u32[]{:S(2)}) %collective-permute-start.9) | collective-permute-done | bytes 65568 | tf_op jit(solution)/shard_map/ppermute | solution.py:22
  44.0 2.6 %shard_map.88 = (f32[128,128]{1,0:T(8,128)S(1)}, bf16[16,128,128]{2,1,0:T(8,128)(2,1)S(1)}, bf16[16,128,128]{2,1,0:T(8,128)(2,1)S(1)}) custom-call(f32[128,128]{1,0:T(8,128)S(1)} %add.32.refs_0_, f32[128,128]{1,0:T(8,128)S(1)} %collective-permute-done.8.refs_1_, f32[128,128]{1,0:T(8,128)S(1)} %collective-permute-done.9.refs_2_, ...), custom_call_target="tpu_custom_call" | custom-call | bytes 2687488 | tf_op jit(solution)/shard_map/pallas_call | solution.py:473
  46.6 1.1 collective-permute-start.12
  47.6 3.2 %collective-permute-done.12 = f32[128,128]{1,0:T(8,128)S(1)} collective-permute-done((f32[128,128]{1,0:T(8,128)S(1)}, f32[128,128]{1,0:T(8,128)S(1)}, u32[]{:S(2)}, u32[]{:S(2)}) %collective-permute-start.12) | collective-permute-done | bytes 65568 | tf_op jit(solution)/shard_map/ppermute | solution.py:22
  50.9 2.6 %collective-permute-start.15 = (f32[128,128]{1,0:T(8,128)S(1)}, f32[128,128]{1,0:T(8,128)S(1)}, u32[]{:S(2)}, u32[]{:S(2)}) collective-permute-start(f32[128,128]{1,0:T(8,128)S(1)} %add.33.refs_0_), channel_id=1, source_target_pairs={{0,24},{4,28},{8,16},{12,20},{16,8},{20,12},{24,0},{28,4},{1,25},{... | collective-permute-start | bytes 196616 | tf_op jit(solution)/shard_map/ppermute | solution.py:22
  53.5 1.8 %collective-permute-start.13 = (f32[128,128]{1,0:T(8,128)S(1)}, f32[128,128]{1,0:T(8,128)S(1)}, u32[]{:S(2)}, u32[]{:S(2)}) collective-permute-start(f32[128,128]{1,0:T(8,128)S(1)} %add.33.refs_0_), channel_id=1, source_target_pairs={{0,8},{4,12},{8,0},{12,4},{16,24},{20,28},{24,16},{28,20},{1,9},{5... | collective-permute-start | bytes 196616 | tf_op jit(solution)/shard_map/ppermute | solution.py:22
  55.4 1.7 %collective-permute-done.15.refs_3_ = f32[128,128]{1,0:T(8,128)S(1)} collective-permute-done((f32[128,128]{1,0:T(8,128)S(1)}, f32[128,128]{1,0:T(8,128)S(1)}, u32[]{:S(2)}, u32[]{:S(2)}) %collective-permute-start.15) | collective-permute-done | bytes 65568 | tf_op jit(solution)/shard_map/ppermute | solution.py:22
  57.0 1.7 %collective-permute-done.14.refs_2_ = f32[128,128]{1,0:T(8,128)S(1)} collective-permute-done((f32[128,128]{1,0:T(8,128)S(1)}, f32[128,128]{1,0:T(8,128)S(1)}, u32[]{:S(2)}, u32[]{:S(2)}) %collective-permute-start.14) | collective-permute-done | bytes 65568 | tf_op jit(solution)/shard_map/ppermute | solution.py:22
  58.7 2.6 %shard_map.89 = (f32[128,128]{1,0:T(8,128)S(1)}, bf16[16,128,128]{2,1,0:T(8,128)(2,1)S(1)}, bf16[16,128,128]{2,1,0:T(8,128)(2,1)S(1)}) custom-call(f32[128,128]{1,0:T(8,128)S(1)} %add.33.refs_0_, f32[128,128]{1,0:T(8,128)S(1)} %collective-permute-done.13.refs_1_, f32[128,128]{1,0:T(8,128)S(1)} %collective-permute-done.14.refs_2_, ...), custom_call_target="tpu_custom_call" | custom-call | bytes 2687488 | tf_op jit(solution)/shard_map/pallas_call | solution.py:473
  61.3 1.1 collective-permute-start.17
  62.4 3.2 %collective-permute-done.17 = f32[128,128]{1,0:T(8,128)S(1)} collective-permute-done((f32[128,128]{1,0:T(8,128)S(1)}, f32[128,128]{1,0:T(8,128)S(1)}, u32[]{:S(2)}, u32[]{:S(2)}) %collective-permute-start.17) | collective-permute-done | bytes 65568 | tf_op jit(solution)/shard_map/ppermute | solution.py:22
  65.6 2.4 %collective-permute-start.20 = (f32[128,128]{1,0:T(8,128)S(1)}, f32[128,128]{1,0:T(8,128)S(1)}, u32[]{:S(2)}, u32[]{:S(2)}) collective-permute-start(f32[128,128]{1,0:T(8,128)S(1)} %add.34.refs_0_), channel_id=1, source_target_pairs={{0,24},{4,28},{8,16},{12,20},{16,8},{20,12},{24,0},{28,4},{1,25},{... | collective-permute-start | bytes 196616 | tf_op jit(solution)/shard_map/ppermute | solution.py:22
  68.1 2.0 %collective-permute-start.18 = (f32[128,128]{1,0:T(8,128)S(1)}, f32[128,128]{1,0:T(8,128)S(1)}, u32[]{:S(2)}, u32[]{:S(2)}) collective-permute-start(f32[128,128]{1,0:T(8,128)S(1)} %add.34.refs_0_), channel_id=1, source_target_pairs={{0,8},{4,12},{8,0},{12,4},{16,24},{20,28},{24,16},{28,20},{1,9},{5... | collective-permute-start | bytes 196616 | tf_op jit(solution)/shard_map/ppermute | solution.py:22
  70.1 1.7 %collective-permute-done.20.refs_3_ = f32[128,128]{1,0:T(8,128)S(1)} collective-permute-done((f32[128,128]{1,0:T(8,128)S(1)}, f32[128,128]{1,0:T(8,128)S(1)}, u32[]{:S(2)}, u32[]{:S(2)}) %collective-permute-start.20) | collective-permute-done | bytes 65568 | tf_op jit(solution)/shard_map/ppermute | solution.py:22
  71.8 1.8 %collective-permute-done.19.refs_2_ = f32[128,128]{1,0:T(8,128)S(1)} collective-permute-done((f32[128,128]{1,0:T(8,128)S(1)}, f32[128,128]{1,0:T(8,128)S(1)}, u32[]{:S(2)}, u32[]{:S(2)}) %collective-permute-start.19) | collective-permute-done | bytes 65568 | tf_op jit(solution)/shard_map/ppermute | solution.py:22
  74.0 1.2 collective-permute-done.21.other
  75.2 3.6 %shard_map.91 = (f32[64,128]{1,0:T(8,128)}, f32[128,128]{1,0:T(8,128)S(1)}, f32[16,128]{1,0:T(8,128)S(1)}, f32[512,128]{1,0:T(8,128)S(1)}) custom-call(f32[128,128]{1,0:T(8,128)S(1)} %shard_map.90.kept, f32[128,128]{1,0:T(8,128)S(1)} %collective-permute-done.21.other, f32[192,128]{1,0:T(8,128)S(1)} %shard_map.86.refs_0_.refs_4_, ...), custom_call_target="tpu_custom_call" | custom-call | bytes 1942016 | tf_op jit(solution)/shard_map/pallas_call | solution.py:473
  79.1 1.4 collective-permute-done.22.theirs
  80.5 1.6 %shard_map.92 = (f32[512,128]{1,0:T(8,128)S(1)}, f32[160,128]{1,0:T(8,128)S(1)}) custom-call(f32[512,128]{1,0:T(8,128)S(1)} %get-tuple-element.43.mine, f32[512,128]{1,0:T(8,128)S(1)} %collective-permute-done.22.theirs, f32[128,128]{1,0:T(8,128)S(1)} %get-tuple-element.44.carried, f32[2,512,128]{2,1,0:T(8,128)S(1)} %bitcast.47, ...), custom_call_target="tpu_custom_call" | custom-call | bytes 1982464 | tf_op jit(solution)/shard_map/pallas_call | solution.py:473
  82.0 1.1 collective-permute-start.23
  83.1 3.4 %collective-permute-done.23 = f32[160,128]{1,0:T(8,128)S(1)} collective-permute-done((f32[160,128]{1,0:T(8,128)S(1)}, f32[160,128]{1,0:T(8,128)S(1)}, u32[]{:S(2)}, u32[]{:S(2)}) %collective-permute-start.23) | collective-permute-done | bytes 81952 | tf_op jit(solution)/shard_map/ppermute | solution.py:22
  86.6 2.1 %collective-permute-start.26 = (f32[160,128]{1,0:T(8,128)S(1)}, f32[160,128]{1,0:T(8,128)S(1)}, u32[]{:S(2)}, u32[]{:S(2)}) collective-permute-start(f32[160,128]{1,0:T(8,128)S(1)} %add.35.refs_0_), channel_id=1, source_target_pairs={{0,24},{4,28},{8,16},{12,20},{16,8},{20,12},{24,0},{28,4},{1,25},{... | collective-permute-start | bytes 245768 | tf_op jit(solution)/shard_map/ppermute | solution.py:22
  88.9 2.2 %collective-permute-start.24 = (f32[160,128]{1,0:T(8,128)S(1)}, f32[160,128]{1,0:T(8,128)S(1)}, u32[]{:S(2)}, u32[]{:S(2)}) collective-permute-start(f32[160,128]{1,0:T(8,128)S(1)} %add.35.refs_0_), channel_id=1, source_target_pairs={{0,8},{4,12},{8,0},{12,4},{16,24},{20,28},{24,16},{28,20},{1,9},{5... | collective-permute-start | bytes 245768 | tf_op jit(solution)/shard_map/ppermute | solution.py:22
  91.1 2.6 %collective-permute-done.26.refs_3_ = f32[160,128]{1,0:T(8,128)S(1)} collective-permute-done((f32[160,128]{1,0:T(8,128)S(1)}, f32[160,128]{1,0:T(8,128)S(1)}, u32[]{:S(2)}, u32[]{:S(2)}) %collective-permute-start.26) | collective-permute-done | bytes 81952 | tf_op jit(solution)/shard_map/ppermute | solution.py:22
  93.7 2.8 %collective-permute-done.25.refs_2_ = f32[160,128]{1,0:T(8,128)S(1)} collective-permute-done((f32[160,128]{1,0:T(8,128)S(1)}, f32[160,128]{1,0:T(8,128)S(1)}, u32[]{:S(2)}, u32[]{:S(2)}) %collective-permute-start.25) | collective-permute-done | bytes 81952 | tf_op jit(solution)/shard_map/ppermute | solution.py:22
  96.5 3.6 %shard_map.93 = (f32[64,128]{1,0:T(8,128)S(1)}, f32[128,128]{1,0:T(8,128)S(1)}, f32[512,128]{1,0:T(8,128)S(1)}) custom-call(f32[160,128]{1,0:T(8,128)S(1)} %add.35.refs_0_, f32[160,128]{1,0:T(8,128)S(1)} %collective-permute-done.24.refs_1_, f32[160,128]{1,0:T(8,128)S(1)} %collective-permute-done.25.refs_2_, f32[160,128]{1,0:T(8,128)S(1)} %collective-permute-done.26.refs_3_, ...), custom_call_target="tpu_custom_call" | custom-call | bytes 1737216 | tf_op jit(solution)/shard_map/pallas_call | solution.py:473
  100.1 1.5 %collective-permute-done.27.theirs = f32[512,128]{1,0:T(8,128)S(1)} collective-permute-done((f32[512,128]{1,0:T(8,128)S(1)}, f32[512,128]{1,0:T(8,128)S(1)}, u32[]{:S(2)}, u32[]{:S(2)}) %collective-permute-start.27) | collective-permute-done | bytes 262176 | tf_op jit(solution)/shard_map/ppermute | solution.py:22
  101.6 1.6 %shard_map.94 = (f32[512,128]{1,0:T(8,128)S(1)}, f32[160,128]{1,0:T(8,128)S(1)}) custom-call(f32[512,128]{1,0:T(8,128)S(1)} %get-tuple-element.48.mine, f32[512,128]{1,0:T(8,128)S(1)} %collective-permute-done.27.theirs, f32[128,128]{1,0:T(8,128)S(1)} %get-tuple-element.49.carried, f32[2,512,128]{2,1,0:T(8,128)S(1)} %bitcast.45, ...), custom_call_target="tpu_custom_call" | custom-call | bytes 1982464 | tf_op jit(solution)/shard_map/pallas_call | solution.py:473
  103.2 1.1 collective-permute-start.28
  104.3 3.4 %collective-permute-done.28 = f32[160,128]{1,0:T(8,128)S(1)} collective-permute-done((f32[160,128]{1,0:T(8,128)S(1)}, f32[160,128]{1,0:T(8,128)S(1)}, u32[]{:S(2)}, u32[]{:S(2)}) %collective-permute-start.28) | collective-permute-done | bytes 81952 | tf_op jit(solution)/shard_map/ppermute | solution.py:22
  107.8 2.1 %collective-permute-start.31 = (f32[160,128]{1,0:T(8,128)S(1)}, f32[160,128]{1,0:T(8,128)S(1)}, u32[]{:S(2)}, u32[]{:S(2)}) collective-permute-start(f32[160,128]{1,0:T(8,128)S(1)} %add.36.refs_0_), channel_id=1, source_target_pairs={{0,24},{4,28},{8,16},{12,20},{16,8},{20,12},{24,0},{28,4},{1,25},{... | collective-permute-start | bytes 245768 | tf_op jit(solution)/shard_map/ppermute | solution.py:22
  109.9 2.4 %collective-permute-start.29 = (f32[160,128]{1,0:T(8,128)S(1)}, f32[160,128]{1,0:T(8,128)S(1)}, u32[]{:S(2)}, u32[]{:S(2)}) collective-permute-start(f32[160,128]{1,0:T(8,128)S(1)} %add.36.refs_0_), channel_id=1, source_target_pairs={{0,8},{4,12},{8,0},{12,4},{16,24},{20,28},{24,16},{28,20},{1,9},{5... | collective-permute-start | bytes 245768 | tf_op jit(solution)/shard_map/ppermute | solution.py:22
  112.2 2.5 %collective-permute-done.31.refs_3_ = f32[160,128]{1,0:T(8,128)S(1)} collective-permute-done((f32[160,128]{1,0:T(8,128)S(1)}, f32[160,128]{1,0:T(8,128)S(1)}, u32[]{:S(2)}, u32[]{:S(2)}) %collective-permute-start.31) | collective-permute-done | bytes 81952 | tf_op jit(solution)/shard_map/ppermute | solution.py:22
  114.8 2.0 %collective-permute-done.30.refs_2_ = f32[160,128]{1,0:T(8,128)S(1)} collective-permute-done((f32[160,128]{1,0:T(8,128)S(1)}, f32[160,128]{1,0:T(8,128)S(1)}, u32[]{:S(2)}, u32[]{:S(2)}) %collective-permute-start.30) | collective-permute-done | bytes 81952 | tf_op jit(solution)/shard_map/ppermute | solution.py:22
  116.8 3.4 %shard_map.95 = (f32[64,128]{1,0:T(8,128)S(1)}, f32[128,128]{1,0:T(8,128)S(1)}, f32[512,128]{1,0:T(8,128)S(1)}) custom-call(f32[160,128]{1,0:T(8,128)S(1)} %add.36.refs_0_, f32[160,128]{1,0:T(8,128)S(1)} %collective-permute-done.29.refs_1_, f32[160,128]{1,0:T(8,128)S(1)} %collective-permute-done.30.refs_2_, f32[160,128]{1,0:T(8,128)S(1)} %collective-permute-done.31.refs_3_, ...), custom_call_target="tpu_custom_call" | custom-call | bytes 1737216 | tf_op jit(solution)/shard_map/pallas_call | solution.py:473
  120.5 1.1 collective-permute-start.42
  121.7 1.6 %shard_map.96 = (f32[512,128]{1,0:T(8,128)S(1)}, f32[160,128]{1,0:T(8,128)S(1)}) custom-call(f32[512,128]{1,0:T(8,128)S(1)} %get-tuple-element.53.mine, f32[512,128]{1,0:T(8,128)S(1)} %collective-permute-done.32.theirs, f32[128,128]{1,0:T(8,128)S(1)} %get-tuple-element.54.carried, f32[2,512,128]{2,1,0:T(8,128)S(1)} %bitcast.43, ...), custom_call_target="tpu_custom_call" | custom-call | bytes 1982464 | tf_op jit(solution)/shard_map/pallas_call | solution.py:473
  123.3 1.1 collective-permute-start.33
  124.7 1.1 collective-permute-start.41
  125.8 1.0 collective-permute-start.40
  126.8 1.0 collective-permute-done.33
  127.8 2.1 %collective-permute-start.36 = (f32[160,128]{1,0:T(8,128)S(1)}, f32[160,128]{1,0:T(8,128)S(1)}, u32[]{:S(2)}, u32[]{:S(2)}) collective-permute-start(f32[160,128]{1,0:T(8,128)S(1)} %add.37.refs_0_), channel_id=1, source_target_pairs={{0,24},{4,28},{8,16},{12,20},{16,8},{20,12},{24,0},{28,4},{1,25},{... | collective-permute-start | bytes 245768 | tf_op jit(solution)/shard_map/ppermute | solution.py:22
  129.9 4.4 %collective-permute-done.36.refs_3_ = f32[160,128]{1,0:T(8,128)S(1)} collective-permute-done((f32[160,128]{1,0:T(8,128)S(1)}, f32[160,128]{1,0:T(8,128)S(1)}, u32[]{:S(2)}, u32[]{:S(2)}) %collective-permute-start.36) | collective-permute-done | bytes 81952 | tf_op jit(solution)/shard_map/ppermute | solution.py:22
  134.3 2.1 %collective-permute-start.34 = (f32[160,128]{1,0:T(8,128)S(1)}, f32[160,128]{1,0:T(8,128)S(1)}, u32[]{:S(2)}, u32[]{:S(2)}) collective-permute-start(f32[160,128]{1,0:T(8,128)S(1)} %add.37.refs_0_), channel_id=1, source_target_pairs={{0,8},{4,12},{8,0},{12,4},{16,24},{20,28},{24,16},{28,20},{1,9},{5... | collective-permute-start | bytes 245768 | tf_op jit(solution)/shard_map/ppermute | solution.py:22
  136.4 1.0 collective-permute-done.35.refs_2_
  137.4 1.5 collective-permute-done.34.refs_1_
  138.8 2.8 %shard_map.97.mine = f32[80,128]{1,0:T(8,128)S(1)} custom-call(f32[160,128]{1,0:T(8,128)S(1)} %add.37.refs_0_, f32[160,128]{1,0:T(8,128)S(1)} %collective-permute-done.34.refs_1_, f32[160,128]{1,0:T(8,128)S(1)} %collective-permute-done.35.refs_2_, f32[160,128]{1,0:T(8,128)S(1)} %collective-permute-done.36.refs_3_, f32[1,128]{1,0:T(1,128)S(1)} %get-tuple-element.76.refs_4_, ...), custom_call_target="tpu_custom_call" | custom-call | bytes 401924 | tf_op jit(solution)/shard_map/pallas_call | solution.py:473
  141.7 1.1 collective-permute-start.38
  146.0 1.9 %shard_map.102 = (f32[2,16,64]{2,1,0:T(8,128)}, f32[2,16,64]{2,1,0:T(8,128)}, f32[2,3,512,128]{3,2,1,0:T(8,128)}) custom-call(s32[1]{0:T(128)} %bitcast.member.refs_5_, f32[80,128]{1,0:T(8,128)S(1)} %shard_map.97.mine, f32[80,128]{1,0:T(8,128)S(1)} %collective-permute-done.37.near, ...), custom_call_target="tpu_custom_call", output_to_operand_aliasing={{2}: (7, {})} | custom-call | bytes 3850244 | tf_op jit(solution)/shard_map/pallas_call | solution.py:473
  (59 shorter events, 10.2 us)
Async XLA Ops:
  2.5 8.9 %collective-permute-start.2 = (f32[96,128]{1,0:T(8,128)}, f32[96,128]{1,0:T(8,128)S(1)}, u32[]{:S(2)}, u32[]{:S(2)}) collective-permute-start(f32[96,128]{1,0:T(8,128)} %get-tuple-element.35), channel_id=1, source_target_pairs={{0,6},{1,7},{2,4},{3,5},{4,2},{5,3},{6,0},{7,1},{8,14},{9,15},{10,... | collective-permute-start | bytes 147464 | tf_op jit(solution)/shard_map/ppermute | solution.py:568
  6.4 4.9 %collective-permute-start.1 = (f32[96,128]{1,0:T(8,128)}, f32[96,128]{1,0:T(8,128)S(1)}, u32[]{:S(2)}, u32[]{:S(2)}) collective-permute-start(f32[96,128]{1,0:T(8,128)} %get-tuple-element.35), channel_id=1, source_target_pairs={{0,2},{1,3},{2,0},{3,1},{4,6},{5,7},{6,4},{7,5},{8,10},{9,11},{10,... | collective-permute-start | bytes 147464 | tf_op jit(solution)/shard_map/ppermute | solution.py:22
  7.0 4.3 %collective-permute-start = (f32[80,128]{1,0:T(8,128)}, f32[80,128]{1,0:T(8,128)S(1)}, u32[]{:S(2)}, u32[]{:S(2)}) collective-permute-start(f32[80,128]{1,0:T(8,128)} %get-tuple-element.34.refs_0_), channel_id=1, source_target_pairs={{0,4},{4,0},{8,12},{12,8},{16,20},{20,16},{24,28},{28,24},{1,5},{5... | collective-permute-start | bytes 122888 | tf_op jit(solution)/shard_map/ppermute | solution.py:22
  8.2 20.1 %collective-permute-start.6 = (f32[2,512,128]{2,1,0:T(8,128)S(1)}, f32[2,512,128]{2,1,0:T(8,128)S(1)}, u32[]{:S(2)}, u32[]{:S(2)}) collective-permute-start(f32[2,512,128]{2,1,0:T(8,128)S(1)} %bitcast.53), channel_id=1, source_target_pairs={{0,2},{1,3},{2,0},{3,1},{4,6},{5,7},{6,4},{7,5},{8,10},{9,11},{10,... | collective-permute-start | bytes 1572872 | tf_op jit(solution)/shard_map/ppermute | solution.py:22
  11.3 4.2 %copy-start.2 = (s32[4]{0:T(128)S(1)}, s32[4]{0:T(128)}, u32[]{:S(2)}) copy-start(s32[4]{0:T(128)} %param.11) | copy-start | bytes 52
  11.3 0.8 copy-start.1
  14.0 25.7 %collective-permute-start.11 = (f32[2,512,128]{2,1,0:T(8,128)S(1)}, f32[2,512,128]{2,1,0:T(8,128)S(1)}, u32[]{:S(2)}, u32[]{:S(2)}) collective-permute-start(f32[2,512,128]{2,1,0:T(8,128)S(1)} %bitcast.55), channel_id=1, source_target_pairs={{0,2},{1,3},{2,0},{3,1},{4,6},{5,7},{6,4},{7,5},{8,10},{9,11},{10,... | collective-permute-start | bytes 1572872 | tf_op jit(solution)/shard_map/ppermute | solution.py:22
  15.5 7.0 %collective-permute-start.5 = (f32[192,128]{1,0:T(8,128)S(1)}, f32[192,128]{1,0:T(8,128)S(1)}, u32[]{:S(2)}, u32[]{:S(2)}) collective-permute-start(f32[192,128]{1,0:T(8,128)S(1)} %shard_map.86.refs_0_.refs_4_), channel_id=1, source_target_pairs={{0,24},{4,28},{8,16},{12,20},{16,8},{20,12},{24,0},{28,4},{1,25},{... | collective-permute-start | bytes 294920 | tf_op jit(solution)/shard_map/ppermute | solution.py:22
  19.1 36.2 %collective-permute-start.16 = (f32[2,512,128]{2,1,0:T(8,128)S(1)}, f32[2,512,128]{2,1,0:T(8,128)S(1)}, u32[]{:S(2)}, u32[]{:S(2)}) collective-permute-start(f32[2,512,128]{2,1,0:T(8,128)S(1)} %bitcast.54), channel_id=1, source_target_pairs={{0,2},{1,3},{2,0},{3,1},{4,6},{5,7},{6,4},{7,5},{8,10},{9,11},{10,... | collective-permute-start | bytes 1572872 | tf_op jit(solution)/shard_map/ppermute | solution.py:22
  19.9 6.5 %collective-permute-start.4 = (f32[192,128]{1,0:T(8,128)S(1)}, f32[192,128]{1,0:T(8,128)S(1)}, u32[]{:S(2)}, u32[]{:S(2)}) collective-permute-start(f32[192,128]{1,0:T(8,128)S(1)} %shard_map.86.refs_0_.refs_4_), channel_id=1, source_target_pairs={{0,16},{4,20},{8,24},{12,28},{16,0},{20,4},{24,8},{28,12},{1,17},{... | collective-permute-start | bytes 294920 | tf_op jit(solution)/shard_map/ppermute | solution.py:22
  22.5 5.8 %collective-permute-start.3 = (f32[192,128]{1,0:T(8,128)S(1)}, f32[192,128]{1,0:T(8,128)S(1)}, u32[]{:S(2)}, u32[]{:S(2)}) collective-permute-start(f32[192,128]{1,0:T(8,128)S(1)} %shard_map.86.refs_0_.refs_4_), channel_id=1, source_target_pairs={{0,8},{4,12},{8,0},{12,4},{16,24},{20,28},{24,16},{28,20},{1,9},{5... | collective-permute-start | bytes 294920 | tf_op jit(solution)/shard_map/ppermute | solution.py:22
  30.9 4.3 %collective-permute-start.7 = (f32[128,128]{1,0:T(8,128)S(1)}, f32[128,128]{1,0:T(8,128)S(1)}, u32[]{:S(2)}, u32[]{:S(2)}) collective-permute-start(f32[128,128]{1,0:T(8,128)S(1)} %get-tuple-element.38), channel_id=1, source_target_pairs={{0,4},{4,0},{8,12},{12,8},{16,20},{20,16},{24,28},{28,24},{1,5},{5... | collective-permute-start | bytes 196616 | tf_op jit(solution)/shard_map/ppermute | solution.py:22
  35.2 6.2 %collective-permute-start.10 = (f32[128,128]{1,0:T(8,128)S(1)}, f32[128,128]{1,0:T(8,128)S(1)}, u32[]{:S(2)}, u32[]{:S(2)}) collective-permute-start(f32[128,128]{1,0:T(8,128)S(1)} %add.32.refs_0_), channel_id=1, source_target_pairs={{0,24},{4,28},{8,16},{12,20},{16,8},{20,12},{24,0},{28,4},{1,25},{... | collective-permute-start | bytes 196616 | tf_op jit(solution)/shard_map/ppermute | solution.py:22
  38.1 5.9 %collective-permute-start.9 = (f32[128,128]{1,0:T(8,128)S(1)}, f32[128,128]{1,0:T(8,128)S(1)}, u32[]{:S(2)}, u32[]{:S(2)}) collective-permute-start(f32[128,128]{1,0:T(8,128)S(1)} %add.32.refs_0_), channel_id=1, source_target_pairs={{0,16},{4,20},{8,24},{12,28},{16,0},{20,4},{24,8},{28,12},{1,17},{... | collective-permute-start | bytes 196616 | tf_op jit(solution)/shard_map/ppermute | solution.py:22
  38.8 5.2 %collective-permute-start.8 = (f32[128,128]{1,0:T(8,128)S(1)}, f32[128,128]{1,0:T(8,128)S(1)}, u32[]{:S(2)}, u32[]{:S(2)}) collective-permute-start(f32[128,128]{1,0:T(8,128)S(1)} %add.32.refs_0_), channel_id=1, source_target_pairs={{0,8},{4,12},{8,0},{12,4},{16,24},{20,28},{24,16},{28,20},{1,9},{5... | collective-permute-start | bytes 196616 | tf_op jit(solution)/shard_map/ppermute | solution.py:22
  46.6 4.3 %collective-permute-start.12 = (f32[128,128]{1,0:T(8,128)S(1)}, f32[128,128]{1,0:T(8,128)S(1)}, u32[]{:S(2)}, u32[]{:S(2)}) collective-permute-start(f32[128,128]{1,0:T(8,128)S(1)} %get-tuple-element.39), channel_id=1, source_target_pairs={{0,4},{4,0},{8,12},{12,8},{16,20},{20,16},{24,28},{28,24},{1,5},{5... | collective-permute-start | bytes 196616 | tf_op jit(solution)/shard_map/ppermute | solution.py:22
  50.9 6.1 %collective-permute-start.15 = (f32[128,128]{1,0:T(8,128)S(1)}, f32[128,128]{1,0:T(8,128)S(1)}, u32[]{:S(2)}, u32[]{:S(2)}) collective-permute-start(f32[128,128]{1,0:T(8,128)S(1)} %add.33.refs_0_), channel_id=1, source_target_pairs={{0,24},{4,28},{8,16},{12,20},{16,8},{20,12},{24,0},{28,4},{1,25},{... | collective-permute-start | bytes 196616 | tf_op jit(solution)/shard_map/ppermute | solution.py:22
  53.5 5.2 %collective-permute-start.14 = (f32[128,128]{1,0:T(8,128)S(1)}, f32[128,128]{1,0:T(8,128)S(1)}, u32[]{:S(2)}, u32[]{:S(2)}) collective-permute-start(f32[128,128]{1,0:T(8,128)S(1)} %add.33.refs_0_), channel_id=1, source_target_pairs={{0,16},{4,20},{8,24},{12,28},{16,0},{20,4},{24,8},{28,12},{1,17},{... | collective-permute-start | bytes 196616 | tf_op jit(solution)/shard_map/ppermute | solution.py:22
  53.5 5.2 %collective-permute-start.13 = (f32[128,128]{1,0:T(8,128)S(1)}, f32[128,128]{1,0:T(8,128)S(1)}, u32[]{:S(2)}, u32[]{:S(2)}) collective-permute-start(f32[128,128]{1,0:T(8,128)S(1)} %add.33.refs_0_), channel_id=1, source_target_pairs={{0,8},{4,12},{8,0},{12,4},{16,24},{20,28},{24,16},{28,20},{1,9},{5... | collective-permute-start | bytes 196616 | tf_op jit(solution)/shard_map/ppermute | solution.py:22
  61.3 4.3 %collective-permute-start.17 = (f32[128,128]{1,0:T(8,128)S(1)}, f32[128,128]{1,0:T(8,128)S(1)}, u32[]{:S(2)}, u32[]{:S(2)}) collective-permute-start(f32[128,128]{1,0:T(8,128)S(1)} %get-tuple-element.40), channel_id=1, source_target_pairs={{0,4},{4,0},{8,12},{12,8},{16,20},{20,16},{24,28},{28,24},{1,5},{5... | collective-permute-start | bytes 196616 | tf_op jit(solution)/shard_map/ppermute | solution.py:22
  65.6 6.1 %collective-permute-start.20 = (f32[128,128]{1,0:T(8,128)S(1)}, f32[128,128]{1,0:T(8,128)S(1)}, u32[]{:S(2)}, u32[]{:S(2)}) collective-permute-start(f32[128,128]{1,0:T(8,128)S(1)} %add.34.refs_0_), channel_id=1, source_target_pairs={{0,24},{4,28},{8,16},{12,20},{16,8},{20,12},{24,0},{28,4},{1,25},{... | collective-permute-start | bytes 196616 | tf_op jit(solution)/shard_map/ppermute | solution.py:22
  68.0 5.6 %collective-permute-start.19 = (f32[128,128]{1,0:T(8,128)S(1)}, f32[128,128]{1,0:T(8,128)S(1)}, u32[]{:S(2)}, u32[]{:S(2)}) collective-permute-start(f32[128,128]{1,0:T(8,128)S(1)} %add.34.refs_0_), channel_id=1, source_target_pairs={{0,16},{4,20},{8,24},{12,28},{16,0},{20,4},{24,8},{28,12},{1,17},{... | collective-permute-start | bytes 196616 | tf_op jit(solution)/shard_map/ppermute | solution.py:22
  68.1 5.5 %collective-permute-start.18 = (f32[128,128]{1,0:T(8,128)S(1)}, f32[128,128]{1,0:T(8,128)S(1)}, u32[]{:S(2)}, u32[]{:S(2)}) collective-permute-start(f32[128,128]{1,0:T(8,128)S(1)} %add.34.refs_0_), channel_id=1, source_target_pairs={{0,8},{4,12},{8,0},{12,4},{16,24},{20,28},{24,16},{28,20},{1,9},{5... | collective-permute-start | bytes 196616 | tf_op jit(solution)/shard_map/ppermute | solution.py:22
  73.9 1.3 collective-permute-start.21
  78.8 1.6 %collective-permute-start.22 = (f32[512,128]{1,0:T(8,128)S(1)}, f32[512,128]{1,0:T(8,128)S(1)}, u32[]{:S(2)}, u32[]{:S(2)}) collective-permute-start(f32[512,128]{1,0:T(8,128)S(1)} %get-tuple-element.43.mine), channel_id=1, source_target_pairs={{0,1},{1,0},{2,3},{3,2},{4,5},{5,4},{6,7},{7,6},{8,9},{9,8},{10,11... | collective-permute-start | bytes 786440 | tf_op jit(solution)/shard_map/ppermute | solution.py:22
  82.0 4.6 %collective-permute-start.23 = (f32[160,128]{1,0:T(8,128)S(1)}, f32[160,128]{1,0:T(8,128)S(1)}, u32[]{:S(2)}, u32[]{:S(2)}) collective-permute-start(f32[160,128]{1,0:T(8,128)S(1)} %get-tuple-element.45), channel_id=1, source_target_pairs={{0,4},{4,0},{8,12},{12,8},{16,20},{20,16},{24,28},{28,24},{1,5},{5... | collective-permute-start | bytes 245768 | tf_op jit(solution)/shard_map/ppermute | solution.py:22
  86.6 7.1 %collective-permute-start.26 = (f32[160,128]{1,0:T(8,128)S(1)}, f32[160,128]{1,0:T(8,128)S(1)}, u32[]{:S(2)}, u32[]{:S(2)}) collective-permute-start(f32[160,128]{1,0:T(8,128)S(1)} %add.35.refs_0_), channel_id=1, source_target_pairs={{0,24},{4,28},{8,16},{12,20},{16,8},{20,12},{24,0},{28,4},{1,25},{... | collective-permute-start | bytes 245768 | tf_op jit(solution)/shard_map/ppermute | solution.py:22
  88.7 7.8 %collective-permute-start.25 = (f32[160,128]{1,0:T(8,128)S(1)}, f32[160,128]{1,0:T(8,128)S(1)}, u32[]{:S(2)}, u32[]{:S(2)}) collective-permute-start(f32[160,128]{1,0:T(8,128)S(1)} %add.35.refs_0_), channel_id=1, source_target_pairs={{0,16},{4,20},{8,24},{12,28},{16,0},{20,4},{24,8},{28,12},{1,17},{... | collective-permute-start | bytes 245768 | tf_op jit(solution)/shard_map/ppermute | solution.py:22
  88.9 7.6 %collective-permute-start.24 = (f32[160,128]{1,0:T(8,128)S(1)}, f32[160,128]{1,0:T(8,128)S(1)}, u32[]{:S(2)}, u32[]{:S(2)}) collective-permute-start(f32[160,128]{1,0:T(8,128)S(1)} %add.35.refs_0_), channel_id=1, source_target_pairs={{0,8},{4,12},{8,0},{12,4},{16,24},{20,28},{24,16},{28,20},{1,9},{5... | collective-permute-start | bytes 245768 | tf_op jit(solution)/shard_map/ppermute | solution.py:22
  100.1 1.6 %collective-permute-start.27 = (f32[512,128]{1,0:T(8,128)S(1)}, f32[512,128]{1,0:T(8,128)S(1)}, u32[]{:S(2)}, u32[]{:S(2)}) collective-permute-start(f32[512,128]{1,0:T(8,128)S(1)} %get-tuple-element.48.mine), channel_id=1, source_target_pairs={{0,1},{1,0},{2,3},{3,2},{4,5},{5,4},{6,7},{7,6},{8,9},{9,8},{10,11... | collective-permute-start | bytes 786440 | tf_op jit(solution)/shard_map/ppermute | solution.py:22
  101.6 37.2 %copy-start = (f32[2,2,16,64]{3,2,1,0:T(8,128)S(1)}, f32[2,2,16,64]{3,2,1,0:T(8,128)}, u32[]{:S(2)}) copy-start(f32[2,2,16,64]{3,2,1,0:T(8,128)} %refs_6_.1) | copy-start | bytes 49156
  103.2 4.5 %collective-permute-start.28 = (f32[160,128]{1,0:T(8,128)S(1)}, f32[160,128]{1,0:T(8,128)S(1)}, u32[]{:S(2)}, u32[]{:S(2)}) collective-permute-start(f32[160,128]{1,0:T(8,128)S(1)} %get-tuple-element.50), channel_id=1, source_target_pairs={{0,4},{4,0},{8,12},{12,8},{16,20},{20,16},{24,28},{28,24},{1,5},{5... | collective-permute-start | bytes 245768 | tf_op jit(solution)/shard_map/ppermute | solution.py:22
  107.8 7.0 %collective-permute-start.31 = (f32[160,128]{1,0:T(8,128)S(1)}, f32[160,128]{1,0:T(8,128)S(1)}, u32[]{:S(2)}, u32[]{:S(2)}) collective-permute-start(f32[160,128]{1,0:T(8,128)S(1)} %add.36.refs_0_), channel_id=1, source_target_pairs={{0,24},{4,28},{8,16},{12,20},{16,8},{20,12},{24,0},{28,4},{1,25},{... | collective-permute-start | bytes 245768 | tf_op jit(solution)/shard_map/ppermute | solution.py:22
  109.9 6.9 %collective-permute-start.30 = (f32[160,128]{1,0:T(8,128)S(1)}, f32[160,128]{1,0:T(8,128)S(1)}, u32[]{:S(2)}, u32[]{:S(2)}) collective-permute-start(f32[160,128]{1,0:T(8,128)S(1)} %add.36.refs_0_), channel_id=1, source_target_pairs={{0,16},{4,20},{8,24},{12,28},{16,0},{20,4},{24,8},{28,12},{1,17},{... | collective-permute-start | bytes 245768 | tf_op jit(solution)/shard_map/ppermute | solution.py:22
  109.9 6.9 %collective-permute-start.29 = (f32[160,128]{1,0:T(8,128)S(1)}, f32[160,128]{1,0:T(8,128)S(1)}, u32[]{:S(2)}, u32[]{:S(2)}) collective-permute-start(f32[160,128]{1,0:T(8,128)S(1)} %add.36.refs_0_), channel_id=1, source_target_pairs={{0,8},{4,12},{8,0},{12,4},{16,24},{20,28},{24,16},{28,20},{1,9},{5... | collective-permute-start | bytes 245768 | tf_op jit(solution)/shard_map/ppermute | solution.py:22
  120.1 1.6 %collective-permute-start.32 = (f32[512,128]{1,0:T(8,128)S(1)}, f32[512,128]{1,0:T(8,128)S(1)}, u32[]{:S(2)}, u32[]{:S(2)}) collective-permute-start(f32[512,128]{1,0:T(8,128)S(1)} %get-tuple-element.53.mine), channel_id=1, source_target_pairs={{0,1},{1,0},{2,3},{3,2},{4,5},{5,4},{6,7},{7,6},{8,9},{9,8},{10,11... | collective-permute-start | bytes 786440 | tf_op jit(solution)/shard_map/ppermute | solution.py:22
  120.5 22.2 %collective-permute-start.42 = (f32[512,128]{1,0:T(8,128)S(1)}, f32[512,128]{1,0:T(8,128)S(1)}, u32[]{:S(2)}, u32[]{:S(2)}) collective-permute-start(f32[512,128]{1,0:T(8,128)S(1)} %shard_map.99.mine), channel_id=1, source_target_pairs={{0,2},{1,3},{2,0},{3,1},{4,6},{5,7},{6,4},{7,5},{8,10},{9,11},{10,... | collective-permute-start | bytes 786440 | tf_op jit(solution)/shard_map/ppermute | solution.py:22
  123.3 4.5 %collective-permute-start.33 = (f32[160,128]{1,0:T(8,128)S(1)}, f32[160,128]{1,0:T(8,128)S(1)}, u32[]{:S(2)}, u32[]{:S(2)}) collective-permute-start(f32[160,128]{1,0:T(8,128)S(1)} %get-tuple-element.55), channel_id=1, source_target_pairs={{0,4},{4,0},{8,12},{12,8},{16,20},{20,16},{24,28},{28,24},{1,5},{5... | collective-permute-start | bytes 245768 | tf_op jit(solution)/shard_map/ppermute | solution.py:22
  124.7 19.6 %collective-permute-start.41 = (f32[512,128]{1,0:T(8,128)S(1)}, f32[512,128]{1,0:T(8,128)S(1)}, u32[]{:S(2)}, u32[]{:S(2)}) collective-permute-start(f32[512,128]{1,0:T(8,128)S(1)} %shard_map.98.mine), channel_id=1, source_target_pairs={{0,2},{1,3},{2,0},{3,1},{4,6},{5,7},{6,4},{7,5},{8,10},{9,11},{10,... | collective-permute-start | bytes 786440 | tf_op jit(solution)/shard_map/ppermute | solution.py:22
  125.8 20.2 %collective-permute-start.40 = (f32[512,128]{1,0:T(8,128)S(1)}, f32[512,128]{1,0:T(8,128)S(1)}, u32[]{:S(2)}, u32[]{:S(2)}) collective-permute-start(f32[512,128]{1,0:T(8,128)S(1)} %get-tuple-element.57.mixture), channel_id=1, source_target_pairs={{0,2},{1,3},{2,0},{3,1},{4,6},{5,7},{6,4},{7,5},{8,10},{9,11},{10,... | collective-permute-start | bytes 786440 | tf_op jit(solution)/shard_map/ppermute | solution.py:22
  127.8 6.5 %collective-permute-start.36 = (f32[160,128]{1,0:T(8,128)S(1)}, f32[160,128]{1,0:T(8,128)S(1)}, u32[]{:S(2)}, u32[]{:S(2)}) collective-permute-start(f32[160,128]{1,0:T(8,128)S(1)} %add.37.refs_0_), channel_id=1, source_target_pairs={{0,24},{4,28},{8,16},{12,20},{16,8},{20,12},{24,0},{28,4},{1,25},{... | collective-permute-start | bytes 245768 | tf_op jit(solution)/shard_map/ppermute | solution.py:22
  129.9 7.4 %collective-permute-start.35 = (f32[160,128]{1,0:T(8,128)S(1)}, f32[160,128]{1,0:T(8,128)S(1)}, u32[]{:S(2)}, u32[]{:S(2)}) collective-permute-start(f32[160,128]{1,0:T(8,128)S(1)} %add.37.refs_0_), channel_id=1, source_target_pairs={{0,16},{4,20},{8,24},{12,28},{16,0},{20,4},{24,8},{28,12},{1,17},{... | collective-permute-start | bytes 245768 | tf_op jit(solution)/shard_map/ppermute | solution.py:22
  134.3 4.5 %collective-permute-start.34 = (f32[160,128]{1,0:T(8,128)S(1)}, f32[160,128]{1,0:T(8,128)S(1)}, u32[]{:S(2)}, u32[]{:S(2)}) collective-permute-start(f32[160,128]{1,0:T(8,128)S(1)} %add.37.refs_0_), channel_id=1, source_target_pairs={{0,8},{4,12},{8,0},{12,4},{16,24},{20,28},{24,16},{28,20},{1,9},{5... | collective-permute-start | bytes 245768 | tf_op jit(solution)/shard_map/ppermute | solution.py:22
  141.7 3.5 %collective-permute-start.39 = (f32[80,128]{1,0:T(8,128)S(1)}, f32[80,128]{1,0:T(8,128)S(1)}, u32[]{:S(2)}, u32[]{:S(2)}) collective-permute-start(f32[80,128]{1,0:T(8,128)S(1)} %shard_map.97.mine), channel_id=1, source_target_pairs={{0,3},{1,2},{2,1},{3,0},{4,7},{5,6},{6,5},{7,4},{8,11},{9,10},{10,... | collective-permute-start | bytes 122888 | tf_op jit(solution)/shard_map/ppermute | solution.py:22
  141.7 4.3 %collective-permute-start.38 = (f32[80,128]{1,0:T(8,128)S(1)}, f32[80,128]{1,0:T(8,128)S(1)}, u32[]{:S(2)}, u32[]{:S(2)}) collective-permute-start(f32[80,128]{1,0:T(8,128)S(1)} %shard_map.97.mine), channel_id=1, source_target_pairs={{0,2},{1,3},{2,0},{3,1},{4,6},{5,7},{6,4},{7,5},{8,10},{9,11},{10,... | collective-permute-start | bytes 122888 | tf_op jit(solution)/shard_map/ppermute | solution.py:22
  142.7 3.3 %collective-permute-start.37 = (f32[80,128]{1,0:T(8,128)S(1)}, f32[80,128]{1,0:T(8,128)S(1)}, u32[]{:S(2)}, u32[]{:S(2)}) collective-permute-start(f32[80,128]{1,0:T(8,128)S(1)} %shard_map.97.mine), channel_id=1, source_target_pairs={{0,1},{1,0},{2,3},{3,2},{4,5},{5,4},{6,7},{7,6},{8,9},{9,8},{10,11... | collective-permute-start | bytes 122888 | tf_op jit(solution)/shard_map/ppermute | solution.py:22

commit v2 on v1

--- a/solution.py
+++ b/solution.py
@@ -151,7 +151,17 @@
 
 def dot3(left, right, dims=NN):
     (lh, ll), (rh, rl) = left, right
-    return dot(lh, rh, dims) + dot(lh, rl, dims) + dot(ll, rh, dims)
+    at_left, at_right = dims[0][0][0], dims[0][1][0]
+    zero = jnp.zeros_like(rl)
+    wide = jnp.concatenate(
+        [
+            jnp.concatenate([rh, rh], axis=at_right),
+            jnp.concatenate([rl, zero], axis=at_right),
+        ],
+        axis=1 - at_right,
+    )
+    value = dot(jnp.concatenate([lh, ll], axis=at_left), wide, dims)
+    return value[:, :LANES] + value[:, LANES:]
 
 
 def exact(left, right, dims=NN):
@@ -267,40 +277,36 @@
     row = lax.broadcasted_iota(jnp.int32, (size, LANES), 0)
     lane = lax.broadcasted_iota(jnp.int32, (size, LANES), 1)
     scaled = gram * (1.0 / row_count)
+    unit = lax.rsqrt(jnp.broadcast_to(scaled[0:1, 0:1], (1, LANES)))
+    scaled = scaled * unit * unit
     diagonal = jnp.where(lane == row, 1.0 - mask, 0.0)
     work = jnp.where(lane < HALF, scaled + diagonal, jnp.where(lane - HALF == row, 1.0, 0.0))
-    step = 4
     done = []
-    for base in range(0, size, step):
-        start = base - base % SUBLANES
-        if base % SUBLANES == 0 and base:
-            work = work[SUBLANES:]
-        live = size - start
-        offset = base - start
+    for base in range(0, size, SUBLANES):
+        live = size - base
         columns = [
-            jnp.broadcast_to(work[:, base + k : base + k + 1], (live, LANES)) for k in range(step)
+            jnp.broadcast_to(work[:, base + k : base + k + 1], (live, LANES))
+            for k in range(SUBLANES)
         ]
-        factors, pivots = [], []
-        for k in range(step):
-            at = offset + k
-            column, pivot = columns[k], work[at : at + 1]
-            for m in range(k):
-                weight = factors[m][at : at + 1]
-                column = column - factors[m] * weight
-                pivot = pivot - pivots[m] * weight
-            scale = lax.rsqrt(column[at : at + 1])
-            factors.append(column * scale)
-            pivots.append(pivot * scale)
-        update = work
-        for k in range(step):
-            update = update - factors[k] * pivots[k]
-        place = lax.broadcasted_iota(jnp.int32, (live, LANES), 0)
-        work = jnp.where(place >= offset + step, update, work)
-        for k in range(step):
-            work = jnp.where(place == offset + k, pivots[k], work)
-        if offset + step == SUBLANES:
-            done.append(work[:SUBLANES])
-    return jnp.concatenate(done, axis=0)
+        pivots = [work[k : k + 1] for k in range(SUBLANES)]
+        for k in range(0, SUBLANES, 2):
+            first, second = columns[k], columns[k + 1]
+            a, b, c = first[k : k + 1], first[k + 1 : k + 2], second[k + 1 : k + 2]
+            root = lax.rsqrt(a)
+            next_root = lax.rsqrt(a * c - b * b) * (a * root)
+            ratio = b * (root * root)
+            columns[k : k + 2] = first * root, (second - first * ratio) * next_root
+            pivots[k : k + 2] = pivots[k] * root, (pivots[k + 1] - pivots[k] * ratio) * next_root
+            for m in range(k + 2, SUBLANES):
+                for at in (k, k + 1):
+                    weight = columns[at][m : m + 1]
+                    columns[m] = columns[m] - columns[at] * weight
+                    pivots[m] = pivots[m] - pivots[at] * weight
+        done.append(jnp.concatenate(pivots, axis=0))
+        work = work[SUBLANES:]
+        for k in range(SUBLANES):
+            work = work - columns[k][SUBLANES:] * pivots[k]
+    return jnp.concatenate(done, axis=0) * unit
 
 
 def project(raw, gram, mask, row_count, square):

time: 148 us -> 143 us (0.966)
  Pallas kernels: 32.1 us -> 24.7 us
  waiting for transfers between devices: 56.3 us -> 59.8 us
  starting transfers between devices: 53.4 us -> 51.8 us
    pallas_call x18, Pallas kernels: 32.1 us -> 24.7 us  [kernel_call(): pl.pallas_call(body, out_shape=outs, in_specs=specs[:len(operands)], out_...]
    ppermute x42, waiting for transfers between devices: 56.3 us -> 59.8 us  [flip(): lax.ppermute(value, axis, [(index, index ^ bits) for index in range(size)])]
    ppermute x42, starting transfers between devices: 49.4 us -> 47.8 us  [flip(): lax.ppermute(value, axis, [(index, index ^ bits) for index in range(size)])]
  transfers between devices with their start and end apart: 43 -> 43, of which waited for: 27 -> 27; matrix products, arithmetic and copies ran while one was open for 3% -> 3% of each run, Pallas kernels for 8% -> 6%
where the time goes in v2:
time: 143 us; the launch traced here: 142 us
  waiting for transfers between devices  59.8 us (42%)
  starting transfers between devices  51.8 us (36%)
  Pallas kernels  24.7 us (17%)
  local copies, waits for them, and re-layouts  4.9 us (3%)
    ppermute x42, waiting for transfers between devices, flip(): lax.ppermute(value, axis, [(index, index ^ bits) for index in range(size)])  59.8 us
    ppermute x42, starting transfers between devices, flip(): lax.ppermute(value, axis, [(index, index ^ bits) for index in range(size)])  47.8 us
    pallas_call x18, Pallas kernels, kernel_call(): pl.pallas_call(body, out_shape=outs, in_specs=specs[:len(operands)], out_...  24.7 us
    ppermute x1, starting transfers between devices, tiled(): sends.append(lax.ppermute(send, ('mode', 'rep'), pairs))  3.99 us
    dynamic_slice x2, local copies, waits for them, and re-layouts, half_of(): lax.dynamic_slice(source, (index, 0, position, 0, 0), (1, count, 1, slice...  2.95 us
  transfers between devices with their start and end apart: 43, of which 27 were waited for; matrix products, arithmetic and copies ran while one was open for 3% of the time, Pallas kernels for 6%

profile of v2, /device:TPU:0, one launch (start us, length us, event | category | flops | bytes accessed | tf_op | source)
XLA Modules:
  0.0 142.5 jit_solution(4521367382979213310)
XLA Ops:
  0.6 1.8 %shard_map.85 = (f32[80,128]{1,0:T(8,128)}, f32[96,128]{1,0:T(8,128)}) custom-call(s32[1]{0:T(128)} %bitcast.member.refs_5_, f32[2,2,16,64]{3,2,1,0:T(8,128)} %refs_6_.1, f32[2,2,16,64]{3,2,1,0:T(8,128)} %refs_1_.1, f32[16,64]{1,0:T(8,128)} %refs_2_.1), custom_call_target="tpu_custom_call" | custom-call | bytes 126980 | tf_op jit(solution)/shard_map/pallas_call | solution.py:479
  2.5 4.0 %collective-permute-start.2 = (f32[96,128]{1,0:T(8,128)}, f32[96,128]{1,0:T(8,128)S(1)}, u32[]{:S(2)}, u32[]{:S(2)}) collective-permute-start(f32[96,128]{1,0:T(8,128)} %get-tuple-element.35), channel_id=1, source_target_pairs={{0,6},{1,7},{2,4},{3,5},{4,2},{5,3},{6,0},{7,1},{8,14},{9,15},{10,... | collective-permute-start | bytes 147464 | tf_op jit(solution)/shard_map/ppermute | solution.py:574
  7.1 1.1 constant_dynamic-slice_fusion.4
  8.2 2.0 %collective-permute-start.6 = (f32[2,512,128]{2,1,0:T(8,128)S(1)}, f32[2,512,128]{2,1,0:T(8,128)S(1)}, u32[]{:S(2)}, u32[]{:S(2)}) collective-permute-start(f32[2,512,128]{2,1,0:T(8,128)S(1)} %bitcast.53), channel_id=1, source_target_pairs={{0,2},{1,3},{2,0},{3,1},{4,6},{5,7},{6,4},{7,5},{8,10},{9,11},{10,... | collective-permute-start | bytes 1572872 | tf_op jit(solution)/shard_map/ppermute | solution.py:22
  10.1 1.2 fusion
  12.1 1.9 %constant_dynamic-slice_fusion = (f32[1,2,1,16,4096]{4,3,2,1,0:T(8,128)S(1)}, f32[1,2,1,16,4096]{4,3,2,1,0:T(8,128)S(1)}, f32[1,2,1,16,4096]{4,3,2,1,0:T(8,128)S...) fusion(f32[2,2,3,16,4096]{4,3,2,1,0:T(8,128)} %param.7, s32[]{:T(128)S(6)} %select_n.17, s32[]{:T(128)S(6)} %select_n.16), kind=kLoop, calls=%fused_computation.2 | loop fusion | bytes 5242888 | tf_op jit(solution)/shard_map/dynamic_slice | solution.py:542
  14.0 1.4 collective-permute-start.11
  15.5 3.6 %collective-permute-start.5 = (f32[192,128]{1,0:T(8,128)S(1)}, f32[192,128]{1,0:T(8,128)S(1)}, u32[]{:S(2)}, u32[]{:S(2)}) collective-permute-start(f32[192,128]{1,0:T(8,128)S(1)} %shard_map.86.refs_0_.refs_4_), channel_id=1, source_target_pairs={{0,24},{4,28},{8,16},{12,20},{16,8},{20,12},{24,0},{28,4},{1,25},{... | collective-permute-start | bytes 294920 | tf_op jit(solution)/shard_map/ppermute | solution.py:22
  19.9 2.6 %collective-permute-done.5.refs_3_.refs_7_ = f32[192,128]{1,0:T(8,128)S(1)} collective-permute-done((f32[192,128]{1,0:T(8,128)S(1)}, f32[192,128]{1,0:T(8,128)S(1)}, u32[]{:S(2)}, u32[]{:S(2)}) %collective-permute-start.5) | collective-permute-done | bytes 98336 | tf_op jit(solution)/shard_map/ppermute | solution.py:22
  22.5 3.2 %collective-permute-start.3 = (f32[192,128]{1,0:T(8,128)S(1)}, f32[192,128]{1,0:T(8,128)S(1)}, u32[]{:S(2)}, u32[]{:S(2)}) collective-permute-start(f32[192,128]{1,0:T(8,128)S(1)} %shard_map.86.refs_0_.refs_4_), channel_id=1, source_target_pairs={{0,8},{4,12},{8,0},{12,4},{16,24},{20,28},{24,16},{28,20},{1,9},{5... | collective-permute-start | bytes 294920 | tf_op jit(solution)/shard_map/ppermute | solution.py:22
  26.4 1.9 %collective-permute-done.3.refs_1_.refs_5_ = f32[192,128]{1,0:T(8,128)S(1)} collective-permute-done((f32[192,128]{1,0:T(8,128)S(1)}, f32[192,128]{1,0:T(8,128)S(1)}, u32[]{:S(2)}, u32[]{:S(2)}) %collective-permute-start.3) | collective-permute-done | bytes 98336 | tf_op jit(solution)/shard_map/ppermute | solution.py:22
  28.3 1.4 shard_map.87
  30.2 3.8 %collective-permute-done.7 = f32[128,128]{1,0:T(8,128)S(1)} collective-permute-done((f32[128,128]{1,0:T(8,128)S(1)}, f32[128,128]{1,0:T(8,128)S(1)}, u32[]{:S(2)}, u32[]{:S(2)}) %collective-permute-start.7) | collective-permute-done | bytes 65568 | tf_op jit(solution)/shard_map/ppermute | solution.py:22
  34.0 2.9 %collective-permute-start.10 = (f32[128,128]{1,0:T(8,128)S(1)}, f32[128,128]{1,0:T(8,128)S(1)}, u32[]{:S(2)}, u32[]{:S(2)}) collective-permute-start(f32[128,128]{1,0:T(8,128)S(1)} %add.32.refs_0_), channel_id=1, source_target_pairs={{0,24},{4,28},{8,16},{12,20},{16,8},{20,12},{24,0},{28,4},{1,25},{... | collective-permute-start | bytes 196616 | tf_op jit(solution)/shard_map/ppermute | solution.py:22
  37.6 0.9 collective-permute-start.8
  38.5 1.8 %collective-permute-done.10.refs_3_ = f32[128,128]{1,0:T(8,128)S(1)} collective-permute-done((f32[128,128]{1,0:T(8,128)S(1)}, f32[128,128]{1,0:T(8,128)S(1)}, u32[]{:S(2)}, u32[]{:S(2)}) %collective-permute-start.10) | collective-permute-done | bytes 65568 | tf_op jit(solution)/shard_map/ppermute | solution.py:22
  40.3 2.5 %collective-permute-done.9.refs_2_ = f32[128,128]{1,0:T(8,128)S(1)} collective-permute-done((f32[128,128]{1,0:T(8,128)S(1)}, f32[128,128]{1,0:T(8,128)S(1)}, u32[]{:S(2)}, u32[]{:S(2)}) %collective-permute-start.9) | collective-permute-done | bytes 65568 | tf_op jit(solution)/shard_map/ppermute | solution.py:22
  42.8 1.4 shard_map.88
  44.2 1.1 collective-permute-start.12
  45.3 3.3 %collective-permute-done.12 = f32[128,128]{1,0:T(8,128)S(1)} collective-permute-done((f32[128,128]{1,0:T(8,128)S(1)}, f32[128,128]{1,0:T(8,128)S(1)}, u32[]{:S(2)}, u32[]{:S(2)}) %collective-permute-start.12) | collective-permute-done | bytes 65568 | tf_op jit(solution)/shard_map/ppermute | solution.py:22
  48.5 2.6 %collective-permute-start.15 = (f32[128,128]{1,0:T(8,128)S(1)}, f32[128,128]{1,0:T(8,128)S(1)}, u32[]{:S(2)}, u32[]{:S(2)}) collective-permute-start(f32[128,128]{1,0:T(8,128)S(1)} %add.33.refs_0_), channel_id=1, source_target_pairs={{0,24},{4,28},{8,16},{12,20},{16,8},{20,12},{24,0},{28,4},{1,25},{... | collective-permute-start | bytes 196616 | tf_op jit(solution)/shard_map/ppermute | solution.py:22
  51.2 1.8 %collective-permute-start.13 = (f32[128,128]{1,0:T(8,128)S(1)}, f32[128,128]{1,0:T(8,128)S(1)}, u32[]{:S(2)}, u32[]{:S(2)}) collective-permute-start(f32[128,128]{1,0:T(8,128)S(1)} %add.33.refs_0_), channel_id=1, source_target_pairs={{0,8},{4,12},{8,0},{12,4},{16,24},{20,28},{24,16},{28,20},{1,9},{5... | collective-permute-start | bytes 196616 | tf_op jit(solution)/shard_map/ppermute | solution.py:22
  53.0 1.7 %collective-permute-done.15.refs_3_ = f32[128,128]{1,0:T(8,128)S(1)} collective-permute-done((f32[128,128]{1,0:T(8,128)S(1)}, f32[128,128]{1,0:T(8,128)S(1)}, u32[]{:S(2)}, u32[]{:S(2)}) %collective-permute-start.15) | collective-permute-done | bytes 65568 | tf_op jit(solution)/shard_map/ppermute | solution.py:22
  54.7 2.1 %collective-permute-done.14.refs_2_ = f32[128,128]{1,0:T(8,128)S(1)} collective-permute-done((f32[128,128]{1,0:T(8,128)S(1)}, f32[128,128]{1,0:T(8,128)S(1)}, u32[]{:S(2)}, u32[]{:S(2)}) %collective-permute-start.14) | collective-permute-done | bytes 65568 | tf_op jit(solution)/shard_map/ppermute | solution.py:22
  56.8 1.4 shard_map.89
  58.2 1.3 collective-permute-start.17
  59.5 3.0 %collective-permute-done.17 = f32[128,128]{1,0:T(8,128)S(1)} collective-permute-done((f32[128,128]{1,0:T(8,128)S(1)}, f32[128,128]{1,0:T(8,128)S(1)}, u32[]{:S(2)}, u32[]{:S(2)}) %collective-permute-start.17) | collective-permute-done | bytes 65568 | tf_op jit(solution)/shard_map/ppermute | solution.py:22
  62.6 3.9 %collective-permute-start.20 = (f32[128,128]{1,0:T(8,128)S(1)}, f32[128,128]{1,0:T(8,128)S(1)}, u32[]{:S(2)}, u32[]{:S(2)}) collective-permute-start(f32[128,128]{1,0:T(8,128)S(1)} %add.34.refs_0_), channel_id=1, source_target_pairs={{0,24},{4,28},{8,16},{12,20},{16,8},{20,12},{24,0},{28,4},{1,25},{... | collective-permute-start | bytes 196616 | tf_op jit(solution)/shard_map/ppermute | solution.py:22
  67.1 1.6 %collective-permute-done.20.refs_3_ = f32[128,128]{1,0:T(8,128)S(1)} collective-permute-done((f32[128,128]{1,0:T(8,128)S(1)}, f32[128,128]{1,0:T(8,128)S(1)}, u32[]{:S(2)}, u32[]{:S(2)}) %collective-permute-start.20) | collective-permute-done | bytes 65568 | tf_op jit(solution)/shard_map/ppermute | solution.py:22
  68.7 2.9 %collective-permute-done.19.refs_2_ = f32[128,128]{1,0:T(8,128)S(1)} collective-permute-done((f32[128,128]{1,0:T(8,128)S(1)}, f32[128,128]{1,0:T(8,128)S(1)}, u32[]{:S(2)}, u32[]{:S(2)}) %collective-permute-start.19) | collective-permute-done | bytes 65568 | tf_op jit(solution)/shard_map/ppermute | solution.py:22
  72.0 1.2 collective-permute-done.21.other
  73.3 3.2 %shard_map.91 = (f32[64,128]{1,0:T(8,128)}, f32[128,128]{1,0:T(8,128)S(1)}, f32[16,128]{1,0:T(8,128)S(1)}, f32[512,128]{1,0:T(8,128)S(1)}) custom-call(f32[128,128]{1,0:T(8,128)S(1)} %shard_map.90.kept, f32[128,128]{1,0:T(8,128)S(1)} %collective-permute-done.21.other, f32[192,128]{1,0:T(8,128)S(1)} %shard_map.86.refs_0_.refs_4_, ...), custom_call_target="tpu_custom_call" | custom-call | bytes 1942016 | tf_op jit(solution)/shard_map/pallas_call | solution.py:479
  76.7 1.4 collective-permute-done.22.theirs
  78.1 1.3 shard_map.92
  79.5 4.4 %collective-permute-done.23 = f32[160,128]{1,0:T(8,128)S(1)} collective-permute-done((f32[160,128]{1,0:T(8,128)S(1)}, f32[160,128]{1,0:T(8,128)S(1)}, u32[]{:S(2)}, u32[]{:S(2)}) %collective-permute-start.23) | collective-permute-done | bytes 81952 | tf_op jit(solution)/shard_map/ppermute | solution.py:22
  83.9 1.7 %collective-permute-start.26 = (f32[160,128]{1,0:T(8,128)S(1)}, f32[160,128]{1,0:T(8,128)S(1)}, u32[]{:S(2)}, u32[]{:S(2)}) collective-permute-start(f32[160,128]{1,0:T(8,128)S(1)} %add.35.refs_0_), channel_id=1, source_target_pairs={{0,24},{4,28},{8,16},{12,20},{16,8},{20,12},{24,0},{28,4},{1,25},{... | collective-permute-start | bytes 245768 | tf_op jit(solution)/shard_map/ppermute | solution.py:22
  86.1 2.3 %collective-permute-start.24 = (f32[160,128]{1,0:T(8,128)S(1)}, f32[160,128]{1,0:T(8,128)S(1)}, u32[]{:S(2)}, u32[]{:S(2)}) collective-permute-start(f32[160,128]{1,0:T(8,128)S(1)} %add.35.refs_0_), channel_id=1, source_target_pairs={{0,8},{4,12},{8,0},{12,4},{16,24},{20,28},{24,16},{28,20},{1,9},{5... | collective-permute-start | bytes 245768 | tf_op jit(solution)/shard_map/ppermute | solution.py:22
  88.4 2.7 %collective-permute-done.26.refs_3_ = f32[160,128]{1,0:T(8,128)S(1)} collective-permute-done((f32[160,128]{1,0:T(8,128)S(1)}, f32[160,128]{1,0:T(8,128)S(1)}, u32[]{:S(2)}, u32[]{:S(2)}) %collective-permute-start.26) | collective-permute-done | bytes 81952 | tf_op jit(solution)/shard_map/ppermute | solution.py:22
  91.1 2.6 %collective-permute-done.25.refs_2_ = f32[160,128]{1,0:T(8,128)S(1)} collective-permute-done((f32[160,128]{1,0:T(8,128)S(1)}, f32[160,128]{1,0:T(8,128)S(1)}, u32[]{:S(2)}, u32[]{:S(2)}) %collective-permute-start.25) | collective-permute-done | bytes 81952 | tf_op jit(solution)/shard_map/ppermute | solution.py:22
  93.7 2.5 %shard_map.93 = (f32[64,128]{1,0:T(8,128)S(1)}, f32[128,128]{1,0:T(8,128)S(1)}, f32[512,128]{1,0:T(8,128)S(1)}) custom-call(f32[160,128]{1,0:T(8,128)S(1)} %add.35.refs_0_, f32[160,128]{1,0:T(8,128)S(1)} %collective-permute-done.24.refs_1_, f32[160,128]{1,0:T(8,128)S(1)} %collective-permute-done.25.refs_2_, f32[160,128]{1,0:T(8,128)S(1)} %collective-permute-done.26.refs_3_, ...), custom_call_target="tpu_custom_call" | custom-call | bytes 1737216 | tf_op jit(solution)/shard_map/pallas_call | solution.py:479
  96.2 1.5 %collective-permute-done.27.theirs = f32[512,128]{1,0:T(8,128)S(1)} collective-permute-done((f32[512,128]{1,0:T(8,128)S(1)}, f32[512,128]{1,0:T(8,128)S(1)}, u32[]{:S(2)}, u32[]{:S(2)}) %collective-permute-start.27) | collective-permute-done | bytes 262176 | tf_op jit(solution)/shard_map/ppermute | solution.py:22
  97.8 1.4 %shard_map.94 = (f32[512,128]{1,0:T(8,128)S(1)}, f32[160,128]{1,0:T(8,128)S(1)}) custom-call(f32[512,128]{1,0:T(8,128)S(1)} %get-tuple-element.48.mine, f32[512,128]{1,0:T(8,128)S(1)} %collective-permute-done.27.theirs, f32[128,128]{1,0:T(8,128)S(1)} %get-tuple-element.49.carried, f32[2,512,128]{2,1,0:T(8,128)S(1)} %bitcast.45, ...), custom_call_target="tpu_custom_call" | custom-call | bytes 1982464 | tf_op jit(solution)/shard_map/pallas_call | solution.py:479
  99.6 4.2 %collective-permute-done.28 = f32[160,128]{1,0:T(8,128)S(1)} collective-permute-done((f32[160,128]{1,0:T(8,128)S(1)}, f32[160,128]{1,0:T(8,128)S(1)}, u32[]{:S(2)}, u32[]{:S(2)}) %collective-permute-start.28) | collective-permute-done | bytes 81952 | tf_op jit(solution)/shard_map/ppermute | solution.py:22
  103.8 2.2 %collective-permute-start.31 = (f32[160,128]{1,0:T(8,128)S(1)}, f32[160,128]{1,0:T(8,128)S(1)}, u32[]{:S(2)}, u32[]{:S(2)}) collective-permute-start(f32[160,128]{1,0:T(8,128)S(1)} %add.36.refs_0_), channel_id=1, source_target_pairs={{0,24},{4,28},{8,16},{12,20},{16,8},{20,12},{24,0},{28,4},{1,25},{... | collective-permute-start | bytes 245768 | tf_op jit(solution)/shard_map/ppermute | solution.py:22
  106.0 2.2 %collective-permute-start.29 = (f32[160,128]{1,0:T(8,128)S(1)}, f32[160,128]{1,0:T(8,128)S(1)}, u32[]{:S(2)}, u32[]{:S(2)}) collective-permute-start(f32[160,128]{1,0:T(8,128)S(1)} %add.36.refs_0_), channel_id=1, source_target_pairs={{0,8},{4,12},{8,0},{12,4},{16,24},{20,28},{24,16},{28,20},{1,9},{5... | collective-permute-start | bytes 245768 | tf_op jit(solution)/shard_map/ppermute | solution.py:22
  108.2 2.4 %collective-permute-done.31.refs_3_ = f32[160,128]{1,0:T(8,128)S(1)} collective-permute-done((f32[160,128]{1,0:T(8,128)S(1)}, f32[160,128]{1,0:T(8,128)S(1)}, u32[]{:S(2)}, u32[]{:S(2)}) %collective-permute-start.31) | collective-permute-done | bytes 81952 | tf_op jit(solution)/shard_map/ppermute | solution.py:22
  110.6 2.1 %collective-permute-done.30.refs_2_ = f32[160,128]{1,0:T(8,128)S(1)} collective-permute-done((f32[160,128]{1,0:T(8,128)S(1)}, f32[160,128]{1,0:T(8,128)S(1)}, u32[]{:S(2)}, u32[]{:S(2)}) %collective-permute-start.30) | collective-permute-done | bytes 81952 | tf_op jit(solution)/shard_map/ppermute | solution.py:22
  112.8 2.5 %shard_map.95 = (f32[64,128]{1,0:T(8,128)S(1)}, f32[128,128]{1,0:T(8,128)S(1)}, f32[512,128]{1,0:T(8,128)S(1)}) custom-call(f32[160,128]{1,0:T(8,128)S(1)} %add.36.refs_0_, f32[160,128]{1,0:T(8,128)S(1)} %collective-permute-done.29.refs_1_, f32[160,128]{1,0:T(8,128)S(1)} %collective-permute-done.30.refs_2_, f32[160,128]{1,0:T(8,128)S(1)} %collective-permute-done.31.refs_3_, ...), custom_call_target="tpu_custom_call" | custom-call | bytes 1737216 | tf_op jit(solution)/shard_map/pallas_call | solution.py:479
  116.8 1.2 shard_map.96
  118.1 1.0 collective-permute-start.33
  119.4 1.2 collective-permute-start.41
  120.6 0.9 collective-permute-start.40
  121.5 1.1 collective-permute-done.33
  122.7 2.2 %collective-permute-start.36 = (f32[160,128]{1,0:T(8,128)S(1)}, f32[160,128]{1,0:T(8,128)S(1)}, u32[]{:S(2)}, u32[]{:S(2)}) collective-permute-start(f32[160,128]{1,0:T(8,128)S(1)} %add.37.refs_0_), channel_id=1, source_target_pairs={{0,24},{4,28},{8,16},{12,20},{16,8},{20,12},{24,0},{28,4},{1,25},{... | collective-permute-start | bytes 245768 | tf_op jit(solution)/shard_map/ppermute | solution.py:22
  124.9 4.3 %collective-permute-done.36.refs_3_ = f32[160,128]{1,0:T(8,128)S(1)} collective-permute-done((f32[160,128]{1,0:T(8,128)S(1)}, f32[160,128]{1,0:T(8,128)S(1)}, u32[]{:S(2)}, u32[]{:S(2)}) %collective-permute-start.36) | collective-permute-done | bytes 81952 | tf_op jit(solution)/shard_map/ppermute | solution.py:22
  129.1 2.3 %collective-permute-start.34 = (f32[160,128]{1,0:T(8,128)S(1)}, f32[160,128]{1,0:T(8,128)S(1)}, u32[]{:S(2)}, u32[]{:S(2)}) collective-permute-start(f32[160,128]{1,0:T(8,128)S(1)} %add.37.refs_0_), channel_id=1, source_target_pairs={{0,8},{4,12},{8,0},{12,4},{16,24},{20,28},{24,16},{28,20},{1,9},{5... | collective-permute-start | bytes 245768 | tf_op jit(solution)/shard_map/ppermute | solution.py:22
  131.5 0.8 collective-permute-done.35.refs_2_
  132.3 1.6 %collective-permute-done.34.refs_1_ = f32[160,128]{1,0:T(8,128)S(1)} collective-permute-done((f32[160,128]{1,0:T(8,128)S(1)}, f32[160,128]{1,0:T(8,128)S(1)}, u32[]{:S(2)}, u32[]{:S(2)}) %collective-permute-start.34) | collective-permute-done | bytes 81952 | tf_op jit(solution)/shard_map/ppermute | solution.py:22
  133.9 2.1 %shard_map.97.mine = f32[80,128]{1,0:T(8,128)S(1)} custom-call(f32[160,128]{1,0:T(8,128)S(1)} %add.37.refs_0_, f32[160,128]{1,0:T(8,128)S(1)} %collective-permute-done.34.refs_1_, f32[160,128]{1,0:T(8,128)S(1)} %collective-permute-done.35.refs_2_, f32[160,128]{1,0:T(8,128)S(1)} %collective-permute-done.36.refs_3_, f32[1,128]{1,0:T(1,128)S(1)} %get-tuple-element.76.refs_4_, ...), custom_call_target="tpu_custom_call" | custom-call | bytes 401924 | tf_op jit(solution)/shard_map/pallas_call | solution.py:479
  136.0 0.9 collective-permute-start.38
  136.9 0.9 collective-permute-start.37
  138.7 0.8 shard_map.101.before
  139.5 0.9 collective-permute-done.38.far
  140.5 1.8 %shard_map.102 = (f32[2,16,64]{2,1,0:T(8,128)}, f32[2,16,64]{2,1,0:T(8,128)}, f32[2,3,512,128]{3,2,1,0:T(8,128)}) custom-call(s32[1]{0:T(128)} %bitcast.member.refs_5_, f32[80,128]{1,0:T(8,128)S(1)} %shard_map.97.mine, f32[80,128]{1,0:T(8,128)S(1)} %collective-permute-done.37.near, ...), custom_call_target="tpu_custom_call", output_to_operand_aliasing={{2}: (7, {})} | custom-call | bytes 3850244 | tf_op jit(solution)/shard_map/pallas_call | solution.py:479
  (59 shorter events, 9.3 us)
Async XLA Ops:
  2.5 8.9 %collective-permute-start.2 = (f32[96,128]{1,0:T(8,128)}, f32[96,128]{1,0:T(8,128)S(1)}, u32[]{:S(2)}, u32[]{:S(2)}) collective-permute-start(f32[96,128]{1,0:T(8,128)} %get-tuple-element.35), channel_id=1, source_target_pairs={{0,6},{1,7},{2,4},{3,5},{4,2},{5,3},{6,0},{7,1},{8,14},{9,15},{10,... | collective-permute-start | bytes 147464 | tf_op jit(solution)/shard_map/ppermute | solution.py:574
  6.4 4.9 %collective-permute-start.1 = (f32[96,128]{1,0:T(8,128)}, f32[96,128]{1,0:T(8,128)S(1)}, u32[]{:S(2)}, u32[]{:S(2)}) collective-permute-start(f32[96,128]{1,0:T(8,128)} %get-tuple-element.35), channel_id=1, source_target_pairs={{0,2},{1,3},{2,0},{3,1},{4,6},{5,7},{6,4},{7,5},{8,10},{9,11},{10,... | collective-permute-start | bytes 147464 | tf_op jit(solution)/shard_map/ppermute | solution.py:22
  7.0 4.3 %collective-permute-start = (f32[80,128]{1,0:T(8,128)}, f32[80,128]{1,0:T(8,128)S(1)}, u32[]{:S(2)}, u32[]{:S(2)}) collective-permute-start(f32[80,128]{1,0:T(8,128)} %get-tuple-element.34.refs_0_), channel_id=1, source_target_pairs={{0,4},{4,0},{8,12},{12,8},{16,20},{20,16},{24,28},{28,24},{1,5},{5... | collective-permute-start | bytes 122888 | tf_op jit(solution)/shard_map/ppermute | solution.py:22
  8.2 20.1 %collective-permute-start.6 = (f32[2,512,128]{2,1,0:T(8,128)S(1)}, f32[2,512,128]{2,1,0:T(8,128)S(1)}, u32[]{:S(2)}, u32[]{:S(2)}) collective-permute-start(f32[2,512,128]{2,1,0:T(8,128)S(1)} %bitcast.53), channel_id=1, source_target_pairs={{0,2},{1,3},{2,0},{3,1},{4,6},{5,7},{6,4},{7,5},{8,10},{9,11},{10,... | collective-permute-start | bytes 1572872 | tf_op jit(solution)/shard_map/ppermute | solution.py:22
  11.3 4.2 %copy-start.2 = (s32[4]{0:T(128)S(1)}, s32[4]{0:T(128)}, u32[]{:S(2)}) copy-start(s32[4]{0:T(128)} %param.11) | copy-start | bytes 52
  11.3 0.8 copy-start.1
  14.0 24.5 %collective-permute-start.11 = (f32[2,512,128]{2,1,0:T(8,128)S(1)}, f32[2,512,128]{2,1,0:T(8,128)S(1)}, u32[]{:S(2)}, u32[]{:S(2)}) collective-permute-start(f32[2,512,128]{2,1,0:T(8,128)S(1)} %bitcast.55), channel_id=1, source_target_pairs={{0,2},{1,3},{2,0},{3,1},{4,6},{5,7},{6,4},{7,5},{8,10},{9,11},{10,... | collective-permute-start | bytes 1572872 | tf_op jit(solution)/shard_map/ppermute | solution.py:22
  15.5 7.0 %collective-permute-start.5 = (f32[192,128]{1,0:T(8,128)S(1)}, f32[192,128]{1,0:T(8,128)S(1)}, u32[]{:S(2)}, u32[]{:S(2)}) collective-permute-start(f32[192,128]{1,0:T(8,128)S(1)} %shard_map.86.refs_0_.refs_4_), channel_id=1, source_target_pairs={{0,24},{4,28},{8,16},{12,20},{16,8},{20,12},{24,0},{28,4},{1,25},{... | collective-permute-start | bytes 294920 | tf_op jit(solution)/shard_map/ppermute | solution.py:22
  19.1 33.9 %collective-permute-start.16 = (f32[2,512,128]{2,1,0:T(8,128)S(1)}, f32[2,512,128]{2,1,0:T(8,128)S(1)}, u32[]{:S(2)}, u32[]{:S(2)}) collective-permute-start(f32[2,512,128]{2,1,0:T(8,128)S(1)} %bitcast.54), channel_id=1, source_target_pairs={{0,2},{1,3},{2,0},{3,1},{4,6},{5,7},{6,4},{7,5},{8,10},{9,11},{10,... | collective-permute-start | bytes 1572872 | tf_op jit(solution)/shard_map/ppermute | solution.py:22
  19.9 6.5 %collective-permute-start.4 = (f32[192,128]{1,0:T(8,128)S(1)}, f32[192,128]{1,0:T(8,128)S(1)}, u32[]{:S(2)}, u32[]{:S(2)}) collective-permute-start(f32[192,128]{1,0:T(8,128)S(1)} %shard_map.86.refs_0_.refs_4_), channel_id=1, source_target_pairs={{0,16},{4,20},{8,24},{12,28},{16,0},{20,4},{24,8},{28,12},{1,17},{... | collective-permute-start | bytes 294920 | tf_op jit(solution)/shard_map/ppermute | solution.py:22
  22.5 5.8 %collective-permute-start.3 = (f32[192,128]{1,0:T(8,128)S(1)}, f32[192,128]{1,0:T(8,128)S(1)}, u32[]{:S(2)}, u32[]{:S(2)}) collective-permute-start(f32[192,128]{1,0:T(8,128)S(1)} %shard_map.86.refs_0_.refs_4_), channel_id=1, source_target_pairs={{0,8},{4,12},{8,0},{12,4},{16,24},{20,28},{24,16},{28,20},{1,9},{5... | collective-permute-start | bytes 294920 | tf_op jit(solution)/shard_map/ppermute | solution.py:22
  29.7 4.3 %collective-permute-start.7 = (f32[128,128]{1,0:T(8,128)S(1)}, f32[128,128]{1,0:T(8,128)S(1)}, u32[]{:S(2)}, u32[]{:S(2)}) collective-permute-start(f32[128,128]{1,0:T(8,128)S(1)} %get-tuple-element.38), channel_id=1, source_target_pairs={{0,4},{4,0},{8,12},{12,8},{16,20},{20,16},{24,28},{28,24},{1,5},{5... | collective-permute-start | bytes 196616 | tf_op jit(solution)/shard_map/ppermute | solution.py:22
  34.0 6.2 %collective-permute-start.10 = (f32[128,128]{1,0:T(8,128)S(1)}, f32[128,128]{1,0:T(8,128)S(1)}, u32[]{:S(2)}, u32[]{:S(2)}) collective-permute-start(f32[128,128]{1,0:T(8,128)S(1)} %add.32.refs_0_), channel_id=1, source_target_pairs={{0,24},{4,28},{8,16},{12,20},{16,8},{20,12},{24,0},{28,4},{1,25},{... | collective-permute-start | bytes 196616 | tf_op jit(solution)/shard_map/ppermute | solution.py:22
  36.9 5.9 %collective-permute-start.9 = (f32[128,128]{1,0:T(8,128)S(1)}, f32[128,128]{1,0:T(8,128)S(1)}, u32[]{:S(2)}, u32[]{:S(2)}) collective-permute-start(f32[128,128]{1,0:T(8,128)S(1)} %add.32.refs_0_), channel_id=1, source_target_pairs={{0,16},{4,20},{8,24},{12,28},{16,0},{20,4},{24,8},{28,12},{1,17},{... | collective-permute-start | bytes 196616 | tf_op jit(solution)/shard_map/ppermute | solution.py:22
  37.6 5.2 %collective-permute-start.8 = (f32[128,128]{1,0:T(8,128)S(1)}, f32[128,128]{1,0:T(8,128)S(1)}, u32[]{:S(2)}, u32[]{:S(2)}) collective-permute-start(f32[128,128]{1,0:T(8,128)S(1)} %add.32.refs_0_), channel_id=1, source_target_pairs={{0,8},{4,12},{8,0},{12,4},{16,24},{20,28},{24,16},{28,20},{1,9},{5... | collective-permute-start | bytes 196616 | tf_op jit(solution)/shard_map/ppermute | solution.py:22
  44.2 4.3 %collective-permute-start.12 = (f32[128,128]{1,0:T(8,128)S(1)}, f32[128,128]{1,0:T(8,128)S(1)}, u32[]{:S(2)}, u32[]{:S(2)}) collective-permute-start(f32[128,128]{1,0:T(8,128)S(1)} %get-tuple-element.39), channel_id=1, source_target_pairs={{0,4},{4,0},{8,12},{12,8},{16,20},{20,16},{24,28},{28,24},{1,5},{5... | collective-permute-start | bytes 196616 | tf_op jit(solution)/shard_map/ppermute | solution.py:22
  48.5 6.1 %collective-permute-start.15 = (f32[128,128]{1,0:T(8,128)S(1)}, f32[128,128]{1,0:T(8,128)S(1)}, u32[]{:S(2)}, u32[]{:S(2)}) collective-permute-start(f32[128,128]{1,0:T(8,128)S(1)} %add.33.refs_0_), channel_id=1, source_target_pairs={{0,24},{4,28},{8,16},{12,20},{16,8},{20,12},{24,0},{28,4},{1,25},{... | collective-permute-start | bytes 196616 | tf_op jit(solution)/shard_map/ppermute | solution.py:22
  51.1 5.7 %collective-permute-start.14 = (f32[128,128]{1,0:T(8,128)S(1)}, f32[128,128]{1,0:T(8,128)S(1)}, u32[]{:S(2)}, u32[]{:S(2)}) collective-permute-start(f32[128,128]{1,0:T(8,128)S(1)} %add.33.refs_0_), channel_id=1, source_target_pairs={{0,16},{4,20},{8,24},{12,28},{16,0},{20,4},{24,8},{28,12},{1,17},{... | collective-permute-start | bytes 196616 | tf_op jit(solution)/shard_map/ppermute | solution.py:22
  51.2 5.7 %collective-permute-start.13 = (f32[128,128]{1,0:T(8,128)S(1)}, f32[128,128]{1,0:T(8,128)S(1)}, u32[]{:S(2)}, u32[]{:S(2)}) collective-permute-start(f32[128,128]{1,0:T(8,128)S(1)} %add.33.refs_0_), channel_id=1, source_target_pairs={{0,8},{4,12},{8,0},{12,4},{16,24},{20,28},{24,16},{28,20},{1,9},{5... | collective-permute-start | bytes 196616 | tf_op jit(solution)/shard_map/ppermute | solution.py:22
  58.2 4.3 %collective-permute-start.17 = (f32[128,128]{1,0:T(8,128)S(1)}, f32[128,128]{1,0:T(8,128)S(1)}, u32[]{:S(2)}, u32[]{:S(2)}) collective-permute-start(f32[128,128]{1,0:T(8,128)S(1)} %get-tuple-element.40), channel_id=1, source_target_pairs={{0,4},{4,0},{8,12},{12,8},{16,20},{20,16},{24,28},{28,24},{1,5},{5... | collective-permute-start | bytes 196616 | tf_op jit(solution)/shard_map/ppermute | solution.py:22
  62.6 6.1 %collective-permute-start.20 = (f32[128,128]{1,0:T(8,128)S(1)}, f32[128,128]{1,0:T(8,128)S(1)}, u32[]{:S(2)}, u32[]{:S(2)}) collective-permute-start(f32[128,128]{1,0:T(8,128)S(1)} %add.34.refs_0_), channel_id=1, source_target_pairs={{0,24},{4,28},{8,16},{12,20},{16,8},{20,12},{24,0},{28,4},{1,25},{... | collective-permute-start | bytes 196616 | tf_op jit(solution)/shard_map/ppermute | solution.py:22
  66.4 5.2 %collective-permute-start.19 = (f32[128,128]{1,0:T(8,128)S(1)}, f32[128,128]{1,0:T(8,128)S(1)}, u32[]{:S(2)}, u32[]{:S(2)}) collective-permute-start(f32[128,128]{1,0:T(8,128)S(1)} %add.34.refs_0_), channel_id=1, source_target_pairs={{0,16},{4,20},{8,24},{12,28},{16,0},{20,4},{24,8},{28,12},{1,17},{... | collective-permute-start | bytes 196616 | tf_op jit(solution)/shard_map/ppermute | solution.py:22
  66.5 5.2 %collective-permute-start.18 = (f32[128,128]{1,0:T(8,128)S(1)}, f32[128,128]{1,0:T(8,128)S(1)}, u32[]{:S(2)}, u32[]{:S(2)}) collective-permute-start(f32[128,128]{1,0:T(8,128)S(1)} %add.34.refs_0_), channel_id=1, source_target_pairs={{0,8},{4,12},{8,0},{12,4},{16,24},{20,28},{24,16},{28,20},{1,9},{5... | collective-permute-start | bytes 196616 | tf_op jit(solution)/shard_map/ppermute | solution.py:22
  72.0 1.3 collective-permute-start.21
  76.5 1.5 %collective-permute-start.22 = (f32[512,128]{1,0:T(8,128)S(1)}, f32[512,128]{1,0:T(8,128)S(1)}, u32[]{:S(2)}, u32[]{:S(2)}) collective-permute-start(f32[512,128]{1,0:T(8,128)S(1)} %get-tuple-element.43.mine), channel_id=1, source_target_pairs={{0,1},{1,0},{2,3},{3,2},{4,5},{5,4},{6,7},{7,6},{8,9},{9,8},{10,11... | collective-permute-start | bytes 786440 | tf_op jit(solution)/shard_map/ppermute | solution.py:22
  79.3 4.6 %collective-permute-start.23 = (f32[160,128]{1,0:T(8,128)S(1)}, f32[160,128]{1,0:T(8,128)S(1)}, u32[]{:S(2)}, u32[]{:S(2)}) collective-permute-start(f32[160,128]{1,0:T(8,128)S(1)} %get-tuple-element.45), channel_id=1, source_target_pairs={{0,4},{4,0},{8,12},{12,8},{16,20},{20,16},{24,28},{28,24},{1,5},{5... | collective-permute-start | bytes 245768 | tf_op jit(solution)/shard_map/ppermute | solution.py:22
  83.9 7.2 %collective-permute-start.26 = (f32[160,128]{1,0:T(8,128)S(1)}, f32[160,128]{1,0:T(8,128)S(1)}, u32[]{:S(2)}, u32[]{:S(2)}) collective-permute-start(f32[160,128]{1,0:T(8,128)S(1)} %add.35.refs_0_), channel_id=1, source_target_pairs={{0,24},{4,28},{8,16},{12,20},{16,8},{20,12},{24,0},{28,4},{1,25},{... | collective-permute-start | bytes 245768 | tf_op jit(solution)/shard_map/ppermute | solution.py:22
  85.6 8.1 %collective-permute-start.25 = (f32[160,128]{1,0:T(8,128)S(1)}, f32[160,128]{1,0:T(8,128)S(1)}, u32[]{:S(2)}, u32[]{:S(2)}) collective-permute-start(f32[160,128]{1,0:T(8,128)S(1)} %add.35.refs_0_), channel_id=1, source_target_pairs={{0,16},{4,20},{8,24},{12,28},{16,0},{20,4},{24,8},{28,12},{1,17},{... | collective-permute-start | bytes 245768 | tf_op jit(solution)/shard_map/ppermute | solution.py:22
  86.1 7.6 %collective-permute-start.24 = (f32[160,128]{1,0:T(8,128)S(1)}, f32[160,128]{1,0:T(8,128)S(1)}, u32[]{:S(2)}, u32[]{:S(2)}) collective-permute-start(f32[160,128]{1,0:T(8,128)S(1)} %add.35.refs_0_), channel_id=1, source_target_pairs={{0,8},{4,12},{8,0},{12,4},{16,24},{20,28},{24,16},{28,20},{1,9},{5... | collective-permute-start | bytes 245768 | tf_op jit(solution)/shard_map/ppermute | solution.py:22
  96.2 1.6 %collective-permute-start.27 = (f32[512,128]{1,0:T(8,128)S(1)}, f32[512,128]{1,0:T(8,128)S(1)}, u32[]{:S(2)}, u32[]{:S(2)}) collective-permute-start(f32[512,128]{1,0:T(8,128)S(1)} %get-tuple-element.48.mine), channel_id=1, source_target_pairs={{0,1},{1,0},{2,3},{3,2},{4,5},{5,4},{6,7},{7,6},{8,9},{9,8},{10,11... | collective-permute-start | bytes 786440 | tf_op jit(solution)/shard_map/ppermute | solution.py:22
  97.8 36.1 %copy-start = (f32[2,2,16,64]{3,2,1,0:T(8,128)S(1)}, f32[2,2,16,64]{3,2,1,0:T(8,128)}, u32[]{:S(2)}) copy-start(f32[2,2,16,64]{3,2,1,0:T(8,128)} %refs_6_.1) | copy-start | bytes 49156
  99.2 4.5 %collective-permute-start.28 = (f32[160,128]{1,0:T(8,128)S(1)}, f32[160,128]{1,0:T(8,128)S(1)}, u32[]{:S(2)}, u32[]{:S(2)}) collective-permute-start(f32[160,128]{1,0:T(8,128)S(1)} %get-tuple-element.50), channel_id=1, source_target_pairs={{0,4},{4,0},{8,12},{12,8},{16,20},{20,16},{24,28},{28,24},{1,5},{5... | collective-permute-start | bytes 245768 | tf_op jit(solution)/shard_map/ppermute | solution.py:22
  103.8 6.9 %collective-permute-start.31 = (f32[160,128]{1,0:T(8,128)S(1)}, f32[160,128]{1,0:T(8,128)S(1)}, u32[]{:S(2)}, u32[]{:S(2)}) collective-permute-start(f32[160,128]{1,0:T(8,128)S(1)} %add.36.refs_0_), channel_id=1, source_target_pairs={{0,24},{4,28},{8,16},{12,20},{16,8},{20,12},{24,0},{28,4},{1,25},{... | collective-permute-start | bytes 245768 | tf_op jit(solution)/shard_map/ppermute | solution.py:22
  106.0 6.8 %collective-permute-start.30 = (f32[160,128]{1,0:T(8,128)S(1)}, f32[160,128]{1,0:T(8,128)S(1)}, u32[]{:S(2)}, u32[]{:S(2)}) collective-permute-start(f32[160,128]{1,0:T(8,128)S(1)} %add.36.refs_0_), channel_id=1, source_target_pairs={{0,16},{4,20},{8,24},{12,28},{16,0},{20,4},{24,8},{28,12},{1,17},{... | collective-permute-start | bytes 245768 | tf_op jit(solution)/shard_map/ppermute | solution.py:22
  106.0 6.8 %collective-permute-start.29 = (f32[160,128]{1,0:T(8,128)S(1)}, f32[160,128]{1,0:T(8,128)S(1)}, u32[]{:S(2)}, u32[]{:S(2)}) collective-permute-start(f32[160,128]{1,0:T(8,128)S(1)} %add.36.refs_0_), channel_id=1, source_target_pairs={{0,8},{4,12},{8,0},{12,4},{16,24},{20,28},{24,16},{28,20},{1,9},{5... | collective-permute-start | bytes 245768 | tf_op jit(solution)/shard_map/ppermute | solution.py:22
  115.3 1.6 %collective-permute-start.32 = (f32[512,128]{1,0:T(8,128)S(1)}, f32[512,128]{1,0:T(8,128)S(1)}, u32[]{:S(2)}, u32[]{:S(2)}) collective-permute-start(f32[512,128]{1,0:T(8,128)S(1)} %get-tuple-element.53.mine), channel_id=1, source_target_pairs={{0,1},{1,0},{2,3},{3,2},{4,5},{5,4},{6,7},{7,6},{8,9},{9,8},{10,11... | collective-permute-start | bytes 786440 | tf_op jit(solution)/shard_map/ppermute | solution.py:22
  115.6 21.3 %collective-permute-start.42 = (f32[512,128]{1,0:T(8,128)S(1)}, f32[512,128]{1,0:T(8,128)S(1)}, u32[]{:S(2)}, u32[]{:S(2)}) collective-permute-start(f32[512,128]{1,0:T(8,128)S(1)} %shard_map.99.mine), channel_id=1, source_target_pairs={{0,2},{1,3},{2,0},{3,1},{4,6},{5,7},{6,4},{7,5},{8,10},{9,11},{10,... | collective-permute-start | bytes 786440 | tf_op jit(solution)/shard_map/ppermute | solution.py:22
  118.1 4.5 %collective-permute-start.33 = (f32[160,128]{1,0:T(8,128)S(1)}, f32[160,128]{1,0:T(8,128)S(1)}, u32[]{:S(2)}, u32[]{:S(2)}) collective-permute-start(f32[160,128]{1,0:T(8,128)S(1)} %get-tuple-element.55), channel_id=1, source_target_pairs={{0,4},{4,0},{8,12},{12,8},{16,20},{20,16},{24,28},{28,24},{1,5},{5... | collective-permute-start | bytes 245768 | tf_op jit(solution)/shard_map/ppermute | solution.py:22
  119.4 19.3 %collective-permute-start.41 = (f32[512,128]{1,0:T(8,128)S(1)}, f32[512,128]{1,0:T(8,128)S(1)}, u32[]{:S(2)}, u32[]{:S(2)}) collective-permute-start(f32[512,128]{1,0:T(8,128)S(1)} %shard_map.98.mine), channel_id=1, source_target_pairs={{0,2},{1,3},{2,0},{3,1},{4,6},{5,7},{6,4},{7,5},{8,10},{9,11},{10,... | collective-permute-start | bytes 786440 | tf_op jit(solution)/shard_map/ppermute | solution.py:22
  120.6 19.9 %collective-permute-start.40 = (f32[512,128]{1,0:T(8,128)S(1)}, f32[512,128]{1,0:T(8,128)S(1)}, u32[]{:S(2)}, u32[]{:S(2)}) collective-permute-start(f32[512,128]{1,0:T(8,128)S(1)} %get-tuple-element.57.mixture), channel_id=1, source_target_pairs={{0,2},{1,3},{2,0},{3,1},{4,6},{5,7},{6,4},{7,5},{8,10},{9,11},{10,... | collective-permute-start | bytes 786440 | tf_op jit(solution)/shard_map/ppermute | solution.py:22
  122.7 6.5 %collective-permute-start.36 = (f32[160,128]{1,0:T(8,128)S(1)}, f32[160,128]{1,0:T(8,128)S(1)}, u32[]{:S(2)}, u32[]{:S(2)}) collective-permute-start(f32[160,128]{1,0:T(8,128)S(1)} %add.37.refs_0_), channel_id=1, source_target_pairs={{0,24},{4,28},{8,16},{12,20},{16,8},{20,12},{24,0},{28,4},{1,25},{... | collective-permute-start | bytes 245768 | tf_op jit(solution)/shard_map/ppermute | solution.py:22
  124.9 7.4 %collective-permute-start.35 = (f32[160,128]{1,0:T(8,128)S(1)}, f32[160,128]{1,0:T(8,128)S(1)}, u32[]{:S(2)}, u32[]{:S(2)}) collective-permute-start(f32[160,128]{1,0:T(8,128)S(1)} %add.37.refs_0_), channel_id=1, source_target_pairs={{0,16},{4,20},{8,24},{12,28},{16,0},{20,4},{24,8},{28,12},{1,17},{... | collective-permute-start | bytes 245768 | tf_op jit(solution)/shard_map/ppermute | solution.py:22
  129.1 4.8 %collective-permute-start.34 = (f32[160,128]{1,0:T(8,128)S(1)}, f32[160,128]{1,0:T(8,128)S(1)}, u32[]{:S(2)}, u32[]{:S(2)}) collective-permute-start(f32[160,128]{1,0:T(8,128)S(1)} %add.37.refs_0_), channel_id=1, source_target_pairs={{0,8},{4,12},{8,0},{12,4},{16,24},{20,28},{24,16},{28,20},{1,9},{5... | collective-permute-start | bytes 245768 | tf_op jit(solution)/shard_map/ppermute | solution.py:22
  136.0 3.5 %collective-permute-start.39 = (f32[80,128]{1,0:T(8,128)S(1)}, f32[80,128]{1,0:T(8,128)S(1)}, u32[]{:S(2)}, u32[]{:S(2)}) collective-permute-start(f32[80,128]{1,0:T(8,128)S(1)} %shard_map.97.mine), channel_id=1, source_target_pairs={{0,3},{1,2},{2,1},{3,0},{4,7},{5,6},{6,5},{7,4},{8,11},{9,10},{10,... | collective-permute-start | bytes 122888 | tf_op jit(solution)/shard_map/ppermute | solution.py:22
  136.0 4.5 %collective-permute-start.38 = (f32[80,128]{1,0:T(8,128)S(1)}, f32[80,128]{1,0:T(8,128)S(1)}, u32[]{:S(2)}, u32[]{:S(2)}) collective-permute-start(f32[80,128]{1,0:T(8,128)S(1)} %shard_map.97.mine), channel_id=1, source_target_pairs={{0,2},{1,3},{2,0},{3,1},{4,6},{5,7},{6,4},{7,5},{8,10},{9,11},{10,... | collective-permute-start | bytes 122888 | tf_op jit(solution)/shard_map/ppermute | solution.py:22
  136.9 3.5 %collective-permute-start.37 = (f32[80,128]{1,0:T(8,128)S(1)}, f32[80,128]{1,0:T(8,128)S(1)}, u32[]{:S(2)}, u32[]{:S(2)}) collective-permute-start(f32[80,128]{1,0:T(8,128)S(1)} %shard_map.97.mine), channel_id=1, source_target_pairs={{0,1},{1,0},{2,3},{3,2},{4,5},{5,4},{6,7},{7,6},{8,9},{9,8},{10,11... | collective-permute-start | bytes 122888 | tf_op jit(solution)/shard_map/ppermute | solution.py:22

commit v3 on v2

--- a/solution.py
+++ b/solution.py
@@ -232,9 +232,7 @@
     return value
 
 
-def sketch_kernel(n_parts, *refs):
-    parts, refs = refs[:n_parts], refs[n_parts:]
-    mask, kept, other, sketch, out, high, low, wide, product, narrow = refs
+def sketch_step(parts, mask, kept, other, sketch, high, low, wide, product, narrow):
     count = kept.shape[0]
     rows = kept.shape[1]
     tiles = rows // 256
@@ -250,7 +248,7 @@
                     tile * 256 : (tile + 1) * 256
                 ]
     height = 2 * count * 32
-    total_value = jnp.zeros(out.shape, jnp.float32)
+    total_value = None
     for tile in range(tiles):
         for sub in range(SUBLANES):
             i = tile * SUBLANES + sub
@@ -259,17 +257,47 @@
             own = split(product[pl.ds(tile * height * SUBLANES + sub, height, stride=SUBLANES), :])
             high[i] = own[0]
             low[i] = own[1]
-            total_value = total_value + dot3(own, weight, NT)
-    out[...] = total_value
-
-
-def first_kernel(n_parts, *refs):
+            term = dot3(own, weight, NT)
+            total_value = term if total_value is None else total_value + term
+    return total_value
+
+
+def sketch_kernel(n_parts, *refs):
     parts, refs = refs[:n_parts], refs[n_parts:]
-    heads, (mask, out, wide) = refs[:n_parts], refs[n_parts:]
-    natural = spread_rows(added(parts) * mask[...], wide)
+    mask, kept, other, sketch, out, *rest = refs
+    out[...] = sketch_step(parts, mask, kept, other, sketch, *rest)
+
+
+SHIFTS = (1, 3, 2)
+
+
+def slice_blocks(spot, n_inner, n_outer):
+    inner, outer = spot % n_inner, spot // n_inner
+    return [
+        (outer + n_outer - by) % n_outer * n_inner + (inner ^ step)
+        for by in (0,) + SHIFTS
+        for step in range(n_inner)
+    ]
+
+
+def block_rows(block, count):
+    return pl.ds(pl.multiple_of(block * count, SUBLANES), count)
+
+
+def first_kernel(n_parts, *refs, slices):
+    parts, heads, refs = refs[:n_parts], refs[n_parts : 2 * n_parts], refs[2 * n_parts :]
+    spot, mask, next_mask, kept, other, sketch, out, *rest = refs
+    value = sketch_step(parts, mask, kept, other, sketch, *rest)
+    natural = spread_rows(value * next_mask[...], rest[2])
     natural = pick(natural, jnp.zeros_like(natural))
     value = exact(heads_of(heads, 0), natural[:LANES])
-    out[...] = value + exact(heads_of(heads, 1), natural[LANES:])
+    value = value + exact(heads_of(heads, 1), natural[LANES:])
+    shared = rest[2]
+    blocks = slice_blocks(spot[0], LANES // slices // n_parts, n_parts)
+    for at, block in enumerate(blocks):
+        shared[block_rows(block, slices), :] = value[at * slices : (at + 1) * slices]
+    value = shared[pl.ds(0, LANES), :]
+    out[...] = pick(value[:HALF], swap(value[HALF:]))
 
 
 def eliminate(gram, mask, row_count):
@@ -341,10 +369,15 @@
     return jnp.concatenate([packed, swap(packed)], axis=0)
 
 
-def bond_one_kernel(row_count, n_parts, kept, other, *refs):
-    heads, (mask, high, low, *refs) = refs[:n_parts], refs[n_parts:]
-    inverse, carried, basis, out, square = refs
-    mixture = kept[...] + other[...]
+def bond_one_kernel(row_count, n_parts, *refs):
+    parts, heads, refs = refs[:n_parts], refs[n_parts : 2 * n_parts], refs[2 * n_parts :]
+    spot, mask, high, low, inverse, carried, basis, out, square = refs
+    packed = added(parts)
+    zero = jnp.zeros_like(packed)
+    square[...] = jnp.concatenate([pick(packed, zero), pick(swap(packed), zero)], axis=0)
+    slices = basis.shape[0]
+    blocks = slice_blocks(spot[0], LANES // slices // n_parts, n_parts)
+    mixture = jnp.concatenate([square[block_rows(block, slices), :] for block in blocks], axis=0)
     gram = exact(mixture, mixture, TN)[:HALF]
     raw = []
     for pair in range(2):
@@ -353,7 +386,6 @@
     solved, moved = project(jnp.concatenate(raw, axis=0), gram, mask[...], row_count, square)
     inverse[...] = solved
     carried[...] = moved
-    slices = basis.shape[0]
     full = jnp.concatenate([pick(solved, jnp.zeros_like(solved)), jnp.zeros_like(solved)], axis=0)
     basis[...] = exact(mixture[:slices], full, NT)
     mix(moved, high, low, out)
@@ -403,19 +435,31 @@
         copy.wait()
 
 
-def final_kernel(position, member, mine, near, far, across, mixture, away, before, *refs):
+def own_kernel(position, member, mine, mixture, before, *refs):
+    out, block, sem = refs
+    slices = mine.shape[0] - HALF
+    weight = split(block_diagonal(mine[pl.ds(slices, HALF), :]))
+    block[...] = dot3(split(mixture[...]), weight, NT)
+    copy = pltpu.make_async_copy(block, out.at[member[0], position], sem)
+    copy.start()
+    copy.wait()
+
+
+def final_kernel(position, member, mine, near, far, across, away, before, *refs):
     first, last, out, blocks, sems = refs
     here = member[0]
     slices = first.shape[1]
+    weight = split(block_diagonal(far[pl.ds(slices, HALF), :]))
+    count = blocks.shape[0]
+    height = away.shape[0] // count
     copies = []
-    for at, (place, value, terms) in enumerate(
-        ((here, mixture, (mine, near)), (1 - here, away, (far, across)))
-    ):
-        weight = split(block_diagonal(terms[0][pl.ds(slices, HALF), :]))
-        blocks[at] = dot3(split(value[...]), weight, NT)
-        copy = pltpu.make_async_copy(blocks.at[at], out.at[place, position], sems.at[at])
-        copy.start()
-        copies.append(copy)
+    for at in range(count):
+        value = away[pl.ds(at * height, height), :]
+        blocks[at] = dot3(split(value), weight, NT)
+        place = out.at[1 - here, position, pl.ds(at * height, height), :]
+        copies.append(pltpu.make_async_copy(blocks.at[at], place, sems.at[at]))
+        copies[-1].start()
+    for place, terms in ((here, (mine, near)), (1 - here, (far, across))):
         head = terms[0][pl.ds(0, slices), :]
         first[place] = swap(head)[:, :HALF]
         last[place] = (head + terms[1][pl.ds(0, slices), :])[:, :HALF]
@@ -512,7 +556,17 @@
 
 def spread(value, axis, step):
     radix, stride = step
-    return [value] + [flip(value, axis, other * stride) for other in range(1, radix)]
+    if radix == 2:
+        return [value, flip(value, axis, stride)]
+    size = lax.axis_size(axis)
+    parts = [value]
+    for by in SHIFTS:
+        pairs = [
+            (index, index + ((index // stride + by) % 4 - index // stride % 4) * stride)
+            for index in range(size)
+        ]
+        parts.append(lax.ppermute(value, axis, pairs))
+    return parts
 
 
 def exchanged(value, axis):
@@ -532,8 +586,7 @@
     low = lax.axis_size("rep") // members
     member = lax.axis_index("rep") // low
     here = member[None].astype(jnp.int32)
-    masks = (jnp.arange(rank_size, dtype=jnp.int32)[None, :] < ranks[:, None]).astype(jnp.float32)
-    masks = jnp.concatenate([masks, masks], axis=1)[:, None, :]
+    spot = lax.axis_index("mode")[None].astype(jnp.int32)
     height = 2 * count * 32
     rows = slices * 32
     inner, outer = radices(lax.axis_size("mode"))
@@ -581,51 +634,55 @@
         *sends,
     )
     cores = [None] * middle
-    late_cores, part = lax.optimization_barrier((mid_cores, part))
+    late_cores, late_sketch, late_ranks, part = lax.optimization_barrier(
+        (mid_cores, sketch_mid, ranks, part)
+    )
+    masks = (jnp.arange(rank_size, dtype=jnp.int32)[None, :] < late_ranks[:, None]).astype(
+        jnp.float32
+    )
+    masks = jnp.concatenate([masks, masks], axis=1)[:, None, :]
+    sketch_rows = in_rows(late_sketch)
+    sketch_rows = [sketch_rows[position] for position in range(middle)]
     for position in range(middle - 1, -1, -1):
         if position == middle - 1:
             sent = half_of(mid_cores, position, 1 - member)
         else:
             sent = half_of(late_cores, position, 1 - member)
         cores[position] = (half_of(late_cores, position, member), flip(sent, "rep", low))
-    sketch_rows = in_rows(sketch_mid)
     mixed = [None] * middle
     heads = None
+    wide = shape(slices, height, LANES, dtype=jnp.bfloat16)
     for position in range(middle - 1, -1, -1):
         parts = exchanged(part, "mode") if heads else spread(part, "mode", outer)
         heads = heads or parts
-        wide = shape(slices, height, LANES, dtype=jnp.bfloat16)
+        body, more, result = sketch_kernel, (), shape(height, LANES)
+        if position == 0:
+            body = functools.partial(first_kernel, slices=slices)
+            more, result = (*heads, spot), shape(total_slices // 2, LANES)
         part, *mixed[position] = kernel_call(
-            functools.partial(sketch_kernel, len(parts)),
-            [shape(height, LANES), wide, wide],
+            functools.partial(body, len(parts)),
+            [result, wide, wide],
             [
                 scratch(2 * height, LANES),
                 scratch(height * slices, LANES),
                 scratch(slices, HALF, LANES),
             ],
             *parts,
-            masks[position + 1],
+            *more,
+            *((masks[1], masks[0]) if position == 0 else (masks[position + 1],)),
             *cores[position],
             sketch_rows[position],
         )
+    square = scratch(count * HALF, LANES)
+    part = part + flip(part, "rep", 1)
     parts = exchanged(part, "mode")
-    (part,) = kernel_call(
-        functools.partial(first_kernel, len(parts)),
-        [shape(total_slices, LANES)],
-        [scratch(2 * height, LANES)],
+    inverse, carried, basis, part = kernel_call(
+        functools.partial(bond_one_kernel, float(total_slices), len(parts)),
+        [shape(HALF, LANES), shape(height, LANES), shape(slices, LANES), shape(rows, LANES)],
+        [square],
         *parts,
         *heads,
-        masks[0],
-    )
-    square = scratch(count * HALF, LANES)
-    near = flip(part, "rep", 1)
-    inverse, carried, basis, part = kernel_call(
-        functools.partial(bond_one_kernel, float(total_slices), len(heads)),
-        [shape(HALF, LANES), shape(height, LANES), shape(slices, LANES), shape(rows, LANES)],
-        [square],
-        part,
-        near,
-        *heads,
+        spot,
         masks[0],
         *mixed[0],
     )
@@ -680,20 +737,31 @@
         basis,
     )
     near, far, across = (flip(last, "rep", bits) for bits in (1, low, low + 1))
+    blocks = kernel_call(
+        functools.partial(own_kernel, middle - 1),
+        [whole],
+        [scratch(rows, LANES), pltpu.SemaphoreType.DMA],
+        here,
+        last,
+        mixture,
+        *blocks,
+        aliases={3: 0},
+        in_hbm=(3, 4),
+    )
+    pieces = slices // SUBLANES
     rounded_first, rounded_last, blocks = kernel_call(
         functools.partial(final_kernel, middle - 1),
         [shape(members, slices, rank_size), shape(members, slices, rank_size), whole],
-        [pltpu.VMEM((2, rows, LANES), jnp.float32), pltpu.SemaphoreType.DMA((2,))],
+        [scratch(pieces, rows // pieces, LANES), pltpu.SemaphoreType.DMA((pieces,))],
         here,
         last,
         near,
         far,
         across,
-        mixture,
         away,
         *blocks,
-        aliases={7: 2},
-        in_hbm=(7, 10),
+        aliases={6: 2},
+        in_hbm=(6, 9),
     )
     return (rounded_first, out_of_rows(blocks, slices), rounded_last)
 

time: 143 us -> 147 us (1.028)
  starting transfers between devices: 51.8 us -> 42.7 us
  local copies, waits for them, and re-layouts: 4.9 us -> 12.4 us
  waiting for transfers between devices: 59.8 us -> 62.9 us
  Pallas kernels: 24.7 us -> 26.6 us
    ppermute x0 -> x21, waiting for transfers between devices: none -> 42.6 us  [spread(): parts.append(lax.ppermute(value, axis, pairs))]
    ppermute x42 -> x21, waiting for transfers between devices: 59.8 us -> 20.3 us  [flip(): lax.ppermute(value, axis, [(index, index ^ bits) for index in range(size)])]
    ppermute x42 -> x21, starting transfers between devices: 47.8 us -> 18.3 us  [flip(): lax.ppermute(value, axis, [(index, index ^ bits) for index in range(size)])]
    ppermute x0 -> x21, starting transfers between devices: none -> 20.4 us  [spread(): parts.append(lax.ppermute(value, axis, pairs))]
    unnamed x6 -> x52, local copies, waits for them, and re-layouts: 0.78 us -> 7.24 us
    pallas_call x18, Pallas kernels: 24.7 us -> 26.6 us  [kernel_call(): pl.pallas_call(body, out_shape=outs, in_specs=specs[:len(operands)], out_...]
    dynamic_slice x2, local copies, waits for them, and re-layouts: 2.95 us -> 4.59 us  [half_of(): lax.dynamic_slice(source, (index, 0, position, 0, 0), (1, count, 1, slice...]
  transfers between devices with their start and end apart: 43 -> 43, of which waited for: 27 -> 23; matrix products, arithmetic and copies ran while one was open for 3% -> 4% of each run, Pallas kernels for 6% -> 6%
where the time goes in v3:
time: 147 us
  waiting for transfers between devices  62.9 us (43%)
  starting transfers between devices  42.7 us (29%)
  Pallas kernels  26.6 us (18%)
  local copies, waits for them, and re-layouts  12.4 us (8%)
    ppermute x21, waiting for transfers between devices, spread(): parts.append(lax.ppermute(value, axis, pairs))  42.6 us
    pallas_call x18, Pallas kernels, kernel_call(): pl.pallas_call(body, out_shape=outs, in_specs=specs[:len(operands)], out_...  26.6 us
    ppermute x21, starting transfers between devices, spread(): parts.append(lax.ppermute(value, axis, pairs))  20.4 us
    ppermute x21, waiting for transfers between devices, flip(): lax.ppermute(value, axis, [(index, index ^ bits) for index in range(size)])  20.3 us
    ppermute x21, starting transfers between devices, flip(): lax.ppermute(value, axis, [(index, index ^ bits) for index in range(size)])  18.3 us
    unnamed x52, local copies, waits for them, and re-layouts  7.24 us
    dynamic_slice x2, local copies, waits for them, and re-layouts, half_of(): lax.dynamic_slice(source, (index, 0, position, 0, 0), (1, count, 1, slice...  4.59 us
    ppermute x1, starting transfers between devices, tiled(): sends.append(lax.ppermute(send, ('mode', 'rep'), pairs))  3.99 us
  transfers between devices with their start and end apart: 43, of which 23 were waited for; matrix products, arithmetic and copies ran while one was open for 4% of the time, Pallas kernels for 6%

profile of v3, /device:TPU:0, one launch (start us, length us, event | category | flops | bytes accessed | tf_op | source)
XLA Modules:
  0.0 146.6 jit_solution(6798896022188363426)
XLA Ops:
  0.7 1.9 %shard_map.85 = (f32[80,128]{1,0:T(8,128)}, f32[96,128]{1,0:T(8,128)}) custom-call(s32[1]{0:T(128)} %bitcast.member.refs_5_, f32[2,2,16,64]{3,2,1,0:T(8,128)} %refs_6_.1, f32[2,2,16,64]{3,2,1,0:T(8,128)} %refs_1_.1, f32[16,64]{1,0:T(8,128)} %refs_2_.1), custom_call_target="tpu_custom_call" | custom-call | bytes 126980 | tf_op jit(solution)/shard_map/pallas_call | solution.py:523
  2.5 4.0 %collective-permute-start.2 = (f32[96,128]{1,0:T(8,128)}, f32[96,128]{1,0:T(8,128)S(1)}, u32[]{:S(2)}, u32[]{:S(2)}) collective-permute-start(f32[96,128]{1,0:T(8,128)} %get-tuple-element.37), channel_id=1, source_target_pairs={{0,6},{1,7},{2,4},{3,5},{4,2},{5,3},{6,0},{7,1},{8,14},{9,15},{10,... | collective-permute-start | bytes 147464 | tf_op jit(solution)/shard_map/ppermute | solution.py:627
  7.2 1.9 %constant_dynamic-slice_fusion.4 = f32[1,2,1,16,4096]{4,3,2,1,0:T(8,128)} fusion(f32[2,2,3,16,4096]{4,3,2,1,0:T(8,128)} %param.7, s32[]{:T(128)S(6)} %select_n.17), kind=kLoop, calls=%fused_computation.6 | loop fusion | bytes 1048580 | tf_op jit(solution)/shard_map/dynamic_slice | solution.py:595
  9.1 1.9 %collective-permute-start.6 = (f32[2,512,128]{2,1,0:T(8,128)}, f32[2,512,128]{2,1,0:T(8,128)S(1)}, u32[]{:S(2)}, u32[]{:S(2)}) collective-permute-start(f32[2,512,128]{2,1,0:T(8,128)} %bitcast.6), channel_id=1, source_target_pairs={{0,2},{1,3},{2,0},{3,1},{4,6},{5,7},{6,4},{7,5},{8,10},{9,11},{10,... | collective-permute-start | bytes 1572872 | tf_op jit(solution)/shard_map/ppermute | solution.py:22
  12.1 2.7 %collective-permute-start.5 = (f32[192,128]{1,0:T(8,128)S(1)}, f32[192,128]{1,0:T(8,128)S(1)}, u32[]{:S(2)}, u32[]{:S(2)}) collective-permute-start(f32[192,128]{1,0:T(8,128)S(1)} %shard_map.86.refs_0_.refs_4_), channel_id=1, source_target_pairs={{0,16},{4,20},{8,24},{12,28},{16,0},{20,4},{24,8},{28,12},{1,17},{... | collective-permute-start | bytes 294920 | tf_op jit(solution)/shard_map/ppermute | solution.py:568
  14.7 1.3 collective-permute-start.4
  16.2 2.7 %constant_dynamic-slice_fusion = (f32[1,2,1,16,4096]{4,3,2,1,0:T(8,128)}, f32[1,2,1,16,4096]{4,3,2,1,0:T(8,128)S(1)}, f32[1,2,1,16,4096]{4,3,2,1,0:T(8,128)S(1)}...) fusion(f32[2,2,3,16,4096]{4,3,2,1,0:T(8,128)} %param.7, s32[]{:T(128)S(6)} %select_n.17, s32[]{:T(128)S(6)} %select_n.16), kind=kLoop, calls=%fused_computation.2 | loop fusion | bytes 5242888 | tf_op jit(solution)/shard_map/dynamic_slice | solution.py:595
  18.8 1.5 %collective-permute-start.11 = (f32[2,512,128]{2,1,0:T(8,128)S(1)}, f32[2,512,128]{2,1,0:T(8,128)S(1)}, u32[]{:S(2)}, u32[]{:S(2)}) collective-permute-start(f32[2,512,128]{2,1,0:T(8,128)S(1)} %bitcast.54), channel_id=1, source_target_pairs={{0,2},{1,3},{2,0},{3,1},{4,6},{5,7},{6,4},{7,5},{8,10},{9,11},{10,... | collective-permute-start | bytes 1572872 | tf_op jit(solution)/shard_map/ppermute | solution.py:22
  22.2 5.2 %collective-permute-done.3.refs_1_.refs_5_ = f32[192,128]{1,0:T(8,128)S(1)} collective-permute-done((f32[192,128]{1,0:T(8,128)S(1)}, f32[192,128]{1,0:T(8,128)S(1)}, u32[]{:S(2)}, u32[]{:S(2)}) %collective-permute-start.3) | collective-permute-done | bytes 98336 | tf_op jit(solution)/shard_map/ppermute | solution.py:568
  27.5 1.4 shard_map.87
  29.7 1.2 collective-permute-start.7
  30.9 3.1 %collective-permute-done.7 = f32[128,128]{1,0:T(8,128)S(1)} collective-permute-done((f32[128,128]{1,0:T(8,128)S(1)}, f32[128,128]{1,0:T(8,128)S(1)}, u32[]{:S(2)}, u32[]{:S(2)}) %collective-permute-start.7) | collective-permute-done | bytes 65568 | tf_op jit(solution)/shard_map/ppermute | solution.py:22
  34.0 1.2 collective-permute-start.9
  35.3 0.8 collective-permute-start.8
  36.1 3.1 %collective-permute-done.10.refs_3_ = f32[128,128]{1,0:T(8,128)S(1)} collective-permute-done((f32[128,128]{1,0:T(8,128)S(1)}, f32[128,128]{1,0:T(8,128)S(1)}, u32[]{:S(2)}, u32[]{:S(2)}) %collective-permute-start.10) | collective-permute-done | bytes 65568 | tf_op jit(solution)/shard_map/ppermute | solution.py:568
  39.6 1.7 %collective-permute-done.8.refs_1_ = f32[128,128]{1,0:T(8,128)S(1)} collective-permute-done((f32[128,128]{1,0:T(8,128)S(1)}, f32[128,128]{1,0:T(8,128)S(1)}, u32[]{:S(2)}, u32[]{:S(2)}) %collective-permute-start.8) | collective-permute-done | bytes 65568 | tf_op jit(solution)/shard_map/ppermute | solution.py:568
  41.3 1.4 shard_map.88
  44.4 1.4 collective-permute-start.12
  45.7 2.9 %collective-permute-done.12 = f32[128,128]{1,0:T(8,128)S(1)} collective-permute-done((f32[128,128]{1,0:T(8,128)S(1)}, f32[128,128]{1,0:T(8,128)S(1)}, u32[]{:S(2)}, u32[]{:S(2)}) %collective-permute-start.12) | collective-permute-done | bytes 65568 | tf_op jit(solution)/shard_map/ppermute | solution.py:22
  49.4 1.3 collective-permute-start.14
  51.4 3.3 %collective-permute-done.15.refs_3_ = f32[128,128]{1,0:T(8,128)} collective-permute-done((f32[128,128]{1,0:T(8,128)}, f32[128,128]{1,0:T(8,128)}, u32[]{:S(2)}, u32[]{:S(2)}) %collective-permute-start.15) | collective-permute-done | bytes 65568 | tf_op jit(solution)/shard_map/ppermute | solution.py:568
  54.8 2.4 %collective-permute-done.13.refs_1_ = f32[128,128]{1,0:T(8,128)} collective-permute-done((f32[128,128]{1,0:T(8,128)}, f32[128,128]{1,0:T(8,128)}, u32[]{:S(2)}, u32[]{:S(2)}) %collective-permute-start.13) | collective-permute-done | bytes 65568 | tf_op jit(solution)/shard_map/ppermute | solution.py:568
  57.1 0.9 copy-done.1
  58.0 0.9 copy-done.3
  58.9 0.9 copy-done.5
  61.1 2.8 %shard_map.89 = (f32[64,128]{1,0:T(8,128)S(1)}, bf16[16,128,128]{2,1,0:T(8,128)(2,1)S(1)}, bf16[16,128,128]{2,1,0:T(8,128)(2,1)S(1)}) custom-call(f32[128,128]{1,0:T(8,128)} %add.36.refs_0_, f32[128,128]{1,0:T(8,128)} %collective-permute-done.13.refs_1_, f32[128,128]{1,0:T(8,128)} %collective-permute-done.14.refs_2_, ...), custom_call_target="tpu_custom_call" | custom-call | bytes 3048452 | tf_op jit(solution)/shard_map/pallas_call | solution.py:523
  64.0 1.2 collective-permute-done.17
  65.2 1.3 collective-permute-start.18
  66.5 2.6 %collective-permute-done.18 = f32[64,128]{1,0:T(8,128)S(1)} collective-permute-done((f32[64,128]{1,0:T(8,128)S(1)}, f32[64,128]{1,0:T(8,128)S(1)}, u32[]{:S(2)}, u32[]{:S(2)}) %collective-permute-start.18) | collective-permute-done | bytes 32800 | tf_op jit(solution)/shard_map/ppermute | solution.py:22
  69.2 1.2 collective-permute-start.20
  71.2 2.9 %collective-permute-done.21.refs_3_ = f32[64,128]{1,0:T(8,128)S(1)} collective-permute-done((f32[64,128]{1,0:T(8,128)S(1)}, f32[64,128]{1,0:T(8,128)S(1)}, u32[]{:S(2)}, u32[]{:S(2)}) %collective-permute-start.21) | collective-permute-done | bytes 32800 | tf_op jit(solution)/shard_map/ppermute | solution.py:568
  74.1 2.0 %collective-permute-done.19.refs_1_ = f32[64,128]{1,0:T(8,128)S(1)} collective-permute-done((f32[64,128]{1,0:T(8,128)S(1)}, f32[64,128]{1,0:T(8,128)S(1)}, u32[]{:S(2)}, u32[]{:S(2)}) %collective-permute-start.19) | collective-permute-done | bytes 32800 | tf_op jit(solution)/shard_map/ppermute | solution.py:568
  76.1 3.3 %shard_map.90 = (f32[64,128]{1,0:T(8,128)}, f32[128,128]{1,0:T(8,128)S(1)}, f32[16,128]{1,0:T(8,128)S(1)}, f32[512,128]{1,0:T(8,128)S(1)}) custom-call(f32[64,128]{1,0:T(8,128)S(1)} %add.38.refs_0_, f32[64,128]{1,0:T(8,128)S(1)} %collective-permute-done.19.refs_1_, f32[64,128]{1,0:T(8,128)S(1)} %collective-permute-done.20.refs_2_, ...), custom_call_target="tpu_custom_call" | custom-call | bytes 1942020 | tf_op jit(solution)/shard_map/pallas_call | solution.py:523
  79.4 1.5 %collective-permute-done.22.theirs = f32[512,128]{1,0:T(8,128)S(1)} collective-permute-done((f32[512,128]{1,0:T(8,128)S(1)}, f32[512,128]{1,0:T(8,128)S(1)}, u32[]{:S(2)}, u32[]{:S(2)}) %collective-permute-start.22) | collective-permute-done | bytes 262176 | tf_op jit(solution)/shard_map/ppermute | solution.py:22
  81.0 1.2 shard_map.91
  82.2 1.5 collective-permute-start.23
  83.7 3.1 %collective-permute-done.23 = f32[160,128]{1,0:T(8,128)S(1)} collective-permute-done((f32[160,128]{1,0:T(8,128)S(1)}, f32[160,128]{1,0:T(8,128)S(1)}, u32[]{:S(2)}, u32[]{:S(2)}) %collective-permute-start.23) | collective-permute-done | bytes 81952 | tf_op jit(solution)/shard_map/ppermute | solution.py:22
  86.9 1.3 collective-permute-start.25
  88.9 5.9 %collective-permute-done.26.refs_3_ = f32[160,128]{1,0:T(8,128)S(1)} collective-permute-done((f32[160,128]{1,0:T(8,128)S(1)}, f32[160,128]{1,0:T(8,128)S(1)}, u32[]{:S(2)}, u32[]{:S(2)}) %collective-permute-start.26) | collective-permute-done | bytes 81952 | tf_op jit(solution)/shard_map/ppermute | solution.py:568
  94.9 2.5 %shard_map.92 = (f32[64,128]{1,0:T(8,128)S(1)}, f32[128,128]{1,0:T(8,128)S(1)}, f32[512,128]{1,0:T(8,128)S(1)}) custom-call(f32[160,128]{1,0:T(8,128)S(1)} %add.39.refs_0_, f32[160,128]{1,0:T(8,128)S(1)} %collective-permute-done.24.refs_1_, f32[160,128]{1,0:T(8,128)S(1)} %collective-permute-done.25.refs_2_, f32[160,128]{1,0:T(8,128)S(1)} %collective-permute-done.26.refs_3_, ...), custom_call_target="tpu_custom_call" | custom-call | bytes 1737216 | tf_op jit(solution)/shard_map/pallas_call | solution.py:523
  97.4 1.5 %collective-permute-done.27.theirs = f32[512,128]{1,0:T(8,128)S(1)} collective-permute-done((f32[512,128]{1,0:T(8,128)S(1)}, f32[512,128]{1,0:T(8,128)S(1)}, u32[]{:S(2)}, u32[]{:S(2)}) %collective-permute-start.27) | collective-permute-done | bytes 262176 | tf_op jit(solution)/shard_map/ppermute | solution.py:22
  99.0 1.2 shard_map.93
  100.2 1.5 collective-permute-start.28
  101.6 3.1 %collective-permute-done.28 = f32[160,128]{1,0:T(8,128)S(1)} collective-permute-done((f32[160,128]{1,0:T(8,128)S(1)}, f32[160,128]{1,0:T(8,128)S(1)}, u32[]{:S(2)}, u32[]{:S(2)}) %collective-permute-start.28) | collective-permute-done | bytes 81952 | tf_op jit(solution)/shard_map/ppermute | solution.py:22
  104.7 2.2 %collective-permute-start.31 = (f32[160,128]{1,0:T(8,128)S(1)}, f32[160,128]{1,0:T(8,128)S(1)}, u32[]{:S(2)}, u32[]{:S(2)}) collective-permute-start(f32[160,128]{1,0:T(8,128)S(1)} %add.40.refs_0_), channel_id=1, source_target_pairs={{0,16},{4,20},{8,24},{12,28},{16,0},{20,4},{24,8},{28,12},{1,17},{... | collective-permute-start | bytes 245768 | tf_op jit(solution)/shard_map/ppermute | solution.py:568
  106.9 1.7 %collective-permute-start.30 = (f32[160,128]{1,0:T(8,128)S(1)}, f32[160,128]{1,0:T(8,128)S(1)}, u32[]{:S(2)}, u32[]{:S(2)}) collective-permute-start(f32[160,128]{1,0:T(8,128)S(1)} %add.40.refs_0_), channel_id=1, source_target_pairs={{0,24},{4,28},{8,0},{12,4},{16,8},{20,12},{24,16},{28,20},{1,25},{... | collective-permute-start | bytes 245768 | tf_op jit(solution)/shard_map/ppermute | solution.py:568
  109.0 3.3 %collective-permute-done.31.refs_3_ = f32[160,128]{1,0:T(8,128)S(1)} collective-permute-done((f32[160,128]{1,0:T(8,128)S(1)}, f32[160,128]{1,0:T(8,128)S(1)}, u32[]{:S(2)}, u32[]{:S(2)}) %collective-permute-start.31) | collective-permute-done | bytes 81952 | tf_op jit(solution)/shard_map/ppermute | solution.py:568
  112.3 2.6 %collective-permute-done.29.refs_1_ = f32[160,128]{1,0:T(8,128)S(1)} collective-permute-done((f32[160,128]{1,0:T(8,128)S(1)}, f32[160,128]{1,0:T(8,128)S(1)}, u32[]{:S(2)}, u32[]{:S(2)}) %collective-permute-start.29) | collective-permute-done | bytes 81952 | tf_op jit(solution)/shard_map/ppermute | solution.py:568
  114.9 2.5 %shard_map.94 = (f32[64,128]{1,0:T(8,128)S(1)}, f32[128,128]{1,0:T(8,128)S(1)}, f32[512,128]{1,0:T(8,128)S(1)}) custom-call(f32[160,128]{1,0:T(8,128)S(1)} %add.40.refs_0_, f32[160,128]{1,0:T(8,128)S(1)} %collective-permute-done.29.refs_1_, f32[160,128]{1,0:T(8,128)S(1)} %collective-permute-done.30.refs_2_, f32[160,128]{1,0:T(8,128)S(1)} %collective-permute-done.31.refs_3_, ...), custom_call_target="tpu_custom_call" | custom-call | bytes 1737216 | tf_op jit(solution)/shard_map/pallas_call | solution.py:523
  117.8 1.5 %collective-permute-start.42 = (f32[512,128]{1,0:T(8,128)S(1)}, f32[512,128]{1,0:T(8,128)S(1)}, u32[]{:S(2)}, u32[]{:S(2)}) collective-permute-start(f32[512,128]{1,0:T(8,128)S(1)} %shard_map.98.mine), channel_id=1, source_target_pairs={{0,2},{1,3},{2,0},{3,1},{4,6},{5,7},{6,4},{7,5},{8,10},{9,11},{10,... | collective-permute-start | bytes 786440 | tf_op jit(solution)/shard_map/ppermute | solution.py:22
  119.4 1.2 shard_map.95
  120.6 1.3 collective-permute-start.33
  122.2 1.2 collective-permute-start.41
  123.4 0.9 collective-permute-start.40
  124.3 0.9 collective-permute-done.33
  125.2 1.1 collective-permute-start.36
  126.3 1.1 collective-permute-start.35
  127.5 4.3 %collective-permute-done.36.refs_3_ = f32[160,128]{1,0:T(8,128)S(1)} collective-permute-done((f32[160,128]{1,0:T(8,128)S(1)}, f32[160,128]{1,0:T(8,128)S(1)}, u32[]{:S(2)}, u32[]{:S(2)}) %collective-permute-start.36) | collective-permute-done | bytes 81952 | tf_op jit(solution)/shard_map/ppermute | solution.py:568
  132.5 5.5 %collective-permute-done.34.refs_1_ = f32[160,128]{1,0:T(8,128)S(1)} collective-permute-done((f32[160,128]{1,0:T(8,128)S(1)}, f32[160,128]{1,0:T(8,128)S(1)}, u32[]{:S(2)}, u32[]{:S(2)}) %collective-permute-start.34) | collective-permute-done | bytes 81952 | tf_op jit(solution)/shard_map/ppermute | solution.py:568
  138.0 2.1 %shard_map.96.mine = f32[80,128]{1,0:T(8,128)S(1)} custom-call(f32[160,128]{1,0:T(8,128)S(1)} %add.41.refs_0_, f32[160,128]{1,0:T(8,128)S(1)} %collective-permute-done.34.refs_1_, f32[160,128]{1,0:T(8,128)S(1)} %collective-permute-done.35.refs_2_, f32[160,128]{1,0:T(8,128)S(1)} %collective-permute-done.36.refs_3_, f32[1,128]{1,0:T(1,128)S(1)} %copy-done.17, ...), custom_call_target="tpu_custom_call" | custom-call | bytes 401924 | tf_op jit(solution)/shard_map/pallas_call | solution.py:523
  140.2 1.0 collective-permute-start.38
  141.2 0.9 collective-permute-start.37
  143.7 1.0 shard_map.101.before
  144.8 1.7 %shard_map.102 = (f32[2,16,64]{2,1,0:T(8,128)}, f32[2,16,64]{2,1,0:T(8,128)}, f32[2,3,512,128]{3,2,1,0:T(8,128)}) custom-call(s32[1]{0:T(128)} %bitcast.member.refs_5_, f32[80,128]{1,0:T(8,128)S(1)} %shard_map.96.mine, f32[80,128]{1,0:T(8,128)S(1)} %collective-permute-done.37.near, ...), custom_call_target="tpu_custom_call", output_to_operand_aliasing={{2}: (6, {})} | custom-call | bytes 3588100 | tf_op jit(solution)/shard_map/pallas_call | solution.py:523
  (106 shorter events, 14.7 us)
Async XLA Ops:
  0.6 15.5 %copy-start.24 = (f32[3,16,4096]{2,1,0:T(8,128)S(1)}, f32[3,16,4096]{2,1,0:T(8,128)}, u32[]{:S(2)}) copy-start(f32[3,16,4096]{2,1,0:T(8,128)} %param.9) | copy-start | bytes 2359300
  2.5 8.7 %collective-permute-start.2 = (f32[96,128]{1,0:T(8,128)}, f32[96,128]{1,0:T(8,128)S(1)}, u32[]{:S(2)}, u32[]{:S(2)}) collective-permute-start(f32[96,128]{1,0:T(8,128)} %get-tuple-element.37), channel_id=1, source_target_pairs={{0,6},{1,7},{2,4},{3,5},{4,2},{5,3},{6,0},{7,1},{8,14},{9,15},{10,... | collective-permute-start | bytes 147464 | tf_op jit(solution)/shard_map/ppermute | solution.py:627
  6.5 4.8 %collective-permute-start.1 = (f32[96,128]{1,0:T(8,128)}, f32[96,128]{1,0:T(8,128)S(1)}, u32[]{:S(2)}, u32[]{:S(2)}) collective-permute-start(f32[96,128]{1,0:T(8,128)} %get-tuple-element.37), channel_id=1, source_target_pairs={{0,2},{1,3},{2,0},{3,1},{4,6},{5,7},{6,4},{7,5},{8,10},{9,11},{10,... | collective-permute-start | bytes 147464 | tf_op jit(solution)/shard_map/ppermute | solution.py:22
  7.1 4.2 %collective-permute-start = (f32[80,128]{1,0:T(8,128)}, f32[80,128]{1,0:T(8,128)S(1)}, u32[]{:S(2)}, u32[]{:S(2)}) collective-permute-start(f32[80,128]{1,0:T(8,128)} %get-tuple-element.36.refs_0_), channel_id=1, source_target_pairs={{0,4},{4,0},{8,12},{12,8},{16,20},{20,16},{24,28},{28,24},{1,5},{5... | collective-permute-start | bytes 122888 | tf_op jit(solution)/shard_map/ppermute | solution.py:22
  9.1 18.4 %collective-permute-start.6 = (f32[2,512,128]{2,1,0:T(8,128)}, f32[2,512,128]{2,1,0:T(8,128)S(1)}, u32[]{:S(2)}, u32[]{:S(2)}) collective-permute-start(f32[2,512,128]{2,1,0:T(8,128)} %bitcast.6), channel_id=1, source_target_pairs={{0,2},{1,3},{2,0},{3,1},{4,6},{5,7},{6,4},{7,5},{8,10},{9,11},{10,... | collective-permute-start | bytes 1572872 | tf_op jit(solution)/shard_map/ppermute | solution.py:22
  12.1 8.9 %collective-permute-start.5 = (f32[192,128]{1,0:T(8,128)S(1)}, f32[192,128]{1,0:T(8,128)S(1)}, u32[]{:S(2)}, u32[]{:S(2)}) collective-permute-start(f32[192,128]{1,0:T(8,128)S(1)} %shard_map.86.refs_0_.refs_4_), channel_id=1, source_target_pairs={{0,16},{4,20},{8,24},{12,28},{16,0},{20,4},{24,8},{28,12},{1,17},{... | collective-permute-start | bytes 294920 | tf_op jit(solution)/shard_map/ppermute | solution.py:568
  14.7 7.5 %collective-permute-start.4 = (f32[192,128]{1,0:T(8,128)S(1)}, f32[192,128]{1,0:T(8,128)S(1)}, u32[]{:S(2)}, u32[]{:S(2)}) collective-permute-start(f32[192,128]{1,0:T(8,128)S(1)} %shard_map.86.refs_0_.refs_4_), channel_id=1, source_target_pairs={{0,24},{4,28},{8,0},{12,4},{16,8},{20,12},{24,16},{28,20},{1,25},{... | collective-permute-start | bytes 294920 | tf_op jit(solution)/shard_map/ppermute | solution.py:568
  16.1 4.2 %copy-start.25 = (s32[4]{0:T(128)S(1)}, s32[4]{0:T(128)}, u32[]{:S(2)}) copy-start(s32[4]{0:T(128)} %param.11) | copy-start | bytes 52
  18.8 17.3 %collective-permute-start.11 = (f32[2,512,128]{2,1,0:T(8,128)S(1)}, f32[2,512,128]{2,1,0:T(8,128)S(1)}, u32[]{:S(2)}, u32[]{:S(2)}) collective-permute-start(f32[2,512,128]{2,1,0:T(8,128)S(1)} %bitcast.54), channel_id=1, source_target_pairs={{0,2},{1,3},{2,0},{3,1},{4,6},{5,7},{6,4},{7,5},{8,10},{9,11},{10,... | collective-permute-start | bytes 1572872 | tf_op jit(solution)/shard_map/ppermute | solution.py:22
  20.4 31.0 %collective-permute-start.16 = (f32[2,512,128]{2,1,0:T(8,128)}, f32[2,512,128]{2,1,0:T(8,128)S(1)}, u32[]{:S(2)}, u32[]{:S(2)}) collective-permute-start(f32[2,512,128]{2,1,0:T(8,128)} %bitcast.24), channel_id=1, source_target_pairs={{0,2},{1,3},{2,0},{3,1},{4,6},{5,7},{6,4},{7,5},{8,10},{9,11},{10,... | collective-permute-start | bytes 1572872 | tf_op jit(solution)/shard_map/ppermute | solution.py:22
  21.0 15.1 %copy-start = (f32[192,128]{1,0:T(8,128)}, f32[192,128]{1,0:T(8,128)S(1)}, u32[]{:S(2)}) copy-start(f32[192,128]{1,0:T(8,128)S(1)} %collective-permute-done.5.refs_3_.refs_7_) | copy-start | bytes 294916
  21.0 6.4 %collective-permute-start.3 = (f32[192,128]{1,0:T(8,128)S(1)}, f32[192,128]{1,0:T(8,128)S(1)}, u32[]{:S(2)}, u32[]{:S(2)}) collective-permute-start(f32[192,128]{1,0:T(8,128)S(1)} %shard_map.86.refs_0_.refs_4_), channel_id=1, source_target_pairs={{0,8},{4,12},{8,16},{12,20},{16,24},{20,28},{24,0},{28,4},{1,9},{5... | collective-permute-start | bytes 294920 | tf_op jit(solution)/shard_map/ppermute | solution.py:568
  22.2 11.7 %copy-start.16 = (f32[1,128]{1,0:T(1,128)}, f32[1,128]{1,0:T(1,128)S(1)}, u32[]{:S(2)}) copy-start(f32[1,128]{1,0:T(1,128)S(1)} %get-tuple-element.80.refs_4_) | copy-start | bytes 1540
  22.2 20.5 %copy-start.18 = (f32[1,128]{1,0:T(1,128)}, f32[1,128]{1,0:T(1,128)S(1)}, u32[]{:S(2)}) copy-start(f32[1,128]{1,0:T(1,128)S(1)} %get-tuple-element.79.refs_4_) | copy-start | bytes 1540
  22.2 20.5 %copy-start.2 = (f32[192,128]{1,0:T(8,128)}, f32[192,128]{1,0:T(8,128)S(1)}, u32[]{:S(2)}) copy-start(f32[192,128]{1,0:T(8,128)S(1)} %collective-permute-done.4.refs_2_.refs_6_) | copy-start | bytes 294916
  27.4 11.7 %copy-start.4 = (f32[192,128]{1,0:T(8,128)}, f32[192,128]{1,0:T(8,128)S(1)}, u32[]{:S(2)}) copy-start(f32[192,128]{1,0:T(8,128)S(1)} %collective-permute-done.3.refs_1_.refs_5_) | copy-start | bytes 294916
  28.8 0.8 copy-start.6
  29.7 14.7 %copy-start.8 = (bf16[16,128,128]{2,1,0:T(8,128)(2,1)}, bf16[16,128,128]{2,1,0:T(8,128)(2,1)S(1)}, u32[]{:S(2)}) copy-start(bf16[16,128,128]{2,1,0:T(8,128)(2,1)S(1)} %get-tuple-element.56.refs_6_) | copy-start | bytes 1572868
  29.7 4.3 %collective-permute-start.7 = (f32[128,128]{1,0:T(8,128)S(1)}, f32[128,128]{1,0:T(8,128)S(1)}, u32[]{:S(2)}, u32[]{:S(2)}) collective-permute-start(f32[128,128]{1,0:T(8,128)S(1)} %get-tuple-element.42), channel_id=1, source_target_pairs={{0,4},{4,0},{8,12},{12,8},{16,20},{20,16},{24,28},{28,24},{1,5},{5... | collective-permute-start | bytes 196616 | tf_op jit(solution)/shard_map/ppermute | solution.py:22
  34.0 5.2 %collective-permute-start.10 = (f32[128,128]{1,0:T(8,128)S(1)}, f32[128,128]{1,0:T(8,128)S(1)}, u32[]{:S(2)}, u32[]{:S(2)}) collective-permute-start(f32[128,128]{1,0:T(8,128)S(1)} %add.35.refs_0_), channel_id=1, source_target_pairs={{0,16},{4,20},{8,24},{12,28},{16,0},{20,4},{24,8},{28,12},{1,17},{... | collective-permute-start | bytes 196616 | tf_op jit(solution)/shard_map/ppermute | solution.py:568
  34.0 5.6 %collective-permute-start.9 = (f32[128,128]{1,0:T(8,128)S(1)}, f32[128,128]{1,0:T(8,128)S(1)}, u32[]{:S(2)}, u32[]{:S(2)}) collective-permute-start(f32[128,128]{1,0:T(8,128)S(1)} %add.35.refs_0_), channel_id=1, source_target_pairs={{0,24},{4,28},{8,0},{12,4},{16,8},{20,12},{24,16},{28,20},{1,25},{... | collective-permute-start | bytes 196616 | tf_op jit(solution)/shard_map/ppermute | solution.py:568
  35.3 6.1 %collective-permute-start.8 = (f32[128,128]{1,0:T(8,128)S(1)}, f32[128,128]{1,0:T(8,128)S(1)}, u32[]{:S(2)}, u32[]{:S(2)}) collective-permute-start(f32[128,128]{1,0:T(8,128)S(1)} %add.35.refs_0_), channel_id=1, source_target_pairs={{0,8},{4,12},{8,16},{12,20},{16,24},{20,28},{24,0},{28,4},{1,9},{5... | collective-permute-start | bytes 196616 | tf_op jit(solution)/shard_map/ppermute | solution.py:568
  44.4 4.3 %collective-permute-start.12 = (f32[128,128]{1,0:T(8,128)S(1)}, f32[128,128]{1,0:T(8,128)S(1)}, u32[]{:S(2)}, u32[]{:S(2)}) collective-permute-start(f32[128,128]{1,0:T(8,128)S(1)} %get-tuple-element.43), channel_id=1, source_target_pairs={{0,4},{4,0},{8,12},{12,8},{16,20},{20,16},{24,28},{28,24},{1,5},{5... | collective-permute-start | bytes 196616 | tf_op jit(solution)/shard_map/ppermute | solution.py:22
  49.3 5.5 %collective-permute-start.15 = (f32[128,128]{1,0:T(8,128)}, f32[128,128]{1,0:T(8,128)}, u32[]{:S(2)}, u32[]{:S(2)}) collective-permute-start(f32[128,128]{1,0:T(8,128)} %add.36.refs_0_), channel_id=1, source_target_pairs={{0,16},{4,20},{8,24},{12,28},{16,0},{20,4},{24,8},{28,12},{1,17},{... | collective-permute-start | bytes 196616 | tf_op jit(solution)/shard_map/ppermute | solution.py:568
  49.4 5.3 %collective-permute-start.14 = (f32[128,128]{1,0:T(8,128)}, f32[128,128]{1,0:T(8,128)}, u32[]{:S(2)}, u32[]{:S(2)}) collective-permute-start(f32[128,128]{1,0:T(8,128)} %add.36.refs_0_), channel_id=1, source_target_pairs={{0,24},{4,28},{8,0},{12,4},{16,8},{20,12},{24,16},{28,20},{1,25},{... | collective-permute-start | bytes 196616 | tf_op jit(solution)/shard_map/ppermute | solution.py:568
  50.7 6.4 %collective-permute-start.13 = (f32[128,128]{1,0:T(8,128)}, f32[128,128]{1,0:T(8,128)}, u32[]{:S(2)}, u32[]{:S(2)}) collective-permute-start(f32[128,128]{1,0:T(8,128)} %add.36.refs_0_), channel_id=1, source_target_pairs={{0,8},{4,12},{8,16},{12,20},{16,24},{20,28},{24,0},{28,4},{1,9},{5... | collective-permute-start | bytes 196616 | tf_op jit(solution)/shard_map/ppermute | solution.py:568
  51.4 24.7 %copy-start.23 = (f32[1,128]{1,0:T(1,128)S(1)}, f32[1,128]{1,0:T(1,128)}, u32[]{:S(2)}) copy-start(f32[1,128]{1,0:T(1,128)} %get-tuple-element.77.refs_10_.refs_9_) | copy-start | bytes 1540
  57.1 0.9 copy-start.1
  58.0 0.9 copy-start.3
  58.9 0.9 copy-start.5
  63.9 1.2 collective-permute-start.17
  65.2 3.9 %collective-permute-start.18 = (f32[64,128]{1,0:T(8,128)S(1)}, f32[64,128]{1,0:T(8,128)S(1)}, u32[]{:S(2)}, u32[]{:S(2)}) collective-permute-start(f32[64,128]{1,0:T(8,128)S(1)} %add.37), channel_id=1, source_target_pairs={{0,4},{4,0},{8,12},{12,8},{16,20},{20,16},{24,28},{28,24},{1,5},{5... | collective-permute-start | bytes 98312 | tf_op jit(solution)/shard_map/ppermute | solution.py:22
  69.1 5.0 %collective-permute-start.21 = (f32[64,128]{1,0:T(8,128)S(1)}, f32[64,128]{1,0:T(8,128)S(1)}, u32[]{:S(2)}, u32[]{:S(2)}) collective-permute-start(f32[64,128]{1,0:T(8,128)S(1)} %add.38.refs_0_), channel_id=1, source_target_pairs={{0,16},{4,20},{8,24},{12,28},{16,0},{20,4},{24,8},{28,12},{1,17},{... | collective-permute-start | bytes 98312 | tf_op jit(solution)/shard_map/ppermute | solution.py:568
  69.2 4.9 %collective-permute-start.20 = (f32[64,128]{1,0:T(8,128)S(1)}, f32[64,128]{1,0:T(8,128)S(1)}, u32[]{:S(2)}, u32[]{:S(2)}) collective-permute-start(f32[64,128]{1,0:T(8,128)S(1)} %add.38.refs_0_), channel_id=1, source_target_pairs={{0,24},{4,28},{8,0},{12,4},{16,8},{20,12},{24,16},{28,20},{1,25},{... | collective-permute-start | bytes 98312 | tf_op jit(solution)/shard_map/ppermute | solution.py:568
  70.4 5.7 %collective-permute-start.19 = (f32[64,128]{1,0:T(8,128)S(1)}, f32[64,128]{1,0:T(8,128)S(1)}, u32[]{:S(2)}, u32[]{:S(2)}) collective-permute-start(f32[64,128]{1,0:T(8,128)S(1)} %add.38.refs_0_), channel_id=1, source_target_pairs={{0,8},{4,12},{8,16},{12,20},{16,24},{20,28},{24,0},{28,4},{1,9},{5... | collective-permute-start | bytes 98312 | tf_op jit(solution)/shard_map/ppermute | solution.py:568
  76.1 18.7 %copy-start.11 = (bf16[16,128,128]{2,1,0:T(8,128)(2,1)S(1)}, bf16[16,128,128]{2,1,0:T(8,128)(2,1)}, u32[]{:S(2)}) copy-start(bf16[16,128,128]{2,1,0:T(8,128)(2,1)} %copy-done.10) | copy-start | bytes 1572868
  76.1 18.7 %copy-start.13 = (bf16[16,128,128]{2,1,0:T(8,128)(2,1)S(1)}, bf16[16,128,128]{2,1,0:T(8,128)(2,1)}, u32[]{:S(2)}) copy-start(bf16[16,128,128]{2,1,0:T(8,128)(2,1)} %copy-done.12) | copy-start | bytes 1572868
  76.1 18.7 %copy-start.21 = (f32[1,128]{1,0:T(1,128)S(1)}, f32[1,128]{1,0:T(1,128)}, u32[]{:S(2)}) copy-start(f32[1,128]{1,0:T(1,128)} %get-tuple-element.78.refs_9_.refs_4_) | copy-start | bytes 1540
  79.4 1.5 %collective-permute-start.22 = (f32[512,128]{1,0:T(8,128)S(1)}, f32[512,128]{1,0:T(8,128)S(1)}, u32[]{:S(2)}, u32[]{:S(2)}) collective-permute-start(f32[512,128]{1,0:T(8,128)S(1)} %get-tuple-element.47.mine), channel_id=1, source_target_pairs={{0,1},{1,0},{2,3},{3,2},{4,5},{5,4},{6,7},{7,6},{8,9},{9,8},{10,11... | collective-permute-start | bytes 786440 | tf_op jit(solution)/shard_map/ppermute | solution.py:22
  82.2 4.5 %collective-permute-start.23 = (f32[160,128]{1,0:T(8,128)S(1)}, f32[160,128]{1,0:T(8,128)S(1)}, u32[]{:S(2)}, u32[]{:S(2)}) collective-permute-start(f32[160,128]{1,0:T(8,128)S(1)} %get-tuple-element.49), channel_id=1, source_target_pairs={{0,4},{4,0},{8,12},{12,8},{16,20},{20,16},{24,28},{28,24},{1,5},{5... | collective-permute-start | bytes 245768 | tf_op jit(solution)/shard_map/ppermute | solution.py:22
  86.8 8.0 %collective-permute-start.26 = (f32[160,128]{1,0:T(8,128)S(1)}, f32[160,128]{1,0:T(8,128)S(1)}, u32[]{:S(2)}, u32[]{:S(2)}) collective-permute-start(f32[160,128]{1,0:T(8,128)S(1)} %add.39.refs_0_), channel_id=1, source_target_pairs={{0,16},{4,20},{8,24},{12,28},{16,0},{20,4},{24,8},{28,12},{1,17},{... | collective-permute-start | bytes 245768 | tf_op jit(solution)/shard_map/ppermute | solution.py:568
  86.9 7.9 %collective-permute-start.25 = (f32[160,128]{1,0:T(8,128)S(1)}, f32[160,128]{1,0:T(8,128)S(1)}, u32[]{:S(2)}, u32[]{:S(2)}) collective-permute-start(f32[160,128]{1,0:T(8,128)S(1)} %add.39.refs_0_), channel_id=1, source_target_pairs={{0,24},{4,28},{8,0},{12,4},{16,8},{20,12},{24,16},{28,20},{1,25},{... | collective-permute-start | bytes 245768 | tf_op jit(solution)/shard_map/ppermute | solution.py:568
  88.2 6.6 %collective-permute-start.24 = (f32[160,128]{1,0:T(8,128)S(1)}, f32[160,128]{1,0:T(8,128)S(1)}, u32[]{:S(2)}, u32[]{:S(2)}) collective-permute-start(f32[160,128]{1,0:T(8,128)S(1)} %add.39.refs_0_), channel_id=1, source_target_pairs={{0,8},{4,12},{8,16},{12,20},{16,24},{20,28},{24,0},{28,4},{1,9},{5... | collective-permute-start | bytes 245768 | tf_op jit(solution)/shard_map/ppermute | solution.py:568
  94.8 20.1 %copy-start.7 = (bf16[16,128,128]{2,1,0:T(8,128)(2,1)S(1)}, bf16[16,128,128]{2,1,0:T(8,128)(2,1)}, u32[]{:S(2)}) copy-start(bf16[16,128,128]{2,1,0:T(8,128)(2,1)} %copy-done.6) | copy-start | bytes 1572868
  94.9 20.1 %copy-start.9 = (bf16[16,128,128]{2,1,0:T(8,128)(2,1)S(1)}, bf16[16,128,128]{2,1,0:T(8,128)(2,1)}, u32[]{:S(2)}) copy-start(bf16[16,128,128]{2,1,0:T(8,128)(2,1)} %copy-done.8) | copy-start | bytes 1572868
  94.9 20.1 %copy-start.19 = (f32[1,128]{1,0:T(1,128)S(1)}, f32[1,128]{1,0:T(1,128)}, u32[]{:S(2)}) copy-start(f32[1,128]{1,0:T(1,128)} %copy-done.18) | copy-start | bytes 1540
  97.4 1.6 %collective-permute-start.27 = (f32[512,128]{1,0:T(8,128)S(1)}, f32[512,128]{1,0:T(8,128)S(1)}, u32[]{:S(2)}, u32[]{:S(2)}) collective-permute-start(f32[512,128]{1,0:T(8,128)S(1)} %get-tuple-element.52.mine), channel_id=1, source_target_pairs={{0,1},{1,0},{2,3},{3,2},{4,5},{5,4},{6,7},{7,6},{8,9},{9,8},{10,11... | collective-permute-start | bytes 786440 | tf_op jit(solution)/shard_map/ppermute | solution.py:22
  100.2 4.6 %collective-permute-start.28 = (f32[160,128]{1,0:T(8,128)S(1)}, f32[160,128]{1,0:T(8,128)S(1)}, u32[]{:S(2)}, u32[]{:S(2)}) collective-permute-start(f32[160,128]{1,0:T(8,128)S(1)} %get-tuple-element.54), channel_id=1, source_target_pairs={{0,4},{4,0},{8,12},{12,8},{16,20},{20,16},{24,28},{28,24},{1,5},{5... | collective-permute-start | bytes 245768 | tf_op jit(solution)/shard_map/ppermute | solution.py:22
  104.7 7.5 %collective-permute-start.31 = (f32[160,128]{1,0:T(8,128)S(1)}, f32[160,128]{1,0:T(8,128)S(1)}, u32[]{:S(2)}, u32[]{:S(2)}) collective-permute-start(f32[160,128]{1,0:T(8,128)S(1)} %add.40.refs_0_), channel_id=1, source_target_pairs={{0,16},{4,20},{8,24},{12,28},{16,0},{20,4},{24,8},{28,12},{1,17},{... | collective-permute-start | bytes 245768 | tf_op jit(solution)/shard_map/ppermute | solution.py:568
  106.9 5.3 %collective-permute-start.30 = (f32[160,128]{1,0:T(8,128)S(1)}, f32[160,128]{1,0:T(8,128)S(1)}, u32[]{:S(2)}, u32[]{:S(2)}) collective-permute-start(f32[160,128]{1,0:T(8,128)S(1)} %add.40.refs_0_), channel_id=1, source_target_pairs={{0,24},{4,28},{8,0},{12,4},{16,8},{20,12},{24,16},{28,20},{1,25},{... | collective-permute-start | bytes 245768 | tf_op jit(solution)/shard_map/ppermute | solution.py:568
  108.7 6.2 %collective-permute-start.29 = (f32[160,128]{1,0:T(8,128)S(1)}, f32[160,128]{1,0:T(8,128)S(1)}, u32[]{:S(2)}, u32[]{:S(2)}) collective-permute-start(f32[160,128]{1,0:T(8,128)S(1)} %add.40.refs_0_), channel_id=1, source_target_pairs={{0,8},{4,12},{8,16},{12,20},{16,24},{20,28},{24,0},{28,4},{1,9},{5... | collective-permute-start | bytes 245768 | tf_op jit(solution)/shard_map/ppermute | solution.py:568
  117.4 20.6 %copy-start.14 = (f32[2,2,16,64]{3,2,1,0:T(8,128)S(1)}, f32[2,2,16,64]{3,2,1,0:T(8,128)}, u32[]{:S(2)}) copy-start(f32[2,2,16,64]{3,2,1,0:T(8,128)} %refs_6_.1) | copy-start | bytes 49156
  117.4 20.6 %copy-start.17 = (f32[1,128]{1,0:T(1,128)S(1)}, f32[1,128]{1,0:T(1,128)}, u32[]{:S(2)}) copy-start(f32[1,128]{1,0:T(1,128)} %copy-done.16) | copy-start | bytes 1540
  117.4 1.9 %collective-permute-start.32 = (f32[512,128]{1,0:T(8,128)S(1)}, f32[512,128]{1,0:T(8,128)S(1)}, u32[]{:S(2)}, u32[]{:S(2)}) collective-permute-start(f32[512,128]{1,0:T(8,128)S(1)} %get-tuple-element.57.mine), channel_id=1, source_target_pairs={{0,1},{1,0},{2,3},{3,2},{4,5},{5,4},{6,7},{7,6},{8,9},{9,8},{10,11... | collective-permute-start | bytes 786440 | tf_op jit(solution)/shard_map/ppermute | solution.py:22
  117.8 23.4 %collective-permute-start.42 = (f32[512,128]{1,0:T(8,128)S(1)}, f32[512,128]{1,0:T(8,128)S(1)}, u32[]{:S(2)}, u32[]{:S(2)}) collective-permute-start(f32[512,128]{1,0:T(8,128)S(1)} %shard_map.98.mine), channel_id=1, source_target_pairs={{0,2},{1,3},{2,0},{3,1},{4,6},{5,7},{6,4},{7,5},{8,10},{9,11},{10,... | collective-permute-start | bytes 786440 | tf_op jit(solution)/shard_map/ppermute | solution.py:22
  120.6 4.6 %collective-permute-start.33 = (f32[160,128]{1,0:T(8,128)S(1)}, f32[160,128]{1,0:T(8,128)S(1)}, u32[]{:S(2)}, u32[]{:S(2)}) collective-permute-start(f32[160,128]{1,0:T(8,128)S(1)} %get-tuple-element.59), channel_id=1, source_target_pairs={{0,4},{4,0},{8,12},{12,8},{16,20},{20,16},{24,28},{28,24},{1,5},{5... | collective-permute-start | bytes 245768 | tf_op jit(solution)/shard_map/ppermute | solution.py:22
  122.2 20.6 %collective-permute-start.41 = (f32[512,128]{1,0:T(8,128)S(1)}, f32[512,128]{1,0:T(8,128)S(1)}, u32[]{:S(2)}, u32[]{:S(2)}) collective-permute-start(f32[512,128]{1,0:T(8,128)S(1)} %shard_map.97.mine), channel_id=1, source_target_pairs={{0,2},{1,3},{2,0},{3,1},{4,6},{5,7},{6,4},{7,5},{8,10},{9,11},{10,... | collective-permute-start | bytes 786440 | tf_op jit(solution)/shard_map/ppermute | solution.py:22
  123.4 21.3 %collective-permute-start.40 = (f32[512,128]{1,0:T(8,128)S(1)}, f32[512,128]{1,0:T(8,128)S(1)}, u32[]{:S(2)}, u32[]{:S(2)}) collective-permute-start(f32[512,128]{1,0:T(8,128)S(1)} %get-tuple-element.61.mixture), channel_id=1, source_target_pairs={{0,2},{1,3},{2,0},{3,1},{4,6},{5,7},{6,4},{7,5},{8,10},{9,11},{10,... | collective-permute-start | bytes 786440 | tf_op jit(solution)/shard_map/ppermute | solution.py:22
  125.2 6.5 %collective-permute-start.36 = (f32[160,128]{1,0:T(8,128)S(1)}, f32[160,128]{1,0:T(8,128)S(1)}, u32[]{:S(2)}, u32[]{:S(2)}) collective-permute-start(f32[160,128]{1,0:T(8,128)S(1)} %add.41.refs_0_), channel_id=1, source_target_pairs={{0,16},{4,20},{8,24},{12,28},{16,0},{20,4},{24,8},{28,12},{1,17},{... | collective-permute-start | bytes 245768 | tf_op jit(solution)/shard_map/ppermute | solution.py:568
  126.3 6.2 %collective-permute-start.35 = (f32[160,128]{1,0:T(8,128)S(1)}, f32[160,128]{1,0:T(8,128)S(1)}, u32[]{:S(2)}, u32[]{:S(2)}) collective-permute-start(f32[160,128]{1,0:T(8,128)S(1)} %add.41.refs_0_), channel_id=1, source_target_pairs={{0,24},{4,28},{8,0},{12,4},{16,8},{20,12},{24,16},{28,20},{1,25},{... | collective-permute-start | bytes 245768 | tf_op jit(solution)/shard_map/ppermute | solution.py:568
  131.8 6.2 %collective-permute-start.34 = (f32[160,128]{1,0:T(8,128)S(1)}, f32[160,128]{1,0:T(8,128)S(1)}, u32[]{:S(2)}, u32[]{:S(2)}) collective-permute-start(f32[160,128]{1,0:T(8,128)S(1)} %add.41.refs_0_), channel_id=1, source_target_pairs={{0,8},{4,12},{8,16},{12,20},{16,24},{20,28},{24,0},{28,4},{1,9},{5... | collective-permute-start | bytes 245768 | tf_op jit(solution)/shard_map/ppermute | solution.py:568
  140.2 4.6 %collective-permute-start.39 = (f32[80,128]{1,0:T(8,128)S(1)}, f32[80,128]{1,0:T(8,128)S(1)}, u32[]{:S(2)}, u32[]{:S(2)}) collective-permute-start(f32[80,128]{1,0:T(8,128)S(1)} %shard_map.96.mine), channel_id=1, source_target_pairs={{0,3},{1,2},{2,1},{3,0},{4,7},{5,6},{6,5},{7,4},{8,11},{9,10},{10,... | collective-permute-start | bytes 122888 | tf_op jit(solution)/shard_map/ppermute | solution.py:22
  140.2 4.6 %collective-permute-start.38 = (f32[80,128]{1,0:T(8,128)S(1)}, f32[80,128]{1,0:T(8,128)S(1)}, u32[]{:S(2)}, u32[]{:S(2)}) collective-permute-start(f32[80,128]{1,0:T(8,128)S(1)} %shard_map.96.mine), channel_id=1, source_target_pairs={{0,2},{1,3},{2,0},{3,1},{4,6},{5,7},{6,4},{7,5},{8,10},{9,11},{10,... | collective-permute-start | bytes 122888 | tf_op jit(solution)/shard_map/ppermute | solution.py:22
  141.2 3.6 %collective-permute-start.37 = (f32[80,128]{1,0:T(8,128)S(1)}, f32[80,128]{1,0:T(8,128)S(1)}, u32[]{:S(2)}, u32[]{:S(2)}) collective-permute-start(f32[80,128]{1,0:T(8,128)S(1)} %shard_map.96.mine), channel_id=1, source_target_pairs={{0,1},{1,0},{2,3},{3,2},{4,5},{5,4},{6,7},{7,6},{8,9},{9,8},{10,11... | collective-permute-start | bytes 122888 | tf_op jit(solution)/shard_map/ppermute | solution.py:22
  (5 other events, 3.7 us)

commit v4 on v3

--- a/solution.py
+++ b/solution.py
@@ -182,7 +182,7 @@
     return scratch[pl.ds(0, 2 * count), :]
 
 
-def start_kernel(member, *refs):
+def start_kernel(member, _, *refs):
     sources, (keep, send), (*local, sems, scratch) = refs[:3], refs[3:5], refs[5:]
     copies = [
         pltpu.make_async_copy(source, target, sems.at[at])
@@ -608,10 +608,11 @@
             scratch(2 * height, LANES),
         ],
         here,
+        spot,
         last_cores,
         first_cores,
         sketch_last,
-        in_hbm=(1, 2, 3),
+        in_hbm=(2, 3, 4),
         limit=None,
     )
     keeps, sends = [keep], []

time: 147 us -> 139 us (0.946)
  local copies, waits for them, and re-layouts: 12.4 us -> 3.81 us
  waiting for transfers between devices: 62.9 us -> 67 us
  starting transfers between devices: 42.7 us -> 40.6 us
    unnamed x52 -> x8, local copies, waits for them, and re-layouts: 7.24 us -> 0.79 us
    ppermute x21, waiting for transfers between devices: 20.3 us -> 23.9 us  [flip(): lax.ppermute(value, axis, [(index, index ^ bits) for index in range(size)])]
    ppermute x21, starting transfers between devices: 18.3 us -> 15.7 us  [flip(): lax.ppermute(value, axis, [(index, index ^ bits) for index in range(size)])]
    dynamic_slice x2, local copies, waits for them, and re-layouts: 4.59 us -> 2.96 us  [half_of(): lax.dynamic_slice(source, (index, 0, position, 0, 0), (1, count, 1, slice...]
  transfers between devices with their start and end apart: 43 -> 43, of which waited for: 23 -> 24; matrix products, arithmetic and copies ran while one was open for 4% -> 2% of each run, Pallas kernels for 6% -> 7%
where the time goes in v4:
time: 139 us; the launch traced here: 138 us
  waiting for transfers between devices  67 us (48%)
  starting transfers between devices  40.6 us (29%)
  Pallas kernels  25.8 us (19%)
  local copies, waits for them, and re-layouts  3.81 us (3%)
    ppermute x21, waiting for transfers between devices, spread(): parts.append(lax.ppermute(value, axis, pairs))  43.1 us
    pallas_call x18, Pallas kernels, kernel_call(): pl.pallas_call(body, out_shape=outs, in_specs=specs[:len(operands)], out_...  25.8 us
    ppermute x21, waiting for transfers between devices, flip(): lax.ppermute(value, axis, [(index, index ^ bits) for index in range(size)])  23.9 us
    ppermute x21, starting transfers between devices, spread(): parts.append(lax.ppermute(value, axis, pairs))  20.9 us
    ppermute x21, starting transfers between devices, flip(): lax.ppermute(value, axis, [(index, index ^ bits) for index in range(size)])  15.7 us
    ppermute x1, starting transfers between devices, tiled(): sends.append(lax.ppermute(send, ('mode', 'rep'), pairs))  3.99 us
    dynamic_slice x2, local copies, waits for them, and re-layouts, half_of(): lax.dynamic_slice(source, (index, 0, position, 0, 0), (1, count, 1, slice...  2.96 us
  transfers between devices with their start and end apart: 43, of which 24 were waited for; matrix products, arithmetic and copies ran while one was open for 2% of the time, Pallas kernels for 7%

profile of v4, /device:TPU:0, one launch (start us, length us, event | category | flops | bytes accessed | tf_op | source)
XLA Modules:
  0.0 138.4 jit_solution(5704437319209704196)
XLA Ops:
  0.7 1.9 %shard_map.85 = (f32[80,128]{1,0:T(8,128)}, f32[96,128]{1,0:T(8,128)}) custom-call(s32[1]{0:T(128)} %bitcast.member.refs_5_, s32[1]{0:T(128)} %bitcast.1._.refs_8_, f32[2,2,16,64]{3,2,1,0:T(8,128)} %refs_6_.1, f32[2,2,16,64]{3,2,1,0:T(8,128)} %refs_1_.1, f32[16,64]{1,0:T(8,128)} %refs_2_.1), custom_call_target="tpu_custom_call" | custom-call | bytes 126984 | tf_op jit(solution)/shard_map/pallas_call | solution.py:523
  2.5 4.0 %collective-permute-start.2 = (f32[96,128]{1,0:T(8,128)}, f32[96,128]{1,0:T(8,128)S(1)}, u32[]{:S(2)}, u32[]{:S(2)}) collective-permute-start(f32[96,128]{1,0:T(8,128)} %get-tuple-element.37), channel_id=1, source_target_pairs={{0,6},{1,7},{2,4},{3,5},{4,2},{5,3},{6,0},{7,1},{8,14},{9,15},{10,... | collective-permute-start | bytes 147464 | tf_op jit(solution)/shard_map/ppermute | solution.py:628
  7.2 1.1 constant_dynamic-slice_fusion.4
  8.3 2.0 %collective-permute-start.6 = (f32[2,512,128]{2,1,0:T(8,128)S(1)}, f32[2,512,128]{2,1,0:T(8,128)S(1)}, u32[]{:S(2)}, u32[]{:S(2)}) collective-permute-start(f32[2,512,128]{2,1,0:T(8,128)S(1)} %bitcast.54), channel_id=1, source_target_pairs={{0,2},{1,3},{2,0},{3,1},{4,6},{5,7},{6,4},{7,5},{8,10},{9,11},{10,... | collective-permute-start | bytes 1572872 | tf_op jit(solution)/shard_map/ppermute | solution.py:22
  10.2 1.1 collective-permute-done.refs_1_
  12.1 2.6 %collective-permute-start.5 = (f32[192,128]{1,0:T(8,128)S(1)}, f32[192,128]{1,0:T(8,128)S(1)}, u32[]{:S(2)}, u32[]{:S(2)}) collective-permute-start(f32[192,128]{1,0:T(8,128)S(1)} %shard_map.86.refs_0_.refs_4_), channel_id=1, source_target_pairs={{0,16},{4,20},{8,24},{12,28},{16,0},{20,4},{24,8},{28,12},{1,17},{... | collective-permute-start | bytes 294920 | tf_op jit(solution)/shard_map/ppermute | solution.py:568
  14.8 1.4 collective-permute-start.4
  16.2 1.9 %constant_dynamic-slice_fusion = (f32[1,2,1,16,4096]{4,3,2,1,0:T(8,128)S(1)}, f32[1,2,1,16,4096]{4,3,2,1,0:T(8,128)S(1)}, f32[1,2,1,16,4096]{4,3,2,1,0:T(8,128)S...) fusion(f32[2,2,3,16,4096]{4,3,2,1,0:T(8,128)} %param.7, s32[]{:T(128)S(6)} %select_n.17, s32[]{:T(128)S(6)} %select_n.16), kind=kLoop, calls=%fused_computation.2 | loop fusion | bytes 5242888 | tf_op jit(solution)/shard_map/dynamic_slice | solution.py:595
  18.1 1.5 %collective-permute-start.11 = (f32[2,512,128]{2,1,0:T(8,128)S(1)}, f32[2,512,128]{2,1,0:T(8,128)S(1)}, u32[]{:S(2)}, u32[]{:S(2)}) collective-permute-start(f32[2,512,128]{2,1,0:T(8,128)S(1)} %bitcast.56), channel_id=1, source_target_pairs={{0,2},{1,3},{2,0},{3,1},{4,6},{5,7},{6,4},{7,5},{8,10},{9,11},{10,... | collective-permute-start | bytes 1572872 | tf_op jit(solution)/shard_map/ppermute | solution.py:22
  20.4 0.8 collective-permute-start.3
  21.2 5.6 %collective-permute-done.3.refs_1_.refs_5_ = f32[192,128]{1,0:T(8,128)S(1)} collective-permute-done((f32[192,128]{1,0:T(8,128)S(1)}, f32[192,128]{1,0:T(8,128)S(1)}, u32[]{:S(2)}, u32[]{:S(2)}) %collective-permute-start.3) | collective-permute-done | bytes 98336 | tf_op jit(solution)/shard_map/ppermute | solution.py:568
  26.8 1.4 %shard_map.87 = (f32[128,128]{1,0:T(8,128)S(1)}, bf16[16,128,128]{2,1,0:T(8,128)(2,1)S(1)}, bf16[16,128,128]{2,1,0:T(8,128)(2,1)S(1)}) custom-call(f32[192,128]{1,0:T(8,128)S(1)} %shard_map.86.refs_0_.refs_4_, f32[192,128]{1,0:T(8,128)S(1)} %collective-permute-done.3.refs_1_.refs_5_, f32[192,128]{1,0:T(8,128)S(1)} %collective-permute-done.4.refs_2_.refs_6_, ...), custom_call_target="tpu_custom_call" | custom-call | bytes 2818560 | tf_op jit(solution)/shard_map/pallas_call | solution.py:523
  28.2 0.8 collective-permute-start.7
  29.0 3.5 %collective-permute-done.7 = f32[128,128]{1,0:T(8,128)S(1)} collective-permute-done((f32[128,128]{1,0:T(8,128)S(1)}, f32[128,128]{1,0:T(8,128)S(1)}, u32[]{:S(2)}, u32[]{:S(2)}) %collective-permute-start.7) | collective-permute-done | bytes 65568 | tf_op jit(solution)/shard_map/ppermute | solution.py:22
  32.6 1.9 %collective-permute-start.9 = (f32[128,128]{1,0:T(8,128)S(1)}, f32[128,128]{1,0:T(8,128)S(1)}, u32[]{:S(2)}, u32[]{:S(2)}) collective-permute-start(f32[128,128]{1,0:T(8,128)S(1)} %add.35.refs_0_), channel_id=1, source_target_pairs={{0,24},{4,28},{8,0},{12,4},{16,8},{20,12},{24,16},{28,20},{1,25},{... | collective-permute-start | bytes 196616 | tf_op jit(solution)/shard_map/ppermute | solution.py:568
  35.0 3.2 %collective-permute-done.10.refs_3_ = f32[128,128]{1,0:T(8,128)S(1)} collective-permute-done((f32[128,128]{1,0:T(8,128)S(1)}, f32[128,128]{1,0:T(8,128)S(1)}, u32[]{:S(2)}, u32[]{:S(2)}) %collective-permute-start.10) | collective-permute-done | bytes 65568 | tf_op jit(solution)/shard_map/ppermute | solution.py:568
  38.7 1.9 %collective-permute-done.8.refs_1_ = f32[128,128]{1,0:T(8,128)S(1)} collective-permute-done((f32[128,128]{1,0:T(8,128)S(1)}, f32[128,128]{1,0:T(8,128)S(1)}, u32[]{:S(2)}, u32[]{:S(2)}) %collective-permute-start.8) | collective-permute-done | bytes 65568 | tf_op jit(solution)/shard_map/ppermute | solution.py:568
  40.6 1.4 %shard_map.88 = (f32[128,128]{1,0:T(8,128)S(1)}, bf16[16,128,128]{2,1,0:T(8,128)(2,1)S(1)}, bf16[16,128,128]{2,1,0:T(8,128)(2,1)S(1)}) custom-call(f32[128,128]{1,0:T(8,128)S(1)} %add.35.refs_0_, f32[128,128]{1,0:T(8,128)S(1)} %collective-permute-done.8.refs_1_, f32[128,128]{1,0:T(8,128)S(1)} %collective-permute-done.9.refs_2_, ...), custom_call_target="tpu_custom_call" | custom-call | bytes 2687488 | tf_op jit(solution)/shard_map/pallas_call | solution.py:523
  42.7 3.6 %collective-permute-done.12 = f32[128,128]{1,0:T(8,128)S(1)} collective-permute-done((f32[128,128]{1,0:T(8,128)S(1)}, f32[128,128]{1,0:T(8,128)S(1)}, u32[]{:S(2)}, u32[]{:S(2)}) %collective-permute-start.12) | collective-permute-done | bytes 65568 | tf_op jit(solution)/shard_map/ppermute | solution.py:22
  46.5 1.1 collective-permute-start.14
  47.6 0.9 collective-permute-start.13
  48.6 3.0 %collective-permute-done.15.refs_3_ = f32[128,128]{1,0:T(8,128)S(1)} collective-permute-done((f32[128,128]{1,0:T(8,128)S(1)}, f32[128,128]{1,0:T(8,128)S(1)}, u32[]{:S(2)}, u32[]{:S(2)}) %collective-permute-start.15) | collective-permute-done | bytes 65568 | tf_op jit(solution)/shard_map/ppermute | solution.py:568
  51.6 2.2 %collective-permute-done.13.refs_1_ = f32[128,128]{1,0:T(8,128)S(1)} collective-permute-done((f32[128,128]{1,0:T(8,128)S(1)}, f32[128,128]{1,0:T(8,128)S(1)}, u32[]{:S(2)}, u32[]{:S(2)}) %collective-permute-start.13) | collective-permute-done | bytes 65568 | tf_op jit(solution)/shard_map/ppermute | solution.py:568
  53.7 1.9 %shard_map.89 = (f32[64,128]{1,0:T(8,128)S(1)}, bf16[16,128,128]{2,1,0:T(8,128)(2,1)S(1)}, bf16[16,128,128]{2,1,0:T(8,128)(2,1)S(1)}) custom-call(f32[128,128]{1,0:T(8,128)S(1)} %add.36.refs_0_, f32[128,128]{1,0:T(8,128)S(1)} %collective-permute-done.13.refs_1_, f32[128,128]{1,0:T(8,128)S(1)} %collective-permute-done.14.refs_2_, ...), custom_call_target="tpu_custom_call" | custom-call | bytes 3048452 | tf_op jit(solution)/shard_map/pallas_call | solution.py:523
  55.7 1.2 collective-permute-done.17
  56.9 1.1 collective-permute-start.18
  58.0 2.8 %collective-permute-done.18 = f32[64,128]{1,0:T(8,128)S(1)} collective-permute-done((f32[64,128]{1,0:T(8,128)S(1)}, f32[64,128]{1,0:T(8,128)S(1)}, u32[]{:S(2)}, u32[]{:S(2)}) %collective-permute-start.18) | collective-permute-done | bytes 32800 | tf_op jit(solution)/shard_map/ppermute | solution.py:22
  60.8 1.5 %collective-permute-start.20 = (f32[64,128]{1,0:T(8,128)S(1)}, f32[64,128]{1,0:T(8,128)S(1)}, u32[]{:S(2)}, u32[]{:S(2)}) collective-permute-start(f32[64,128]{1,0:T(8,128)S(1)} %add.38.refs_0_), channel_id=1, source_target_pairs={{0,24},{4,28},{8,0},{12,4},{16,8},{20,12},{24,16},{28,20},{1,25},{... | collective-permute-start | bytes 98312 | tf_op jit(solution)/shard_map/ppermute | solution.py:568
  62.9 3.1 %collective-permute-done.21.refs_3_ = f32[64,128]{1,0:T(8,128)S(1)} collective-permute-done((f32[64,128]{1,0:T(8,128)S(1)}, f32[64,128]{1,0:T(8,128)S(1)}, u32[]{:S(2)}, u32[]{:S(2)}) %collective-permute-start.21) | collective-permute-done | bytes 32800 | tf_op jit(solution)/shard_map/ppermute | solution.py:568
  65.9 2.0 %collective-permute-done.19.refs_1_ = f32[64,128]{1,0:T(8,128)S(1)} collective-permute-done((f32[64,128]{1,0:T(8,128)S(1)}, f32[64,128]{1,0:T(8,128)S(1)}, u32[]{:S(2)}, u32[]{:S(2)}) %collective-permute-start.19) | collective-permute-done | bytes 32800 | tf_op jit(solution)/shard_map/ppermute | solution.py:568
  68.0 3.3 %shard_map.90 = (f32[64,128]{1,0:T(8,128)}, f32[128,128]{1,0:T(8,128)S(1)}, f32[16,128]{1,0:T(8,128)S(1)}, f32[512,128]{1,0:T(8,128)S(1)}) custom-call(f32[64,128]{1,0:T(8,128)S(1)} %add.38.refs_0_, f32[64,128]{1,0:T(8,128)S(1)} %collective-permute-done.19.refs_1_, f32[64,128]{1,0:T(8,128)S(1)} %collective-permute-done.20.refs_2_, ...), custom_call_target="tpu_custom_call" | custom-call | bytes 1942020 | tf_op jit(solution)/shard_map/pallas_call | solution.py:523
  71.3 1.5 %collective-permute-done.22.theirs = f32[512,128]{1,0:T(8,128)S(1)} collective-permute-done((f32[512,128]{1,0:T(8,128)S(1)}, f32[512,128]{1,0:T(8,128)S(1)}, u32[]{:S(2)}, u32[]{:S(2)}) %collective-permute-start.22) | collective-permute-done | bytes 262176 | tf_op jit(solution)/shard_map/ppermute | solution.py:22
  72.8 1.3 shard_map.91
  74.1 1.0 collective-permute-start.23
  75.1 3.5 %collective-permute-done.23 = f32[160,128]{1,0:T(8,128)S(1)} collective-permute-done((f32[160,128]{1,0:T(8,128)S(1)}, f32[160,128]{1,0:T(8,128)S(1)}, u32[]{:S(2)}, u32[]{:S(2)}) %collective-permute-start.23) | collective-permute-done | bytes 81952 | tf_op jit(solution)/shard_map/ppermute | solution.py:22
  78.8 1.2 collective-permute-start.25
  80.0 0.8 collective-permute-start.24
  80.8 5.9 %collective-permute-done.26.refs_3_ = f32[160,128]{1,0:T(8,128)S(1)} collective-permute-done((f32[160,128]{1,0:T(8,128)S(1)}, f32[160,128]{1,0:T(8,128)S(1)}, u32[]{:S(2)}, u32[]{:S(2)}) %collective-permute-start.26) | collective-permute-done | bytes 81952 | tf_op jit(solution)/shard_map/ppermute | solution.py:568
  86.7 2.5 %shard_map.92 = (f32[64,128]{1,0:T(8,128)S(1)}, f32[128,128]{1,0:T(8,128)S(1)}, f32[512,128]{1,0:T(8,128)S(1)}) custom-call(f32[160,128]{1,0:T(8,128)S(1)} %add.39.refs_0_, f32[160,128]{1,0:T(8,128)S(1)} %collective-permute-done.24.refs_1_, f32[160,128]{1,0:T(8,128)S(1)} %collective-permute-done.25.refs_2_, f32[160,128]{1,0:T(8,128)S(1)} %collective-permute-done.26.refs_3_, ...), custom_call_target="tpu_custom_call" | custom-call | bytes 1737216 | tf_op jit(solution)/shard_map/pallas_call | solution.py:523
  89.2 1.5 %collective-permute-done.27.theirs = f32[512,128]{1,0:T(8,128)S(1)} collective-permute-done((f32[512,128]{1,0:T(8,128)S(1)}, f32[512,128]{1,0:T(8,128)S(1)}, u32[]{:S(2)}, u32[]{:S(2)}) %collective-permute-start.27) | collective-permute-done | bytes 262176 | tf_op jit(solution)/shard_map/ppermute | solution.py:22
  90.8 1.3 shard_map.93
  92.0 1.0 collective-permute-start.28
  93.1 3.5 %collective-permute-done.28 = f32[160,128]{1,0:T(8,128)S(1)} collective-permute-done((f32[160,128]{1,0:T(8,128)S(1)}, f32[160,128]{1,0:T(8,128)S(1)}, u32[]{:S(2)}, u32[]{:S(2)}) %collective-permute-start.28) | collective-permute-done | bytes 81952 | tf_op jit(solution)/shard_map/ppermute | solution.py:22
  96.6 2.2 %collective-permute-start.31 = (f32[160,128]{1,0:T(8,128)S(1)}, f32[160,128]{1,0:T(8,128)S(1)}, u32[]{:S(2)}, u32[]{:S(2)}) collective-permute-start(f32[160,128]{1,0:T(8,128)S(1)} %add.40.refs_0_), channel_id=1, source_target_pairs={{0,16},{4,20},{8,24},{12,28},{16,0},{20,4},{24,8},{28,12},{1,17},{... | collective-permute-start | bytes 245768 | tf_op jit(solution)/shard_map/ppermute | solution.py:568
  98.8 1.8 %collective-permute-start.30 = (f32[160,128]{1,0:T(8,128)S(1)}, f32[160,128]{1,0:T(8,128)S(1)}, u32[]{:S(2)}, u32[]{:S(2)}) collective-permute-start(f32[160,128]{1,0:T(8,128)S(1)} %add.40.refs_0_), channel_id=1, source_target_pairs={{0,24},{4,28},{8,0},{12,4},{16,8},{20,12},{24,16},{28,20},{1,25},{... | collective-permute-start | bytes 245768 | tf_op jit(solution)/shard_map/ppermute | solution.py:568
  100.8 3.3 %collective-permute-done.31.refs_3_ = f32[160,128]{1,0:T(8,128)S(1)} collective-permute-done((f32[160,128]{1,0:T(8,128)S(1)}, f32[160,128]{1,0:T(8,128)S(1)}, u32[]{:S(2)}, u32[]{:S(2)}) %collective-permute-start.31) | collective-permute-done | bytes 81952 | tf_op jit(solution)/shard_map/ppermute | solution.py:568
  104.1 2.6 %collective-permute-done.29.refs_1_ = f32[160,128]{1,0:T(8,128)S(1)} collective-permute-done((f32[160,128]{1,0:T(8,128)S(1)}, f32[160,128]{1,0:T(8,128)S(1)}, u32[]{:S(2)}, u32[]{:S(2)}) %collective-permute-start.29) | collective-permute-done | bytes 81952 | tf_op jit(solution)/shard_map/ppermute | solution.py:568
  106.8 2.5 %shard_map.94 = (f32[64,128]{1,0:T(8,128)S(1)}, f32[128,128]{1,0:T(8,128)S(1)}, f32[512,128]{1,0:T(8,128)S(1)}) custom-call(f32[160,128]{1,0:T(8,128)S(1)} %add.40.refs_0_, f32[160,128]{1,0:T(8,128)S(1)} %collective-permute-done.29.refs_1_, f32[160,128]{1,0:T(8,128)S(1)} %collective-permute-done.30.refs_2_, f32[160,128]{1,0:T(8,128)S(1)} %collective-permute-done.31.refs_3_, ...), custom_call_target="tpu_custom_call" | custom-call | bytes 1737216 | tf_op jit(solution)/shard_map/pallas_call | solution.py:523
  109.7 1.5 %collective-permute-start.42 = (f32[512,128]{1,0:T(8,128)S(1)}, f32[512,128]{1,0:T(8,128)S(1)}, u32[]{:S(2)}, u32[]{:S(2)}) collective-permute-start(f32[512,128]{1,0:T(8,128)S(1)} %shard_map.98.mine), channel_id=1, source_target_pairs={{0,2},{1,3},{2,0},{3,1},{4,6},{5,7},{6,4},{7,5},{8,10},{9,11},{10,... | collective-permute-start | bytes 786440 | tf_op jit(solution)/shard_map/ppermute | solution.py:22
  111.2 1.2 shard_map.95
  113.4 1.0 collective-permute-start.41
  114.4 1.1 collective-permute-start.40
  115.5 1.6 %collective-permute-done.33 = f32[160,128]{1,0:T(8,128)S(1)} collective-permute-done((f32[160,128]{1,0:T(8,128)S(1)}, f32[160,128]{1,0:T(8,128)S(1)}, u32[]{:S(2)}, u32[]{:S(2)}) %collective-permute-start.33) | collective-permute-done | bytes 81952 | tf_op jit(solution)/shard_map/ppermute | solution.py:22
  117.1 1.1 collective-permute-start.36
  118.2 1.1 collective-permute-start.35
  119.3 4.3 %collective-permute-done.36.refs_3_ = f32[160,128]{1,0:T(8,128)S(1)} collective-permute-done((f32[160,128]{1,0:T(8,128)S(1)}, f32[160,128]{1,0:T(8,128)S(1)}, u32[]{:S(2)}, u32[]{:S(2)}) %collective-permute-start.36) | collective-permute-done | bytes 81952 | tf_op jit(solution)/shard_map/ppermute | solution.py:568
  124.3 5.5 %collective-permute-done.34.refs_1_ = f32[160,128]{1,0:T(8,128)S(1)} collective-permute-done((f32[160,128]{1,0:T(8,128)S(1)}, f32[160,128]{1,0:T(8,128)S(1)}, u32[]{:S(2)}, u32[]{:S(2)}) %collective-permute-start.34) | collective-permute-done | bytes 81952 | tf_op jit(solution)/shard_map/ppermute | solution.py:568
  129.9 2.1 %shard_map.96.mine = f32[80,128]{1,0:T(8,128)S(1)} custom-call(f32[160,128]{1,0:T(8,128)S(1)} %add.41.refs_0_, f32[160,128]{1,0:T(8,128)S(1)} %collective-permute-done.34.refs_1_, f32[160,128]{1,0:T(8,128)S(1)} %collective-permute-done.35.refs_2_, f32[160,128]{1,0:T(8,128)S(1)} %collective-permute-done.36.refs_3_, f32[1,128]{1,0:T(1,128)S(1)} %get-tuple-element.80.refs_4_, ...), custom_call_target="tpu_custom_call" | custom-call | bytes 401924 | tf_op jit(solution)/shard_map/pallas_call | solution.py:523
  132.0 1.0 collective-permute-start.38
  133.0 0.9 collective-permute-start.37
  133.9 0.8 shard_map.99.refs_0_
  134.7 0.8 shard_map.100.before
  135.5 1.0 shard_map.101.before
  136.6 1.7 %shard_map.102 = (f32[2,16,64]{2,1,0:T(8,128)}, f32[2,16,64]{2,1,0:T(8,128)}, f32[2,3,512,128]{3,2,1,0:T(8,128)}) custom-call(s32[1]{0:T(128)} %bitcast.member.refs_5_, f32[80,128]{1,0:T(8,128)S(1)} %shard_map.96.mine, f32[80,128]{1,0:T(8,128)S(1)} %collective-permute-done.37.near, ...), custom_call_target="tpu_custom_call", output_to_operand_aliasing={{2}: (6, {})} | custom-call | bytes 3588100 | tf_op jit(solution)/shard_map/pallas_call | solution.py:523
  (62 shorter events, 7.5 us)
Async XLA Ops:
  0.6 15.5 %copy-start.2 = (f32[3,16,4096]{2,1,0:T(8,128)S(1)}, f32[3,16,4096]{2,1,0:T(8,128)}, u32[]{:S(2)}) copy-start(f32[3,16,4096]{2,1,0:T(8,128)} %param.9) | copy-start | bytes 2359300
  2.5 8.7 %collective-permute-start.2 = (f32[96,128]{1,0:T(8,128)}, f32[96,128]{1,0:T(8,128)S(1)}, u32[]{:S(2)}, u32[]{:S(2)}) collective-permute-start(f32[96,128]{1,0:T(8,128)} %get-tuple-element.37), channel_id=1, source_target_pairs={{0,6},{1,7},{2,4},{3,5},{4,2},{5,3},{6,0},{7,1},{8,14},{9,15},{10,... | collective-permute-start | bytes 147464 | tf_op jit(solution)/shard_map/ppermute | solution.py:628
  6.5 4.8 %collective-permute-start.1 = (f32[96,128]{1,0:T(8,128)}, f32[96,128]{1,0:T(8,128)S(1)}, u32[]{:S(2)}, u32[]{:S(2)}) collective-permute-start(f32[96,128]{1,0:T(8,128)} %get-tuple-element.37), channel_id=1, source_target_pairs={{0,2},{1,3},{2,0},{3,1},{4,6},{5,7},{6,4},{7,5},{8,10},{9,11},{10,... | collective-permute-start | bytes 147464 | tf_op jit(solution)/shard_map/ppermute | solution.py:22
  7.1 4.2 %collective-permute-start = (f32[80,128]{1,0:T(8,128)}, f32[80,128]{1,0:T(8,128)S(1)}, u32[]{:S(2)}, u32[]{:S(2)}) collective-permute-start(f32[80,128]{1,0:T(8,128)} %get-tuple-element.36.refs_0_), channel_id=1, source_target_pairs={{0,4},{4,0},{8,12},{12,8},{16,20},{20,16},{24,28},{28,24},{1,5},{5... | collective-permute-start | bytes 122888 | tf_op jit(solution)/shard_map/ppermute | solution.py:22
  8.3 18.5 %collective-permute-start.6 = (f32[2,512,128]{2,1,0:T(8,128)S(1)}, f32[2,512,128]{2,1,0:T(8,128)S(1)}, u32[]{:S(2)}, u32[]{:S(2)}) collective-permute-start(f32[2,512,128]{2,1,0:T(8,128)S(1)} %bitcast.54), channel_id=1, source_target_pairs={{0,2},{1,3},{2,0},{3,1},{4,6},{5,7},{6,4},{7,5},{8,10},{9,11},{10,... | collective-permute-start | bytes 1572872 | tf_op jit(solution)/shard_map/ppermute | solution.py:22
  11.4 0.8 copy-start.1
  12.1 8.2 %collective-permute-start.5 = (f32[192,128]{1,0:T(8,128)S(1)}, f32[192,128]{1,0:T(8,128)S(1)}, u32[]{:S(2)}, u32[]{:S(2)}) collective-permute-start(f32[192,128]{1,0:T(8,128)S(1)} %shard_map.86.refs_0_.refs_4_), channel_id=1, source_target_pairs={{0,16},{4,20},{8,24},{12,28},{16,0},{20,4},{24,8},{28,12},{1,17},{... | collective-permute-start | bytes 294920 | tf_op jit(solution)/shard_map/ppermute | solution.py:568
  14.8 6.4 %collective-permute-start.4 = (f32[192,128]{1,0:T(8,128)S(1)}, f32[192,128]{1,0:T(8,128)S(1)}, u32[]{:S(2)}, u32[]{:S(2)}) collective-permute-start(f32[192,128]{1,0:T(8,128)S(1)} %shard_map.86.refs_0_.refs_4_), channel_id=1, source_target_pairs={{0,24},{4,28},{8,0},{12,4},{16,8},{20,12},{24,16},{28,20},{1,25},{... | collective-permute-start | bytes 294920 | tf_op jit(solution)/shard_map/ppermute | solution.py:568
  16.2 3.4 %copy-start.3 = (s32[4]{0:T(128)S(1)}, s32[4]{0:T(128)}, u32[]{:S(2)}) copy-start(s32[4]{0:T(128)} %param.11) | copy-start | bytes 52
  18.1 16.9 %collective-permute-start.11 = (f32[2,512,128]{2,1,0:T(8,128)S(1)}, f32[2,512,128]{2,1,0:T(8,128)S(1)}, u32[]{:S(2)}, u32[]{:S(2)}) collective-permute-start(f32[2,512,128]{2,1,0:T(8,128)S(1)} %bitcast.56), channel_id=1, source_target_pairs={{0,2},{1,3},{2,0},{3,1},{4,6},{5,7},{6,4},{7,5},{8,10},{9,11},{10,... | collective-permute-start | bytes 1572872 | tf_op jit(solution)/shard_map/ppermute | solution.py:22
  19.7 28.9 %collective-permute-start.16 = (f32[2,512,128]{2,1,0:T(8,128)S(1)}, f32[2,512,128]{2,1,0:T(8,128)S(1)}, u32[]{:S(2)}, u32[]{:S(2)}) collective-permute-start(f32[2,512,128]{2,1,0:T(8,128)S(1)} %bitcast.55), channel_id=1, source_target_pairs={{0,2},{1,3},{2,0},{3,1},{4,6},{5,7},{6,4},{7,5},{8,10},{9,11},{10,... | collective-permute-start | bytes 1572872 | tf_op jit(solution)/shard_map/ppermute | solution.py:22
  20.4 6.4 %collective-permute-start.3 = (f32[192,128]{1,0:T(8,128)S(1)}, f32[192,128]{1,0:T(8,128)S(1)}, u32[]{:S(2)}, u32[]{:S(2)}) collective-permute-start(f32[192,128]{1,0:T(8,128)S(1)} %shard_map.86.refs_0_.refs_4_), channel_id=1, source_target_pairs={{0,8},{4,12},{8,16},{12,20},{16,24},{20,28},{24,0},{28,4},{1,9},{5... | collective-permute-start | bytes 294920 | tf_op jit(solution)/shard_map/ppermute | solution.py:568
  28.2 4.3 %collective-permute-start.7 = (f32[128,128]{1,0:T(8,128)S(1)}, f32[128,128]{1,0:T(8,128)S(1)}, u32[]{:S(2)}, u32[]{:S(2)}) collective-permute-start(f32[128,128]{1,0:T(8,128)S(1)} %get-tuple-element.42), channel_id=1, source_target_pairs={{0,4},{4,0},{8,12},{12,8},{16,20},{20,16},{24,28},{28,24},{1,5},{5... | collective-permute-start | bytes 196616 | tf_op jit(solution)/shard_map/ppermute | solution.py:22
  32.5 5.7 %collective-permute-start.10 = (f32[128,128]{1,0:T(8,128)S(1)}, f32[128,128]{1,0:T(8,128)S(1)}, u32[]{:S(2)}, u32[]{:S(2)}) collective-permute-start(f32[128,128]{1,0:T(8,128)S(1)} %add.35.refs_0_), channel_id=1, source_target_pairs={{0,16},{4,20},{8,24},{12,28},{16,0},{20,4},{24,8},{28,12},{1,17},{... | collective-permute-start | bytes 196616 | tf_op jit(solution)/shard_map/ppermute | solution.py:568
  32.6 6.0 %collective-permute-start.9 = (f32[128,128]{1,0:T(8,128)S(1)}, f32[128,128]{1,0:T(8,128)S(1)}, u32[]{:S(2)}, u32[]{:S(2)}) collective-permute-start(f32[128,128]{1,0:T(8,128)S(1)} %add.35.refs_0_), channel_id=1, source_target_pairs={{0,24},{4,28},{8,0},{12,4},{16,8},{20,12},{24,16},{28,20},{1,25},{... | collective-permute-start | bytes 196616 | tf_op jit(solution)/shard_map/ppermute | solution.py:568
  34.5 6.1 %collective-permute-start.8 = (f32[128,128]{1,0:T(8,128)S(1)}, f32[128,128]{1,0:T(8,128)S(1)}, u32[]{:S(2)}, u32[]{:S(2)}) collective-permute-start(f32[128,128]{1,0:T(8,128)S(1)} %add.35.refs_0_), channel_id=1, source_target_pairs={{0,8},{4,12},{8,16},{12,20},{16,24},{20,28},{24,0},{28,4},{1,9},{5... | collective-permute-start | bytes 196616 | tf_op jit(solution)/shard_map/ppermute | solution.py:568
  42.0 4.3 %collective-permute-start.12 = (f32[128,128]{1,0:T(8,128)S(1)}, f32[128,128]{1,0:T(8,128)S(1)}, u32[]{:S(2)}, u32[]{:S(2)}) collective-permute-start(f32[128,128]{1,0:T(8,128)S(1)} %get-tuple-element.43), channel_id=1, source_target_pairs={{0,4},{4,0},{8,12},{12,8},{16,20},{20,16},{24,28},{28,24},{1,5},{5... | collective-permute-start | bytes 196616 | tf_op jit(solution)/shard_map/ppermute | solution.py:22
  46.3 5.2 %collective-permute-start.15 = (f32[128,128]{1,0:T(8,128)S(1)}, f32[128,128]{1,0:T(8,128)S(1)}, u32[]{:S(2)}, u32[]{:S(2)}) collective-permute-start(f32[128,128]{1,0:T(8,128)S(1)} %add.36.refs_0_), channel_id=1, source_target_pairs={{0,16},{4,20},{8,24},{12,28},{16,0},{20,4},{24,8},{28,12},{1,17},{... | collective-permute-start | bytes 196616 | tf_op jit(solution)/shard_map/ppermute | solution.py:568
  46.5 5.0 %collective-permute-start.14 = (f32[128,128]{1,0:T(8,128)S(1)}, f32[128,128]{1,0:T(8,128)S(1)}, u32[]{:S(2)}, u32[]{:S(2)}) collective-permute-start(f32[128,128]{1,0:T(8,128)S(1)} %add.36.refs_0_), channel_id=1, source_target_pairs={{0,24},{4,28},{8,0},{12,4},{16,8},{20,12},{24,16},{28,20},{1,25},{... | collective-permute-start | bytes 196616 | tf_op jit(solution)/shard_map/ppermute | solution.py:568
  47.6 6.1 %collective-permute-start.13 = (f32[128,128]{1,0:T(8,128)S(1)}, f32[128,128]{1,0:T(8,128)S(1)}, u32[]{:S(2)}, u32[]{:S(2)}) collective-permute-start(f32[128,128]{1,0:T(8,128)S(1)} %add.36.refs_0_), channel_id=1, source_target_pairs={{0,8},{4,12},{8,16},{12,20},{16,24},{20,28},{24,0},{28,4},{1,9},{5... | collective-permute-start | bytes 196616 | tf_op jit(solution)/shard_map/ppermute | solution.py:568
  55.6 1.2 collective-permute-start.17
  56.9 3.9 %collective-permute-start.18 = (f32[64,128]{1,0:T(8,128)S(1)}, f32[64,128]{1,0:T(8,128)S(1)}, u32[]{:S(2)}, u32[]{:S(2)}) collective-permute-start(f32[64,128]{1,0:T(8,128)S(1)} %add.37), channel_id=1, source_target_pairs={{0,4},{4,0},{8,12},{12,8},{16,20},{20,16},{24,28},{28,24},{1,5},{5... | collective-permute-start | bytes 98312 | tf_op jit(solution)/shard_map/ppermute | solution.py:22
  60.8 5.2 %collective-permute-start.21 = (f32[64,128]{1,0:T(8,128)S(1)}, f32[64,128]{1,0:T(8,128)S(1)}, u32[]{:S(2)}, u32[]{:S(2)}) collective-permute-start(f32[64,128]{1,0:T(8,128)S(1)} %add.38.refs_0_), channel_id=1, source_target_pairs={{0,16},{4,20},{8,24},{12,28},{16,0},{20,4},{24,8},{28,12},{1,17},{... | collective-permute-start | bytes 98312 | tf_op jit(solution)/shard_map/ppermute | solution.py:568
  60.8 5.2 %collective-permute-start.20 = (f32[64,128]{1,0:T(8,128)S(1)}, f32[64,128]{1,0:T(8,128)S(1)}, u32[]{:S(2)}, u32[]{:S(2)}) collective-permute-start(f32[64,128]{1,0:T(8,128)S(1)} %add.38.refs_0_), channel_id=1, source_target_pairs={{0,24},{4,28},{8,0},{12,4},{16,8},{20,12},{24,16},{28,20},{1,25},{... | collective-permute-start | bytes 98312 | tf_op jit(solution)/shard_map/ppermute | solution.py:568
  62.2 5.7 %collective-permute-start.19 = (f32[64,128]{1,0:T(8,128)S(1)}, f32[64,128]{1,0:T(8,128)S(1)}, u32[]{:S(2)}, u32[]{:S(2)}) collective-permute-start(f32[64,128]{1,0:T(8,128)S(1)} %add.38.refs_0_), channel_id=1, source_target_pairs={{0,8},{4,12},{8,16},{12,20},{16,24},{20,28},{24,0},{28,4},{1,9},{5... | collective-permute-start | bytes 98312 | tf_op jit(solution)/shard_map/ppermute | solution.py:568
  71.3 1.5 %collective-permute-start.22 = (f32[512,128]{1,0:T(8,128)S(1)}, f32[512,128]{1,0:T(8,128)S(1)}, u32[]{:S(2)}, u32[]{:S(2)}) collective-permute-start(f32[512,128]{1,0:T(8,128)S(1)} %get-tuple-element.47.mine), channel_id=1, source_target_pairs={{0,1},{1,0},{2,3},{3,2},{4,5},{5,4},{6,7},{7,6},{8,9},{9,8},{10,11... | collective-permute-start | bytes 786440 | tf_op jit(solution)/shard_map/ppermute | solution.py:22
  74.1 4.5 %collective-permute-start.23 = (f32[160,128]{1,0:T(8,128)S(1)}, f32[160,128]{1,0:T(8,128)S(1)}, u32[]{:S(2)}, u32[]{:S(2)}) collective-permute-start(f32[160,128]{1,0:T(8,128)S(1)} %get-tuple-element.49), channel_id=1, source_target_pairs={{0,4},{4,0},{8,12},{12,8},{16,20},{20,16},{24,28},{28,24},{1,5},{5... | collective-permute-start | bytes 245768 | tf_op jit(solution)/shard_map/ppermute | solution.py:22
  78.6 8.0 %collective-permute-start.26 = (f32[160,128]{1,0:T(8,128)S(1)}, f32[160,128]{1,0:T(8,128)S(1)}, u32[]{:S(2)}, u32[]{:S(2)}) collective-permute-start(f32[160,128]{1,0:T(8,128)S(1)} %add.39.refs_0_), channel_id=1, source_target_pairs={{0,16},{4,20},{8,24},{12,28},{16,0},{20,4},{24,8},{28,12},{1,17},{... | collective-permute-start | bytes 245768 | tf_op jit(solution)/shard_map/ppermute | solution.py:568
  78.8 7.9 %collective-permute-start.25 = (f32[160,128]{1,0:T(8,128)S(1)}, f32[160,128]{1,0:T(8,128)S(1)}, u32[]{:S(2)}, u32[]{:S(2)}) collective-permute-start(f32[160,128]{1,0:T(8,128)S(1)} %add.39.refs_0_), channel_id=1, source_target_pairs={{0,24},{4,28},{8,0},{12,4},{16,8},{20,12},{24,16},{28,20},{1,25},{... | collective-permute-start | bytes 245768 | tf_op jit(solution)/shard_map/ppermute | solution.py:568
  80.0 6.7 %collective-permute-start.24 = (f32[160,128]{1,0:T(8,128)S(1)}, f32[160,128]{1,0:T(8,128)S(1)}, u32[]{:S(2)}, u32[]{:S(2)}) collective-permute-start(f32[160,128]{1,0:T(8,128)S(1)} %add.39.refs_0_), channel_id=1, source_target_pairs={{0,8},{4,12},{8,16},{12,20},{16,24},{20,28},{24,0},{28,4},{1,9},{5... | collective-permute-start | bytes 245768 | tf_op jit(solution)/shard_map/ppermute | solution.py:568
  89.2 1.6 %collective-permute-start.27 = (f32[512,128]{1,0:T(8,128)S(1)}, f32[512,128]{1,0:T(8,128)S(1)}, u32[]{:S(2)}, u32[]{:S(2)}) collective-permute-start(f32[512,128]{1,0:T(8,128)S(1)} %get-tuple-element.52.mine), channel_id=1, source_target_pairs={{0,1},{1,0},{2,3},{3,2},{4,5},{5,4},{6,7},{7,6},{8,9},{9,8},{10,11... | collective-permute-start | bytes 786440 | tf_op jit(solution)/shard_map/ppermute | solution.py:22
  92.0 4.5 %collective-permute-start.28 = (f32[160,128]{1,0:T(8,128)S(1)}, f32[160,128]{1,0:T(8,128)S(1)}, u32[]{:S(2)}, u32[]{:S(2)}) collective-permute-start(f32[160,128]{1,0:T(8,128)S(1)} %get-tuple-element.54), channel_id=1, source_target_pairs={{0,4},{4,0},{8,12},{12,8},{16,20},{20,16},{24,28},{28,24},{1,5},{5... | collective-permute-start | bytes 245768 | tf_op jit(solution)/shard_map/ppermute | solution.py:22
  96.6 7.5 %collective-permute-start.31 = (f32[160,128]{1,0:T(8,128)S(1)}, f32[160,128]{1,0:T(8,128)S(1)}, u32[]{:S(2)}, u32[]{:S(2)}) collective-permute-start(f32[160,128]{1,0:T(8,128)S(1)} %add.40.refs_0_), channel_id=1, source_target_pairs={{0,16},{4,20},{8,24},{12,28},{16,0},{20,4},{24,8},{28,12},{1,17},{... | collective-permute-start | bytes 245768 | tf_op jit(solution)/shard_map/ppermute | solution.py:568
  98.8 5.4 %collective-permute-start.30 = (f32[160,128]{1,0:T(8,128)S(1)}, f32[160,128]{1,0:T(8,128)S(1)}, u32[]{:S(2)}, u32[]{:S(2)}) collective-permute-start(f32[160,128]{1,0:T(8,128)S(1)} %add.40.refs_0_), channel_id=1, source_target_pairs={{0,24},{4,28},{8,0},{12,4},{16,8},{20,12},{24,16},{28,20},{1,25},{... | collective-permute-start | bytes 245768 | tf_op jit(solution)/shard_map/ppermute | solution.py:568
  100.5 6.2 %collective-permute-start.29 = (f32[160,128]{1,0:T(8,128)S(1)}, f32[160,128]{1,0:T(8,128)S(1)}, u32[]{:S(2)}, u32[]{:S(2)}) collective-permute-start(f32[160,128]{1,0:T(8,128)S(1)} %add.40.refs_0_), channel_id=1, source_target_pairs={{0,8},{4,12},{8,16},{12,20},{16,24},{20,28},{24,0},{28,4},{1,9},{5... | collective-permute-start | bytes 245768 | tf_op jit(solution)/shard_map/ppermute | solution.py:568
  109.3 20.6 %copy-start = (f32[2,2,16,64]{3,2,1,0:T(8,128)S(1)}, f32[2,2,16,64]{3,2,1,0:T(8,128)}, u32[]{:S(2)}) copy-start(f32[2,2,16,64]{3,2,1,0:T(8,128)} %refs_6_.1) | copy-start | bytes 49156
  109.3 1.9 %collective-permute-start.32 = (f32[512,128]{1,0:T(8,128)S(1)}, f32[512,128]{1,0:T(8,128)S(1)}, u32[]{:S(2)}, u32[]{:S(2)}) collective-permute-start(f32[512,128]{1,0:T(8,128)S(1)} %get-tuple-element.57.mine), channel_id=1, source_target_pairs={{0,1},{1,0},{2,3},{3,2},{4,5},{5,4},{6,7},{7,6},{8,9},{9,8},{10,11... | collective-permute-start | bytes 786440 | tf_op jit(solution)/shard_map/ppermute | solution.py:22
  109.7 23.3 %collective-permute-start.42 = (f32[512,128]{1,0:T(8,128)S(1)}, f32[512,128]{1,0:T(8,128)S(1)}, u32[]{:S(2)}, u32[]{:S(2)}) collective-permute-start(f32[512,128]{1,0:T(8,128)S(1)} %shard_map.98.mine), channel_id=1, source_target_pairs={{0,2},{1,3},{2,0},{3,1},{4,6},{5,7},{6,4},{7,5},{8,10},{9,11},{10,... | collective-permute-start | bytes 786440 | tf_op jit(solution)/shard_map/ppermute | solution.py:22
  112.5 4.6 %collective-permute-start.33 = (f32[160,128]{1,0:T(8,128)S(1)}, f32[160,128]{1,0:T(8,128)S(1)}, u32[]{:S(2)}, u32[]{:S(2)}) collective-permute-start(f32[160,128]{1,0:T(8,128)S(1)} %get-tuple-element.59), channel_id=1, source_target_pairs={{0,4},{4,0},{8,12},{12,8},{16,20},{20,16},{24,28},{28,24},{1,5},{5... | collective-permute-start | bytes 245768 | tf_op jit(solution)/shard_map/ppermute | solution.py:22
  113.4 21.3 %collective-permute-start.41 = (f32[512,128]{1,0:T(8,128)S(1)}, f32[512,128]{1,0:T(8,128)S(1)}, u32[]{:S(2)}, u32[]{:S(2)}) collective-permute-start(f32[512,128]{1,0:T(8,128)S(1)} %shard_map.97.mine), channel_id=1, source_target_pairs={{0,2},{1,3},{2,0},{3,1},{4,6},{5,7},{6,4},{7,5},{8,10},{9,11},{10,... | collective-permute-start | bytes 786440 | tf_op jit(solution)/shard_map/ppermute | solution.py:22
  114.4 22.2 %collective-permute-start.40 = (f32[512,128]{1,0:T(8,128)S(1)}, f32[512,128]{1,0:T(8,128)S(1)}, u32[]{:S(2)}, u32[]{:S(2)}) collective-permute-start(f32[512,128]{1,0:T(8,128)S(1)} %get-tuple-element.61.mixture), channel_id=1, source_target_pairs={{0,2},{1,3},{2,0},{3,1},{4,6},{5,7},{6,4},{7,5},{8,10},{9,11},{10,... | collective-permute-start | bytes 786440 | tf_op jit(solution)/shard_map/ppermute | solution.py:22
  117.1 6.5 %collective-permute-start.36 = (f32[160,128]{1,0:T(8,128)S(1)}, f32[160,128]{1,0:T(8,128)S(1)}, u32[]{:S(2)}, u32[]{:S(2)}) collective-permute-start(f32[160,128]{1,0:T(8,128)S(1)} %add.41.refs_0_), channel_id=1, source_target_pairs={{0,16},{4,20},{8,24},{12,28},{16,0},{20,4},{24,8},{28,12},{1,17},{... | collective-permute-start | bytes 245768 | tf_op jit(solution)/shard_map/ppermute | solution.py:568
  118.2 6.1 %collective-permute-start.35 = (f32[160,128]{1,0:T(8,128)S(1)}, f32[160,128]{1,0:T(8,128)S(1)}, u32[]{:S(2)}, u32[]{:S(2)}) collective-permute-start(f32[160,128]{1,0:T(8,128)S(1)} %add.41.refs_0_), channel_id=1, source_target_pairs={{0,24},{4,28},{8,0},{12,4},{16,8},{20,12},{24,16},{28,20},{1,25},{... | collective-permute-start | bytes 245768 | tf_op jit(solution)/shard_map/ppermute | solution.py:568
  123.6 6.2 %collective-permute-start.34 = (f32[160,128]{1,0:T(8,128)S(1)}, f32[160,128]{1,0:T(8,128)S(1)}, u32[]{:S(2)}, u32[]{:S(2)}) collective-permute-start(f32[160,128]{1,0:T(8,128)S(1)} %add.41.refs_0_), channel_id=1, source_target_pairs={{0,8},{4,12},{8,16},{12,20},{16,24},{20,28},{24,0},{28,4},{1,9},{5... | collective-permute-start | bytes 245768 | tf_op jit(solution)/shard_map/ppermute | solution.py:568
  132.0 4.6 %collective-permute-start.39 = (f32[80,128]{1,0:T(8,128)S(1)}, f32[80,128]{1,0:T(8,128)S(1)}, u32[]{:S(2)}, u32[]{:S(2)}) collective-permute-start(f32[80,128]{1,0:T(8,128)S(1)} %shard_map.96.mine), channel_id=1, source_target_pairs={{0,3},{1,2},{2,1},{3,0},{4,7},{5,6},{6,5},{7,4},{8,11},{9,10},{10,... | collective-permute-start | bytes 122888 | tf_op jit(solution)/shard_map/ppermute | solution.py:22
  132.0 4.6 %collective-permute-start.38 = (f32[80,128]{1,0:T(8,128)S(1)}, f32[80,128]{1,0:T(8,128)S(1)}, u32[]{:S(2)}, u32[]{:S(2)}) collective-permute-start(f32[80,128]{1,0:T(8,128)S(1)} %shard_map.96.mine), channel_id=1, source_target_pairs={{0,2},{1,3},{2,0},{3,1},{4,6},{5,7},{6,4},{7,5},{8,10},{9,11},{10,... | collective-permute-start | bytes 122888 | tf_op jit(solution)/shard_map/ppermute | solution.py:22
  133.0 3.6 %collective-permute-start.37 = (f32[80,128]{1,0:T(8,128)S(1)}, f32[80,128]{1,0:T(8,128)S(1)}, u32[]{:S(2)}, u32[]{:S(2)}) collective-permute-start(f32[80,128]{1,0:T(8,128)S(1)} %shard_map.96.mine), channel_id=1, source_target_pairs={{0,1},{1,0},{2,3},{3,2},{4,5},{5,4},{6,7},{7,6},{8,9},{9,8},{10,11... | collective-permute-start | bytes 122888 | tf_op jit(solution)/shard_map/ppermute | solution.py:22

commit v5 on v4

--- a/solution.py
+++ b/solution.py
@@ -183,7 +183,7 @@
 
 
 def start_kernel(member, _, *refs):
-    sources, (keep, send), (*local, sems, scratch) = refs[:3], refs[3:5], refs[5:]
+    sources, (part, heads, tail), (*local, sems, scratch) = refs[:3], refs[3:6], refs[6:]
     copies = [
         pltpu.make_async_copy(source, target, sems.at[at])
         for at, (source, target) in enumerate(zip(sources, local))
@@ -193,36 +193,29 @@
     for copy in copies:
         copy.wait()
     last, first, sketch = local
-    count = last.shape[1]
-    for out, index in ((keep, member[0]), (send, 1 - member[0])):
-        cores, heads = last[index], first[index]
+    count, slices = last.shape[1:3]
+    for half, index in enumerate((member[0], 1 - member[0])):
+        cores, fronts = last[index], first[index]
         for s in range(count):
-            scratch[pl.ds(s * HALF, HALF), pl.ds(0, HALF)] = exact(cores[s], sketch[...], TN)
-        rows = count * 32
-        even = scratch[pl.ds(0, rows, stride=2), :]
-        odd = scratch[pl.ds(1, rows, stride=2), :]
-        out[pl.ds(0, rows), :] = pick(even, swap(odd))
-        slices = heads.shape[1]
-        out[pl.ds(rows, slices), :] = jnp.concatenate([heads[0], heads[1]], axis=1)
-        if out.shape[0] > rows + slices:
-            out[pl.ds(rows + slices, slices), :] = jnp.concatenate([cores[0], cores[1]], axis=1)
-
-
-def merge_kernel(n_parts, rows, slices, *refs):
-    keeps, sends, out = refs[:n_parts], refs[n_parts : 2 * n_parts], refs[-1]
-    for pair, parts in enumerate((keeps, sends)):
-        out[pl.ds(pair * rows, rows), :] = added([part.at[pl.ds(0, rows)] for part in parts])
-        for at, part in enumerate(parts):
-            out[pl.ds(2 * rows + (pair * n_parts + at) * slices, slices), :] = part[
-                pl.ds(rows, slices), :
-            ]
-
-
-def heads_of(parts, pair):
-    rows = (parts[0].shape[0] - LANES) // 2
-    return jnp.concatenate(
-        [part[pl.ds(LANES + pair * rows, rows), :] for part in parts], axis=0
-    )
+            scratch[pl.ds((half * count + s) * HALF, HALF), pl.ds(0, HALF)] = exact(
+                cores[s], sketch[...], TN
+            )
+        heads[pl.ds(half * slices, slices), :] = jnp.concatenate([fronts[0], fronts[1]], axis=1)
+        if half:
+            tail[...] = jnp.concatenate([cores[0], cores[1]], axis=1)
+    rows = part.shape[0]
+    even = scratch[pl.ds(0, rows, stride=2), :]
+    odd = scratch[pl.ds(1, rows, stride=2), :]
+    part[...] = pick(even, swap(odd))
+
+
+def merge_kernel(n_parts, rows, *refs):
+    keeps, sends, (part, heads) = refs[:n_parts], refs[n_parts : 2 * n_parts], refs[2 * n_parts :]
+    height = keeps[0].shape[0] - rows
+    for pair, terms in enumerate((keeps, sends)):
+        part[pl.ds(pair * rows, rows), :] = added([term.at[pl.ds(0, rows)] for term in terms])
+        for at, term in enumerate(terms):
+            heads[pair, pl.ds(at * height, height), :] = term[pl.ds(rows, height), :]
 
 
 def added(parts):
@@ -236,8 +229,7 @@
     count = kept.shape[0]
     rows = kept.shape[1]
     tiles = rows // 256
-    value = added([part.at[pl.ds(0, LANES)] for part in parts])
-    natural = spread_rows(value * mask[...], wide)
+    natural = spread_rows(added(parts) * mask[...], wide)
     for half, cores in enumerate((kept, other)):
         for index in range(count):
             s = half * count + index
@@ -268,6 +260,40 @@
     out[...] = sketch_step(parts, mask, kept, other, sketch, *rest)
 
 
+def meet_kernel(n_parts, n_heads, *refs):
+    parts, heads, refs = refs[:n_parts], refs[n_parts : n_parts + n_heads], refs[n_parts + n_heads :]
+    mask, tail, kept, other, sketch, keep, send, relay, *rest = refs
+    value = sketch_step(parts, mask, kept, other, sketch, *rest)
+    rows = value.shape[0] // 2
+    slices = tail.shape[0]
+    keep[pl.ds(0, rows), :] = value[:rows]
+    send[pl.ds(0, rows), :] = value[rows:]
+    for at, head in enumerate(heads):
+        keep[pl.ds(rows + at * slices, slices), :] = head[pl.ds(0, slices), :]
+        send[pl.ds(rows + at * slices, slices), :] = head[pl.ds(slices, slices), :]
+    relay[pl.ds(0, rows), :] = added([part.at[pl.ds(rows, rows)] for part in parts]) * mask[...]
+    relay[pl.ds(rows, slices), :] = tail[...]
+
+
+def mixed_kernel(relay, cores, own_high, own_low, high, low, wide, product):
+    count, rows = cores.shape[:2]
+    tiles = rows // 256
+    height = count * 32
+    natural = spread_rows(relay[pl.ds(0, height), :], wide)
+    for index in range(count):
+        weight = split(block_diagonal(natural[index * HALF : (index + 1) * HALF]))
+        result = dot3(split(cores[index]), weight)
+        for tile in range(tiles):
+            product[pl.ds((tile * count + index) * 256, 256), :] = result[
+                tile * 256 : (tile + 1) * 256
+            ]
+    for i in range(high.shape[0]):
+        start = i // SUBLANES * height * SUBLANES + i % SUBLANES
+        value = split(product[pl.ds(start, height, stride=SUBLANES), :])
+        high[i] = jnp.concatenate([own_high[i][:height], value[0]], axis=0)
+        low[i] = jnp.concatenate([own_low[i][:height], value[1]], axis=0)
+
+
 SHIFTS = (1, 3, 2)
 
 
@@ -275,8 +301,8 @@
     inner, outer = spot % n_inner, spot // n_inner
     return [
         (outer + n_outer - by) % n_outer * n_inner + (inner ^ step)
+        for step in range(n_inner)
         for by in (0,) + SHIFTS
-        for step in range(n_inner)
     ]
 
 
@@ -285,13 +311,13 @@
 
 
 def first_kernel(n_parts, *refs, slices):
-    parts, heads, refs = refs[:n_parts], refs[n_parts : 2 * n_parts], refs[2 * n_parts :]
+    parts, (heads, *refs) = refs[:n_parts], refs[n_parts:]
     spot, mask, next_mask, kept, other, sketch, out, *rest = refs
     value = sketch_step(parts, mask, kept, other, sketch, *rest)
     natural = spread_rows(value * next_mask[...], rest[2])
     natural = pick(natural, jnp.zeros_like(natural))
-    value = exact(heads_of(heads, 0), natural[:LANES])
-    value = value + exact(heads_of(heads, 1), natural[LANES:])
+    value = exact(heads[0], natural[:LANES])
+    value = value + exact(heads[1], natural[LANES:])
     shared = rest[2]
     blocks = slice_blocks(spot[0], LANES // slices // n_parts, n_parts)
     for at, block in enumerate(blocks):
@@ -370,7 +396,7 @@
 
 
 def bond_one_kernel(row_count, n_parts, *refs):
-    parts, heads, refs = refs[:n_parts], refs[n_parts : 2 * n_parts], refs[2 * n_parts :]
+    parts, (heads, *refs) = refs[:n_parts], refs[n_parts:]
     spot, mask, high, low, inverse, carried, basis, out, square = refs
     packed = added(parts)
     zero = jnp.zeros_like(packed)
@@ -381,7 +407,7 @@
     gram = exact(mixture, mixture, TN)[:HALF]
     raw = []
     for pair in range(2):
-        value = exact(heads_of(heads, pair), mixture, TN)
+        value = exact(heads[pair], mixture, TN)
         raw.append(pick(value[:HALF], swap(value[HALF:])))
     solved, moved = project(jnp.concatenate(raw, axis=0), gram, mask[...], row_count, square)
     inverse[...] = solved
@@ -405,7 +431,7 @@
 
 def last_kernel(row_count, n_parts, *refs):
     parts, refs = refs[:n_parts], refs[n_parts:]
-    mask, member, kept, traded, basis, out = refs
+    mask, member, kept, relay, basis, out = refs
     value = added(parts)
     solved = swap(eliminate(unpack_gram(value[LANES:]), mask[...], row_count))
     carried = exact(value[:LANES], block_diagonal(solved), NT) * (1.0 / row_count)
@@ -413,7 +439,7 @@
     slices = cores.shape[1]
     own = jnp.concatenate([cores[0], cores[1]], axis=1)
     term = None
-    for pair, both in enumerate((own, traded[...])):
+    for pair, both in enumerate((own, relay[pl.ds(HALF, slices), :])):
         side = carried[pair * HALF : (pair + 1) * HALF]
         zero = jnp.zeros_like(side)
         both = exact(both, jnp.concatenate([pick(side, zero), pick(swap(side), zero)], axis=0))
@@ -597,9 +623,9 @@
         )
         return in_rows(part.reshape(count, slices, width))
 
-    keep, send = kernel_call(
+    part, heads, tail = kernel_call(
         start_kernel,
-        [shape(count * 32 + slices, LANES), shape(count * 32 + 2 * slices, LANES)],
+        [shape(height, LANES), shape(2 * slices, LANES), shape(slices, LANES)],
         [
             scratch(*last_cores.shape),
             scratch(*first_cores.shape),
@@ -615,6 +641,41 @@
         in_hbm=(2, 3, 4),
         limit=None,
     )
+    late_cores, late_sketch, late_ranks, part = lax.optimization_barrier(
+        (mid_cores, sketch_mid, ranks, part)
+    )
+    masks = (jnp.arange(rank_size, dtype=jnp.int32)[None, :] < late_ranks[:, None]).astype(
+        jnp.float32
+    )
+    masks = jnp.concatenate([masks, masks], axis=1)[:, None, :]
+    sketch_rows = in_rows(late_sketch)
+    sketch_rows = [sketch_rows[position] for position in range(middle)]
+    kept = [half_of(late_cores, position, member) for position in range(middle)]
+    sent = [half_of(late_cores, position, 1 - member) for position in range(middle)]
+    sent[middle - 2] = half_of(mid_cores, middle - 2, 1 - member)
+    traded = [flip(sent[position], "rep", low) for position in range(middle)]
+    cores = list(zip(kept, traded))
+    wide = shape(slices, height, LANES, dtype=jnp.bfloat16)
+    room = [
+        scratch(2 * height, LANES),
+        scratch(height * slices, LANES),
+        scratch(slices, HALF, LANES),
+    ]
+    heads = spread(heads, "mode", outer)
+    parts = exchanged(part, "mode")
+    block = shape(height // 2 + len(heads) * slices, LANES)
+    keep, send, relay, *own_mixed = kernel_call(
+        functools.partial(meet_kernel, len(parts), len(heads)),
+        [block, block, shape(height // 2 + slices, LANES), wide, wide],
+        room,
+        *parts,
+        *heads,
+        masks[middle],
+        tail,
+        kept[-1],
+        sent[-1],
+        sketch_rows[-1],
+    )
     keeps, sends = [keep], []
     sends.append(flip(send, "rep", low))
     for step in range(1, inner[0]):
@@ -626,48 +687,36 @@
             for r in range(2 * low)
         ]
         sends.append(lax.ppermute(send, ("mode", "rep"), pairs))
-    traded = sends[0][count * 32 + slices :]
-    (part,) = kernel_call(
-        functools.partial(merge_kernel, len(keeps), count * 32, slices),
-        [shape(height + 2 * len(keeps) * slices, LANES)],
+    part, heads = kernel_call(
+        functools.partial(merge_kernel, len(keeps), height // 2),
+        [shape(height, LANES), shape(2, total_slices, LANES)],
         [],
         *keeps,
         *sends,
     )
-    cores = [None] * middle
-    late_cores, late_sketch, late_ranks, part = lax.optimization_barrier(
-        (mid_cores, sketch_mid, ranks, part)
-    )
-    masks = (jnp.arange(rank_size, dtype=jnp.int32)[None, :] < late_ranks[:, None]).astype(
-        jnp.float32
-    )
-    masks = jnp.concatenate([masks, masks], axis=1)[:, None, :]
-    sketch_rows = in_rows(late_sketch)
-    sketch_rows = [sketch_rows[position] for position in range(middle)]
-    for position in range(middle - 1, -1, -1):
-        if position == middle - 1:
-            sent = half_of(mid_cores, position, 1 - member)
+    relay = flip(relay, "rep", low)
+    mixed = [None] * middle
+    mixed[-1] = kernel_call(
+        mixed_kernel,
+        [wide, wide],
+        [scratch(height, LANES), scratch(height // 2 * slices, LANES)],
+        relay,
+        traded[-1],
+        *own_mixed,
+    )
+    for position in range(middle - 2, -1, -1):
+        if position == middle - 2:
+            parts = spread(part, "mode", outer)
         else:
-            sent = half_of(late_cores, position, 1 - member)
-        cores[position] = (half_of(late_cores, position, member), flip(sent, "rep", low))
-    mixed = [None] * middle
-    heads = None
-    wide = shape(slices, height, LANES, dtype=jnp.bfloat16)
-    for position in range(middle - 1, -1, -1):
-        parts = exchanged(part, "mode") if heads else spread(part, "mode", outer)
-        heads = heads or parts
+            parts = exchanged(part, "mode")
         body, more, result = sketch_kernel, (), shape(height, LANES)
         if position == 0:
             body = functools.partial(first_kernel, slices=slices)
-            more, result = (*heads, spot), shape(total_slices // 2, LANES)
+            more, result = (heads, spot), shape(total_slices // 2, LANES)
         part, *mixed[position] = kernel_call(
             functools.partial(body, len(parts)),
             [result, wide, wide],
-            [
-                scratch(2 * height, LANES),
-                scratch(height * slices, LANES),
-                scratch(slices, HALF, LANES),
-            ],
+            room,
             *parts,
             *more,
             *((masks[1], masks[0]) if position == 0 else (masks[position + 1],)),
@@ -682,7 +731,7 @@
         [shape(HALF, LANES), shape(height, LANES), shape(slices, LANES), shape(rows, LANES)],
         [square],
         *parts,
-        *heads,
+        heads,
         spot,
         masks[0],
         *mixed[0],
@@ -734,7 +783,7 @@
         mask,
         here,
         last_cores,
-        traded,
+        relay,
         basis,
     )
     near, far, across = (flip(last, "rep", bits) for bits in (1, low, low + 1))

time: 139 us -> 146 us (1.050)
  starting transfers between devices: 40.6 us -> 47.5 us
    ppermute x21 -> x24, starting transfers between devices: 20.9 us -> 27.6 us  [spread(): parts.append(lax.ppermute(value, axis, pairs))]
    ppermute x1, waiting for transfers between devices: 0.01 us -> 5.76 us  [tiled(): sends.append(lax.ppermute(send, ('mode', 'rep'), pairs))]
    ppermute x21 -> x24, waiting for transfers between devices: 43.1 us -> 39.7 us  [spread(): parts.append(lax.ppermute(value, axis, pairs))]
    ppermute x21 -> x22, starting transfers between devices: 15.7 us -> 17.6 us  [flip(): lax.ppermute(value, axis, [(index, index ^ bits) for index in range(size)])]
    ppermute x1, starting transfers between devices: 3.99 us -> 2.28 us  [tiled(): sends.append(lax.ppermute(send, ('mode', 'rep'), pairs))]
    ppermute x21 -> x22, waiting for transfers between devices: 23.9 us -> 22.3 us  [flip(): lax.ppermute(value, axis, [(index, index ^ bits) for index in range(size)])]
    pallas_call x18 -> x19, Pallas kernels: 25.8 us -> 26.3 us  [kernel_call(): pl.pallas_call(body, out_shape=outs, in_specs=specs[:len(operands)], out_...]
  transfers between devices with their start and end apart: 43 -> 47, of which waited for: 24 -> 26; matrix products, arithmetic and copies ran while one was open for 2% -> 2% of each run, Pallas kernels for 7% -> 9%
where the time goes in v5:
time: 146 us
  waiting for transfers between devices  67.8 us (46%)
  starting transfers between devices  47.5 us (33%)
  Pallas kernels  26.3 us (18%)
  local copies, waits for them, and re-layouts  3.06 us (2%)
    ppermute x24, waiting for transfers between devices, spread(): parts.append(lax.ppermute(value, axis, pairs))  39.7 us
    ppermute x24, starting transfers between devices, spread(): parts.append(lax.ppermute(value, axis, pairs))  27.6 us
    pallas_call x19, Pallas kernels, kernel_call(): pl.pallas_call(body, out_shape=outs, in_specs=specs[:len(operands)], out_...  26.3 us
    ppermute x22, waiting for transfers between devices, flip(): lax.ppermute(value, axis, [(index, index ^ bits) for index in range(size)])  22.3 us
    ppermute x22, starting transfers between devices, flip(): lax.ppermute(value, axis, [(index, index ^ bits) for index in range(size)])  17.6 us
    ppermute x1, waiting for transfers between devices, tiled(): sends.append(lax.ppermute(send, ('mode', 'rep'), pairs))  5.76 us
    dynamic_slice x2, local copies, waits for them, and re-layouts, half_of(): lax.dynamic_slice(source, (index, 0, position, 0, 0), (1, count, 1, slice...  2.97 us
  transfers between devices with their start and end apart: 47, of which 26 were waited for; matrix products, arithmetic and copies ran while one was open for 2% of the time, Pallas kernels for 9%

profile of v5, /device:TPU:0, one launch (start us, length us, event | category | flops | bytes accessed | tf_op | source)
XLA Modules:
  0.0 146.0 jit_solution(1948698698044858308)
XLA Ops:
  0.7 1.9 %shard_map.85 = (f32[128,128]{1,0:T(8,128)}, f32[32,128]{1,0:T(8,128)}, f32[16,128]{1,0:T(8,128)}) custom-call(s32[1]{0:T(128)} %bitcast.member.refs_5_, s32[1]{0:T(128)} %bitcast.1._.refs_5_, f32[2,2,16,64]{3,2,1,0:T(8,128)} %refs_6_.1, f32[2,2,16,64]{3,2,1,0:T(8,128)} %refs_1_.1, f32[16,64]{1,0:T(8,128)} %refs_2_.1), custom_call_target="tpu_custom_call" | custom-call | bytes 126984 | tf_op jit(solution)/shard_map/pallas_call | solution.py:549
  2.5 4.1 %collective-permute-start.6 = (f32[32,128]{1,0:T(8,128)}, f32[32,128]{1,0:T(8,128)S(1)}, u32[]{:S(2)}, u32[]{:S(2)}) collective-permute-start(f32[32,128]{1,0:T(8,128)} %get-tuple-element.45.refs_4_), channel_id=1, source_target_pairs={{0,16},{4,20},{8,24},{12,28},{16,0},{20,4},{24,8},{28,12},{1,17},{... | collective-permute-start | bytes 49160 | tf_op jit(solution)/shard_map/ppermute | solution.py:594
  6.7 1.3 collective-permute-start.5
  8.7 1.5 %collective-permute-start = (f32[128,128]{1,0:T(8,128)}, f32[128,128]{1,0:T(8,128)S(1)}, u32[]{:S(2)}, u32[]{:S(2)}) collective-permute-start(f32[128,128]{1,0:T(8,128)} %get-tuple-element.44), channel_id=1, source_target_pairs={{0,4},{4,0},{8,12},{12,8},{16,20},{20,16},{24,28},{28,24},{1,5},{5... | collective-permute-start | bytes 196616 | tf_op jit(solution)/shard_map/ppermute | solution.py:22
  10.2 1.1 constant_dynamic-slice_fusion.2
  11.3 1.6 %collective-permute-start.13 = (f32[2,512,128]{2,1,0:T(8,128)S(1)}, f32[2,512,128]{2,1,0:T(8,128)S(1)}, u32[]{:S(2)}, u32[]{:S(2)}) collective-permute-start(f32[2,512,128]{2,1,0:T(8,128)S(1)} %bitcast.56), channel_id=1, source_target_pairs={{0,2},{1,3},{2,0},{3,1},{4,6},{5,7},{6,4},{7,5},{8,10},{9,11},{10,... | collective-permute-start | bytes 1572872 | tf_op jit(solution)/shard_map/ppermute | solution.py:22
  13.0 1.9 %constant_dynamic-slice_fusion = (f32[1,2,1,16,4096]{4,3,2,1,0:T(8,128)S(1)}, f32[1,2,1,16,4096]{4,3,2,1,0:T(8,128)S(1)}, f32[1,2,1,16,4096]{4,3,2,1,0:T(8,128)S...) fusion(f32[2,2,3,16,4096]{4,3,2,1,0:T(8,128)} %param.7, s32[]{:T(128)S(6)} %select_n.17, s32[]{:T(128)S(6)} %select_n.16), kind=kLoop, calls=%fused_computation.2 | loop fusion | bytes 5242888 | tf_op jit(solution)/shard_map/dynamic_slice | solution.py:621
  15.6 1.1 collective-permute-start.3
  16.7 2.9 %collective-permute-start.2 = (f32[128,128]{1,0:T(8,128)S(1)}, f32[128,128]{1,0:T(8,128)S(1)}, u32[]{:S(2)}, u32[]{:S(2)}) collective-permute-start(f32[128,128]{1,0:T(8,128)S(1)} %add.33.refs_0_), channel_id=1, source_target_pairs={{0,24},{4,28},{8,0},{12,4},{16,8},{20,12},{24,16},{28,20},{1,25},{... | collective-permute-start | bytes 196616 | tf_op jit(solution)/shard_map/ppermute | solution.py:594
  19.6 1.2 collective-permute-done.3.refs_3_
  21.7 4.0 %collective-permute-done.1.refs_1_ = f32[128,128]{1,0:T(8,128)S(1)} collective-permute-done((f32[128,128]{1,0:T(8,128)S(1)}, f32[128,128]{1,0:T(8,128)S(1)}, u32[]{:S(2)}, u32[]{:S(2)}) %collective-permute-start.1) | collective-permute-done | bytes 65568 | tf_op jit(solution)/shard_map/ppermute | solution.py:594
  25.7 1.4 shard_map.86
  27.9 2.3 %collective-permute-start.9 = (f32[128,128]{1,0:T(8,128)S(1)}, f32[128,128]{1,0:T(8,128)S(1)}, u32[]{:S(2)}, u32[]{:S(2)}) collective-permute-start(f32[128,128]{1,0:T(8,128)S(1)} %get-tuple-element.51), channel_id=1, source_target_pairs={{0,6},{1,7},{2,4},{3,5},{4,2},{5,3},{6,0},{7,1},{8,14},{9,15},{10,... | collective-permute-start | bytes 196616 | tf_op jit(solution)/shard_map/ppermute | solution.py:689
  31.4 5.8 %collective-permute-done.9.refs_3_ = f32[128,128]{1,0:T(8,128)S(1)} collective-permute-done((f32[128,128]{1,0:T(8,128)S(1)}, f32[128,128]{1,0:T(8,128)S(1)}, u32[]{:S(2)}, u32[]{:S(2)}) %collective-permute-start.9) | collective-permute-done | bytes 65568 | tf_op jit(solution)/shard_map/ppermute | solution.py:689
  38.0 1.4 collective-permute-start.12
  39.3 2.6 %collective-permute-start.11 = (f32[128,128]{1,0:T(8,128)S(1)}, f32[128,128]{1,0:T(8,128)S(1)}, u32[]{:S(2)}, u32[]{:S(2)}) collective-permute-start(f32[128,128]{1,0:T(8,128)S(1)} %get-tuple-element.52.refs_0_), channel_id=1, source_target_pairs={{0,24},{4,28},{8,0},{12,4},{16,8},{20,12},{24,16},{28,20},{1,25},{... | collective-permute-start | bytes 196616 | tf_op jit(solution)/shard_map/ppermute | solution.py:594
  42.0 1.2 collective-permute-done.12.refs_3_
  43.2 1.1 collective-permute-done.11.refs_2_
  44.3 3.7 %collective-permute-done.10.refs_1_ = f32[128,128]{1,0:T(8,128)S(1)} collective-permute-done((f32[128,128]{1,0:T(8,128)S(1)}, f32[128,128]{1,0:T(8,128)S(1)}, u32[]{:S(2)}, u32[]{:S(2)}) %collective-permute-start.10) | collective-permute-done | bytes 65568 | tf_op jit(solution)/shard_map/ppermute | solution.py:594
  48.1 1.4 shard_map.88
  49.4 0.8 collective-permute-start.14
  50.3 3.5 %collective-permute-done.14 = f32[128,128]{1,0:T(8,128)S(1)} collective-permute-done((f32[128,128]{1,0:T(8,128)S(1)}, f32[128,128]{1,0:T(8,128)S(1)}, u32[]{:S(2)}, u32[]{:S(2)}) %collective-permute-start.14) | collective-permute-done | bytes 65568 | tf_op jit(solution)/shard_map/ppermute | solution.py:22
  53.9 1.3 collective-permute-start.16
  55.9 3.1 %collective-permute-done.17.refs_3_ = f32[128,128]{1,0:T(8,128)S(1)} collective-permute-done((f32[128,128]{1,0:T(8,128)S(1)}, f32[128,128]{1,0:T(8,128)S(1)}, u32[]{:S(2)}, u32[]{:S(2)}) %collective-permute-start.17) | collective-permute-done | bytes 65568 | tf_op jit(solution)/shard_map/ppermute | solution.py:594
  59.0 2.2 %collective-permute-done.15.refs_1_ = f32[128,128]{1,0:T(8,128)S(1)} collective-permute-done((f32[128,128]{1,0:T(8,128)S(1)}, f32[128,128]{1,0:T(8,128)S(1)}, u32[]{:S(2)}, u32[]{:S(2)}) %collective-permute-start.15) | collective-permute-done | bytes 65568 | tf_op jit(solution)/shard_map/ppermute | solution.py:594
  61.2 1.9 %shard_map.89 = (f32[64,128]{1,0:T(8,128)S(1)}, bf16[16,128,128]{2,1,0:T(8,128)(2,1)S(1)}, bf16[16,128,128]{2,1,0:T(8,128)(2,1)S(1)}) custom-call(f32[128,128]{1,0:T(8,128)S(1)} %add.36.refs_0_, f32[128,128]{1,0:T(8,128)S(1)} %collective-permute-done.15.refs_1_, f32[128,128]{1,0:T(8,128)S(1)} %collective-permute-done.16.refs_2_, ...), custom_call_target="tpu_custom_call" | custom-call | bytes 2786308 | tf_op jit(solution)/shard_map/pallas_call | solution.py:549
  63.1 1.2 collective-permute-done.19
  65.1 3.2 %collective-permute-done.20 = f32[64,128]{1,0:T(8,128)S(1)} collective-permute-done((f32[64,128]{1,0:T(8,128)S(1)}, f32[64,128]{1,0:T(8,128)S(1)}, u32[]{:S(2)}, u32[]{:S(2)}) %collective-permute-start.20) | collective-permute-done | bytes 32800 | tf_op jit(solution)/shard_map/ppermute | solution.py:22
  68.2 1.5 collective-permute-start.22
  70.3 3.1 %collective-permute-done.23.refs_3_ = f32[64,128]{1,0:T(8,128)S(1)} collective-permute-done((f32[64,128]{1,0:T(8,128)S(1)}, f32[64,128]{1,0:T(8,128)S(1)}, u32[]{:S(2)}, u32[]{:S(2)}) %collective-permute-start.23) | collective-permute-done | bytes 32800 | tf_op jit(solution)/shard_map/ppermute | solution.py:594
  73.4 2.0 %collective-permute-done.21.refs_1_ = f32[64,128]{1,0:T(8,128)S(1)} collective-permute-done((f32[64,128]{1,0:T(8,128)S(1)}, f32[64,128]{1,0:T(8,128)S(1)}, u32[]{:S(2)}, u32[]{:S(2)}) %collective-permute-start.21) | collective-permute-done | bytes 32800 | tf_op jit(solution)/shard_map/ppermute | solution.py:594
  75.4 3.3 %shard_map.90 = (f32[64,128]{1,0:T(8,128)}, f32[128,128]{1,0:T(8,128)S(1)}, f32[16,128]{1,0:T(8,128)S(1)}, f32[512,128]{1,0:T(8,128)S(1)}) custom-call(f32[64,128]{1,0:T(8,128)S(1)} %add.38.refs_0_, f32[64,128]{1,0:T(8,128)S(1)} %collective-permute-done.21.refs_1_, f32[64,128]{1,0:T(8,128)S(1)} %collective-permute-done.22.refs_2_, ...), custom_call_target="tpu_custom_call" | custom-call | bytes 1679876 | tf_op jit(solution)/shard_map/pallas_call | solution.py:549
  78.7 1.5 %collective-permute-done.24.theirs = f32[512,128]{1,0:T(8,128)S(1)} collective-permute-done((f32[512,128]{1,0:T(8,128)S(1)}, f32[512,128]{1,0:T(8,128)S(1)}, u32[]{:S(2)}, u32[]{:S(2)}) %collective-permute-start.24) | collective-permute-done | bytes 262176 | tf_op jit(solution)/shard_map/ppermute | solution.py:22
  80.2 1.2 shard_map.91
  81.5 0.8 collective-permute-start.25
  82.3 1.5 %collective-permute-start.35 = (f32[2,512,128]{2,1,0:T(8,128)S(1)}, f32[2,512,128]{2,1,0:T(8,128)S(1)}, u32[]{:S(2)}, u32[]{:S(2)}) collective-permute-start(f32[2,512,128]{2,1,0:T(8,128)S(1)} %bitcast.50), channel_id=1, source_target_pairs={{0,2},{1,3},{2,0},{3,1},{4,6},{5,7},{6,4},{7,5},{8,10},{9,11},{10,... | collective-permute-start | bytes 1572872 | tf_op jit(solution)/shard_map/ppermute | solution.py:22
  83.8 2.2 %collective-permute-done.25 = f32[160,128]{1,0:T(8,128)S(1)} collective-permute-done((f32[160,128]{1,0:T(8,128)S(1)}, f32[160,128]{1,0:T(8,128)S(1)}, u32[]{:S(2)}, u32[]{:S(2)}) %collective-permute-start.25) | collective-permute-done | bytes 81952 | tf_op jit(solution)/shard_map/ppermute | solution.py:22
  86.2 1.2 collective-permute-start.27
  87.4 0.8 collective-permute-start.26
  88.2 5.9 %collective-permute-done.28.refs_3_ = f32[160,128]{1,0:T(8,128)S(1)} collective-permute-done((f32[160,128]{1,0:T(8,128)S(1)}, f32[160,128]{1,0:T(8,128)S(1)}, u32[]{:S(2)}, u32[]{:S(2)}) %collective-permute-start.28) | collective-permute-done | bytes 81952 | tf_op jit(solution)/shard_map/ppermute | solution.py:594
  94.1 2.5 %shard_map.92 = (f32[64,128]{1,0:T(8,128)S(1)}, f32[128,128]{1,0:T(8,128)S(1)}, f32[512,128]{1,0:T(8,128)S(1)}) custom-call(f32[160,128]{1,0:T(8,128)S(1)} %add.39.refs_0_, f32[160,128]{1,0:T(8,128)S(1)} %collective-permute-done.26.refs_1_, f32[160,128]{1,0:T(8,128)S(1)} %collective-permute-done.27.refs_2_, f32[160,128]{1,0:T(8,128)S(1)} %collective-permute-done.28.refs_3_, ...), custom_call_target="tpu_custom_call" | custom-call | bytes 1737216 | tf_op jit(solution)/shard_map/pallas_call | solution.py:549
  96.7 1.5 %collective-permute-done.29.theirs = f32[512,128]{1,0:T(8,128)S(1)} collective-permute-done((f32[512,128]{1,0:T(8,128)S(1)}, f32[512,128]{1,0:T(8,128)S(1)}, u32[]{:S(2)}, u32[]{:S(2)}) %collective-permute-start.29) | collective-permute-done | bytes 262176 | tf_op jit(solution)/shard_map/ppermute | solution.py:22
  98.2 1.3 shard_map.93
  99.4 0.8 collective-permute-start.30
  100.3 3.7 %collective-permute-done.30 = f32[160,128]{1,0:T(8,128)S(1)} collective-permute-done((f32[160,128]{1,0:T(8,128)S(1)}, f32[160,128]{1,0:T(8,128)S(1)}, u32[]{:S(2)}, u32[]{:S(2)}) %collective-permute-start.30) | collective-permute-done | bytes 81952 | tf_op jit(solution)/shard_map/ppermute | solution.py:22
  104.0 2.2 %collective-permute-start.33 = (f32[160,128]{1,0:T(8,128)S(1)}, f32[160,128]{1,0:T(8,128)S(1)}, u32[]{:S(2)}, u32[]{:S(2)}) collective-permute-start(f32[160,128]{1,0:T(8,128)S(1)} %add.40.refs_0_), channel_id=1, source_target_pairs={{0,16},{4,20},{8,24},{12,28},{16,0},{20,4},{24,8},{28,12},{1,17},{... | collective-permute-start | bytes 245768 | tf_op jit(solution)/shard_map/ppermute | solution.py:594
  106.2 1.8 %collective-permute-start.32 = (f32[160,128]{1,0:T(8,128)S(1)}, f32[160,128]{1,0:T(8,128)S(1)}, u32[]{:S(2)}, u32[]{:S(2)}) collective-permute-start(f32[160,128]{1,0:T(8,128)S(1)} %add.40.refs_0_), channel_id=1, source_target_pairs={{0,24},{4,28},{8,0},{12,4},{16,8},{20,12},{24,16},{28,20},{1,25},{... | collective-permute-start | bytes 245768 | tf_op jit(solution)/shard_map/ppermute | solution.py:594
  108.2 1.5 %collective-permute-start.34 = (f32[80,128]{1,0:T(8,128)S(1)}, f32[80,128]{1,0:T(8,128)S(1)}, u32[]{:S(2)}, u32[]{:S(2)}) collective-permute-start(f32[80,128]{1,0:T(8,128)S(1)} %get-tuple-element.66), channel_id=1, source_target_pairs={{0,2},{1,3},{2,0},{3,1},{4,6},{5,7},{6,4},{7,5},{8,10},{9,11},{10,... | collective-permute-start | bytes 122888 | tf_op jit(solution)/shard_map/ppermute | solution.py:22
  109.7 2.5 %collective-permute-done.34.relay.refs_7_ = f32[80,128]{1,0:T(8,128)S(1)} collective-permute-done((f32[80,128]{1,0:T(8,128)S(1)}, f32[80,128]{1,0:T(8,128)S(1)}, u32[]{:S(2)}, u32[]{:S(2)}) %collective-permute-start.34) | collective-permute-done | bytes 40992 | tf_op jit(solution)/shard_map/ppermute | solution.py:22
  112.8 1.4 collective-permute-done.31.refs_1_
  114.2 2.5 %shard_map.95 = (f32[64,128]{1,0:T(8,128)S(1)}, f32[128,128]{1,0:T(8,128)S(1)}, f32[512,128]{1,0:T(8,128)S(1)}) custom-call(f32[160,128]{1,0:T(8,128)S(1)} %add.40.refs_0_, f32[160,128]{1,0:T(8,128)S(1)} %collective-permute-done.31.refs_1_, f32[160,128]{1,0:T(8,128)S(1)} %collective-permute-done.32.refs_2_, f32[160,128]{1,0:T(8,128)S(1)} %collective-permute-done.33.refs_3_, ...), custom_call_target="tpu_custom_call" | custom-call | bytes 1737216 | tf_op jit(solution)/shard_map/pallas_call | solution.py:549
  117.1 1.6 %collective-permute-start.46 = (f32[512,128]{1,0:T(8,128)S(1)}, f32[512,128]{1,0:T(8,128)S(1)}, u32[]{:S(2)}, u32[]{:S(2)}) collective-permute-start(f32[512,128]{1,0:T(8,128)S(1)} %shard_map.99.mine), channel_id=1, source_target_pairs={{0,2},{1,3},{2,0},{3,1},{4,6},{5,7},{6,4},{7,5},{8,10},{9,11},{10,... | collective-permute-start | bytes 786440 | tf_op jit(solution)/shard_map/ppermute | solution.py:22
  118.6 1.3 shard_map.96
  121.0 1.2 collective-permute-start.45
  122.2 0.9 collective-permute-start.44
  123.1 1.4 collective-permute-done.37
  124.5 1.0 collective-permute-start.40
  125.5 1.3 collective-permute-start.39
  126.9 4.3 %collective-permute-done.40.refs_3_ = f32[160,128]{1,0:T(8,128)S(1)} collective-permute-done((f32[160,128]{1,0:T(8,128)S(1)}, f32[160,128]{1,0:T(8,128)S(1)}, u32[]{:S(2)}, u32[]{:S(2)}) %collective-permute-start.40) | collective-permute-done | bytes 81952 | tf_op jit(solution)/shard_map/ppermute | solution.py:594
  131.7 5.7 %collective-permute-done.38.refs_1_ = f32[160,128]{1,0:T(8,128)S(1)} collective-permute-done((f32[160,128]{1,0:T(8,128)S(1)}, f32[160,128]{1,0:T(8,128)S(1)}, u32[]{:S(2)}, u32[]{:S(2)}) %collective-permute-start.38) | collective-permute-done | bytes 81952 | tf_op jit(solution)/shard_map/ppermute | solution.py:594
  137.4 2.1 %shard_map.97.mine = f32[80,128]{1,0:T(8,128)S(1)} custom-call(f32[160,128]{1,0:T(8,128)S(1)} %add.41.refs_0_, f32[160,128]{1,0:T(8,128)S(1)} %collective-permute-done.38.refs_1_, f32[160,128]{1,0:T(8,128)S(1)} %collective-permute-done.39.refs_2_, f32[160,128]{1,0:T(8,128)S(1)} %collective-permute-done.40.refs_3_, ...), custom_call_target="tpu_custom_call" | custom-call | bytes 434692 | tf_op jit(solution)/shard_map/pallas_call | solution.py:549
  139.6 1.1 collective-permute-start.42
  143.1 1.0 shard_map.102.before
  144.2 1.7 %shard_map.103 = (f32[2,16,64]{2,1,0:T(8,128)}, f32[2,16,64]{2,1,0:T(8,128)}, f32[2,3,512,128]{3,2,1,0:T(8,128)}) custom-call(s32[1]{0:T(128)} %bitcast.member.refs_5_, f32[80,128]{1,0:T(8,128)S(1)} %shard_map.97.mine, f32[80,128]{1,0:T(8,128)S(1)} %collective-permute-done.41.near, ...), custom_call_target="tpu_custom_call", output_to_operand_aliasing={{2}: (6, {})} | custom-call | bytes 3588100 | tf_op jit(solution)/shard_map/pallas_call | solution.py:549
  (74 shorter events, 13.0 us)
Async XLA Ops:
  0.6 12.2 %copy-start.3 = (f32[3,16,4096]{2,1,0:T(8,128)S(1)}, f32[3,16,4096]{2,1,0:T(8,128)}, u32[]{:S(2)}) copy-start(f32[3,16,4096]{2,1,0:T(8,128)} %param.9) | copy-start | bytes 2359300
  2.5 13.1 %collective-permute-start.6 = (f32[32,128]{1,0:T(8,128)}, f32[32,128]{1,0:T(8,128)S(1)}, u32[]{:S(2)}, u32[]{:S(2)}) collective-permute-start(f32[32,128]{1,0:T(8,128)} %get-tuple-element.45.refs_4_), channel_id=1, source_target_pairs={{0,16},{4,20},{8,24},{12,28},{16,0},{20,4},{24,8},{28,12},{1,17},{... | collective-permute-start | bytes 49160 | tf_op jit(solution)/shard_map/ppermute | solution.py:594
  6.7 10.0 %collective-permute-start.5 = (f32[32,128]{1,0:T(8,128)}, f32[32,128]{1,0:T(8,128)S(1)}, u32[]{:S(2)}, u32[]{:S(2)}) collective-permute-start(f32[32,128]{1,0:T(8,128)} %get-tuple-element.45.refs_4_), channel_id=1, source_target_pairs={{0,24},{4,28},{8,0},{12,4},{16,8},{20,12},{24,16},{28,20},{1,25},{... | collective-permute-start | bytes 49160 | tf_op jit(solution)/shard_map/ppermute | solution.py:594
  8.0 11.6 %collective-permute-start.4 = (f32[32,128]{1,0:T(8,128)}, f32[32,128]{1,0:T(8,128)S(1)}, u32[]{:S(2)}, u32[]{:S(2)}) collective-permute-start(f32[32,128]{1,0:T(8,128)} %get-tuple-element.45.refs_4_), channel_id=1, source_target_pairs={{0,8},{4,12},{8,16},{12,20},{16,24},{20,28},{24,0},{28,4},{1,9},{5... | collective-permute-start | bytes 49160 | tf_op jit(solution)/shard_map/ppermute | solution.py:594
  8.7 6.3 %collective-permute-start = (f32[128,128]{1,0:T(8,128)}, f32[128,128]{1,0:T(8,128)S(1)}, u32[]{:S(2)}, u32[]{:S(2)}) collective-permute-start(f32[128,128]{1,0:T(8,128)} %get-tuple-element.44), channel_id=1, source_target_pairs={{0,4},{4,0},{8,12},{12,8},{16,20},{20,16},{24,28},{28,24},{1,5},{5... | collective-permute-start | bytes 196616 | tf_op jit(solution)/shard_map/ppermute | solution.py:22
  11.3 36.7 %collective-permute-start.13 = (f32[2,512,128]{2,1,0:T(8,128)S(1)}, f32[2,512,128]{2,1,0:T(8,128)S(1)}, u32[]{:S(2)}, u32[]{:S(2)}) collective-permute-start(f32[2,512,128]{2,1,0:T(8,128)S(1)} %bitcast.56), channel_id=1, source_target_pairs={{0,2},{1,3},{2,0},{3,1},{4,6},{5,7},{6,4},{7,5},{8,10},{9,11},{10,... | collective-permute-start | bytes 1572872 | tf_op jit(solution)/shard_map/ppermute | solution.py:22
  12.9 2.0 %copy-start.5 = (s32[4]{0:T(128)S(1)}, s32[4]{0:T(128)}, u32[]{:S(2)}) copy-start(s32[4]{0:T(128)} %param.11) | copy-start | bytes 52
  12.9 2.7 %copy-start.4 = (f32[128,128]{1,0:T(8,128)S(1)}, f32[128,128]{1,0:T(8,128)}, u32[]{:S(2)}) copy-start(f32[128,128]{1,0:T(8,128)} %get-tuple-element.44) | copy-start | bytes 196612
  13.0 12.7 %copy-start.1 = (f32[32,128]{1,0:T(8,128)S(1)}, f32[32,128]{1,0:T(8,128)}, u32[]{:S(2)}) copy-start(f32[32,128]{1,0:T(8,128)} %get-tuple-element.45.refs_4_) | copy-start | bytes 49156
  13.0 12.7 %copy-start.2 = (f32[16,128]{1,0:T(8,128)S(1)}, f32[16,128]{1,0:T(8,128)}, u32[]{:S(2)}) copy-start(f32[16,128]{1,0:T(8,128)} %get-tuple-element.47.refs_9_) | copy-start | bytes 24580
  15.0 41.0 %collective-permute-start.18 = (f32[2,512,128]{2,1,0:T(8,128)S(1)}, f32[2,512,128]{2,1,0:T(8,128)S(1)}, u32[]{:S(2)}, u32[]{:S(2)}) collective-permute-start(f32[2,512,128]{2,1,0:T(8,128)S(1)} %bitcast.57), channel_id=1, source_target_pairs={{0,2},{1,3},{2,0},{3,1},{4,6},{5,7},{6,4},{7,5},{8,10},{9,11},{10,... | collective-permute-start | bytes 1572872 | tf_op jit(solution)/shard_map/ppermute | solution.py:22
  15.6 5.2 %collective-permute-start.3 = (f32[128,128]{1,0:T(8,128)S(1)}, f32[128,128]{1,0:T(8,128)S(1)}, u32[]{:S(2)}, u32[]{:S(2)}) collective-permute-start(f32[128,128]{1,0:T(8,128)S(1)} %add.33.refs_0_), channel_id=1, source_target_pairs={{0,16},{4,20},{8,24},{12,28},{16,0},{20,4},{24,8},{28,12},{1,17},{... | collective-permute-start | bytes 196616 | tf_op jit(solution)/shard_map/ppermute | solution.py:594
  16.7 5.0 %collective-permute-start.2 = (f32[128,128]{1,0:T(8,128)S(1)}, f32[128,128]{1,0:T(8,128)S(1)}, u32[]{:S(2)}, u32[]{:S(2)}) collective-permute-start(f32[128,128]{1,0:T(8,128)S(1)} %add.33.refs_0_), channel_id=1, source_target_pairs={{0,24},{4,28},{8,0},{12,4},{16,8},{20,12},{24,16},{28,20},{1,25},{... | collective-permute-start | bytes 196616 | tf_op jit(solution)/shard_map/ppermute | solution.py:594
  19.6 6.1 %collective-permute-start.1 = (f32[128,128]{1,0:T(8,128)S(1)}, f32[128,128]{1,0:T(8,128)S(1)}, u32[]{:S(2)}, u32[]{:S(2)}) collective-permute-start(f32[128,128]{1,0:T(8,128)S(1)} %add.33.refs_0_), channel_id=1, source_target_pairs={{0,8},{4,12},{8,16},{12,20},{16,24},{20,28},{24,0},{28,4},{1,9},{5... | collective-permute-start | bytes 196616 | tf_op jit(solution)/shard_map/ppermute | solution.py:594
  27.1 4.3 %collective-permute-start.7 = (f32[128,128]{1,0:T(8,128)S(1)}, f32[128,128]{1,0:T(8,128)S(1)}, u32[]{:S(2)}, u32[]{:S(2)}) collective-permute-start(f32[128,128]{1,0:T(8,128)S(1)} %get-tuple-element.50.refs_0_), channel_id=1, source_target_pairs={{0,4},{4,0},{8,12},{12,8},{16,20},{20,16},{24,28},{28,24},{1,5},{5... | collective-permute-start | bytes 196616 | tf_op jit(solution)/shard_map/ppermute | solution.py:22
  27.9 9.3 %collective-permute-start.9 = (f32[128,128]{1,0:T(8,128)S(1)}, f32[128,128]{1,0:T(8,128)S(1)}, u32[]{:S(2)}, u32[]{:S(2)}) collective-permute-start(f32[128,128]{1,0:T(8,128)S(1)} %get-tuple-element.51), channel_id=1, source_target_pairs={{0,6},{1,7},{2,4},{3,5},{4,2},{5,3},{6,0},{7,1},{8,14},{9,15},{10,... | collective-permute-start | bytes 196616 | tf_op jit(solution)/shard_map/ppermute | solution.py:689
  30.1 7.8 %collective-permute-start.8 = (f32[128,128]{1,0:T(8,128)S(1)}, f32[128,128]{1,0:T(8,128)S(1)}, u32[]{:S(2)}, u32[]{:S(2)}) collective-permute-start(f32[128,128]{1,0:T(8,128)S(1)} %get-tuple-element.51), channel_id=1, source_target_pairs={{0,2},{1,3},{2,0},{3,1},{4,6},{5,7},{6,4},{7,5},{8,10},{9,11},{10,... | collective-permute-start | bytes 196616 | tf_op jit(solution)/shard_map/ppermute | solution.py:22
  38.0 5.2 %collective-permute-start.12 = (f32[128,128]{1,0:T(8,128)S(1)}, f32[128,128]{1,0:T(8,128)S(1)}, u32[]{:S(2)}, u32[]{:S(2)}) collective-permute-start(f32[128,128]{1,0:T(8,128)S(1)} %get-tuple-element.52.refs_0_), channel_id=1, source_target_pairs={{0,16},{4,20},{8,24},{12,28},{16,0},{20,4},{24,8},{28,12},{1,17},{... | collective-permute-start | bytes 196616 | tf_op jit(solution)/shard_map/ppermute | solution.py:594
  39.3 5.0 %collective-permute-start.11 = (f32[128,128]{1,0:T(8,128)S(1)}, f32[128,128]{1,0:T(8,128)S(1)}, u32[]{:S(2)}, u32[]{:S(2)}) collective-permute-start(f32[128,128]{1,0:T(8,128)S(1)} %get-tuple-element.52.refs_0_), channel_id=1, source_target_pairs={{0,24},{4,28},{8,0},{12,4},{16,8},{20,12},{24,16},{28,20},{1,25},{... | collective-permute-start | bytes 196616 | tf_op jit(solution)/shard_map/ppermute | solution.py:594
  42.0 6.1 %collective-permute-start.10 = (f32[128,128]{1,0:T(8,128)S(1)}, f32[128,128]{1,0:T(8,128)S(1)}, u32[]{:S(2)}, u32[]{:S(2)}) collective-permute-start(f32[128,128]{1,0:T(8,128)S(1)} %get-tuple-element.52.refs_0_), channel_id=1, source_target_pairs={{0,8},{4,12},{8,16},{12,20},{16,24},{20,28},{24,0},{28,4},{1,9},{5... | collective-permute-start | bytes 196616 | tf_op jit(solution)/shard_map/ppermute | solution.py:594
  49.4 4.3 %collective-permute-start.14 = (f32[128,128]{1,0:T(8,128)S(1)}, f32[128,128]{1,0:T(8,128)S(1)}, u32[]{:S(2)}, u32[]{:S(2)}) collective-permute-start(f32[128,128]{1,0:T(8,128)S(1)} %get-tuple-element.53), channel_id=1, source_target_pairs={{0,4},{4,0},{8,12},{12,8},{16,20},{20,16},{24,28},{28,24},{1,5},{5... | collective-permute-start | bytes 196616 | tf_op jit(solution)/shard_map/ppermute | solution.py:22
  53.8 5.2 %collective-permute-start.17 = (f32[128,128]{1,0:T(8,128)S(1)}, f32[128,128]{1,0:T(8,128)S(1)}, u32[]{:S(2)}, u32[]{:S(2)}) collective-permute-start(f32[128,128]{1,0:T(8,128)S(1)} %add.36.refs_0_), channel_id=1, source_target_pairs={{0,16},{4,20},{8,24},{12,28},{16,0},{20,4},{24,8},{28,12},{1,17},{... | collective-permute-start | bytes 196616 | tf_op jit(solution)/shard_map/ppermute | solution.py:594
  53.9 5.2 %collective-permute-start.16 = (f32[128,128]{1,0:T(8,128)S(1)}, f32[128,128]{1,0:T(8,128)S(1)}, u32[]{:S(2)}, u32[]{:S(2)}) collective-permute-start(f32[128,128]{1,0:T(8,128)S(1)} %add.36.refs_0_), channel_id=1, source_target_pairs={{0,24},{4,28},{8,0},{12,4},{16,8},{20,12},{24,16},{28,20},{1,25},{... | collective-permute-start | bytes 196616 | tf_op jit(solution)/shard_map/ppermute | solution.py:594
  55.1 6.1 %collective-permute-start.15 = (f32[128,128]{1,0:T(8,128)S(1)}, f32[128,128]{1,0:T(8,128)S(1)}, u32[]{:S(2)}, u32[]{:S(2)}) collective-permute-start(f32[128,128]{1,0:T(8,128)S(1)} %add.36.refs_0_), channel_id=1, source_target_pairs={{0,8},{4,12},{8,16},{12,20},{16,24},{20,28},{24,0},{28,4},{1,9},{5... | collective-permute-start | bytes 196616 | tf_op jit(solution)/shard_map/ppermute | solution.py:594
  63.1 1.2 collective-permute-start.19
  64.3 3.9 %collective-permute-start.20 = (f32[64,128]{1,0:T(8,128)S(1)}, f32[64,128]{1,0:T(8,128)S(1)}, u32[]{:S(2)}, u32[]{:S(2)}) collective-permute-start(f32[64,128]{1,0:T(8,128)S(1)} %add.37), channel_id=1, source_target_pairs={{0,4},{4,0},{8,12},{12,8},{16,20},{20,16},{24,28},{28,24},{1,5},{5... | collective-permute-start | bytes 98312 | tf_op jit(solution)/shard_map/ppermute | solution.py:22
  68.2 5.2 %collective-permute-start.23 = (f32[64,128]{1,0:T(8,128)S(1)}, f32[64,128]{1,0:T(8,128)S(1)}, u32[]{:S(2)}, u32[]{:S(2)}) collective-permute-start(f32[64,128]{1,0:T(8,128)S(1)} %add.38.refs_0_), channel_id=1, source_target_pairs={{0,16},{4,20},{8,24},{12,28},{16,0},{20,4},{24,8},{28,12},{1,17},{... | collective-permute-start | bytes 98312 | tf_op jit(solution)/shard_map/ppermute | solution.py:594
  68.2 5.2 %collective-permute-start.22 = (f32[64,128]{1,0:T(8,128)S(1)}, f32[64,128]{1,0:T(8,128)S(1)}, u32[]{:S(2)}, u32[]{:S(2)}) collective-permute-start(f32[64,128]{1,0:T(8,128)S(1)} %add.38.refs_0_), channel_id=1, source_target_pairs={{0,24},{4,28},{8,0},{12,4},{16,8},{20,12},{24,16},{28,20},{1,25},{... | collective-permute-start | bytes 98312 | tf_op jit(solution)/shard_map/ppermute | solution.py:594
  69.7 5.7 %collective-permute-start.21 = (f32[64,128]{1,0:T(8,128)S(1)}, f32[64,128]{1,0:T(8,128)S(1)}, u32[]{:S(2)}, u32[]{:S(2)}) collective-permute-start(f32[64,128]{1,0:T(8,128)S(1)} %add.38.refs_0_), channel_id=1, source_target_pairs={{0,8},{4,12},{8,16},{12,20},{16,24},{20,28},{24,0},{28,4},{1,9},{5... | collective-permute-start | bytes 98312 | tf_op jit(solution)/shard_map/ppermute | solution.py:594
  78.7 1.5 %collective-permute-start.24 = (f32[512,128]{1,0:T(8,128)S(1)}, f32[512,128]{1,0:T(8,128)S(1)}, u32[]{:S(2)}, u32[]{:S(2)}) collective-permute-start(f32[512,128]{1,0:T(8,128)S(1)} %get-tuple-element.58.mine), channel_id=1, source_target_pairs={{0,1},{1,0},{2,3},{3,2},{4,5},{5,4},{6,7},{7,6},{8,9},{9,8},{10,11... | collective-permute-start | bytes 786440 | tf_op jit(solution)/shard_map/ppermute | solution.py:22
  81.5 4.6 %collective-permute-start.25 = (f32[160,128]{1,0:T(8,128)S(1)}, f32[160,128]{1,0:T(8,128)S(1)}, u32[]{:S(2)}, u32[]{:S(2)}) collective-permute-start(f32[160,128]{1,0:T(8,128)S(1)} %get-tuple-element.60), channel_id=1, source_target_pairs={{0,4},{4,0},{8,12},{12,8},{16,20},{20,16},{24,28},{28,24},{1,5},{5... | collective-permute-start | bytes 245768 | tf_op jit(solution)/shard_map/ppermute | solution.py:22
  82.3 29.9 %collective-permute-start.35 = (f32[2,512,128]{2,1,0:T(8,128)S(1)}, f32[2,512,128]{2,1,0:T(8,128)S(1)}, u32[]{:S(2)}, u32[]{:S(2)}) collective-permute-start(f32[2,512,128]{2,1,0:T(8,128)S(1)} %bitcast.50), channel_id=1, source_target_pairs={{0,2},{1,3},{2,0},{3,1},{4,6},{5,7},{6,4},{7,5},{8,10},{9,11},{10,... | collective-permute-start | bytes 1572872 | tf_op jit(solution)/shard_map/ppermute | solution.py:22
  86.1 8.0 %collective-permute-start.28 = (f32[160,128]{1,0:T(8,128)S(1)}, f32[160,128]{1,0:T(8,128)S(1)}, u32[]{:S(2)}, u32[]{:S(2)}) collective-permute-start(f32[160,128]{1,0:T(8,128)S(1)} %add.39.refs_0_), channel_id=1, source_target_pairs={{0,16},{4,20},{8,24},{12,28},{16,0},{20,4},{24,8},{28,12},{1,17},{... | collective-permute-start | bytes 245768 | tf_op jit(solution)/shard_map/ppermute | solution.py:594
  86.2 7.9 %collective-permute-start.27 = (f32[160,128]{1,0:T(8,128)S(1)}, f32[160,128]{1,0:T(8,128)S(1)}, u32[]{:S(2)}, u32[]{:S(2)}) collective-permute-start(f32[160,128]{1,0:T(8,128)S(1)} %add.39.refs_0_), channel_id=1, source_target_pairs={{0,24},{4,28},{8,0},{12,4},{16,8},{20,12},{24,16},{28,20},{1,25},{... | collective-permute-start | bytes 245768 | tf_op jit(solution)/shard_map/ppermute | solution.py:594
  87.4 6.7 %collective-permute-start.26 = (f32[160,128]{1,0:T(8,128)S(1)}, f32[160,128]{1,0:T(8,128)S(1)}, u32[]{:S(2)}, u32[]{:S(2)}) collective-permute-start(f32[160,128]{1,0:T(8,128)S(1)} %add.39.refs_0_), channel_id=1, source_target_pairs={{0,8},{4,12},{8,16},{12,20},{16,24},{20,28},{24,0},{28,4},{1,9},{5... | collective-permute-start | bytes 245768 | tf_op jit(solution)/shard_map/ppermute | solution.py:594
  96.6 1.6 %collective-permute-start.29 = (f32[512,128]{1,0:T(8,128)S(1)}, f32[512,128]{1,0:T(8,128)S(1)}, u32[]{:S(2)}, u32[]{:S(2)}) collective-permute-start(f32[512,128]{1,0:T(8,128)S(1)} %get-tuple-element.63.mine), channel_id=1, source_target_pairs={{0,1},{1,0},{2,3},{3,2},{4,5},{5,4},{6,7},{7,6},{8,9},{9,8},{10,11... | collective-permute-start | bytes 786440 | tf_op jit(solution)/shard_map/ppermute | solution.py:22
  99.4 4.5 %collective-permute-start.30 = (f32[160,128]{1,0:T(8,128)S(1)}, f32[160,128]{1,0:T(8,128)S(1)}, u32[]{:S(2)}, u32[]{:S(2)}) collective-permute-start(f32[160,128]{1,0:T(8,128)S(1)} %get-tuple-element.65), channel_id=1, source_target_pairs={{0,4},{4,0},{8,12},{12,8},{16,20},{20,16},{24,28},{28,24},{1,5},{5... | collective-permute-start | bytes 245768 | tf_op jit(solution)/shard_map/ppermute | solution.py:22
  104.0 8.8 %collective-permute-start.33 = (f32[160,128]{1,0:T(8,128)S(1)}, f32[160,128]{1,0:T(8,128)S(1)}, u32[]{:S(2)}, u32[]{:S(2)}) collective-permute-start(f32[160,128]{1,0:T(8,128)S(1)} %add.40.refs_0_), channel_id=1, source_target_pairs={{0,16},{4,20},{8,24},{12,28},{16,0},{20,4},{24,8},{28,12},{1,17},{... | collective-permute-start | bytes 245768 | tf_op jit(solution)/shard_map/ppermute | solution.py:594
  106.2 6.6 %collective-permute-start.32 = (f32[160,128]{1,0:T(8,128)S(1)}, f32[160,128]{1,0:T(8,128)S(1)}, u32[]{:S(2)}, u32[]{:S(2)}) collective-permute-start(f32[160,128]{1,0:T(8,128)S(1)} %add.40.refs_0_), channel_id=1, source_target_pairs={{0,24},{4,28},{8,0},{12,4},{16,8},{20,12},{24,16},{28,20},{1,25},{... | collective-permute-start | bytes 245768 | tf_op jit(solution)/shard_map/ppermute | solution.py:594
  107.9 6.2 %collective-permute-start.31 = (f32[160,128]{1,0:T(8,128)S(1)}, f32[160,128]{1,0:T(8,128)S(1)}, u32[]{:S(2)}, u32[]{:S(2)}) collective-permute-start(f32[160,128]{1,0:T(8,128)S(1)} %add.40.refs_0_), channel_id=1, source_target_pairs={{0,8},{4,12},{8,16},{12,20},{16,24},{20,28},{24,0},{28,4},{1,9},{5... | collective-permute-start | bytes 245768 | tf_op jit(solution)/shard_map/ppermute | solution.py:594
  108.2 4.0 %collective-permute-start.34 = (f32[80,128]{1,0:T(8,128)S(1)}, f32[80,128]{1,0:T(8,128)S(1)}, u32[]{:S(2)}, u32[]{:S(2)}) collective-permute-start(f32[80,128]{1,0:T(8,128)S(1)} %get-tuple-element.66), channel_id=1, source_target_pairs={{0,2},{1,3},{2,0},{3,1},{4,6},{5,7},{6,4},{7,5},{8,10},{9,11},{10,... | collective-permute-start | bytes 122888 | tf_op jit(solution)/shard_map/ppermute | solution.py:22
  116.7 20.7 %copy-start = (f32[2,2,16,64]{3,2,1,0:T(8,128)S(1)}, f32[2,2,16,64]{3,2,1,0:T(8,128)}, u32[]{:S(2)}) copy-start(f32[2,2,16,64]{3,2,1,0:T(8,128)} %refs_6_.1) | copy-start | bytes 49156
  116.7 2.0 %collective-permute-start.36 = (f32[512,128]{1,0:T(8,128)S(1)}, f32[512,128]{1,0:T(8,128)S(1)}, u32[]{:S(2)}, u32[]{:S(2)}) collective-permute-start(f32[512,128]{1,0:T(8,128)S(1)} %get-tuple-element.71.mine), channel_id=1, source_target_pairs={{0,1},{1,0},{2,3},{3,2},{4,5},{5,4},{6,7},{7,6},{8,9},{9,8},{10,11... | collective-permute-start | bytes 786440 | tf_op jit(solution)/shard_map/ppermute | solution.py:22
  117.1 23.6 %collective-permute-start.46 = (f32[512,128]{1,0:T(8,128)S(1)}, f32[512,128]{1,0:T(8,128)S(1)}, u32[]{:S(2)}, u32[]{:S(2)}) collective-permute-start(f32[512,128]{1,0:T(8,128)S(1)} %shard_map.99.mine), channel_id=1, source_target_pairs={{0,2},{1,3},{2,0},{3,1},{4,6},{5,7},{6,4},{7,5},{8,10},{9,11},{10,... | collective-permute-start | bytes 786440 | tf_op jit(solution)/shard_map/ppermute | solution.py:22
  119.9 4.6 %collective-permute-start.37 = (f32[160,128]{1,0:T(8,128)S(1)}, f32[160,128]{1,0:T(8,128)S(1)}, u32[]{:S(2)}, u32[]{:S(2)}) collective-permute-start(f32[160,128]{1,0:T(8,128)S(1)} %get-tuple-element.73), channel_id=1, source_target_pairs={{0,4},{4,0},{8,12},{12,8},{16,20},{20,16},{24,28},{28,24},{1,5},{5... | collective-permute-start | bytes 245768 | tf_op jit(solution)/shard_map/ppermute | solution.py:22
  121.0 21.2 %collective-permute-start.45 = (f32[512,128]{1,0:T(8,128)S(1)}, f32[512,128]{1,0:T(8,128)S(1)}, u32[]{:S(2)}, u32[]{:S(2)}) collective-permute-start(f32[512,128]{1,0:T(8,128)S(1)} %shard_map.98.mine), channel_id=1, source_target_pairs={{0,2},{1,3},{2,0},{3,1},{4,6},{5,7},{6,4},{7,5},{8,10},{9,11},{10,... | collective-permute-start | bytes 786440 | tf_op jit(solution)/shard_map/ppermute | solution.py:22
  122.2 21.9 %collective-permute-start.44 = (f32[512,128]{1,0:T(8,128)S(1)}, f32[512,128]{1,0:T(8,128)S(1)}, u32[]{:S(2)}, u32[]{:S(2)}) collective-permute-start(f32[512,128]{1,0:T(8,128)S(1)} %get-tuple-element.75.mixture), channel_id=1, source_target_pairs={{0,2},{1,3},{2,0},{3,1},{4,6},{5,7},{6,4},{7,5},{8,10},{9,11},{10,... | collective-permute-start | bytes 786440 | tf_op jit(solution)/shard_map/ppermute | solution.py:22
  124.5 6.6 %collective-permute-start.40 = (f32[160,128]{1,0:T(8,128)S(1)}, f32[160,128]{1,0:T(8,128)S(1)}, u32[]{:S(2)}, u32[]{:S(2)}) collective-permute-start(f32[160,128]{1,0:T(8,128)S(1)} %add.41.refs_0_), channel_id=1, source_target_pairs={{0,16},{4,20},{8,24},{12,28},{16,0},{20,4},{24,8},{28,12},{1,17},{... | collective-permute-start | bytes 245768 | tf_op jit(solution)/shard_map/ppermute | solution.py:594
  125.5 6.2 %collective-permute-start.39 = (f32[160,128]{1,0:T(8,128)S(1)}, f32[160,128]{1,0:T(8,128)S(1)}, u32[]{:S(2)}, u32[]{:S(2)}) collective-permute-start(f32[160,128]{1,0:T(8,128)S(1)} %add.41.refs_0_), channel_id=1, source_target_pairs={{0,24},{4,28},{8,0},{12,4},{16,8},{20,12},{24,16},{28,20},{1,25},{... | collective-permute-start | bytes 245768 | tf_op jit(solution)/shard_map/ppermute | solution.py:594
  131.2 6.2 %collective-permute-start.38 = (f32[160,128]{1,0:T(8,128)S(1)}, f32[160,128]{1,0:T(8,128)S(1)}, u32[]{:S(2)}, u32[]{:S(2)}) collective-permute-start(f32[160,128]{1,0:T(8,128)S(1)} %add.41.refs_0_), channel_id=1, source_target_pairs={{0,8},{4,12},{8,16},{12,20},{16,24},{20,28},{24,0},{28,4},{1,9},{5... | collective-permute-start | bytes 245768 | tf_op jit(solution)/shard_map/ppermute | solution.py:594
  139.6 4.6 %collective-permute-start.43 = (f32[80,128]{1,0:T(8,128)S(1)}, f32[80,128]{1,0:T(8,128)S(1)}, u32[]{:S(2)}, u32[]{:S(2)}) collective-permute-start(f32[80,128]{1,0:T(8,128)S(1)} %shard_map.97.mine), channel_id=1, source_target_pairs={{0,3},{1,2},{2,1},{3,0},{4,7},{5,6},{6,5},{7,4},{8,11},{9,10},{10,... | collective-permute-start | bytes 122888 | tf_op jit(solution)/shard_map/ppermute | solution.py:22
  139.6 4.6 %collective-permute-start.42 = (f32[80,128]{1,0:T(8,128)S(1)}, f32[80,128]{1,0:T(8,128)S(1)}, u32[]{:S(2)}, u32[]{:S(2)}) collective-permute-start(f32[80,128]{1,0:T(8,128)S(1)} %shard_map.97.mine), channel_id=1, source_target_pairs={{0,2},{1,3},{2,0},{3,1},{4,6},{5,7},{6,4},{7,5},{8,10},{9,11},{10,... | collective-permute-start | bytes 122888 | tf_op jit(solution)/shard_map/ppermute | solution.py:22
  140.7 3.5 %collective-permute-start.41 = (f32[80,128]{1,0:T(8,128)S(1)}, f32[80,128]{1,0:T(8,128)S(1)}, u32[]{:S(2)}, u32[]{:S(2)}) collective-permute-start(f32[80,128]{1,0:T(8,128)S(1)} %shard_map.97.mine), channel_id=1, source_target_pairs={{0,1},{1,0},{2,3},{3,2},{4,5},{5,4},{6,7},{7,6},{8,9},{9,8},{10,11... | collective-permute-start | bytes 122888 | tf_op jit(solution)/shard_map/ppermute | solution.py:22

commit v6 on v5

--- a/solution.py
+++ b/solution.py
@@ -182,31 +182,18 @@
     return scratch[pl.ds(0, 2 * count), :]
 
 
-def start_kernel(member, _, *refs):
-    sources, (part, heads, tail), (*local, sems, scratch) = refs[:3], refs[3:6], refs[6:]
-    copies = [
-        pltpu.make_async_copy(source, target, sems.at[at])
-        for at, (source, target) in enumerate(zip(sources, local))
-    ]
-    for copy in copies:
-        copy.start()
-    for copy in copies:
-        copy.wait()
-    last, first, sketch = local
-    count, slices = last.shape[1:3]
+def start_kernel(member, _, last, sketch, out, scratch):
+    count = last.shape[1]
     for half, index in enumerate((member[0], 1 - member[0])):
-        cores, fronts = last[index], first[index]
+        cores = last[index]
         for s in range(count):
             scratch[pl.ds((half * count + s) * HALF, HALF), pl.ds(0, HALF)] = exact(
                 cores[s], sketch[...], TN
             )
-        heads[pl.ds(half * slices, slices), :] = jnp.concatenate([fronts[0], fronts[1]], axis=1)
-        if half:
-            tail[...] = jnp.concatenate([cores[0], cores[1]], axis=1)
-    rows = part.shape[0]
+    rows = out.shape[0]
     even = scratch[pl.ds(0, rows, stride=2), :]
     odd = scratch[pl.ds(1, rows, stride=2), :]
-    part[...] = pick(even, swap(odd))
+    out[...] = pick(even, swap(odd))
 
 
 def merge_kernel(n_parts, rows, *refs):
@@ -215,7 +202,13 @@
     for pair, terms in enumerate((keeps, sends)):
         part[pl.ds(pair * rows, rows), :] = added([term.at[pl.ds(0, rows)] for term in terms])
         for at, term in enumerate(terms):
-            heads[pair, pl.ds(at * height, height), :] = term[pl.ds(rows, height), :]
+            place = pl.ds((pair * n_parts + at) * height, height)
+            heads[place, :] = term[pl.ds(rows, height), :]
+
+
+def heads_of(parts, pair):
+    rows = parts[0].shape[0] // 2
+    return jnp.concatenate([part[pl.ds(pair * rows, rows), :] for part in parts], axis=0)
 
 
 def added(parts):
@@ -260,19 +253,19 @@
     out[...] = sketch_step(parts, mask, kept, other, sketch, *rest)
 
 
-def meet_kernel(n_parts, n_heads, *refs):
-    parts, heads, refs = refs[:n_parts], refs[n_parts : n_parts + n_heads], refs[n_parts + n_heads :]
-    mask, tail, kept, other, sketch, keep, send, relay, *rest = refs
+def meet_kernel(n_parts, *refs):
+    parts, refs = refs[:n_parts], refs[n_parts:]
+    member, first, last, mask, kept, other, sketch, keep, send, relay, *rest = refs
     value = sketch_step(parts, mask, kept, other, sketch, *rest)
     rows = value.shape[0] // 2
-    slices = tail.shape[0]
-    keep[pl.ds(0, rows), :] = value[:rows]
-    send[pl.ds(0, rows), :] = value[rows:]
-    for at, head in enumerate(heads):
-        keep[pl.ds(rows + at * slices, slices), :] = head[pl.ds(0, slices), :]
-        send[pl.ds(rows + at * slices, slices), :] = head[pl.ds(slices, slices), :]
+    slices = first.shape[2]
+    for out, half, index in ((keep, 0, member[0]), (send, 1, 1 - member[0])):
+        out[pl.ds(0, rows), :] = value[half * rows : (half + 1) * rows]
+        heads = first[index]
+        out[pl.ds(rows, slices), :] = jnp.concatenate([heads[0], heads[1]], axis=1)
+    tail = last[1 - member[0]]
     relay[pl.ds(0, rows), :] = added([part.at[pl.ds(rows, rows)] for part in parts]) * mask[...]
-    relay[pl.ds(rows, slices), :] = tail[...]
+    relay[pl.ds(rows, slices), :] = jnp.concatenate([tail[0], tail[1]], axis=1)
 
 
 def mixed_kernel(relay, cores, own_high, own_low, high, low, wide, product):
@@ -301,8 +294,8 @@
     inner, outer = spot % n_inner, spot // n_inner
     return [
         (outer + n_outer - by) % n_outer * n_inner + (inner ^ step)
+        for by in (0,) + SHIFTS
         for step in range(n_inner)
-        for by in (0,) + SHIFTS
     ]
 
 
@@ -311,13 +304,13 @@
 
 
 def first_kernel(n_parts, *refs, slices):
-    parts, (heads, *refs) = refs[:n_parts], refs[n_parts:]
+    parts, heads, refs = refs[:n_parts], refs[n_parts : 2 * n_parts], refs[2 * n_parts :]
     spot, mask, next_mask, kept, other, sketch, out, *rest = refs
     value = sketch_step(parts, mask, kept, other, sketch, *rest)
     natural = spread_rows(value * next_mask[...], rest[2])
     natural = pick(natural, jnp.zeros_like(natural))
-    value = exact(heads[0], natural[:LANES])
-    value = value + exact(heads[1], natural[LANES:])
+    value = dot3(split(heads_of(heads, 0)), split(natural[:LANES]))
+    value = value + dot3(split(heads_of(heads, 1)), split(natural[LANES:]))
     shared = rest[2]
     blocks = slice_blocks(spot[0], LANES // slices // n_parts, n_parts)
     for at, block in enumerate(blocks):
@@ -369,7 +362,7 @@
     planar = jnp.concatenate(
         [square[pl.ds(0, HALF // 2, stride=2), :], square[pl.ds(1, HALF // 2, stride=2), :]], axis=0
     )
-    carried = exact(raw, block_diagonal(swap(planar)), NT) * (1.0 / row_count)
+    carried = dot3(split(raw), split(block_diagonal(swap(planar))), NT) * (1.0 / row_count)
     square[...] = carried
     pairs = carried.shape[0] // HALF
     even = square[pl.ds(0, pairs * 32, stride=2), :]
@@ -396,7 +389,7 @@
 
 
 def bond_one_kernel(row_count, n_parts, *refs):
-    parts, (heads, *refs) = refs[:n_parts], refs[n_parts:]
+    parts, heads, refs = refs[:n_parts], refs[n_parts : 2 * n_parts], refs[2 * n_parts :]
     spot, mask, high, low, inverse, carried, basis, out, square = refs
     packed = added(parts)
     zero = jnp.zeros_like(packed)
@@ -407,7 +400,7 @@
     gram = exact(mixture, mixture, TN)[:HALF]
     raw = []
     for pair in range(2):
-        value = exact(heads[pair], mixture, TN)
+        value = dot3(split(heads_of(heads, pair)), split(mixture), TN)
         raw.append(pick(value[:HALF], swap(value[HALF:])))
     solved, moved = project(jnp.concatenate(raw, axis=0), gram, mask[...], row_count, square)
     inverse[...] = solved
@@ -497,8 +490,8 @@
     count, rows = kept.shape[0], kept.shape[1]
     tiles = rows // 256
     mixture[...] = mine[...] + theirs[...]
-    everything = mixture[...]
-    gram = exact(everything, everything, TN)
+    everything = split(mixture[...])
+    gram = dot3(everything, everything, TN)
     weight = split(carried[...])
     height = 2 * count * 32
     for tile in range(tiles):
@@ -623,23 +616,14 @@
         )
         return in_rows(part.reshape(count, slices, width))
 
-    part, heads, tail = kernel_call(
+    (part,) = kernel_call(
         start_kernel,
-        [shape(height, LANES), shape(2 * slices, LANES), shape(slices, LANES)],
-        [
-            scratch(*last_cores.shape),
-            scratch(*first_cores.shape),
-            scratch(*sketch_last.shape),
-            pltpu.SemaphoreType.DMA((3,)),
-            scratch(2 * height, LANES),
-        ],
+        [shape(height, LANES)],
+        [scratch(2 * height, LANES)],
         here,
         spot,
         last_cores,
-        first_cores,
         sketch_last,
-        in_hbm=(2, 3, 4),
-        limit=None,
     )
     late_cores, late_sketch, late_ranks, part = lax.optimization_barrier(
         (mid_cores, sketch_mid, ranks, part)
@@ -650,32 +634,38 @@
     masks = jnp.concatenate([masks, masks], axis=1)[:, None, :]
     sketch_rows = in_rows(late_sketch)
     sketch_rows = [sketch_rows[position] for position in range(middle)]
-    kept = [half_of(late_cores, position, member) for position in range(middle)]
-    sent = [half_of(late_cores, position, 1 - member) for position in range(middle)]
-    sent[middle - 2] = half_of(mid_cores, middle - 2, 1 - member)
-    traded = [flip(sent[position], "rep", low) for position in range(middle)]
-    cores = list(zip(kept, traded))
+    kept = [None] * (middle - 1) + [half_of(late_cores, middle - 1, member)]
+    sent = [None] * (middle - 1) + [half_of(late_cores, middle - 1, 1 - member)]
     wide = shape(slices, height, LANES, dtype=jnp.bfloat16)
     room = [
         scratch(2 * height, LANES),
         scratch(height * slices, LANES),
         scratch(slices, HALF, LANES),
     ]
-    heads = spread(heads, "mode", outer)
     parts = exchanged(part, "mode")
-    block = shape(height // 2 + len(heads) * slices, LANES)
+    block = shape(height // 2 + slices, LANES)
     keep, send, relay, *own_mixed = kernel_call(
-        functools.partial(meet_kernel, len(parts), len(heads)),
+        functools.partial(meet_kernel, len(parts)),
         [block, block, shape(height // 2 + slices, LANES), wide, wide],
         room,
         *parts,
-        *heads,
+        here,
+        first_cores,
+        last_cores,
         masks[middle],
-        tail,
         kept[-1],
         sent[-1],
         sketch_rows[-1],
     )
+    later_cores, keep, send = lax.optimization_barrier((late_cores, keep, send))
+    for position in range(middle - 1):
+        if position == middle - 2:
+            sent[position] = half_of(mid_cores, position, 1 - member)
+        else:
+            sent[position] = half_of(later_cores, position, 1 - member)
+        kept[position] = half_of(later_cores, position, member)
+    traded = [flip(sent[position], "rep", low) for position in range(middle)]
+    cores = list(zip(kept, traded))
     keeps, sends = [keep], []
     sends.append(flip(send, "rep", low))
     for step in range(1, inner[0]):
@@ -689,11 +679,12 @@
         sends.append(lax.ppermute(send, ("mode", "rep"), pairs))
     part, heads = kernel_call(
         functools.partial(merge_kernel, len(keeps), height // 2),
-        [shape(height, LANES), shape(2, total_slices, LANES)],
+        [shape(height, LANES), shape(2 * len(keeps) * slices, LANES)],
         [],
         *keeps,
         *sends,
     )
+    heads = spread(heads, "mode", outer)
     relay = flip(relay, "rep", low)
     mixed = [None] * middle
     mixed[-1] = kernel_call(
@@ -712,7 +703,7 @@
         body, more, result = sketch_kernel, (), shape(height, LANES)
         if position == 0:
             body = functools.partial(first_kernel, slices=slices)
-            more, result = (heads, spot), shape(total_slices // 2, LANES)
+            more, result = (*heads, spot), shape(total_slices // 2, LANES)
         part, *mixed[position] = kernel_call(
             functools.partial(body, len(parts)),
             [result, wide, wide],
@@ -731,7 +722,7 @@
         [shape(HALF, LANES), shape(height, LANES), shape(slices, LANES), shape(rows, LANES)],
         [square],
         *parts,
-        heads,
+        *heads,
         spot,
         masks[0],
         *mixed[0],

time: 146 us -> 144 us (0.986)
  Pallas kernels: 26.3 us -> 23.1 us
  local copies, waits for them, and re-layouts: 3.06 us -> 5.3 us
  waiting for transfers between devices: 67.8 us -> 65.6 us
    pallas_call x19, Pallas kernels: 26.3 us -> 23.1 us  [kernel_call(): pl.pallas_call(body, out_shape=outs, in_specs=specs[:len(operands)], out_...]
    ppermute x24, waiting for transfers between devices: 39.7 us -> 37.2 us  [spread(): parts.append(lax.ppermute(value, axis, pairs))]
    ppermute x1, waiting for transfers between devices: 5.76 us -> 8.18 us  [tiled(): sends.append(lax.ppermute(send, ('mode', 'rep'), pairs))]
    ppermute x22, waiting for transfers between devices: 22.3 us -> 20.2 us  [flip(): lax.ppermute(value, axis, [(index, index ^ bits) for index in range(size)])]
    unnamed x12 -> x10, local copies, waits for them, and re-layouts: 0.03 us -> 1.51 us
    dynamic_slice x2 -> x3, local copies, waits for them, and re-layouts: 2.97 us -> 2.63 us  [half_of(): lax.dynamic_slice(source, (index, 0, position, 0, 0), (1, count, 1, slice...]
  transfers between devices with their start and end apart: 47 -> 47, of which waited for: 26 -> 27; matrix products, arithmetic and copies ran while one was open for 2% -> 3% of each run, Pallas kernels for 9% -> 9%
where the time goes in v6:
time: 144 us; the launch traced here: 143 us
  waiting for transfers between devices  65.6 us (46%)
  starting transfers between devices  47.5 us (33%)
  Pallas kernels  23.1 us (16%)
  local copies, waits for them, and re-layouts  5.3 us (4%)
    ppermute x24, waiting for transfers between devices, spread(): parts.append(lax.ppermute(value, axis, pairs))  37.2 us
    ppermute x24, starting transfers between devices, spread(): parts.append(lax.ppermute(value, axis, pairs))  27.1 us
    pallas_call x19, Pallas kernels, kernel_call(): pl.pallas_call(body, out_shape=outs, in_specs=specs[:len(operands)], out_...  23.1 us
    ppermute x22, waiting for transfers between devices, flip(): lax.ppermute(value, axis, [(index, index ^ bits) for index in range(size)])  20.2 us
    ppermute x22, starting transfers between devices, flip(): lax.ppermute(value, axis, [(index, index ^ bits) for index in range(size)])  18 us
    ppermute x1, waiting for transfers between devices, tiled(): sends.append(lax.ppermute(send, ('mode', 'rep'), pairs))  8.18 us
  transfers between devices with their start and end apart: 47, of which 27 were waited for; matrix products, arithmetic and copies ran while one was open for 3% of the time, Pallas kernels for 9%

profile of v6, /device:TPU:0, one launch (start us, length us, event | category | flops | bytes accessed | tf_op | source)
XLA Modules:
  0.0 143.5 jit_solution(11464857016333181414)
XLA Ops:
  2.5 3.0 %collective-permute-start = (f32[128,128]{1,0:T(8,128)S(1)}, f32[128,128]{1,0:T(8,128)S(1)}, u32[]{:S(2)}, u32[]{:S(2)}) collective-permute-start(f32[128,128]{1,0:T(8,128)S(1)} %shard_map.85), channel_id=1, source_target_pairs={{0,4},{4,0},{8,12},{12,8},{16,20},{20,16},{24,28},{28,24},{1,5},{5... | collective-permute-start | bytes 196616 | tf_op jit(solution)/shard_map/ppermute | solution.py:22
  5.6 1.1 constant_dynamic-slice_fusion.2
  6.7 1.6 %collective-permute-start.10 = (f32[2,512,128]{2,1,0:T(8,128)S(1)}, f32[2,512,128]{2,1,0:T(8,128)S(1)}, u32[]{:S(2)}, u32[]{:S(2)}) collective-permute-start(f32[2,512,128]{2,1,0:T(8,128)S(1)} %bitcast.56), channel_id=1, source_target_pairs={{0,2},{1,3},{2,0},{3,1},{4,6},{5,7},{6,4},{7,5},{8,10},{9,11},{10,... | collective-permute-start | bytes 1572872 | tf_op jit(solution)/shard_map/ppermute | solution.py:22
  8.9 1.2 fusion
  10.1 1.4 constant_dynamic-slice_fusion.4
  11.7 2.7 %collective-permute-start.3 = (f32[128,128]{1,0:T(8,128)S(1)}, f32[128,128]{1,0:T(8,128)S(1)}, u32[]{:S(2)}, u32[]{:S(2)}) collective-permute-start(f32[128,128]{1,0:T(8,128)S(1)} %add.33.refs_0_), channel_id=1, source_target_pairs={{0,16},{4,20},{8,24},{12,28},{16,0},{20,4},{24,8},{28,12},{1,17},{... | collective-permute-start | bytes 196616 | tf_op jit(solution)/shard_map/ppermute | solution.py:587
  14.3 1.3 collective-permute-start.2
  17.0 1.6 %collective-permute-done.2.refs_2_ = f32[128,128]{1,0:T(8,128)S(1)} collective-permute-done((f32[128,128]{1,0:T(8,128)S(1)}, f32[128,128]{1,0:T(8,128)S(1)}, u32[]{:S(2)}, u32[]{:S(2)}) %collective-permute-start.2) | collective-permute-done | bytes 65568 | tf_op jit(solution)/shard_map/ppermute | solution.py:587
  18.6 3.1 %collective-permute-done.1.refs_1_ = f32[128,128]{1,0:T(8,128)S(1)} collective-permute-done((f32[128,128]{1,0:T(8,128)S(1)}, f32[128,128]{1,0:T(8,128)S(1)}, u32[]{:S(2)}, u32[]{:S(2)}) %collective-permute-start.1) | collective-permute-done | bytes 65568 | tf_op jit(solution)/shard_map/ppermute | solution.py:587
  21.7 1.4 shard_map.86
  24.4 2.5 %collective-permute-start.6 = (f32[80,128]{1,0:T(8,128)S(1)}, f32[80,128]{1,0:T(8,128)S(1)}, u32[]{:S(2)}, u32[]{:S(2)}) collective-permute-start(f32[80,128]{1,0:T(8,128)S(1)} %get-tuple-element.50), channel_id=1, source_target_pairs={{0,6},{1,7},{2,4},{3,5},{4,2},{5,3},{6,0},{7,1},{8,14},{9,15},{10,... | collective-permute-start | bytes 122888 | tf_op jit(solution)/shard_map/ppermute | solution.py:679
  27.9 8.2 %collective-permute-done.6.refs_3_ = f32[80,128]{1,0:T(8,128)S(1)} collective-permute-done((f32[80,128]{1,0:T(8,128)S(1)}, f32[80,128]{1,0:T(8,128)S(1)}, u32[]{:S(2)}, u32[]{:S(2)}) %collective-permute-start.6) | collective-permute-done | bytes 40992 | tf_op jit(solution)/shard_map/ppermute | solution.py:679
  36.6 3.1 %collective-permute-start.9 = (f32[128,128]{1,0:T(8,128)S(1)}, f32[128,128]{1,0:T(8,128)S(1)}, u32[]{:S(2)}, u32[]{:S(2)}) collective-permute-start(f32[128,128]{1,0:T(8,128)S(1)} %get-tuple-element.51.refs_0_), channel_id=1, source_target_pairs={{0,16},{4,20},{8,24},{12,28},{16,0},{20,4},{24,8},{28,12},{1,17},{... | collective-permute-start | bytes 196616 | tf_op jit(solution)/shard_map/ppermute | solution.py:587
  40.2 1.6 %collective-permute-start.7 = (f32[128,128]{1,0:T(8,128)S(1)}, f32[128,128]{1,0:T(8,128)S(1)}, u32[]{:S(2)}, u32[]{:S(2)}) collective-permute-start(f32[128,128]{1,0:T(8,128)S(1)} %get-tuple-element.51.refs_0_), channel_id=1, source_target_pairs={{0,8},{4,12},{8,16},{12,20},{16,24},{20,28},{24,0},{28,4},{1,9},{5... | collective-permute-start | bytes 196616 | tf_op jit(solution)/shard_map/ppermute | solution.py:587
  41.8 1.3 collective-permute-done.9.refs_3_
  43.0 1.5 %collective-permute-done.8.refs_2_ = f32[128,128]{1,0:T(8,128)S(1)} collective-permute-done((f32[128,128]{1,0:T(8,128)S(1)}, f32[128,128]{1,0:T(8,128)S(1)}, u32[]{:S(2)}, u32[]{:S(2)}) %collective-permute-start.8) | collective-permute-done | bytes 65568 | tf_op jit(solution)/shard_map/ppermute | solution.py:587
  44.5 1.7 %collective-permute-done.7.refs_1_ = f32[128,128]{1,0:T(8,128)S(1)} collective-permute-done((f32[128,128]{1,0:T(8,128)S(1)}, f32[128,128]{1,0:T(8,128)S(1)}, u32[]{:S(2)}, u32[]{:S(2)}) %collective-permute-start.7) | collective-permute-done | bytes 65568 | tf_op jit(solution)/shard_map/ppermute | solution.py:587
  46.2 1.4 shard_map.88
  47.6 1.1 collective-permute-start.11
  49.0 1.9 %collective-permute-start.16 = (f32[64,128]{1,0:T(8,128)S(1)}, f32[64,128]{1,0:T(8,128)S(1)}, u32[]{:S(2)}, u32[]{:S(2)}) collective-permute-start(f32[64,128]{1,0:T(8,128)S(1)} %get-tuple-element.54.refs_4_), channel_id=1, source_target_pairs={{0,24},{4,28},{8,0},{12,4},{16,8},{20,12},{24,16},{28,20},{1,25},{... | collective-permute-start | bytes 98312 | tf_op jit(solution)/shard_map/ppermute | solution.py:587
  50.9 1.1 collective-permute-done.11
  52.0 0.8 collective-permute-start.14
  52.8 1.4 collective-permute-start.13
  54.9 0.9 collective-permute-start.15
  55.8 5.0 %collective-permute-done.15.refs_5_ = f32[64,128]{1,0:T(8,128)S(1)} collective-permute-done((f32[64,128]{1,0:T(8,128)S(1)}, f32[64,128]{1,0:T(8,128)S(1)}, u32[]{:S(2)}, u32[]{:S(2)}) %collective-permute-start.15) | collective-permute-done | bytes 32800 | tf_op jit(solution)/shard_map/ppermute | solution.py:587
  60.8 1.7 %shard_map.89 = (f32[64,128]{1,0:T(8,128)S(1)}, bf16[16,128,128]{2,1,0:T(8,128)(2,1)S(1)}, bf16[16,128,128]{2,1,0:T(8,128)(2,1)S(1)}) custom-call(f32[128,128]{1,0:T(8,128)S(1)} %add.36.refs_0_, f32[128,128]{1,0:T(8,128)S(1)} %collective-permute-done.12.refs_1_, f32[128,128]{1,0:T(8,128)S(1)} %collective-permute-done.13.refs_2_, ...), custom_call_target="tpu_custom_call" | custom-call | bytes 2786308 | tf_op jit(solution)/shard_map/pallas_call | solution.py:542
  62.6 1.2 collective-permute-done.19
  63.8 1.2 collective-permute-start.20
  64.9 2.8 %collective-permute-done.20 = f32[64,128]{1,0:T(8,128)S(1)} collective-permute-done((f32[64,128]{1,0:T(8,128)S(1)}, f32[64,128]{1,0:T(8,128)S(1)}, u32[]{:S(2)}, u32[]{:S(2)}) %collective-permute-start.20) | collective-permute-done | bytes 32800 | tf_op jit(solution)/shard_map/ppermute | solution.py:22
  67.8 1.2 collective-permute-start.22
  69.9 3.0 %collective-permute-done.23.refs_3_ = f32[64,128]{1,0:T(8,128)S(1)} collective-permute-done((f32[64,128]{1,0:T(8,128)S(1)}, f32[64,128]{1,0:T(8,128)S(1)}, u32[]{:S(2)}, u32[]{:S(2)}) %collective-permute-start.23) | collective-permute-done | bytes 32800 | tf_op jit(solution)/shard_map/ppermute | solution.py:587
  72.9 1.9 %collective-permute-done.21.refs_1_ = f32[64,128]{1,0:T(8,128)S(1)} collective-permute-done((f32[64,128]{1,0:T(8,128)S(1)}, f32[64,128]{1,0:T(8,128)S(1)}, u32[]{:S(2)}, u32[]{:S(2)}) %collective-permute-start.21) | collective-permute-done | bytes 32800 | tf_op jit(solution)/shard_map/ppermute | solution.py:587
  74.8 2.7 %shard_map.90 = (f32[64,128]{1,0:T(8,128)}, f32[128,128]{1,0:T(8,128)S(1)}, f32[16,128]{1,0:T(8,128)S(1)}, f32[512,128]{1,0:T(8,128)S(1)}) custom-call(f32[64,128]{1,0:T(8,128)S(1)} %add.38.refs_0_, f32[64,128]{1,0:T(8,128)S(1)} %collective-permute-done.21.refs_1_, f32[64,128]{1,0:T(8,128)S(1)} %collective-permute-done.22.refs_2_, ...), custom_call_target="tpu_custom_call" | custom-call | bytes 1679876 | tf_op jit(solution)/shard_map/pallas_call | solution.py:542
  77.5 1.5 %collective-permute-done.24.theirs = f32[512,128]{1,0:T(8,128)S(1)} collective-permute-done((f32[512,128]{1,0:T(8,128)S(1)}, f32[512,128]{1,0:T(8,128)S(1)}, u32[]{:S(2)}, u32[]{:S(2)}) %collective-permute-start.24) | collective-permute-done | bytes 262176 | tf_op jit(solution)/shard_map/ppermute | solution.py:22
  79.0 1.1 shard_map.91
  80.1 1.2 collective-permute-start.25
  81.9 2.8 %collective-permute-done.25 = f32[160,128]{1,0:T(8,128)S(1)} collective-permute-done((f32[160,128]{1,0:T(8,128)S(1)}, f32[160,128]{1,0:T(8,128)S(1)}, u32[]{:S(2)}, u32[]{:S(2)}) %collective-permute-start.25) | collective-permute-done | bytes 81952 | tf_op jit(solution)/shard_map/ppermute | solution.py:22
  84.9 1.2 collective-permute-start.27
  86.1 0.8 collective-permute-start.26
  86.9 5.8 %collective-permute-done.28.refs_3_ = f32[160,128]{1,0:T(8,128)S(1)} collective-permute-done((f32[160,128]{1,0:T(8,128)S(1)}, f32[160,128]{1,0:T(8,128)S(1)}, u32[]{:S(2)}, u32[]{:S(2)}) %collective-permute-start.28) | collective-permute-done | bytes 81952 | tf_op jit(solution)/shard_map/ppermute | solution.py:587
  92.7 2.3 %shard_map.92 = (f32[64,128]{1,0:T(8,128)S(1)}, f32[128,128]{1,0:T(8,128)S(1)}, f32[512,128]{1,0:T(8,128)S(1)}) custom-call(f32[160,128]{1,0:T(8,128)S(1)} %add.39.refs_0_, f32[160,128]{1,0:T(8,128)S(1)} %collective-permute-done.26.refs_1_, f32[160,128]{1,0:T(8,128)S(1)} %collective-permute-done.27.refs_2_, f32[160,128]{1,0:T(8,128)S(1)} %collective-permute-done.28.refs_3_, ...), custom_call_target="tpu_custom_call" | custom-call | bytes 1737216 | tf_op jit(solution)/shard_map/pallas_call | solution.py:542
  95.1 1.5 %collective-permute-done.29.theirs = f32[512,128]{1,0:T(8,128)S(1)} collective-permute-done((f32[512,128]{1,0:T(8,128)S(1)}, f32[512,128]{1,0:T(8,128)S(1)}, u32[]{:S(2)}, u32[]{:S(2)}) %collective-permute-start.29) | collective-permute-done | bytes 262176 | tf_op jit(solution)/shard_map/ppermute | solution.py:22
  96.6 1.1 shard_map.93
  97.7 1.2 collective-permute-start.30
  98.9 3.3 %collective-permute-done.30 = f32[160,128]{1,0:T(8,128)S(1)} collective-permute-done((f32[160,128]{1,0:T(8,128)S(1)}, f32[160,128]{1,0:T(8,128)S(1)}, u32[]{:S(2)}, u32[]{:S(2)}) %collective-permute-start.30) | collective-permute-done | bytes 81952 | tf_op jit(solution)/shard_map/ppermute | solution.py:22
  102.3 2.2 %collective-permute-start.33 = (f32[160,128]{1,0:T(8,128)S(1)}, f32[160,128]{1,0:T(8,128)S(1)}, u32[]{:S(2)}, u32[]{:S(2)}) collective-permute-start(f32[160,128]{1,0:T(8,128)S(1)} %add.40.refs_0_), channel_id=1, source_target_pairs={{0,16},{4,20},{8,24},{12,28},{16,0},{20,4},{24,8},{28,12},{1,17},{... | collective-permute-start | bytes 245768 | tf_op jit(solution)/shard_map/ppermute | solution.py:587
  104.5 1.7 %collective-permute-start.32 = (f32[160,128]{1,0:T(8,128)S(1)}, f32[160,128]{1,0:T(8,128)S(1)}, u32[]{:S(2)}, u32[]{:S(2)}) collective-permute-start(f32[160,128]{1,0:T(8,128)S(1)} %add.40.refs_0_), channel_id=1, source_target_pairs={{0,24},{4,28},{8,0},{12,4},{16,8},{20,12},{24,16},{28,20},{1,25},{... | collective-permute-start | bytes 245768 | tf_op jit(solution)/shard_map/ppermute | solution.py:587
  107.0 3.5 %collective-permute-done.34.relay.refs_7_ = f32[80,128]{1,0:T(8,128)S(1)} collective-permute-done((f32[80,128]{1,0:T(8,128)S(1)}, f32[80,128]{1,0:T(8,128)S(1)}, u32[]{:S(2)}, u32[]{:S(2)}) %collective-permute-start.34) | collective-permute-done | bytes 40992 | tf_op jit(solution)/shard_map/ppermute | solution.py:22
  111.1 1.3 collective-permute-done.31.refs_1_
  112.4 2.3 %shard_map.95 = (f32[64,128]{1,0:T(8,128)S(1)}, f32[128,128]{1,0:T(8,128)S(1)}, f32[512,128]{1,0:T(8,128)S(1)}) custom-call(f32[160,128]{1,0:T(8,128)S(1)} %add.40.refs_0_, f32[160,128]{1,0:T(8,128)S(1)} %collective-permute-done.31.refs_1_, f32[160,128]{1,0:T(8,128)S(1)} %collective-permute-done.32.refs_2_, f32[160,128]{1,0:T(8,128)S(1)} %collective-permute-done.33.refs_3_, ...), custom_call_target="tpu_custom_call" | custom-call | bytes 1737216 | tf_op jit(solution)/shard_map/pallas_call | solution.py:542
  116.3 1.1 shard_map.96
  117.4 1.2 collective-permute-start.37
  119.0 1.0 collective-permute-start.45
  119.9 1.1 collective-permute-start.44
  121.0 0.9 collective-permute-done.37
  122.0 1.1 collective-permute-start.40
  123.0 1.3 collective-permute-start.39
  124.3 4.4 %collective-permute-done.40.refs_3_ = f32[160,128]{1,0:T(8,128)S(1)} collective-permute-done((f32[160,128]{1,0:T(8,128)S(1)}, f32[160,128]{1,0:T(8,128)S(1)}, u32[]{:S(2)}, u32[]{:S(2)}) %collective-permute-start.40) | collective-permute-done | bytes 81952 | tf_op jit(solution)/shard_map/ppermute | solution.py:587
  129.1 5.8 %collective-permute-done.38.refs_1_ = f32[160,128]{1,0:T(8,128)S(1)} collective-permute-done((f32[160,128]{1,0:T(8,128)S(1)}, f32[160,128]{1,0:T(8,128)S(1)}, u32[]{:S(2)}, u32[]{:S(2)}) %collective-permute-start.38) | collective-permute-done | bytes 81952 | tf_op jit(solution)/shard_map/ppermute | solution.py:587
  134.9 2.1 %shard_map.97.mine = f32[80,128]{1,0:T(8,128)S(1)} custom-call(f32[160,128]{1,0:T(8,128)S(1)} %add.41.refs_0_, f32[160,128]{1,0:T(8,128)S(1)} %collective-permute-done.38.refs_1_, f32[160,128]{1,0:T(8,128)S(1)} %collective-permute-done.39.refs_2_, f32[160,128]{1,0:T(8,128)S(1)} %collective-permute-done.40.refs_3_, ...), custom_call_target="tpu_custom_call" | custom-call | bytes 434692 | tf_op jit(solution)/shard_map/pallas_call | solution.py:542
  137.0 1.0 collective-permute-start.42
  138.0 0.9 collective-permute-start.41
  140.6 1.0 shard_map.102.before
  141.6 1.7 %shard_map.103 = (f32[2,16,64]{2,1,0:T(8,128)}, f32[2,16,64]{2,1,0:T(8,128)}, f32[2,3,512,128]{3,2,1,0:T(8,128)}) custom-call(s32[1]{0:T(128)} %bitcast.member.refs_4_.refs_5_, f32[80,128]{1,0:T(8,128)S(1)} %shard_map.97.mine, f32[80,128]{1,0:T(8,128)S(1)} %collective-permute-done.41.near, ...), custom_call_target="tpu_custom_call", output_to_operand_aliasing={{2}: (6, {})} | custom-call | bytes 3588100 | tf_op jit(solution)/shard_map/pallas_call | solution.py:542
  (73 shorter events, 15.5 us)
Async XLA Ops:
  0.6 21.1 %copy-start.1 = (f32[2,2,16,64]{3,2,1,0:T(8,128)S(1)}, f32[2,2,16,64]{3,2,1,0:T(8,128)}, u32[]{:S(2)}) copy-start(f32[2,2,16,64]{3,2,1,0:T(8,128)} %refs_6_.3) | copy-start | bytes 49156
  0.7 0.8 copy-start
  1.5 0.7 copy-start.3
  2.2 19.6 %copy-start.2 = (f32[2,2,16,64]{3,2,1,0:T(8,128)S(1)}, f32[2,2,16,64]{3,2,1,0:T(8,128)}, u32[]{:S(2)}) copy-start(f32[2,2,16,64]{3,2,1,0:T(8,128)} %refs_5_.1) | copy-start | bytes 49156
  2.5 9.1 %collective-permute-start = (f32[128,128]{1,0:T(8,128)S(1)}, f32[128,128]{1,0:T(8,128)S(1)}, u32[]{:S(2)}, u32[]{:S(2)}) collective-permute-start(f32[128,128]{1,0:T(8,128)S(1)} %shard_map.85), channel_id=1, source_target_pairs={{0,4},{4,0},{8,12},{12,8},{16,20},{20,16},{24,28},{28,24},{1,5},{5... | collective-permute-start | bytes 196616 | tf_op jit(solution)/shard_map/ppermute | solution.py:22
  6.7 39.6 %collective-permute-start.10 = (f32[2,512,128]{2,1,0:T(8,128)S(1)}, f32[2,512,128]{2,1,0:T(8,128)S(1)}, u32[]{:S(2)}, u32[]{:S(2)}) collective-permute-start(f32[2,512,128]{2,1,0:T(8,128)S(1)} %bitcast.56), channel_id=1, source_target_pairs={{0,2},{1,3},{2,0},{3,1},{4,6},{5,7},{6,4},{7,5},{8,10},{9,11},{10,... | collective-permute-start | bytes 1572872 | tf_op jit(solution)/shard_map/ppermute | solution.py:22
  10.1 13.0 %copy-start.4 = (f32[2,2,3,16,4096]{4,3,2,1,0:T(8,128)S(1)}, f32[2,2,3,16,4096]{4,3,2,1,0:T(8,128)}, u32[]{:S(2)}) copy-start(f32[2,2,3,16,4096]{4,3,2,1,0:T(8,128)} %param.7) | copy-start | bytes 9437188
  11.7 5.3 %collective-permute-start.3 = (f32[128,128]{1,0:T(8,128)S(1)}, f32[128,128]{1,0:T(8,128)S(1)}, u32[]{:S(2)}, u32[]{:S(2)}) collective-permute-start(f32[128,128]{1,0:T(8,128)S(1)} %add.33.refs_0_), channel_id=1, source_target_pairs={{0,16},{4,20},{8,24},{12,28},{16,0},{20,4},{24,8},{28,12},{1,17},{... | collective-permute-start | bytes 196616 | tf_op jit(solution)/shard_map/ppermute | solution.py:587
  14.3 4.3 %collective-permute-start.2 = (f32[128,128]{1,0:T(8,128)S(1)}, f32[128,128]{1,0:T(8,128)S(1)}, u32[]{:S(2)}, u32[]{:S(2)}) collective-permute-start(f32[128,128]{1,0:T(8,128)S(1)} %add.33.refs_0_), channel_id=1, source_target_pairs={{0,24},{4,28},{8,0},{12,4},{16,8},{20,12},{24,16},{28,20},{1,25},{... | collective-permute-start | bytes 196616 | tf_op jit(solution)/shard_map/ppermute | solution.py:587
  15.7 6.1 %collective-permute-start.1 = (f32[128,128]{1,0:T(8,128)S(1)}, f32[128,128]{1,0:T(8,128)S(1)}, u32[]{:S(2)}, u32[]{:S(2)}) collective-permute-start(f32[128,128]{1,0:T(8,128)S(1)} %add.33.refs_0_), channel_id=1, source_target_pairs={{0,8},{4,12},{8,16},{12,20},{16,24},{20,28},{24,0},{28,4},{1,9},{5... | collective-permute-start | bytes 196616 | tf_op jit(solution)/shard_map/ppermute | solution.py:587
  23.3 37.5 %collective-permute-start.18 = (f32[2,512,128]{2,1,0:T(8,128)S(1)}, f32[2,512,128]{2,1,0:T(8,128)S(1)}, u32[]{:S(2)}, u32[]{:S(2)}) collective-permute-start(f32[2,512,128]{2,1,0:T(8,128)S(1)} %bitcast.57), channel_id=1, source_target_pairs={{0,2},{1,3},{2,0},{3,1},{4,6},{5,7},{6,4},{7,5},{8,10},{9,11},{10,... | collective-permute-start | bytes 1572872 | tf_op jit(solution)/shard_map/ppermute | solution.py:22
  23.9 4.0 %collective-permute-start.4 = (f32[80,128]{1,0:T(8,128)S(1)}, f32[80,128]{1,0:T(8,128)S(1)}, u32[]{:S(2)}, u32[]{:S(2)}) collective-permute-start(f32[80,128]{1,0:T(8,128)S(1)} %get-tuple-element.49.refs_0_), channel_id=1, source_target_pairs={{0,4},{4,0},{8,12},{12,8},{16,20},{20,16},{24,28},{28,24},{1,5},{5... | collective-permute-start | bytes 122888 | tf_op jit(solution)/shard_map/ppermute | solution.py:22
  24.4 11.7 %collective-permute-start.6 = (f32[80,128]{1,0:T(8,128)S(1)}, f32[80,128]{1,0:T(8,128)S(1)}, u32[]{:S(2)}, u32[]{:S(2)}) collective-permute-start(f32[80,128]{1,0:T(8,128)S(1)} %get-tuple-element.50), channel_id=1, source_target_pairs={{0,6},{1,7},{2,4},{3,5},{4,2},{5,3},{6,0},{7,1},{8,14},{9,15},{10,... | collective-permute-start | bytes 122888 | tf_op jit(solution)/shard_map/ppermute | solution.py:679
  26.8 9.7 %collective-permute-start.5 = (f32[80,128]{1,0:T(8,128)S(1)}, f32[80,128]{1,0:T(8,128)S(1)}, u32[]{:S(2)}, u32[]{:S(2)}) collective-permute-start(f32[80,128]{1,0:T(8,128)S(1)} %get-tuple-element.50), channel_id=1, source_target_pairs={{0,2},{1,3},{2,0},{3,1},{4,6},{5,7},{6,4},{7,5},{8,10},{9,11},{10,... | collective-permute-start | bytes 122888 | tf_op jit(solution)/shard_map/ppermute | solution.py:22
  36.6 6.5 %collective-permute-start.9 = (f32[128,128]{1,0:T(8,128)S(1)}, f32[128,128]{1,0:T(8,128)S(1)}, u32[]{:S(2)}, u32[]{:S(2)}) collective-permute-start(f32[128,128]{1,0:T(8,128)S(1)} %get-tuple-element.51.refs_0_), channel_id=1, source_target_pairs={{0,16},{4,20},{8,24},{12,28},{16,0},{20,4},{24,8},{28,12},{1,17},{... | collective-permute-start | bytes 196616 | tf_op jit(solution)/shard_map/ppermute | solution.py:587
  39.7 4.8 %collective-permute-start.8 = (f32[128,128]{1,0:T(8,128)S(1)}, f32[128,128]{1,0:T(8,128)S(1)}, u32[]{:S(2)}, u32[]{:S(2)}) collective-permute-start(f32[128,128]{1,0:T(8,128)S(1)} %get-tuple-element.51.refs_0_), channel_id=1, source_target_pairs={{0,24},{4,28},{8,0},{12,4},{16,8},{20,12},{24,16},{28,20},{1,25},{... | collective-permute-start | bytes 196616 | tf_op jit(solution)/shard_map/ppermute | solution.py:587
  40.2 6.1 %collective-permute-start.7 = (f32[128,128]{1,0:T(8,128)S(1)}, f32[128,128]{1,0:T(8,128)S(1)}, u32[]{:S(2)}, u32[]{:S(2)}) collective-permute-start(f32[128,128]{1,0:T(8,128)S(1)} %get-tuple-element.51.refs_0_), channel_id=1, source_target_pairs={{0,8},{4,12},{8,16},{12,20},{16,24},{20,28},{24,0},{28,4},{1,9},{5... | collective-permute-start | bytes 196616 | tf_op jit(solution)/shard_map/ppermute | solution.py:587
  47.6 4.3 %collective-permute-start.11 = (f32[128,128]{1,0:T(8,128)S(1)}, f32[128,128]{1,0:T(8,128)S(1)}, u32[]{:S(2)}, u32[]{:S(2)}) collective-permute-start(f32[128,128]{1,0:T(8,128)S(1)} %get-tuple-element.53), channel_id=1, source_target_pairs={{0,4},{4,0},{8,12},{12,8},{16,20},{20,16},{24,28},{28,24},{1,5},{5... | collective-permute-start | bytes 196616 | tf_op jit(solution)/shard_map/ppermute | solution.py:22
  48.7 5.6 %collective-permute-start.17 = (f32[64,128]{1,0:T(8,128)S(1)}, f32[64,128]{1,0:T(8,128)S(1)}, u32[]{:S(2)}, u32[]{:S(2)}) collective-permute-start(f32[64,128]{1,0:T(8,128)S(1)} %get-tuple-element.54.refs_4_), channel_id=1, source_target_pairs={{0,16},{4,20},{8,24},{12,28},{16,0},{20,4},{24,8},{28,12},{1,17},{... | collective-permute-start | bytes 98312 | tf_op jit(solution)/shard_map/ppermute | solution.py:587
  49.0 5.9 %collective-permute-start.16 = (f32[64,128]{1,0:T(8,128)S(1)}, f32[64,128]{1,0:T(8,128)S(1)}, u32[]{:S(2)}, u32[]{:S(2)}) collective-permute-start(f32[64,128]{1,0:T(8,128)S(1)} %get-tuple-element.54.refs_4_), channel_id=1, source_target_pairs={{0,24},{4,28},{8,0},{12,4},{16,8},{20,12},{24,16},{28,20},{1,25},{... | collective-permute-start | bytes 98312 | tf_op jit(solution)/shard_map/ppermute | solution.py:587
  52.0 8.8 %collective-permute-start.14 = (f32[128,128]{1,0:T(8,128)S(1)}, f32[128,128]{1,0:T(8,128)S(1)}, u32[]{:S(2)}, u32[]{:S(2)}) collective-permute-start(f32[128,128]{1,0:T(8,128)S(1)} %add.36.refs_0_), channel_id=1, source_target_pairs={{0,16},{4,20},{8,24},{12,28},{16,0},{20,4},{24,8},{28,12},{1,17},{... | collective-permute-start | bytes 196616 | tf_op jit(solution)/shard_map/ppermute | solution.py:587
  52.8 8.0 %collective-permute-start.13 = (f32[128,128]{1,0:T(8,128)S(1)}, f32[128,128]{1,0:T(8,128)S(1)}, u32[]{:S(2)}, u32[]{:S(2)}) collective-permute-start(f32[128,128]{1,0:T(8,128)S(1)} %add.36.refs_0_), channel_id=1, source_target_pairs={{0,24},{4,28},{8,0},{12,4},{16,8},{20,12},{24,16},{28,20},{1,25},{... | collective-permute-start | bytes 196616 | tf_op jit(solution)/shard_map/ppermute | solution.py:587
  54.4 6.4 %collective-permute-start.12 = (f32[128,128]{1,0:T(8,128)S(1)}, f32[128,128]{1,0:T(8,128)S(1)}, u32[]{:S(2)}, u32[]{:S(2)}) collective-permute-start(f32[128,128]{1,0:T(8,128)S(1)} %add.36.refs_0_), channel_id=1, source_target_pairs={{0,8},{4,12},{8,16},{12,20},{16,24},{20,28},{24,0},{28,4},{1,9},{5... | collective-permute-start | bytes 196616 | tf_op jit(solution)/shard_map/ppermute | solution.py:587
  54.9 5.9 %collective-permute-start.15 = (f32[64,128]{1,0:T(8,128)S(1)}, f32[64,128]{1,0:T(8,128)S(1)}, u32[]{:S(2)}, u32[]{:S(2)}) collective-permute-start(f32[64,128]{1,0:T(8,128)S(1)} %get-tuple-element.54.refs_4_), channel_id=1, source_target_pairs={{0,8},{4,12},{8,16},{12,20},{16,24},{20,28},{24,0},{28,4},{1,9},{5... | collective-permute-start | bytes 98312 | tf_op jit(solution)/shard_map/ppermute | solution.py:587
  62.5 1.2 collective-permute-start.19
  63.8 3.9 %collective-permute-start.20 = (f32[64,128]{1,0:T(8,128)S(1)}, f32[64,128]{1,0:T(8,128)S(1)}, u32[]{:S(2)}, u32[]{:S(2)}) collective-permute-start(f32[64,128]{1,0:T(8,128)S(1)} %add.37), channel_id=1, source_target_pairs={{0,4},{4,0},{8,12},{12,8},{16,20},{20,16},{24,28},{28,24},{1,5},{5... | collective-permute-start | bytes 98312 | tf_op jit(solution)/shard_map/ppermute | solution.py:22
  67.7 5.2 %collective-permute-start.23 = (f32[64,128]{1,0:T(8,128)S(1)}, f32[64,128]{1,0:T(8,128)S(1)}, u32[]{:S(2)}, u32[]{:S(2)}) collective-permute-start(f32[64,128]{1,0:T(8,128)S(1)} %add.38.refs_0_), channel_id=1, source_target_pairs={{0,16},{4,20},{8,24},{12,28},{16,0},{20,4},{24,8},{28,12},{1,17},{... | collective-permute-start | bytes 98312 | tf_op jit(solution)/shard_map/ppermute | solution.py:587
  67.8 5.0 %collective-permute-start.22 = (f32[64,128]{1,0:T(8,128)S(1)}, f32[64,128]{1,0:T(8,128)S(1)}, u32[]{:S(2)}, u32[]{:S(2)}) collective-permute-start(f32[64,128]{1,0:T(8,128)S(1)} %add.38.refs_0_), channel_id=1, source_target_pairs={{0,24},{4,28},{8,0},{12,4},{16,8},{20,12},{24,16},{28,20},{1,25},{... | collective-permute-start | bytes 98312 | tf_op jit(solution)/shard_map/ppermute | solution.py:587
  69.1 5.7 %collective-permute-start.21 = (f32[64,128]{1,0:T(8,128)S(1)}, f32[64,128]{1,0:T(8,128)S(1)}, u32[]{:S(2)}, u32[]{:S(2)}) collective-permute-start(f32[64,128]{1,0:T(8,128)S(1)} %add.38.refs_0_), channel_id=1, source_target_pairs={{0,8},{4,12},{8,16},{12,20},{16,24},{20,28},{24,0},{28,4},{1,9},{5... | collective-permute-start | bytes 98312 | tf_op jit(solution)/shard_map/ppermute | solution.py:587
  77.4 1.6 %collective-permute-start.24 = (f32[512,128]{1,0:T(8,128)S(1)}, f32[512,128]{1,0:T(8,128)S(1)}, u32[]{:S(2)}, u32[]{:S(2)}) collective-permute-start(f32[512,128]{1,0:T(8,128)S(1)} %get-tuple-element.58.mine), channel_id=1, source_target_pairs={{0,1},{1,0},{2,3},{3,2},{4,5},{5,4},{6,7},{7,6},{8,9},{9,8},{10,11... | collective-permute-start | bytes 786440 | tf_op jit(solution)/shard_map/ppermute | solution.py:22
  80.1 4.5 %collective-permute-start.25 = (f32[160,128]{1,0:T(8,128)S(1)}, f32[160,128]{1,0:T(8,128)S(1)}, u32[]{:S(2)}, u32[]{:S(2)}) collective-permute-start(f32[160,128]{1,0:T(8,128)S(1)} %get-tuple-element.60), channel_id=1, source_target_pairs={{0,4},{4,0},{8,12},{12,8},{16,20},{20,16},{24,28},{28,24},{1,5},{5... | collective-permute-start | bytes 245768 | tf_op jit(solution)/shard_map/ppermute | solution.py:22
  81.3 29.2 %collective-permute-start.35 = (f32[2,512,128]{2,1,0:T(8,128)S(1)}, f32[2,512,128]{2,1,0:T(8,128)S(1)}, u32[]{:S(2)}, u32[]{:S(2)}) collective-permute-start(f32[2,512,128]{2,1,0:T(8,128)S(1)} %bitcast.50), channel_id=1, source_target_pairs={{0,2},{1,3},{2,0},{3,1},{4,6},{5,7},{6,4},{7,5},{8,10},{9,11},{10,... | collective-permute-start | bytes 1572872 | tf_op jit(solution)/shard_map/ppermute | solution.py:22
  84.7 8.0 %collective-permute-start.28 = (f32[160,128]{1,0:T(8,128)S(1)}, f32[160,128]{1,0:T(8,128)S(1)}, u32[]{:S(2)}, u32[]{:S(2)}) collective-permute-start(f32[160,128]{1,0:T(8,128)S(1)} %add.39.refs_0_), channel_id=1, source_target_pairs={{0,16},{4,20},{8,24},{12,28},{16,0},{20,4},{24,8},{28,12},{1,17},{... | collective-permute-start | bytes 245768 | tf_op jit(solution)/shard_map/ppermute | solution.py:587
  84.9 7.8 %collective-permute-start.27 = (f32[160,128]{1,0:T(8,128)S(1)}, f32[160,128]{1,0:T(8,128)S(1)}, u32[]{:S(2)}, u32[]{:S(2)}) collective-permute-start(f32[160,128]{1,0:T(8,128)S(1)} %add.39.refs_0_), channel_id=1, source_target_pairs={{0,24},{4,28},{8,0},{12,4},{16,8},{20,12},{24,16},{28,20},{1,25},{... | collective-permute-start | bytes 245768 | tf_op jit(solution)/shard_map/ppermute | solution.py:587
  86.1 6.6 %collective-permute-start.26 = (f32[160,128]{1,0:T(8,128)S(1)}, f32[160,128]{1,0:T(8,128)S(1)}, u32[]{:S(2)}, u32[]{:S(2)}) collective-permute-start(f32[160,128]{1,0:T(8,128)S(1)} %add.39.refs_0_), channel_id=1, source_target_pairs={{0,8},{4,12},{8,16},{12,20},{16,24},{20,28},{24,0},{28,4},{1,9},{5... | collective-permute-start | bytes 245768 | tf_op jit(solution)/shard_map/ppermute | solution.py:587
  95.0 1.6 %collective-permute-start.29 = (f32[512,128]{1,0:T(8,128)S(1)}, f32[512,128]{1,0:T(8,128)S(1)}, u32[]{:S(2)}, u32[]{:S(2)}) collective-permute-start(f32[512,128]{1,0:T(8,128)S(1)} %get-tuple-element.63.mine), channel_id=1, source_target_pairs={{0,1},{1,0},{2,3},{3,2},{4,5},{5,4},{6,7},{7,6},{8,9},{9,8},{10,11... | collective-permute-start | bytes 786440 | tf_op jit(solution)/shard_map/ppermute | solution.py:22
  97.7 4.5 %collective-permute-start.30 = (f32[160,128]{1,0:T(8,128)S(1)}, f32[160,128]{1,0:T(8,128)S(1)}, u32[]{:S(2)}, u32[]{:S(2)}) collective-permute-start(f32[160,128]{1,0:T(8,128)S(1)} %get-tuple-element.65), channel_id=1, source_target_pairs={{0,4},{4,0},{8,12},{12,8},{16,20},{20,16},{24,28},{28,24},{1,5},{5... | collective-permute-start | bytes 245768 | tf_op jit(solution)/shard_map/ppermute | solution.py:22
  102.3 8.8 %collective-permute-start.33 = (f32[160,128]{1,0:T(8,128)S(1)}, f32[160,128]{1,0:T(8,128)S(1)}, u32[]{:S(2)}, u32[]{:S(2)}) collective-permute-start(f32[160,128]{1,0:T(8,128)S(1)} %add.40.refs_0_), channel_id=1, source_target_pairs={{0,16},{4,20},{8,24},{12,28},{16,0},{20,4},{24,8},{28,12},{1,17},{... | collective-permute-start | bytes 245768 | tf_op jit(solution)/shard_map/ppermute | solution.py:587
  104.5 6.6 %collective-permute-start.32 = (f32[160,128]{1,0:T(8,128)S(1)}, f32[160,128]{1,0:T(8,128)S(1)}, u32[]{:S(2)}, u32[]{:S(2)}) collective-permute-start(f32[160,128]{1,0:T(8,128)S(1)} %add.40.refs_0_), channel_id=1, source_target_pairs={{0,24},{4,28},{8,0},{12,4},{16,8},{20,12},{24,16},{28,20},{1,25},{... | collective-permute-start | bytes 245768 | tf_op jit(solution)/shard_map/ppermute | solution.py:587
  106.2 6.2 %collective-permute-start.31 = (f32[160,128]{1,0:T(8,128)S(1)}, f32[160,128]{1,0:T(8,128)S(1)}, u32[]{:S(2)}, u32[]{:S(2)}) collective-permute-start(f32[160,128]{1,0:T(8,128)S(1)} %add.40.refs_0_), channel_id=1, source_target_pairs={{0,8},{4,12},{8,16},{12,20},{16,24},{20,28},{24,0},{28,4},{1,9},{5... | collective-permute-start | bytes 245768 | tf_op jit(solution)/shard_map/ppermute | solution.py:587
  106.5 4.0 %collective-permute-start.34 = (f32[80,128]{1,0:T(8,128)S(1)}, f32[80,128]{1,0:T(8,128)S(1)}, u32[]{:S(2)}, u32[]{:S(2)}) collective-permute-start(f32[80,128]{1,0:T(8,128)S(1)} %get-tuple-element.66), channel_id=1, source_target_pairs={{0,2},{1,3},{2,0},{3,1},{4,6},{5,7},{6,4},{7,5},{8,10},{9,11},{10,... | collective-permute-start | bytes 122888 | tf_op jit(solution)/shard_map/ppermute | solution.py:22
  114.7 1.6 %collective-permute-start.36 = (f32[512,128]{1,0:T(8,128)S(1)}, f32[512,128]{1,0:T(8,128)S(1)}, u32[]{:S(2)}, u32[]{:S(2)}) collective-permute-start(f32[512,128]{1,0:T(8,128)S(1)} %get-tuple-element.71.mine), channel_id=1, source_target_pairs={{0,1},{1,0},{2,3},{3,2},{4,5},{5,4},{6,7},{7,6},{8,9},{9,8},{10,11... | collective-permute-start | bytes 786440 | tf_op jit(solution)/shard_map/ppermute | solution.py:22
  115.1 22.9 %collective-permute-start.46 = (f32[512,128]{1,0:T(8,128)S(1)}, f32[512,128]{1,0:T(8,128)S(1)}, u32[]{:S(2)}, u32[]{:S(2)}) collective-permute-start(f32[512,128]{1,0:T(8,128)S(1)} %shard_map.99.mine), channel_id=1, source_target_pairs={{0,2},{1,3},{2,0},{3,1},{4,6},{5,7},{6,4},{7,5},{8,10},{9,11},{10,... | collective-permute-start | bytes 786440 | tf_op jit(solution)/shard_map/ppermute | solution.py:22
  117.4 4.5 %collective-permute-start.37 = (f32[160,128]{1,0:T(8,128)S(1)}, f32[160,128]{1,0:T(8,128)S(1)}, u32[]{:S(2)}, u32[]{:S(2)}) collective-permute-start(f32[160,128]{1,0:T(8,128)S(1)} %get-tuple-element.73), channel_id=1, source_target_pairs={{0,4},{4,0},{8,12},{12,8},{16,20},{20,16},{24,28},{28,24},{1,5},{5... | collective-permute-start | bytes 245768 | tf_op jit(solution)/shard_map/ppermute | solution.py:22
  119.0 20.8 %collective-permute-start.45 = (f32[512,128]{1,0:T(8,128)S(1)}, f32[512,128]{1,0:T(8,128)S(1)}, u32[]{:S(2)}, u32[]{:S(2)}) collective-permute-start(f32[512,128]{1,0:T(8,128)S(1)} %shard_map.98.mine), channel_id=1, source_target_pairs={{0,2},{1,3},{2,0},{3,1},{4,6},{5,7},{6,4},{7,5},{8,10},{9,11},{10,... | collective-permute-start | bytes 786440 | tf_op jit(solution)/shard_map/ppermute | solution.py:22
  119.9 21.7 %collective-permute-start.44 = (f32[512,128]{1,0:T(8,128)S(1)}, f32[512,128]{1,0:T(8,128)S(1)}, u32[]{:S(2)}, u32[]{:S(2)}) collective-permute-start(f32[512,128]{1,0:T(8,128)S(1)} %get-tuple-element.75.mixture), channel_id=1, source_target_pairs={{0,2},{1,3},{2,0},{3,1},{4,6},{5,7},{6,4},{7,5},{8,10},{9,11},{10,... | collective-permute-start | bytes 786440 | tf_op jit(solution)/shard_map/ppermute | solution.py:22
  122.0 6.7 %collective-permute-start.40 = (f32[160,128]{1,0:T(8,128)S(1)}, f32[160,128]{1,0:T(8,128)S(1)}, u32[]{:S(2)}, u32[]{:S(2)}) collective-permute-start(f32[160,128]{1,0:T(8,128)S(1)} %add.41.refs_0_), channel_id=1, source_target_pairs={{0,16},{4,20},{8,24},{12,28},{16,0},{20,4},{24,8},{28,12},{1,17},{... | collective-permute-start | bytes 245768 | tf_op jit(solution)/shard_map/ppermute | solution.py:587
  123.0 6.1 %collective-permute-start.39 = (f32[160,128]{1,0:T(8,128)S(1)}, f32[160,128]{1,0:T(8,128)S(1)}, u32[]{:S(2)}, u32[]{:S(2)}) collective-permute-start(f32[160,128]{1,0:T(8,128)S(1)} %add.41.refs_0_), channel_id=1, source_target_pairs={{0,24},{4,28},{8,0},{12,4},{16,8},{20,12},{24,16},{28,20},{1,25},{... | collective-permute-start | bytes 245768 | tf_op jit(solution)/shard_map/ppermute | solution.py:587
  128.7 6.2 %collective-permute-start.38 = (f32[160,128]{1,0:T(8,128)S(1)}, f32[160,128]{1,0:T(8,128)S(1)}, u32[]{:S(2)}, u32[]{:S(2)}) collective-permute-start(f32[160,128]{1,0:T(8,128)S(1)} %add.41.refs_0_), channel_id=1, source_target_pairs={{0,8},{4,12},{8,16},{12,20},{16,24},{20,28},{24,0},{28,4},{1,9},{5... | collective-permute-start | bytes 245768 | tf_op jit(solution)/shard_map/ppermute | solution.py:587
  137.0 4.6 %collective-permute-start.43 = (f32[80,128]{1,0:T(8,128)S(1)}, f32[80,128]{1,0:T(8,128)S(1)}, u32[]{:S(2)}, u32[]{:S(2)}) collective-permute-start(f32[80,128]{1,0:T(8,128)S(1)} %shard_map.97.mine), channel_id=1, source_target_pairs={{0,3},{1,2},{2,1},{3,0},{4,7},{5,6},{6,5},{7,4},{8,11},{9,10},{10,... | collective-permute-start | bytes 122888 | tf_op jit(solution)/shard_map/ppermute | solution.py:22
  137.0 4.6 %collective-permute-start.42 = (f32[80,128]{1,0:T(8,128)S(1)}, f32[80,128]{1,0:T(8,128)S(1)}, u32[]{:S(2)}, u32[]{:S(2)}) collective-permute-start(f32[80,128]{1,0:T(8,128)S(1)} %shard_map.97.mine), channel_id=1, source_target_pairs={{0,2},{1,3},{2,0},{3,1},{4,6},{5,7},{6,4},{7,5},{8,10},{9,11},{10,... | collective-permute-start | bytes 122888 | tf_op jit(solution)/shard_map/ppermute | solution.py:22
  138.0 3.6 %collective-permute-start.41 = (f32[80,128]{1,0:T(8,128)S(1)}, f32[80,128]{1,0:T(8,128)S(1)}, u32[]{:S(2)}, u32[]{:S(2)}) collective-permute-start(f32[80,128]{1,0:T(8,128)S(1)} %shard_map.97.mine), channel_id=1, source_target_pairs={{0,1},{1,0},{2,3},{3,2},{4,5},{5,4},{6,7},{7,6},{8,9},{9,8},{10,11... | collective-permute-start | bytes 122888 | tf_op jit(solution)/shard_map/ppermute | solution.py:22

commit v7 on v6

--- a/solution.py
+++ b/solution.py
@@ -287,14 +287,14 @@
         low[i] = jnp.concatenate([own_low[i][:height], value[1]], axis=0)
 
 
-SHIFTS = (1, 3, 2)
-
-
-def slice_blocks(spot, n_inner, n_outer):
+OTHERS = (1, 3, 2)
+
+
+def slice_blocks(spot, n_inner):
     inner, outer = spot % n_inner, spot // n_inner
     return [
-        (outer + n_outer - by) % n_outer * n_inner + (inner ^ step)
-        for by in (0,) + SHIFTS
+        (outer ^ by) * n_inner + (inner ^ step)
+        for by in (0,) + OTHERS
         for step in range(n_inner)
     ]
 
@@ -312,7 +312,7 @@
     value = dot3(split(heads_of(heads, 0)), split(natural[:LANES]))
     value = value + dot3(split(heads_of(heads, 1)), split(natural[LANES:]))
     shared = rest[2]
-    blocks = slice_blocks(spot[0], LANES // slices // n_parts, n_parts)
+    blocks = slice_blocks(spot[0], LANES // slices // n_parts)
     for at, block in enumerate(blocks):
         shared[block_rows(block, slices), :] = value[at * slices : (at + 1) * slices]
     value = shared[pl.ds(0, LANES), :]
@@ -395,9 +395,9 @@
     zero = jnp.zeros_like(packed)
     square[...] = jnp.concatenate([pick(packed, zero), pick(swap(packed), zero)], axis=0)
     slices = basis.shape[0]
-    blocks = slice_blocks(spot[0], LANES // slices // n_parts, n_parts)
+    blocks = slice_blocks(spot[0], LANES // slices // n_parts)
     mixture = jnp.concatenate([square[block_rows(block, slices), :] for block in blocks], axis=0)
-    gram = exact(mixture, mixture, TN)[:HALF]
+    gram = dot3(split(mixture), split(mixture), TN)[:HALF]
     raw = []
     for pair in range(2):
         value = dot3(split(heads_of(heads, pair)), split(mixture), TN)
@@ -579,11 +579,8 @@
         return [value, flip(value, axis, stride)]
     size = lax.axis_size(axis)
     parts = [value]
-    for by in SHIFTS:
-        pairs = [
-            (index, index + ((index // stride + by) % 4 - index // stride % 4) * stride)
-            for index in range(size)
-        ]
+    for by in OTHERS:
+        pairs = [(index, index ^ (by * stride)) for index in range(size)]
         parts.append(lax.ppermute(value, axis, pairs))
     return parts
 

time: 144 us -> 143 us (level)
  waiting for transfers between devices: 65.6 us -> 63.1 us
  starting transfers between devices: 47.5 us -> 49.4 us
    ppermute x24, waiting for transfers between devices: 37.2 us -> 33.9 us  [spread(): parts.append(lax.ppermute(value, axis, pairs))]
    ppermute x24, starting transfers between devices: 27.1 us -> 29.4 us  [spread(): parts.append(lax.ppermute(value, axis, pairs))]
  transfers between devices with their start and end apart: 47 -> 47, of which waited for: 27 -> 28; matrix products, arithmetic and copies ran while one was open for 3% -> 3% of each run, Pallas kernels for 9% -> 9%
where the time goes in v7:
time: 143 us
  waiting for transfers between devices  63.1 us (44%)
  starting transfers between devices  49.4 us (35%)
  Pallas kernels  23.4 us (16%)
  local copies, waits for them, and re-layouts  5.3 us (4%)
    ppermute x24, waiting for transfers between devices, spread(): parts.append(lax.ppermute(value, axis, pairs))  33.9 us
    ppermute x24, starting transfers between devices, spread(): parts.append(lax.ppermute(value, axis, pairs))  29.4 us
    pallas_call x19, Pallas kernels, kernel_call(): pl.pallas_call(body, out_shape=outs, in_specs=specs[:len(operands)], out_...  23.4 us
    ppermute x22, waiting for transfers between devices, flip(): lax.ppermute(value, axis, [(index, index ^ bits) for index in range(size)])  20.7 us
    ppermute x22, starting transfers between devices, flip(): lax.ppermute(value, axis, [(index, index ^ bits) for index in range(size)])  17.6 us
    ppermute x1, waiting for transfers between devices, tiled(): sends.append(lax.ppermute(send, ('mode', 'rep'), pairs))  8.46 us
  transfers between devices with their start and end apart: 47, of which 28 were waited for; matrix products, arithmetic and copies ran while one was open for 3% of the time, Pallas kernels for 9%

profile of v7, /device:TPU:0, one launch (start us, length us, event | category | flops | bytes accessed | tf_op | source)
XLA Modules:
  0.0 143.2 jit_solution(6008678558050419193)
XLA Ops:
  2.5 3.0 %collective-permute-start = (f32[128,128]{1,0:T(8,128)S(1)}, f32[128,128]{1,0:T(8,128)S(1)}, u32[]{:S(2)}, u32[]{:S(2)}) collective-permute-start(f32[128,128]{1,0:T(8,128)S(1)} %shard_map.85), channel_id=1, source_target_pairs={{0,4},{4,0},{8,12},{12,8},{16,20},{20,16},{24,28},{28,24},{1,5},{5... | collective-permute-start | bytes 196616 | tf_op jit(solution)/shard_map/ppermute | solution.py:22
  5.6 1.1 constant_dynamic-slice_fusion.2
  6.7 1.6 %collective-permute-start.10 = (f32[2,512,128]{2,1,0:T(8,128)S(1)}, f32[2,512,128]{2,1,0:T(8,128)S(1)}, u32[]{:S(2)}, u32[]{:S(2)}) collective-permute-start(f32[2,512,128]{2,1,0:T(8,128)S(1)} %bitcast.56), channel_id=1, source_target_pairs={{0,2},{1,3},{2,0},{3,1},{4,6},{5,7},{6,4},{7,5},{8,10},{9,11},{10,... | collective-permute-start | bytes 1572872 | tf_op jit(solution)/shard_map/ppermute | solution.py:22
  8.9 1.2 fusion
  10.1 1.4 constant_dynamic-slice_fusion.4
  11.7 2.7 %collective-permute-start.3 = (f32[128,128]{1,0:T(8,128)S(1)}, f32[128,128]{1,0:T(8,128)S(1)}, u32[]{:S(2)}, u32[]{:S(2)}) collective-permute-start(f32[128,128]{1,0:T(8,128)S(1)} %add.33.refs_0_), channel_id=1, source_target_pairs={{0,16},{4,20},{8,24},{12,28},{16,0},{20,4},{24,8},{28,12},{1,17},{... | collective-permute-start | bytes 196616 | tf_op jit(solution)/shard_map/ppermute | solution.py:584
  14.3 1.3 collective-permute-start.2
  15.9 1.0 collective-permute-done.3.refs_3_
  16.9 3.6 %collective-permute-done.2.refs_2_ = f32[128,128]{1,0:T(8,128)S(1)} collective-permute-done((f32[128,128]{1,0:T(8,128)S(1)}, f32[128,128]{1,0:T(8,128)S(1)}, u32[]{:S(2)}, u32[]{:S(2)}) %collective-permute-start.2) | collective-permute-done | bytes 65568 | tf_op jit(solution)/shard_map/ppermute | solution.py:584
  20.6 1.4 shard_map.86
  23.3 2.5 %collective-permute-start.6 = (f32[80,128]{1,0:T(8,128)S(1)}, f32[80,128]{1,0:T(8,128)S(1)}, u32[]{:S(2)}, u32[]{:S(2)}) collective-permute-start(f32[80,128]{1,0:T(8,128)S(1)} %get-tuple-element.50), channel_id=1, source_target_pairs={{0,6},{1,7},{2,4},{3,5},{4,2},{5,3},{6,0},{7,1},{8,14},{9,15},{10,... | collective-permute-start | bytes 122888 | tf_op jit(solution)/shard_map/ppermute | solution.py:676
  26.8 8.5 %collective-permute-done.6.refs_3_ = f32[80,128]{1,0:T(8,128)S(1)} collective-permute-done((f32[80,128]{1,0:T(8,128)S(1)}, f32[80,128]{1,0:T(8,128)S(1)}, u32[]{:S(2)}, u32[]{:S(2)}) %collective-permute-start.6) | collective-permute-done | bytes 40992 | tf_op jit(solution)/shard_map/ppermute | solution.py:676
  35.8 4.0 %collective-permute-start.9 = (f32[128,128]{1,0:T(8,128)S(1)}, f32[128,128]{1,0:T(8,128)S(1)}, u32[]{:S(2)}, u32[]{:S(2)}) collective-permute-start(f32[128,128]{1,0:T(8,128)S(1)} %get-tuple-element.51.refs_0_), channel_id=1, source_target_pairs={{0,16},{4,20},{8,24},{12,28},{16,0},{20,4},{24,8},{28,12},{1,17},{... | collective-permute-start | bytes 196616 | tf_op jit(solution)/shard_map/ppermute | solution.py:584
  40.4 3.3 %collective-permute-done.9.refs_3_ = f32[128,128]{1,0:T(8,128)S(1)} collective-permute-done((f32[128,128]{1,0:T(8,128)S(1)}, f32[128,128]{1,0:T(8,128)S(1)}, u32[]{:S(2)}, u32[]{:S(2)}) %collective-permute-start.9) | collective-permute-done | bytes 65568 | tf_op jit(solution)/shard_map/ppermute | solution.py:584
  43.6 2.1 %collective-permute-done.8.refs_2_ = f32[128,128]{1,0:T(8,128)S(1)} collective-permute-done((f32[128,128]{1,0:T(8,128)S(1)}, f32[128,128]{1,0:T(8,128)S(1)}, u32[]{:S(2)}, u32[]{:S(2)}) %collective-permute-start.8) | collective-permute-done | bytes 65568 | tf_op jit(solution)/shard_map/ppermute | solution.py:584
  45.8 1.4 shard_map.88
  47.2 1.1 collective-permute-start.11
  48.3 1.3 collective-permute-start.17
  50.3 1.2 collective-permute-done.11
  51.5 1.3 collective-permute-start.14
  52.9 1.4 collective-permute-start.13
  54.2 0.9 collective-permute-start.12
  56.2 3.3 %collective-permute-done.15.refs_5_ = f32[64,128]{1,0:T(8,128)S(1)} collective-permute-done((f32[64,128]{1,0:T(8,128)S(1)}, f32[64,128]{1,0:T(8,128)S(1)}, u32[]{:S(2)}, u32[]{:S(2)}) %collective-permute-start.15) | collective-permute-done | bytes 32800 | tf_op jit(solution)/shard_map/ppermute | solution.py:584
  59.6 1.7 %shard_map.89 = (f32[64,128]{1,0:T(8,128)S(1)}, bf16[16,128,128]{2,1,0:T(8,128)(2,1)S(1)}, bf16[16,128,128]{2,1,0:T(8,128)(2,1)S(1)}) custom-call(f32[128,128]{1,0:T(8,128)S(1)} %add.36.refs_0_, f32[128,128]{1,0:T(8,128)S(1)} %collective-permute-done.12.refs_1_, f32[128,128]{1,0:T(8,128)S(1)} %collective-permute-done.13.refs_2_, ...), custom_call_target="tpu_custom_call" | custom-call | bytes 2786308 | tf_op jit(solution)/shard_map/pallas_call | solution.py:542
  61.3 1.2 collective-permute-done.19
  62.5 1.0 collective-permute-start.20
  63.5 2.9 %collective-permute-done.20 = f32[64,128]{1,0:T(8,128)S(1)} collective-permute-done((f32[64,128]{1,0:T(8,128)S(1)}, f32[64,128]{1,0:T(8,128)S(1)}, u32[]{:S(2)}, u32[]{:S(2)}) %collective-permute-start.20) | collective-permute-done | bytes 32800 | tf_op jit(solution)/shard_map/ppermute | solution.py:22
  66.4 1.9 %collective-permute-start.23 = (f32[64,128]{1,0:T(8,128)S(1)}, f32[64,128]{1,0:T(8,128)S(1)}, u32[]{:S(2)}, u32[]{:S(2)}) collective-permute-start(f32[64,128]{1,0:T(8,128)S(1)} %add.38.refs_0_), channel_id=1, source_target_pairs={{0,16},{4,20},{8,24},{12,28},{16,0},{20,4},{24,8},{28,12},{1,17},{... | collective-permute-start | bytes 98312 | tf_op jit(solution)/shard_map/ppermute | solution.py:584
  68.3 1.1 collective-permute-start.22
  69.9 2.0 %collective-permute-done.23.refs_3_ = f32[64,128]{1,0:T(8,128)S(1)} collective-permute-done((f32[64,128]{1,0:T(8,128)S(1)}, f32[64,128]{1,0:T(8,128)S(1)}, u32[]{:S(2)}, u32[]{:S(2)}) %collective-permute-start.23) | collective-permute-done | bytes 32800 | tf_op jit(solution)/shard_map/ppermute | solution.py:584
  72.0 2.1 %collective-permute-done.22.refs_2_ = f32[64,128]{1,0:T(8,128)S(1)} collective-permute-done((f32[64,128]{1,0:T(8,128)S(1)}, f32[64,128]{1,0:T(8,128)S(1)}, u32[]{:S(2)}, u32[]{:S(2)}) %collective-permute-start.22) | collective-permute-done | bytes 32800 | tf_op jit(solution)/shard_map/ppermute | solution.py:584
  74.1 3.0 %shard_map.90 = (f32[64,128]{1,0:T(8,128)}, f32[128,128]{1,0:T(8,128)S(1)}, f32[16,128]{1,0:T(8,128)S(1)}, f32[512,128]{1,0:T(8,128)S(1)}) custom-call(f32[64,128]{1,0:T(8,128)S(1)} %add.38.refs_0_, f32[64,128]{1,0:T(8,128)S(1)} %collective-permute-done.21.refs_1_, f32[64,128]{1,0:T(8,128)S(1)} %collective-permute-done.22.refs_2_, ...), custom_call_target="tpu_custom_call" | custom-call | bytes 1679876 | tf_op jit(solution)/shard_map/pallas_call | solution.py:542
  77.1 1.5 %collective-permute-done.24.theirs = f32[512,128]{1,0:T(8,128)S(1)} collective-permute-done((f32[512,128]{1,0:T(8,128)S(1)}, f32[512,128]{1,0:T(8,128)S(1)}, u32[]{:S(2)}, u32[]{:S(2)}) %collective-permute-start.24) | collective-permute-done | bytes 262176 | tf_op jit(solution)/shard_map/ppermute | solution.py:22
  78.6 1.1 shard_map.91
  79.7 1.2 collective-permute-start.25
  81.4 2.8 %collective-permute-done.25 = f32[160,128]{1,0:T(8,128)S(1)} collective-permute-done((f32[160,128]{1,0:T(8,128)S(1)}, f32[160,128]{1,0:T(8,128)S(1)}, u32[]{:S(2)}, u32[]{:S(2)}) %collective-permute-start.25) | collective-permute-done | bytes 81952 | tf_op jit(solution)/shard_map/ppermute | solution.py:22
  84.2 1.0 collective-permute-start.28
  85.2 1.2 collective-permute-start.27
  86.5 1.3 collective-permute-start.26
  87.8 4.7 %collective-permute-done.28.refs_3_ = f32[160,128]{1,0:T(8,128)S(1)} collective-permute-done((f32[160,128]{1,0:T(8,128)S(1)}, f32[160,128]{1,0:T(8,128)S(1)}, u32[]{:S(2)}, u32[]{:S(2)}) %collective-permute-start.28) | collective-permute-done | bytes 81952 | tf_op jit(solution)/shard_map/ppermute | solution.py:584
  92.6 2.3 %shard_map.92 = (f32[64,128]{1,0:T(8,128)S(1)}, f32[128,128]{1,0:T(8,128)S(1)}, f32[512,128]{1,0:T(8,128)S(1)}) custom-call(f32[160,128]{1,0:T(8,128)S(1)} %add.39.refs_0_, f32[160,128]{1,0:T(8,128)S(1)} %collective-permute-done.26.refs_1_, f32[160,128]{1,0:T(8,128)S(1)} %collective-permute-done.27.refs_2_, f32[160,128]{1,0:T(8,128)S(1)} %collective-permute-done.28.refs_3_, ...), custom_call_target="tpu_custom_call" | custom-call | bytes 1737216 | tf_op jit(solution)/shard_map/pallas_call | solution.py:542
  95.0 1.5 %collective-permute-done.29.theirs = f32[512,128]{1,0:T(8,128)S(1)} collective-permute-done((f32[512,128]{1,0:T(8,128)S(1)}, f32[512,128]{1,0:T(8,128)S(1)}, u32[]{:S(2)}, u32[]{:S(2)}) %collective-permute-start.29) | collective-permute-done | bytes 262176 | tf_op jit(solution)/shard_map/ppermute | solution.py:22
  96.5 1.1 shard_map.93
  97.6 1.1 collective-permute-start.30
  98.8 3.4 %collective-permute-done.30 = f32[160,128]{1,0:T(8,128)S(1)} collective-permute-done((f32[160,128]{1,0:T(8,128)S(1)}, f32[160,128]{1,0:T(8,128)S(1)}, u32[]{:S(2)}, u32[]{:S(2)}) %collective-permute-start.30) | collective-permute-done | bytes 81952 | tf_op jit(solution)/shard_map/ppermute | solution.py:22
  102.2 2.5 %collective-permute-start.33 = (f32[160,128]{1,0:T(8,128)S(1)}, f32[160,128]{1,0:T(8,128)S(1)}, u32[]{:S(2)}, u32[]{:S(2)}) collective-permute-start(f32[160,128]{1,0:T(8,128)S(1)} %add.40.refs_0_), channel_id=1, source_target_pairs={{0,16},{4,20},{8,24},{12,28},{16,0},{20,4},{24,8},{28,12},{1,17},{... | collective-permute-start | bytes 245768 | tf_op jit(solution)/shard_map/ppermute | solution.py:584
  104.6 1.4 collective-permute-start.32
  106.6 3.5 %collective-permute-done.34.relay.refs_7_ = f32[80,128]{1,0:T(8,128)S(1)} collective-permute-done((f32[80,128]{1,0:T(8,128)S(1)}, f32[80,128]{1,0:T(8,128)S(1)}, u32[]{:S(2)}, u32[]{:S(2)}) %collective-permute-start.34) | collective-permute-done | bytes 40992 | tf_op jit(solution)/shard_map/ppermute | solution.py:22
  111.7 2.3 %shard_map.95 = (f32[64,128]{1,0:T(8,128)S(1)}, f32[128,128]{1,0:T(8,128)S(1)}, f32[512,128]{1,0:T(8,128)S(1)}) custom-call(f32[160,128]{1,0:T(8,128)S(1)} %add.40.refs_0_, f32[160,128]{1,0:T(8,128)S(1)} %collective-permute-done.31.refs_1_, f32[160,128]{1,0:T(8,128)S(1)} %collective-permute-done.32.refs_2_, f32[160,128]{1,0:T(8,128)S(1)} %collective-permute-done.33.refs_3_, ...), custom_call_target="tpu_custom_call" | custom-call | bytes 1737216 | tf_op jit(solution)/shard_map/pallas_call | solution.py:542
  115.6 1.1 shard_map.96
  116.7 1.1 collective-permute-start.37
  118.2 1.0 collective-permute-start.45
  119.1 1.1 collective-permute-start.44
  120.2 1.0 collective-permute-done.37
  121.3 2.0 %collective-permute-start.40 = (f32[160,128]{1,0:T(8,128)S(1)}, f32[160,128]{1,0:T(8,128)S(1)}, u32[]{:S(2)}, u32[]{:S(2)}) collective-permute-start(f32[160,128]{1,0:T(8,128)S(1)} %add.41.refs_0_), channel_id=1, source_target_pairs={{0,16},{4,20},{8,24},{12,28},{16,0},{20,4},{24,8},{28,12},{1,17},{... | collective-permute-start | bytes 245768 | tf_op jit(solution)/shard_map/ppermute | solution.py:584
  123.3 1.4 collective-permute-start.39
  124.7 5.5 %collective-permute-done.40.refs_3_ = f32[160,128]{1,0:T(8,128)S(1)} collective-permute-done((f32[160,128]{1,0:T(8,128)S(1)}, f32[160,128]{1,0:T(8,128)S(1)}, u32[]{:S(2)}, u32[]{:S(2)}) %collective-permute-start.40) | collective-permute-done | bytes 81952 | tf_op jit(solution)/shard_map/ppermute | solution.py:584
  130.2 4.4 %collective-permute-done.38.refs_1_ = f32[160,128]{1,0:T(8,128)S(1)} collective-permute-done((f32[160,128]{1,0:T(8,128)S(1)}, f32[160,128]{1,0:T(8,128)S(1)}, u32[]{:S(2)}, u32[]{:S(2)}) %collective-permute-start.38) | collective-permute-done | bytes 81952 | tf_op jit(solution)/shard_map/ppermute | solution.py:584
  134.6 2.1 %shard_map.97.mine = f32[80,128]{1,0:T(8,128)S(1)} custom-call(f32[160,128]{1,0:T(8,128)S(1)} %add.41.refs_0_, f32[160,128]{1,0:T(8,128)S(1)} %collective-permute-done.38.refs_1_, f32[160,128]{1,0:T(8,128)S(1)} %collective-permute-done.39.refs_2_, f32[160,128]{1,0:T(8,128)S(1)} %collective-permute-done.40.refs_3_, ...), custom_call_target="tpu_custom_call" | custom-call | bytes 434692 | tf_op jit(solution)/shard_map/pallas_call | solution.py:542
  136.7 1.0 collective-permute-start.42
  137.8 0.9 collective-permute-start.41
  139.4 0.8 shard_map.101.before
  140.3 1.0 shard_map.102.before
  141.3 1.7 %shard_map.103 = (f32[2,16,64]{2,1,0:T(8,128)}, f32[2,16,64]{2,1,0:T(8,128)}, f32[2,3,512,128]{3,2,1,0:T(8,128)}) custom-call(s32[1]{0:T(128)} %bitcast.member.refs_4_.refs_5_, f32[80,128]{1,0:T(8,128)S(1)} %shard_map.97.mine, f32[80,128]{1,0:T(8,128)S(1)} %collective-permute-done.41.near, ...), custom_call_target="tpu_custom_call", output_to_operand_aliasing={{2}: (6, {})} | custom-call | bytes 3588100 | tf_op jit(solution)/shard_map/pallas_call | solution.py:542
  (73 shorter events, 14.6 us)
Async XLA Ops:
  0.6 20.0 %copy-start.1 = (f32[2,2,16,64]{3,2,1,0:T(8,128)S(1)}, f32[2,2,16,64]{3,2,1,0:T(8,128)}, u32[]{:S(2)}) copy-start(f32[2,2,16,64]{3,2,1,0:T(8,128)} %refs_6_.3) | copy-start | bytes 49156
  0.7 0.8 copy-start
  1.5 0.7 copy-start.3
  2.2 18.5 %copy-start.2 = (f32[2,2,16,64]{3,2,1,0:T(8,128)S(1)}, f32[2,2,16,64]{3,2,1,0:T(8,128)}, u32[]{:S(2)}) copy-start(f32[2,2,16,64]{3,2,1,0:T(8,128)} %refs_5_.1) | copy-start | bytes 49156
  2.5 9.1 %collective-permute-start = (f32[128,128]{1,0:T(8,128)S(1)}, f32[128,128]{1,0:T(8,128)S(1)}, u32[]{:S(2)}, u32[]{:S(2)}) collective-permute-start(f32[128,128]{1,0:T(8,128)S(1)} %shard_map.85), channel_id=1, source_target_pairs={{0,4},{4,0},{8,12},{12,8},{16,20},{20,16},{24,28},{28,24},{1,5},{5... | collective-permute-start | bytes 196616 | tf_op jit(solution)/shard_map/ppermute | solution.py:22
  6.7 39.1 %collective-permute-start.10 = (f32[2,512,128]{2,1,0:T(8,128)S(1)}, f32[2,512,128]{2,1,0:T(8,128)S(1)}, u32[]{:S(2)}, u32[]{:S(2)}) collective-permute-start(f32[2,512,128]{2,1,0:T(8,128)S(1)} %bitcast.56), channel_id=1, source_target_pairs={{0,2},{1,3},{2,0},{3,1},{4,6},{5,7},{6,4},{7,5},{8,10},{9,11},{10,... | collective-permute-start | bytes 1572872 | tf_op jit(solution)/shard_map/ppermute | solution.py:22
  10.1 11.9 %copy-start.4 = (f32[2,2,3,16,4096]{4,3,2,1,0:T(8,128)S(1)}, f32[2,2,3,16,4096]{4,3,2,1,0:T(8,128)}, u32[]{:S(2)}) copy-start(f32[2,2,3,16,4096]{4,3,2,1,0:T(8,128)} %param.7) | copy-start | bytes 9437188
  11.7 5.2 %collective-permute-start.3 = (f32[128,128]{1,0:T(8,128)S(1)}, f32[128,128]{1,0:T(8,128)S(1)}, u32[]{:S(2)}, u32[]{:S(2)}) collective-permute-start(f32[128,128]{1,0:T(8,128)S(1)} %add.33.refs_0_), channel_id=1, source_target_pairs={{0,16},{4,20},{8,24},{12,28},{16,0},{20,4},{24,8},{28,12},{1,17},{... | collective-permute-start | bytes 196616 | tf_op jit(solution)/shard_map/ppermute | solution.py:584
  14.3 6.2 %collective-permute-start.2 = (f32[128,128]{1,0:T(8,128)S(1)}, f32[128,128]{1,0:T(8,128)S(1)}, u32[]{:S(2)}, u32[]{:S(2)}) collective-permute-start(f32[128,128]{1,0:T(8,128)S(1)} %add.33.refs_0_), channel_id=1, source_target_pairs={{0,24},{4,28},{8,16},{12,20},{16,8},{20,12},{24,0},{28,4},{1,25},{... | collective-permute-start | bytes 196616 | tf_op jit(solution)/shard_map/ppermute | solution.py:584
  15.7 5.0 %collective-permute-start.1 = (f32[128,128]{1,0:T(8,128)S(1)}, f32[128,128]{1,0:T(8,128)S(1)}, u32[]{:S(2)}, u32[]{:S(2)}) collective-permute-start(f32[128,128]{1,0:T(8,128)S(1)} %add.33.refs_0_), channel_id=1, source_target_pairs={{0,8},{4,12},{8,0},{12,4},{16,24},{20,28},{24,16},{28,20},{1,9},{5... | collective-permute-start | bytes 196616 | tf_op jit(solution)/shard_map/ppermute | solution.py:584
  22.2 37.4 %collective-permute-start.18 = (f32[2,512,128]{2,1,0:T(8,128)S(1)}, f32[2,512,128]{2,1,0:T(8,128)S(1)}, u32[]{:S(2)}, u32[]{:S(2)}) collective-permute-start(f32[2,512,128]{2,1,0:T(8,128)S(1)} %bitcast.57), channel_id=1, source_target_pairs={{0,2},{1,3},{2,0},{3,1},{4,6},{5,7},{6,4},{7,5},{8,10},{9,11},{10,... | collective-permute-start | bytes 1572872 | tf_op jit(solution)/shard_map/ppermute | solution.py:22
  22.8 4.0 %collective-permute-start.4 = (f32[80,128]{1,0:T(8,128)S(1)}, f32[80,128]{1,0:T(8,128)S(1)}, u32[]{:S(2)}, u32[]{:S(2)}) collective-permute-start(f32[80,128]{1,0:T(8,128)S(1)} %get-tuple-element.49.refs_0_), channel_id=1, source_target_pairs={{0,4},{4,0},{8,12},{12,8},{16,20},{20,16},{24,28},{28,24},{1,5},{5... | collective-permute-start | bytes 122888 | tf_op jit(solution)/shard_map/ppermute | solution.py:22
  23.3 12.0 %collective-permute-start.6 = (f32[80,128]{1,0:T(8,128)S(1)}, f32[80,128]{1,0:T(8,128)S(1)}, u32[]{:S(2)}, u32[]{:S(2)}) collective-permute-start(f32[80,128]{1,0:T(8,128)S(1)} %get-tuple-element.50), channel_id=1, source_target_pairs={{0,6},{1,7},{2,4},{3,5},{4,2},{5,3},{6,0},{7,1},{8,14},{9,15},{10,... | collective-permute-start | bytes 122888 | tf_op jit(solution)/shard_map/ppermute | solution.py:676
  25.7 10.0 %collective-permute-start.5 = (f32[80,128]{1,0:T(8,128)S(1)}, f32[80,128]{1,0:T(8,128)S(1)}, u32[]{:S(2)}, u32[]{:S(2)}) collective-permute-start(f32[80,128]{1,0:T(8,128)S(1)} %get-tuple-element.50), channel_id=1, source_target_pairs={{0,2},{1,3},{2,0},{3,1},{4,6},{5,7},{6,4},{7,5},{8,10},{9,11},{10,... | collective-permute-start | bytes 122888 | tf_op jit(solution)/shard_map/ppermute | solution.py:22
  35.8 7.9 %collective-permute-start.9 = (f32[128,128]{1,0:T(8,128)S(1)}, f32[128,128]{1,0:T(8,128)S(1)}, u32[]{:S(2)}, u32[]{:S(2)}) collective-permute-start(f32[128,128]{1,0:T(8,128)S(1)} %get-tuple-element.51.refs_0_), channel_id=1, source_target_pairs={{0,16},{4,20},{8,24},{12,28},{16,0},{20,4},{24,8},{28,12},{1,17},{... | collective-permute-start | bytes 196616 | tf_op jit(solution)/shard_map/ppermute | solution.py:584
  39.7 6.1 %collective-permute-start.8 = (f32[128,128]{1,0:T(8,128)S(1)}, f32[128,128]{1,0:T(8,128)S(1)}, u32[]{:S(2)}, u32[]{:S(2)}) collective-permute-start(f32[128,128]{1,0:T(8,128)S(1)} %get-tuple-element.51.refs_0_), channel_id=1, source_target_pairs={{0,24},{4,28},{8,16},{12,20},{16,8},{20,12},{24,0},{28,4},{1,25},{... | collective-permute-start | bytes 196616 | tf_op jit(solution)/shard_map/ppermute | solution.py:584
  40.2 5.6 %collective-permute-start.7 = (f32[128,128]{1,0:T(8,128)S(1)}, f32[128,128]{1,0:T(8,128)S(1)}, u32[]{:S(2)}, u32[]{:S(2)}) collective-permute-start(f32[128,128]{1,0:T(8,128)S(1)} %get-tuple-element.51.refs_0_), channel_id=1, source_target_pairs={{0,8},{4,12},{8,0},{12,4},{16,24},{20,28},{24,16},{28,20},{1,9},{5... | collective-permute-start | bytes 196616 | tf_op jit(solution)/shard_map/ppermute | solution.py:584
  47.2 4.3 %collective-permute-start.11 = (f32[128,128]{1,0:T(8,128)S(1)}, f32[128,128]{1,0:T(8,128)S(1)}, u32[]{:S(2)}, u32[]{:S(2)}) collective-permute-start(f32[128,128]{1,0:T(8,128)S(1)} %get-tuple-element.53), channel_id=1, source_target_pairs={{0,4},{4,0},{8,12},{12,8},{16,20},{20,16},{24,28},{28,24},{1,5},{5... | collective-permute-start | bytes 196616 | tf_op jit(solution)/shard_map/ppermute | solution.py:22
  48.3 5.9 %collective-permute-start.17 = (f32[64,128]{1,0:T(8,128)S(1)}, f32[64,128]{1,0:T(8,128)S(1)}, u32[]{:S(2)}, u32[]{:S(2)}) collective-permute-start(f32[64,128]{1,0:T(8,128)S(1)} %get-tuple-element.54.refs_4_), channel_id=1, source_target_pairs={{0,16},{4,20},{8,24},{12,28},{16,0},{20,4},{24,8},{28,12},{1,17},{... | collective-permute-start | bytes 98312 | tf_op jit(solution)/shard_map/ppermute | solution.py:584
  49.5 6.0 %collective-permute-start.16 = (f32[64,128]{1,0:T(8,128)S(1)}, f32[64,128]{1,0:T(8,128)S(1)}, u32[]{:S(2)}, u32[]{:S(2)}) collective-permute-start(f32[64,128]{1,0:T(8,128)S(1)} %get-tuple-element.54.refs_4_), channel_id=1, source_target_pairs={{0,24},{4,28},{8,16},{12,20},{16,8},{20,12},{24,0},{28,4},{1,25},{... | collective-permute-start | bytes 98312 | tf_op jit(solution)/shard_map/ppermute | solution.py:584
  51.5 8.0 %collective-permute-start.14 = (f32[128,128]{1,0:T(8,128)S(1)}, f32[128,128]{1,0:T(8,128)S(1)}, u32[]{:S(2)}, u32[]{:S(2)}) collective-permute-start(f32[128,128]{1,0:T(8,128)S(1)} %add.36.refs_0_), channel_id=1, source_target_pairs={{0,16},{4,20},{8,24},{12,28},{16,0},{20,4},{24,8},{28,12},{1,17},{... | collective-permute-start | bytes 196616 | tf_op jit(solution)/shard_map/ppermute | solution.py:584
  52.9 6.7 %collective-permute-start.13 = (f32[128,128]{1,0:T(8,128)S(1)}, f32[128,128]{1,0:T(8,128)S(1)}, u32[]{:S(2)}, u32[]{:S(2)}) collective-permute-start(f32[128,128]{1,0:T(8,128)S(1)} %add.36.refs_0_), channel_id=1, source_target_pairs={{0,24},{4,28},{8,16},{12,20},{16,8},{20,12},{24,0},{28,4},{1,25},{... | collective-permute-start | bytes 196616 | tf_op jit(solution)/shard_map/ppermute | solution.py:584
  54.2 5.3 %collective-permute-start.12 = (f32[128,128]{1,0:T(8,128)S(1)}, f32[128,128]{1,0:T(8,128)S(1)}, u32[]{:S(2)}, u32[]{:S(2)}) collective-permute-start(f32[128,128]{1,0:T(8,128)S(1)} %add.36.refs_0_), channel_id=1, source_target_pairs={{0,8},{4,12},{8,0},{12,4},{16,24},{20,28},{24,16},{28,20},{1,9},{5... | collective-permute-start | bytes 196616 | tf_op jit(solution)/shard_map/ppermute | solution.py:584
  55.6 4.0 %collective-permute-start.15 = (f32[64,128]{1,0:T(8,128)S(1)}, f32[64,128]{1,0:T(8,128)S(1)}, u32[]{:S(2)}, u32[]{:S(2)}) collective-permute-start(f32[64,128]{1,0:T(8,128)S(1)} %get-tuple-element.54.refs_4_), channel_id=1, source_target_pairs={{0,8},{4,12},{8,0},{12,4},{16,24},{20,28},{24,16},{28,20},{1,9},{5... | collective-permute-start | bytes 98312 | tf_op jit(solution)/shard_map/ppermute | solution.py:584
  61.3 1.2 collective-permute-start.19
  62.5 3.9 %collective-permute-start.20 = (f32[64,128]{1,0:T(8,128)S(1)}, f32[64,128]{1,0:T(8,128)S(1)}, u32[]{:S(2)}, u32[]{:S(2)}) collective-permute-start(f32[64,128]{1,0:T(8,128)S(1)} %add.37), channel_id=1, source_target_pairs={{0,4},{4,0},{8,12},{12,8},{16,20},{20,16},{24,28},{28,24},{1,5},{5... | collective-permute-start | bytes 98312 | tf_op jit(solution)/shard_map/ppermute | solution.py:22
  66.4 5.5 %collective-permute-start.23 = (f32[64,128]{1,0:T(8,128)S(1)}, f32[64,128]{1,0:T(8,128)S(1)}, u32[]{:S(2)}, u32[]{:S(2)}) collective-permute-start(f32[64,128]{1,0:T(8,128)S(1)} %add.38.refs_0_), channel_id=1, source_target_pairs={{0,16},{4,20},{8,24},{12,28},{16,0},{20,4},{24,8},{28,12},{1,17},{... | collective-permute-start | bytes 98312 | tf_op jit(solution)/shard_map/ppermute | solution.py:584
  68.3 5.7 %collective-permute-start.22 = (f32[64,128]{1,0:T(8,128)S(1)}, f32[64,128]{1,0:T(8,128)S(1)}, u32[]{:S(2)}, u32[]{:S(2)}) collective-permute-start(f32[64,128]{1,0:T(8,128)S(1)} %add.38.refs_0_), channel_id=1, source_target_pairs={{0,24},{4,28},{8,16},{12,20},{16,8},{20,12},{24,0},{28,4},{1,25},{... | collective-permute-start | bytes 98312 | tf_op jit(solution)/shard_map/ppermute | solution.py:584
  69.4 4.6 %collective-permute-start.21 = (f32[64,128]{1,0:T(8,128)S(1)}, f32[64,128]{1,0:T(8,128)S(1)}, u32[]{:S(2)}, u32[]{:S(2)}) collective-permute-start(f32[64,128]{1,0:T(8,128)S(1)} %add.38.refs_0_), channel_id=1, source_target_pairs={{0,8},{4,12},{8,0},{12,4},{16,24},{20,28},{24,16},{28,20},{1,9},{5... | collective-permute-start | bytes 98312 | tf_op jit(solution)/shard_map/ppermute | solution.py:584
  77.1 1.5 %collective-permute-start.24 = (f32[512,128]{1,0:T(8,128)S(1)}, f32[512,128]{1,0:T(8,128)S(1)}, u32[]{:S(2)}, u32[]{:S(2)}) collective-permute-start(f32[512,128]{1,0:T(8,128)S(1)} %get-tuple-element.58.mine), channel_id=1, source_target_pairs={{0,1},{1,0},{2,3},{3,2},{4,5},{5,4},{6,7},{7,6},{8,9},{9,8},{10,11... | collective-permute-start | bytes 786440 | tf_op jit(solution)/shard_map/ppermute | solution.py:22
  79.7 4.5 %collective-permute-start.25 = (f32[160,128]{1,0:T(8,128)S(1)}, f32[160,128]{1,0:T(8,128)S(1)}, u32[]{:S(2)}, u32[]{:S(2)}) collective-permute-start(f32[160,128]{1,0:T(8,128)S(1)} %get-tuple-element.60), channel_id=1, source_target_pairs={{0,4},{4,0},{8,12},{12,8},{16,20},{20,16},{24,28},{28,24},{1,5},{5... | collective-permute-start | bytes 245768 | tf_op jit(solution)/shard_map/ppermute | solution.py:22
  80.8 29.2 %collective-permute-start.35 = (f32[2,512,128]{2,1,0:T(8,128)S(1)}, f32[2,512,128]{2,1,0:T(8,128)S(1)}, u32[]{:S(2)}, u32[]{:S(2)}) collective-permute-start(f32[2,512,128]{2,1,0:T(8,128)S(1)} %bitcast.50), channel_id=1, source_target_pairs={{0,2},{1,3},{2,0},{3,1},{4,6},{5,7},{6,4},{7,5},{8,10},{9,11},{10,... | collective-permute-start | bytes 1572872 | tf_op jit(solution)/shard_map/ppermute | solution.py:22
  84.2 8.2 %collective-permute-start.28 = (f32[160,128]{1,0:T(8,128)S(1)}, f32[160,128]{1,0:T(8,128)S(1)}, u32[]{:S(2)}, u32[]{:S(2)}) collective-permute-start(f32[160,128]{1,0:T(8,128)S(1)} %add.39.refs_0_), channel_id=1, source_target_pairs={{0,16},{4,20},{8,24},{12,28},{16,0},{20,4},{24,8},{28,12},{1,17},{... | collective-permute-start | bytes 245768 | tf_op jit(solution)/shard_map/ppermute | solution.py:584
  85.2 7.3 %collective-permute-start.27 = (f32[160,128]{1,0:T(8,128)S(1)}, f32[160,128]{1,0:T(8,128)S(1)}, u32[]{:S(2)}, u32[]{:S(2)}) collective-permute-start(f32[160,128]{1,0:T(8,128)S(1)} %add.39.refs_0_), channel_id=1, source_target_pairs={{0,24},{4,28},{8,16},{12,20},{16,8},{20,12},{24,0},{28,4},{1,25},{... | collective-permute-start | bytes 245768 | tf_op jit(solution)/shard_map/ppermute | solution.py:584
  86.5 6.2 %collective-permute-start.26 = (f32[160,128]{1,0:T(8,128)S(1)}, f32[160,128]{1,0:T(8,128)S(1)}, u32[]{:S(2)}, u32[]{:S(2)}) collective-permute-start(f32[160,128]{1,0:T(8,128)S(1)} %add.39.refs_0_), channel_id=1, source_target_pairs={{0,8},{4,12},{8,0},{12,4},{16,24},{20,28},{24,16},{28,20},{1,9},{5... | collective-permute-start | bytes 245768 | tf_op jit(solution)/shard_map/ppermute | solution.py:584
  94.9 1.6 %collective-permute-start.29 = (f32[512,128]{1,0:T(8,128)S(1)}, f32[512,128]{1,0:T(8,128)S(1)}, u32[]{:S(2)}, u32[]{:S(2)}) collective-permute-start(f32[512,128]{1,0:T(8,128)S(1)} %get-tuple-element.63.mine), channel_id=1, source_target_pairs={{0,1},{1,0},{2,3},{3,2},{4,5},{5,4},{6,7},{7,6},{8,9},{9,8},{10,11... | collective-permute-start | bytes 786440 | tf_op jit(solution)/shard_map/ppermute | solution.py:22
  97.6 4.5 %collective-permute-start.30 = (f32[160,128]{1,0:T(8,128)S(1)}, f32[160,128]{1,0:T(8,128)S(1)}, u32[]{:S(2)}, u32[]{:S(2)}) collective-permute-start(f32[160,128]{1,0:T(8,128)S(1)} %get-tuple-element.65), channel_id=1, source_target_pairs={{0,4},{4,0},{8,12},{12,8},{16,20},{20,16},{24,28},{28,24},{1,5},{5... | collective-permute-start | bytes 245768 | tf_op jit(solution)/shard_map/ppermute | solution.py:22
  102.2 8.5 %collective-permute-start.33 = (f32[160,128]{1,0:T(8,128)S(1)}, f32[160,128]{1,0:T(8,128)S(1)}, u32[]{:S(2)}, u32[]{:S(2)}) collective-permute-start(f32[160,128]{1,0:T(8,128)S(1)} %add.40.refs_0_), channel_id=1, source_target_pairs={{0,16},{4,20},{8,24},{12,28},{16,0},{20,4},{24,8},{28,12},{1,17},{... | collective-permute-start | bytes 245768 | tf_op jit(solution)/shard_map/ppermute | solution.py:584
  104.6 6.6 %collective-permute-start.32 = (f32[160,128]{1,0:T(8,128)S(1)}, f32[160,128]{1,0:T(8,128)S(1)}, u32[]{:S(2)}, u32[]{:S(2)}) collective-permute-start(f32[160,128]{1,0:T(8,128)S(1)} %add.40.refs_0_), channel_id=1, source_target_pairs={{0,24},{4,28},{8,16},{12,20},{16,8},{20,12},{24,0},{28,4},{1,25},{... | collective-permute-start | bytes 245768 | tf_op jit(solution)/shard_map/ppermute | solution.py:584
  106.0 5.7 %collective-permute-start.31 = (f32[160,128]{1,0:T(8,128)S(1)}, f32[160,128]{1,0:T(8,128)S(1)}, u32[]{:S(2)}, u32[]{:S(2)}) collective-permute-start(f32[160,128]{1,0:T(8,128)S(1)} %add.40.refs_0_), channel_id=1, source_target_pairs={{0,8},{4,12},{8,0},{12,4},{16,24},{20,28},{24,16},{28,20},{1,9},{5... | collective-permute-start | bytes 245768 | tf_op jit(solution)/shard_map/ppermute | solution.py:584
  106.0 4.0 %collective-permute-start.34 = (f32[80,128]{1,0:T(8,128)S(1)}, f32[80,128]{1,0:T(8,128)S(1)}, u32[]{:S(2)}, u32[]{:S(2)}) collective-permute-start(f32[80,128]{1,0:T(8,128)S(1)} %get-tuple-element.66), channel_id=1, source_target_pairs={{0,2},{1,3},{2,0},{3,1},{4,6},{5,7},{6,4},{7,5},{8,10},{9,11},{10,... | collective-permute-start | bytes 122888 | tf_op jit(solution)/shard_map/ppermute | solution.py:22
  114.0 1.6 %collective-permute-start.36 = (f32[512,128]{1,0:T(8,128)S(1)}, f32[512,128]{1,0:T(8,128)S(1)}, u32[]{:S(2)}, u32[]{:S(2)}) collective-permute-start(f32[512,128]{1,0:T(8,128)S(1)} %get-tuple-element.71.mine), channel_id=1, source_target_pairs={{0,1},{1,0},{2,3},{3,2},{4,5},{5,4},{6,7},{7,6},{8,9},{9,8},{10,11... | collective-permute-start | bytes 786440 | tf_op jit(solution)/shard_map/ppermute | solution.py:22
  114.4 23.4 %collective-permute-start.46 = (f32[512,128]{1,0:T(8,128)S(1)}, f32[512,128]{1,0:T(8,128)S(1)}, u32[]{:S(2)}, u32[]{:S(2)}) collective-permute-start(f32[512,128]{1,0:T(8,128)S(1)} %shard_map.99.mine), channel_id=1, source_target_pairs={{0,2},{1,3},{2,0},{3,1},{4,6},{5,7},{6,4},{7,5},{8,10},{9,11},{10,... | collective-permute-start | bytes 786440 | tf_op jit(solution)/shard_map/ppermute | solution.py:22
  116.7 4.5 %collective-permute-start.37 = (f32[160,128]{1,0:T(8,128)S(1)}, f32[160,128]{1,0:T(8,128)S(1)}, u32[]{:S(2)}, u32[]{:S(2)}) collective-permute-start(f32[160,128]{1,0:T(8,128)S(1)} %get-tuple-element.73), channel_id=1, source_target_pairs={{0,4},{4,0},{8,12},{12,8},{16,20},{20,16},{24,28},{28,24},{1,5},{5... | collective-permute-start | bytes 245768 | tf_op jit(solution)/shard_map/ppermute | solution.py:22
  118.2 21.3 %collective-permute-start.45 = (f32[512,128]{1,0:T(8,128)S(1)}, f32[512,128]{1,0:T(8,128)S(1)}, u32[]{:S(2)}, u32[]{:S(2)}) collective-permute-start(f32[512,128]{1,0:T(8,128)S(1)} %shard_map.98.mine), channel_id=1, source_target_pairs={{0,2},{1,3},{2,0},{3,1},{4,6},{5,7},{6,4},{7,5},{8,10},{9,11},{10,... | collective-permute-start | bytes 786440 | tf_op jit(solution)/shard_map/ppermute | solution.py:22
  119.1 22.2 %collective-permute-start.44 = (f32[512,128]{1,0:T(8,128)S(1)}, f32[512,128]{1,0:T(8,128)S(1)}, u32[]{:S(2)}, u32[]{:S(2)}) collective-permute-start(f32[512,128]{1,0:T(8,128)S(1)} %get-tuple-element.75.mixture), channel_id=1, source_target_pairs={{0,2},{1,3},{2,0},{3,1},{4,6},{5,7},{6,4},{7,5},{8,10},{9,11},{10,... | collective-permute-start | bytes 786440 | tf_op jit(solution)/shard_map/ppermute | solution.py:22
  121.3 8.9 %collective-permute-start.40 = (f32[160,128]{1,0:T(8,128)S(1)}, f32[160,128]{1,0:T(8,128)S(1)}, u32[]{:S(2)}, u32[]{:S(2)}) collective-permute-start(f32[160,128]{1,0:T(8,128)S(1)} %add.41.refs_0_), channel_id=1, source_target_pairs={{0,16},{4,20},{8,24},{12,28},{16,0},{20,4},{24,8},{28,12},{1,17},{... | collective-permute-start | bytes 245768 | tf_op jit(solution)/shard_map/ppermute | solution.py:584
  123.3 6.9 %collective-permute-start.39 = (f32[160,128]{1,0:T(8,128)S(1)}, f32[160,128]{1,0:T(8,128)S(1)}, u32[]{:S(2)}, u32[]{:S(2)}) collective-permute-start(f32[160,128]{1,0:T(8,128)S(1)} %add.41.refs_0_), channel_id=1, source_target_pairs={{0,24},{4,28},{8,16},{12,20},{16,8},{20,12},{24,0},{28,4},{1,25},{... | collective-permute-start | bytes 245768 | tf_op jit(solution)/shard_map/ppermute | solution.py:584
  130.2 4.4 %collective-permute-start.38 = (f32[160,128]{1,0:T(8,128)S(1)}, f32[160,128]{1,0:T(8,128)S(1)}, u32[]{:S(2)}, u32[]{:S(2)}) collective-permute-start(f32[160,128]{1,0:T(8,128)S(1)} %add.41.refs_0_), channel_id=1, source_target_pairs={{0,8},{4,12},{8,0},{12,4},{16,24},{20,28},{24,16},{28,20},{1,9},{5... | collective-permute-start | bytes 245768 | tf_op jit(solution)/shard_map/ppermute | solution.py:584
  136.7 4.6 %collective-permute-start.43 = (f32[80,128]{1,0:T(8,128)S(1)}, f32[80,128]{1,0:T(8,128)S(1)}, u32[]{:S(2)}, u32[]{:S(2)}) collective-permute-start(f32[80,128]{1,0:T(8,128)S(1)} %shard_map.97.mine), channel_id=1, source_target_pairs={{0,3},{1,2},{2,1},{3,0},{4,7},{5,6},{6,5},{7,4},{8,11},{9,10},{10,... | collective-permute-start | bytes 122888 | tf_op jit(solution)/shard_map/ppermute | solution.py:22
  136.7 4.6 %collective-permute-start.42 = (f32[80,128]{1,0:T(8,128)S(1)}, f32[80,128]{1,0:T(8,128)S(1)}, u32[]{:S(2)}, u32[]{:S(2)}) collective-permute-start(f32[80,128]{1,0:T(8,128)S(1)} %shard_map.97.mine), channel_id=1, source_target_pairs={{0,2},{1,3},{2,0},{3,1},{4,6},{5,7},{6,4},{7,5},{8,10},{9,11},{10,... | collective-permute-start | bytes 122888 | tf_op jit(solution)/shard_map/ppermute | solution.py:22
  137.8 3.6 %collective-permute-start.41 = (f32[80,128]{1,0:T(8,128)S(1)}, f32[80,128]{1,0:T(8,128)S(1)}, u32[]{:S(2)}, u32[]{:S(2)}) collective-permute-start(f32[80,128]{1,0:T(8,128)S(1)} %shard_map.97.mine), channel_id=1, source_target_pairs={{0,1},{1,0},{2,3},{3,2},{4,5},{5,4},{6,7},{7,6},{8,9},{9,8},{10,11... | collective-permute-start | bytes 122888 | tf_op jit(solution)/shard_map/ppermute | solution.py:22
